TPU v7x, 32 devices: a whole 2x2x4 slice. The times are simulated.
32 devices in a mesh: dp: 8 (over y, x, core), mp: 4 (over z).
Axes of the slice: x: 2, y: 2, z: 4, core: 2. Of those that a mesh axis runs over, the one named last changes fastest.
Arguments:
- inputs: bfloat16 [8, 2048, 1024], P('dp', 'mp'), may hold values from -6 to 6
- cotangent: bfloat16 [8, 2048, 1024], P('dp', 'mp'), may hold values from -6 to 6
- segment_ids: int32 [8, 2048], P('dp'), may hold values from 0 to 2048, as said below
- row_length: int32 [8], P('dp'), may hold values from 1792 to 2048, as said below
- w_qkv: float32 [3, 1024, 1024], P(None, 'dp', 'mp'), may hold values from -0.09375 to 0.09375
- m_qkv: float32 [3, 1024, 1024], P(None, 'dp', 'mp'), may hold values from -320 to 320
- v_qkv: float32 [3, 1024, 1024], P(None, 'dp', 'mp'), may hold values from 131.072 to 2097.152
- w_out: float32 [1024, 1024], P('mp', 'dp'), may hold values from -1.5 to 1.5
- m_out: float32 [1024, 1024], P('mp', 'dp'), may hold values from -16 to 16
- v_out: float32 [1024, 1024], P('mp', 'dp'), may hold values from 0.2654208 to 4.25984
- w_gate_up: float32 [2, 1024, 2816], P(None, 'dp', 'mp'), may hold values from -0.1875 to 0.1875
- m_gate_up: float32 [2, 1024, 2816], P(None, 'dp', 'mp'), may hold values from -32 to 32
- v_gate_up: float32 [2, 1024, 2816], P(None, 'dp', 'mp'), may hold values from 1.122304 to 18.0224
- w_down: float32 [2816, 1024], P('mp', 'dp'), may hold values from -0.109375 to 0.109375
- m_down: float32 [2816, 1024], P('mp', 'dp'), may hold values from -56 to 56
- v_down: float32 [2816, 1024], P('mp', 'dp'), may hold values from 3.44064 to 55.7056
- norm_gains: float32 [2, 1024], P(None, 'dp'), may hold values from 0.5 to 1.5
- m_gains: float32 [2, 1024], P(None, 'dp'), may hold values from -128 to 128
- v_gains: float32 [2, 1024], P(None, 'dp'), may hold values from 16.384 to 262.144
Outputs:
- block_output: float32 [8, 2048, 1024], P('dp', 'mp')
- input_grad: float32 [8, 2048, 1024], P('dp', 'mp')
- qkv_new: float32 [3, 1024, 1024], P(None, 'dp', 'mp')
- qkv_copy: bfloat16 [3, 1024, 1024], P(None, 'dp', 'mp')
- qkv_moment: float32 [3, 1024, 1024], P(None, 'dp', 'mp')
- qkv_second: float32 [3, 1024, 1024], P(None, 'dp', 'mp')
- out_new: float32 [1024, 1024], P('mp', 'dp')
- out_copy: bfloat16 [1024, 1024], P('mp', 'dp')
- out_moment: float32 [1024, 1024], P('mp', 'dp')
- out_second: float32 [1024, 1024], P('mp', 'dp')
- gate_up_new: float32 [2, 1024, 2816], P(None, 'dp', 'mp')
- gate_up_copy: bfloat16 [2, 1024, 2816], P(None, 'dp', 'mp')
- gate_up_moment: float32 [2, 1024, 2816], P(None, 'dp', 'mp')
- gate_up_second: float32 [2, 1024, 2816], P(None, 'dp', 'mp')
- down_new: float32 [2816, 1024], P('mp', 'dp')
- down_copy: bfloat16 [2816, 1024], P('mp', 'dp')
- down_moment: float32 [2816, 1024], P('mp', 'dp')
- down_second: float32 [2816, 1024], P('mp', 'dp')
- gains_new: float32 [2, 1024], P(None, 'dp')
- gains_copy: bfloat16 [2, 1024], P(None, 'dp')
- gains_moment: float32 [2, 1024], P(None, 'dp')
- gains_second: float32 [2, 1024], P(None, 'dp')
Inputs may be any that keep to these rules, and one draw needn't show every extreme that they name: A row's live tokens are its positions below row_length; some row is full and some holds exactly the least. `segment_ids`: ids never fall along a row; positions at or past the row's length hold 2048 and live ones less; each run of one id among live positions is one packed document.
All inputs are finite; a program needn't handle non-finite values.
Results may differ from a plain program's by a relative error of at most 0.019.
The roundings to bfloat16 on the way count: a program that leaves them out, or rounds other values in their place, can miss the bound.
Values may be sent and summed in bfloat16 or wider, within the bound.
No kernel may reach another device: no remote copies, remote signals or barrier semaphores. Data moves between devices by JAX's collectives and lax.ppermute only.
A program may use at most 192 MiB of HBM per device.

v0:
```python
import jax
import jax.numpy as jnp
from jax import lax
from jax.sharding import PartitionSpec as P

HEAD = 64
ADAM_STEP = 5


EPS_NORM = 1e-06
BETA_ONE = 0.9
BETA_TWO = 0.999
ADAM_EPS = 1e-08
DECAY_RATE = 0.1
RATES = (0.03, 0.5, 0.06, 0.04, 0.4)
NEG_FILL = -1e30


def rms_scale(values_in):
    return lax.rsqrt(jnp.mean(values_in * values_in, axis=-1, keepdims=True) + EPS_NORM)


def norm_back(d_normed, hat, scale, gain):
    scaled = gain * d_normed
    return scale * (scaled - hat * jnp.mean(scaled * hat, axis=-1, keepdims=True))


def gated(gate_val, lift):
    return jax.nn.gelu(gate_val, approximate=True) * lift


def adam_update(weight, moment, second, grad, step_rate, decay):
    moment_new = BETA_ONE * moment + (1.0 - BETA_ONE) * grad
    second_new = BETA_TWO * second + (1.0 - BETA_TWO) * grad * grad
    moment_hat = moment_new / (1.0 - BETA_ONE**ADAM_STEP)
    second_hat = second_new / (1.0 - BETA_TWO**ADAM_STEP)
    updated = weight - step_rate * (moment_hat / (jnp.sqrt(second_hat) + ADAM_EPS) + decay * weight)
    return (updated, updated.astype(jnp.bfloat16), moment_new, second_new)


def block_scores(query_blk, seg_blk, seg_row, keys_in):
    scores = jnp.einsum("qhd,khd->hqk", query_blk, keys_in, preferred_element_type=jnp.float32)
    same_doc = (seg_blk[:, None] == seg_row[None, :])[None]
    return (scores, same_doc)


def on_device(
    inputs,
    cotangent,
    segment_ids,
    row_length,
    w_qkv,
    m_qkv,
    v_qkv,
    w_out,
    m_out,
    v_out,
    w_gate_up,
    m_gate_up,
    v_gate_up,
    w_down,
    m_down,
    v_down,
    norm_gains,
    m_gains,
    v_gains,
):
    copy_qkv = w_qkv.astype(jnp.bfloat16)
    copy_out = w_out.astype(jnp.bfloat16)
    copy_gate_up = w_gate_up.astype(jnp.bfloat16)
    copy_down = w_down.astype(jnp.bfloat16)
    copy_gains = norm_gains.astype(jnp.bfloat16)
    full_qkv, full_out, full_gate_up, full_down, full_gains = (
        lax.all_gather(copy_qkv, "dp", axis=1, tiled=True),
        lax.all_gather(copy_out, "dp", axis=1, tiled=True),
        lax.all_gather(copy_gate_up, "dp", axis=1, tiled=True),
        lax.all_gather(copy_down, "dp", axis=1, tiled=True),
        lax.all_gather(copy_gains, "dp", axis=1, tiled=True),
    )
    gain_one = full_gains[0].astype(jnp.float32)
    gain_two = full_gains[1].astype(jnp.float32)
    seq_len = segment_ids.shape[1]
    width = full_qkv.shape[2]
    heads_here = width // HEAD
    block_rows = min(512, seq_len)
    blocks = seq_len // block_rows
    seg_row = segment_ids[0]
    positions = jnp.arange(seq_len, dtype=jnp.int32)
    live_row = (positions < row_length[0]).astype(jnp.float32)
    seg_blocks = seg_row.reshape(blocks, block_rows)
    resid_in = inputs[0].astype(jnp.float32)
    scale_one = rms_scale(resid_in)
    hat_one = resid_in * scale_one
    normed_one = (hat_one * gain_one).astype(jnp.bfloat16)
    qkv_rows = jnp.einsum(
        "td,cdf->tcf",
        lax.all_gather(normed_one, "mp", axis=0, tiled=True),
        full_qkv,
        preferred_element_type=jnp.float32,
    ).astype(jnp.bfloat16)
    queries = qkv_rows[:, 0].reshape(seq_len, heads_here, HEAD)
    keys_all = qkv_rows[:, 1].reshape(seq_len, heads_here, HEAD)
    values_all = qkv_rows[:, 2].reshape(seq_len, heads_here, HEAD)

    def forward_block(block_in):
        query_blk, seg_blk = block_in
        scores, same_doc = block_scores(query_blk, seg_blk, seg_row, keys_all)
        scores = jnp.where(same_doc, scores, NEG_FILL)
        row_peak = jnp.max(scores, axis=-1, keepdims=True)
        raised = jnp.exp(scores - row_peak)
        summed = jnp.sum(raised, axis=-1, keepdims=True)
        probs = (raised / summed).astype(jnp.bfloat16)
        attended_blk = jnp.einsum(
            "hqk,khd->qhd", probs, values_all, preferred_element_type=jnp.float32
        )
        return (attended_blk, (row_peak + jnp.log(summed))[..., 0])

    attended, log_sums = lax.map(
        forward_block, (queries.reshape(blocks, block_rows, heads_here, HEAD), seg_blocks)
    )
    attended = (attended.reshape(seq_len, width) * live_row[:, None]).astype(jnp.bfloat16)
    after_attn = resid_in + lax.psum_scatter(
        jnp.dot(attended, full_out, preferred_element_type=jnp.float32),
        "mp",
        scatter_dimension=0,
        tiled=True,
    )
    scale_two = rms_scale(after_attn)
    hat_two = after_attn * scale_two
    normed_two = (hat_two * gain_two).astype(jnp.bfloat16)
    both_rows = jnp.einsum(
        "td,cdf->ctf",
        lax.all_gather(normed_two, "mp", axis=0, tiled=True),
        full_gate_up,
        preferred_element_type=jnp.float32,
    )
    hidden = gated(both_rows[0], both_rows[1]).astype(jnp.bfloat16)
    block_output = after_attn + lax.psum_scatter(
        jnp.dot(hidden, full_down, preferred_element_type=jnp.float32).astype(jnp.bfloat16),
        "mp",
        scatter_dimension=0,
        tiled=True,
    ).astype(jnp.float32)
    grad_all, normed_two_all = (
        lax.all_gather(cotangent[0], "mp", axis=0, tiled=True),
        lax.all_gather(normed_two, "mp", axis=0, tiled=True),
    )
    both_again = jnp.einsum(
        "td,cdf->ctf", normed_two_all, full_gate_up, preferred_element_type=jnp.float32
    )
    hidden_again, gated_pull = jax.vjp(gated, both_again[0], both_again[1])
    hidden_again = hidden_again.astype(jnp.bfloat16)
    d_hidden = jnp.einsum("td,fd->tf", grad_all, full_down, preferred_element_type=jnp.float32)
    d_gate, d_lift = gated_pull(d_hidden)
    d_both = jnp.stack([d_gate, d_lift]).astype(jnp.bfloat16)
    grad_down = jnp.einsum("tf,td->fd", hidden_again, grad_all, preferred_element_type=jnp.float32)
    grad_gate_up = jnp.einsum(
        "td,ctf->cdf", normed_two_all, d_both, preferred_element_type=jnp.float32
    )
    part = d_both
    d_normed_two = lax.psum_scatter(
        jnp.einsum("ctf,cdf->td", part, full_gate_up, preferred_element_type=jnp.float32).astype(
            jnp.bfloat16
        ),
        "mp",
        scatter_dimension=0,
        tiled=True,
    ).astype(jnp.float32)
    d_after = cotangent[0].astype(jnp.float32) + norm_back(
        d_normed_two, hat_two, scale_two, gain_two
    )
    grad_gain_two = jnp.sum(d_normed_two * hat_two, axis=0)
    d_branch = d_after.astype(jnp.bfloat16)
    d_branch_all, normed_one_all = (
        lax.all_gather(d_branch, "mp", axis=0, tiled=True),
        lax.all_gather(normed_one, "mp", axis=0, tiled=True),
    )
    qkv_again = jnp.einsum(
        "td,cdf->tcf", normed_one_all, full_qkv, preferred_element_type=jnp.float32
    ).astype(jnp.bfloat16)
    queries_new = qkv_again[:, 0].reshape(seq_len, heads_here, HEAD)
    keys_new = qkv_again[:, 1].reshape(seq_len, heads_here, HEAD)
    values_new = qkv_again[:, 2].reshape(seq_len, heads_here, HEAD)
    grad_out = jnp.einsum("tf,td->fd", attended, d_branch_all, preferred_element_type=jnp.float32)
    d_attended = jnp.einsum(
        "td,fd->tf", d_branch_all, full_out, preferred_element_type=jnp.float32
    ).astype(jnp.bfloat16)
    d_attended = d_attended * live_row[:, None].astype(jnp.bfloat16)

    def back_block(carry, block_in):
        d_keys, d_values = carry
        query_blk, seg_blk, log_blk, d_out_blk = block_in
        scores, same_doc = block_scores(query_blk, seg_blk, seg_row, keys_new)
        probs = jnp.exp(jnp.where(same_doc, scores - log_blk[..., None], NEG_FILL))
        d_probs = jnp.einsum(
            "qhd,khd->hqk", d_out_blk, values_new, preferred_element_type=jnp.float32
        )
        row_dot = jnp.sum(probs * d_probs, axis=-1, keepdims=True)
        d_scores = (probs * (d_probs - row_dot)).astype(jnp.bfloat16)
        d_query = jnp.einsum("hqk,khd->qhd", d_scores, keys_new, preferred_element_type=jnp.float32)
        d_keys = d_keys + jnp.einsum(
            "hqk,qhd->khd", d_scores, query_blk, preferred_element_type=jnp.float32
        )
        d_values = d_values + jnp.einsum(
            "hqk,qhd->khd",
            probs.astype(jnp.bfloat16),
            d_out_blk,
            preferred_element_type=jnp.float32,
        )
        return ((d_keys, d_values), d_query)

    initial = jnp.zeros((seq_len, heads_here, HEAD), jnp.float32)
    scan_in = (
        queries_new.reshape(blocks, block_rows, heads_here, HEAD),
        seg_blocks,
        log_sums,
        d_attended.reshape(blocks, block_rows, heads_here, HEAD),
    )
    (d_keys, d_values), d_queries = lax.scan(back_block, (initial, initial), scan_in)
    d_qkv = jnp.stack(
        [
            d_queries.reshape(seq_len, width),
            d_keys.reshape(seq_len, width),
            d_values.reshape(seq_len, width),
        ],
        axis=1,
    ).astype(jnp.bfloat16)
    grad_qkv = jnp.einsum("td,tcf->cdf", normed_one_all, d_qkv, preferred_element_type=jnp.float32)
    part = d_qkv
    d_normed_one = lax.psum_scatter(
        jnp.einsum("tcf,cdf->td", part, full_qkv, preferred_element_type=jnp.float32).astype(
            jnp.bfloat16
        ),
        "mp",
        scatter_dimension=0,
        tiled=True,
    ).astype(jnp.float32)
    input_grad = d_after + norm_back(d_normed_one, hat_one, scale_one, gain_one)
    grad_gain_one = jnp.sum(d_normed_one * hat_one, axis=0)
    grad_gains = lax.psum(jnp.stack([grad_gain_one, grad_gain_two]), "mp")
    red_qkv, red_out, red_gate_up, red_down, red_gains = (
        lax.psum_scatter(grad_qkv, "dp", scatter_dimension=1, tiled=True),
        lax.psum_scatter(grad_out, "dp", scatter_dimension=1, tiled=True),
        lax.psum_scatter(grad_gate_up, "dp", scatter_dimension=1, tiled=True),
        lax.psum_scatter(grad_down, "dp", scatter_dimension=1, tiled=True),
        lax.psum_scatter(grad_gains, "dp", scatter_dimension=1, tiled=True),
    )
    new_qkv = adam_update(w_qkv, m_qkv, v_qkv, red_qkv, RATES[0], DECAY_RATE)
    new_out = adam_update(w_out, m_out, v_out, red_out, RATES[1], DECAY_RATE)
    new_gate_up = adam_update(w_gate_up, m_gate_up, v_gate_up, red_gate_up, RATES[2], DECAY_RATE)
    new_down = adam_update(w_down, m_down, v_down, red_down, RATES[3], DECAY_RATE)
    new_gains = adam_update(norm_gains, m_gains, v_gains, red_gains, RATES[4], 0.0)
    return (
        block_output[None],
        input_grad[None],
        new_qkv[0],
        new_qkv[1],
        new_qkv[2],
        new_qkv[3],
        new_out[0],
        new_out[1],
        new_out[2],
        new_out[3],
        new_gate_up[0],
        new_gate_up[1],
        new_gate_up[2],
        new_gate_up[3],
        new_down[0],
        new_down[1],
        new_down[2],
        new_down[3],
        new_gains[0],
        new_gains[1],
        new_gains[2],
        new_gains[3],
    )


def solution(mesh):
    return jax.shard_map(
        on_device,
        mesh=mesh,
        in_specs=(
            P("dp", "mp", None),
            P("dp", "mp", None),
            P("dp", None),
            P("dp"),
            P(None, "dp", "mp"),
            P(None, "dp", "mp"),
            P(None, "dp", "mp"),
            P("mp", "dp"),
            P("mp", "dp"),
            P("mp", "dp"),
            P(None, "dp", "mp"),
            P(None, "dp", "mp"),
            P(None, "dp", "mp"),
            P("mp", "dp"),
            P("mp", "dp"),
            P("mp", "dp"),
            P(None, "dp"),
            P(None, "dp"),
            P(None, "dp"),
        ),
        out_specs=(
            P("dp", "mp", None),
            P("dp", "mp", None),
            P(None, "dp", "mp"),
            P(None, "dp", "mp"),
            P(None, "dp", "mp"),
            P(None, "dp", "mp"),
            P("mp", "dp"),
            P("mp", "dp"),
            P("mp", "dp"),
            P("mp", "dp"),
            P(None, "dp", "mp"),
            P(None, "dp", "mp"),
            P(None, "dp", "mp"),
            P(None, "dp", "mp"),
            P("mp", "dp"),
            P("mp", "dp"),
            P("mp", "dp"),
            P("mp", "dp"),
            P(None, "dp"),
            P(None, "dp"),
            P(None, "dp"),
            P(None, "dp"),
        ),
        check_vma=False,
    )
```

profile of v0, /device:TPU:0, one launch (start us, length us, event | category | flops | bytes accessed | tf_op | source)
XLA Modules:
  0.0 1283.2 jit_solution(16407593226943926335)
XLA Ops:
  10.0 10.3 all_gather.29
  26.3 12.4 all_gather.32
  40.4 82.9 %all-gather.9.cloned.1.call-done = bf16[2048,1024]{1,0:T(8,128)(2,1)} async-done(((bf16[512,1024]{1,0:T(8,128)(2,1)}), bf16[2048,1024]{1,0:T(8,128)(2,1)}) %all-gather.9.cloned.1.call-update) | async-done | bytes 4194320 | tf_op jit(solution)/shard_map/all_gather | solution.py:97
  123.3 6.1 fusion.55
  136.0 99.0 %while.27 = (s32[]{:T(128)}, f32[4,512,4,64]{1,0,3,2:T(4,128)}, f32[4,4,512]{2,1,0:T(4,128)}, s32[4,512]{1,0:T(4,128)S(1)}, s32[1,2048]{1,0:T(1,128)S(1)}, /*ind...) while((s32[]{:T(128)}, f32[4,512,4,64]{1,0,3,2:T(4,128)}, ...), condition=%wide.region_4.5_spmd, body=%wide.region_1.4_spmd.sunk | while | flops 1112537088 | bytes 59586684 | solution.py:118
  140.4 3.9 fusion.150
  144.3 4.2 fusion.151
  149.7 11.1 dynamic_update_slice.18
  165.2 3.9 fusion.150
  169.1 4.2 fusion.151
  174.4 11.1 dynamic_update_slice.18
  193.8 4.2 fusion.151
  199.2 11.1 dynamic_update_slice.18
  218.6 4.2 fusion.151
  223.9 11.1 dynamic_update_slice.18
  239.2 4.6 fusion.87
  245.8 141.3 %reduce-scatter.12.cloned.1.call-done = f32[512,1024]{1,0:T(8,128)} async-done(((f32[2048,1024]{1,0:T(8,128)}), f32[512,1024]{1,0:T(8,128)}) %reduce-scatter.12.cloned.1.call-update) | async-done | bytes 2097168 | tf_op jit(solution)/shard_map/reduce_scatter | solution.py:122
  392.2 29.4 %all-gather.15.cloned.1.call-done = bf16[2,1024,704]{1,2,0:T(8,128)(2,1)} async-done(((bf16[2,128,704]{1,2,0:T(8,128)(2,1)}), bf16[2,1024,704]{1,2,0:T(8,128)(2,1)}) %all-gather.15.cloned.1.call-update) | async-done | bytes 2883600 | tf_op jit(solution)/shard_map/all_gather | solution.py:76
  421.6 82.8 %all-gather.13.cloned.1.call-done = bf16[2048,1024]{1,0:T(8,128)(2,1)} async-done(((bf16[512,1024]{1,0:T(8,128)(2,1)}), bf16[2048,1024]{1,0:T(8,128)(2,1)}) %all-gather.13.cloned.1.call-update) | async-done | bytes 4194320 | tf_op jit(solution)/shard_map/all_gather | solution.py:133
  504.4 11.7 convolution_bitcast_fusion.2
  516.1 14.3 %all-gather.17.cloned.1.call-done = bf16[704,1024]{1,0:T(8,128)(2,1)} async-done(((bf16[704,128]{1,0:T(8,128)(2,1)}), bf16[704,1024]{1,0:T(8,128)(2,1)}) %all-gather.17.cloned.1.call-update) | async-done | bytes 1441808 | tf_op jit(solution)/shard_map/all_gather | solution.py:77
  530.4 82.3 %all-gather.21.cloned.1.call-done = bf16[1,2048,1024]{2,1,0:T(8,128)(2,1)} async-done(((bf16[1,512,1024]{2,1,0:T(8,128)(2,1)}), bf16[1,2048,1024]{2,1,0:T(8,128)(2,1)}) %all-gather.21.cloned.1.call-update) | async-done | bytes 4194320 | tf_op jit(solution)/shard_map/all_gather | solution.py:145
  612.7 13.1 %fusion.63 = (bf16[1,2048,704]{1,2,0:T(8,128)(2,1)S(1)}, bf16[1,2048,704]{1,2,0:T(8,128)(2,1)S(1)}, bf16[2048,704]{0,1:T(8,128)(2,1)}) fusion(f32[2,2048,704]{1,2,0:T(8,128)} %convolution_bitcast_fusion.2, bf16[704,1024]{1,0:T(8,128)(2,1)} %all-gather.17.cloned.1.call-done, bf16[1,2048,1024]{2,1,0:T(8,128)(2,1)} %all-gather.21.cloned.1.call-done), kind=kOutput, calls=%fused_computation.86 | convolution fusion | flops 2990276608 | bytes 25821184 | tf_op jit(solution)/shard_map/td,fd->tf/dot_general | solution.py:153
  628.3 8.3 bitcast_convert_fusion.1
  636.6 75.4 %reduce-scatter.16.cloned.1.call-done = bf16[512,1024]{1,0:T(8,128)(2,1)} async-done(((bf16[2048,1024]{1,0:T(8,128)(2,1)}), bf16[512,1024]{1,0:T(8,128)(2,1)}) %reduce-scatter.16.cloned.1.call-update) | async-done | bytes 1048592 | tf_op jit(solution)/shard_map/reduce_scatter | solution.py:161
  716.9 7.7 fusion.44
  724.7 11.4 fusion.64
  736.3 61.6 %all-gather.19.cloned.1.call-done = bf16[2048,1024]{1,0:T(8,128)(2,1)} async-done(((bf16[512,1024]{1,0:T(8,128)(2,1)}), bf16[2048,1024]{1,0:T(8,128)(2,1)}) %all-gather.19.cloned.1.call-update) | async-done | bytes 4194320 | tf_op jit(solution)/shard_map/all_gather | solution.py:175
  797.9 4.5 fusion.70
  802.3 4.6 reshape.184
  806.9 4.1 copy.83
  811.1 4.5 fusion.86
  815.7 185.1 %while.28 = (s32[]{:T(128)}, f32[2048,4,64]{0,2,1:T(8,128)}, f32[2048,4,64]{0,2,1:T(8,128)}, bf16[4,512,4,64]{1,3,2,0:T(8,128)(2,1)}, bf16[4,512,4,64]{1,3,2,0:T...) while((s32[]{:T(128)}, f32[2048,4,64]{0,2,1:T(8,128)}, ...), condition=%wide.region_12.13_spmd.clone, body=%wide.region_10.12_spmd.clone.sunk | while | flops 2737829888 | bytes 185276784 | solution.py:219
  821.2 6.7 fusion.163
  828.0 11.0 multiply_reduce_fusion.3
  839.0 10.7 multiply_convert_fusion.8
  849.7 7.4 fusion.164
  857.1 4.0 fusion.162
  866.5 7.5 fusion.163
  874.0 11.0 multiply_reduce_fusion.3
  885.0 10.8 multiply_convert_fusion.8
  895.8 7.1 fusion.164
  903.0 4.7 fusion.162
  913.1 7.5 fusion.163
  920.5 11.0 multiply_reduce_fusion.3
  931.6 10.7 multiply_convert_fusion.8
  942.2 7.2 fusion.164
  949.4 4.7 fusion.162
  959.5 7.5 fusion.163
  967.0 11.0 multiply_reduce_fusion.3
  978.0 10.7 multiply_convert_fusion.8
  988.7 7.1 fusion.164
  995.8 4.7 fusion.162
  1000.8 4.2 copy.102
  1005.0 4.3 reshape.185
  1014.0 7.6 fusion.82
  1022.8 6.4 bitcast_convert_fusion
  1030.7 7.2 convolution_convert_fusion
  1047.6 19.6 %reduce-scatter.20.cloned.1.call-done = f32[3,128,256]{1,2,0:T(8,128)} async-done(((f32[3,1024,256]{1,2,0:T(8,128)}), f32[3,128,256]{1,2,0:T(8,128)}) %reduce-scatter.20.cloned.1.call-update) | async-done | bytes 393232 | tf_op jit(solution)/shard_map/reduce_scatter | solution.py:242
  1076.1 70.1 %reduce-scatter.18.cloned.1.call-done = bf16[512,1024]{1,0:T(8,128)(2,1)} async-done(((bf16[2048,1024]{1,0:T(8,128)(2,1)}), bf16[512,1024]{1,0:T(8,128)(2,1)}) %reduce-scatter.18.cloned.1.call-update) | async-done | bytes 1048592 | tf_op jit(solution)/shard_map/reduce_scatter | solution.py:230
  1150.0 75.6 %reduce-scatter.14.cloned.1.call-done = bf16[512,1024]{1,0:T(8,128)(2,1)} async-done(((bf16[2048,1024]{1,0:T(8,128)(2,1)}), bf16[512,1024]{1,0:T(8,128)(2,1)}) %reduce-scatter.14.cloned.1.call-update) | async-done | bytes 1048592 | tf_op jit(solution)/shard_map/reduce_scatter | solution.py:138
  1225.7 4.2 fusion.73
  1229.9 33.4 %reduce-scatter.28.cloned.1.call-done = f32[128,2]{1,0:T(8,128)} async-done(((f32[1024,2]{1,0:T(8,128)}), f32[128,2]{1,0:T(8,128)}) %reduce-scatter.28.cloned.1.call-update) | async-done | bytes 1040
  1264.2 11.7 psum.8
  (268 shorter events, 117.3 us)
Async XLA Ops:
  7.2 15.2 %copy-start.7 = (bf16[1,512,1024]{2,1,0:T(8,128)(2,1)S(1)}, bf16[1,512,1024]{2,1,0:T(8,128)(2,1)}, u32[]{:S(2)}) copy-start(bf16[1,512,1024]{2,1,0:T(8,128)(2,1)} %param.23) | copy-start | bytes 3145732
  7.2 17.8 %copy-start.24 = (s32[1,2048]{1,0:T(1,128)S(1)}, s32[1,2048]{1,0:T(1,128)}, u32[]{:S(2)}) copy-start(s32[1,2048]{1,0:T(1,128)} %param.25) | copy-start | bytes 24580
  7.2 18.5 %copy-start.29 = (f32[256,128]{1,0:T(8,128)S(1)}, f32[256,128]{1,0:T(8,128)}, u32[]{:S(2)}) copy-start(f32[256,128]{1,0:T(8,128)} %param.30) | copy-start | bytes 393220
  7.2 33.2 %all-gather.11.cloned.1.call-start = ((), (), s32[]{:S(2)}) async-start(), calls=%async_computation.10 | async-start | bytes 1769472 | tf_op jit(solution)/shard_map/all_gather | solution.py:74
  8.5 121.0 %copy-start.13 = (f32[3,128,256]{1,2,0:T(8,128)}, f32[3,128,256]{1,2,0:T(8,128)S(1)}, u32[]{:S(2)}) copy-start(f32[3,128,256]{1,2,0:T(8,128)S(1)} %copy.78) | copy-start | bytes 1179652
  9.3 114.0 %all-gather.9.cloned.1.call-start = ((), (), s32[]{:S(2)}) async-start(), calls=%async_computation.9 | async-start | bytes 5242880 | tf_op jit(solution)/shard_map/all_gather | solution.py:97
  21.8 3.8 copy-start.41
  22.4 3.2 copy-start.37
  23.7 363.4 %reduce-scatter.12.cloned.1.call-start = ((), (), s32[]{:S(2)}) async-start(), calls=%async_computation.11 | async-start | bytes 10485760 | tf_op jit(solution)/shard_map/reduce_scatter | solution.py:122
  235.0 8.8 copy-start.6
  235.0 4.2 copy-start.17
  235.0 4.2 copy-start.32
  243.8 145.5 %copy-start.33 = (f32[1,1024]{1,0:T(1,128)S(1)}, f32[1,1024]{1,0:T(1,128)}, u32[]{:S(2)}) copy-start(f32[1,1024]{1,0:T(1,128)} %get-tuple-element.364) | copy-start | bytes 12292
  243.9 177.8 %all-gather.15.cloned.1.call-start = ((), (), s32[]{:S(2)}) async-start(), calls=%async_computation.13 | async-start | bytes 3244032 | tf_op jit(solution)/shard_map/all_gather | solution.py:76
  245.7 258.6 %all-gather.13.cloned.1.call-start = ((), (), s32[]{:S(2)}) async-start(), calls=%async_computation.12 | async-start | bytes 5242880 | tf_op jit(solution)/shard_map/all_gather | solution.py:133
  389.3 325.4 %copy-start.4 = (f32[512,1024]{1,0:T(8,128)}, f32[512,1024]{1,0:T(8,128)S(1)}, u32[]{:S(2)}) copy-start(f32[512,1024]{1,0:T(8,128)S(1)} %get-tuple-element.351) | copy-start | bytes 6291460
  389.3 325.4 %copy-start.39 = (f32[512]{0:T(512)}, f32[512]{0:T(512)S(1)}, u32[]{:S(2)}) copy-start(f32[512]{0:T(512)S(1)} %add_rsqrt_fusion) | copy-start | bytes 6148
  390.6 139.8 %all-gather.17.cloned.1.call-start = ((), (), s32[]{:S(2)}) async-start(), calls=%async_computation.14 | async-start | bytes 1622016 | tf_op jit(solution)/shard_map/all_gather | solution.py:77
  391.4 221.4 %all-gather.21.cloned.1.call-start = ((), (), s32[]{:S(2)}) async-start(), calls=%async_computation.23 | async-start | bytes 5242880 | tf_op jit(solution)/shard_map/all_gather | solution.py:145
  392.1 319.9 %reduce-scatter.16.cloned.1.call-start = ((), (), s32[]{:S(2)}) async-start(), calls=%async_computation.16 | async-start | bytes 5242880 | tf_op jit(solution)/shard_map/reduce_scatter | solution.py:161
  612.7 15.5 %copy-start.47 = (bf16[2,1024,704]{1,2,0:T(8,128)(2,1)S(1)}, bf16[2,1024,704]{1,2,0:T(8,128)(2,1)}, u32[]{:S(2)}) copy-start(bf16[2,1024,704]{1,2,0:T(8,128)(2,1)} %all-gather.15.cloned.1.call-done) | copy-start | bytes 8650756
  636.6 161.3 %all-gather.19.cloned.1.call-start = ((), (), s32[]{:S(2)}) async-start(), calls=%async_computation.17 | async-start | bytes 5242880 | tf_op jit(solution)/shard_map/all_gather | solution.py:175
  716.5 323.7 %reduce-scatter.26.cloned.1.call-start = ((), (), s32[]{:S(2)}) async-start(), calls=%async_computation.22 | async-start | bytes 3244032 | tf_op jit(solution)/shard_map/reduce_scatter | solution.py:245
  724.7 317.9 %reduce-scatter.24.cloned.1.call-start = ((), (), s32[]{:S(2)}) async-start(), calls=%async_computation.21 | async-start | bytes 6488064 | tf_op jit(solution)/shard_map/reduce_scatter | solution.py:244
  736.2 61.7 %copy-start.18 = (bf16[256,1024]{1,0:T(8,128)(2,1)S(1)}, bf16[256,1024]{1,0:T(8,128)(2,1)}, u32[]{:S(2)}) copy-start(bf16[256,1024]{1,0:T(8,128)(2,1)} %all_gather.32) | copy-start | bytes 1572868
  736.2 309.5 %reduce-scatter.22.cloned.1.call-start = ((), (), s32[]{:S(2)}) async-start(), calls=%async_computation.20 | async-start | bytes 1179648 | tf_op jit(solution)/shard_map/reduce_scatter | solution.py:243
  802.3 8.8 copy-start.10
  815.6 251.6 %reduce-scatter.20.cloned.1.call-start = ((), (), s32[]{:S(2)}) async-start(), calls=%async_computation.19 | async-start | bytes 3538944 | tf_op jit(solution)/shard_map/reduce_scatter | solution.py:242
  849.7 7.4 copy-start
  857.1 4.0 copy-start.2
  857.1 4.0 copy-start.26
  857.1 4.0 copy-start.36
  895.8 7.1 copy-start
  903.0 4.7 copy-start.2
  903.0 4.7 copy-start.26
  903.0 4.7 copy-start.36
  942.2 7.2 copy-start
  949.4 4.7 copy-start.2
  949.4 4.7 copy-start.26
  949.4 4.7 copy-start.36
  988.7 7.1 copy-start
  995.8 4.7 copy-start.2
  995.8 4.7 copy-start.26
  995.8 4.7 copy-start.36
  1000.8 8.5 copy-start.3
  1010.8 3.2 copy-start.21
  1010.8 3.2 copy-start.22
  1021.6 124.6 %reduce-scatter.18.cloned.1.call-start = ((), (), s32[]{:S(2)}) async-start(), calls=%async_computation.18 | async-start | bytes 5242880 | tf_op jit(solution)/shard_map/reduce_scatter | solution.py:230
  1029.2 196.5 %reduce-scatter.14.cloned.1.call-start = ((), (), s32[]{:S(2)}) async-start(), calls=%async_computation.15 | async-start | bytes 5242880 | tf_op jit(solution)/shard_map/reduce_scatter | solution.py:138
  1037.9 4.8 copy-start.16
  1037.9 4.8 copy-start.27
  1037.9 4.7 copy-start.28
  1037.9 225.4 %reduce-scatter.28.cloned.1.call-start = ((), (), s32[]{:S(2)}) async-start(), calls=%async_computation.24 | async-start | bytes 589824
  1042.6 3.1 copy-start.30
  1042.6 24.6 %copy-start.14 = (f32[3,128,256]{1,2,0:T(8,128)S(1)}, f32[3,128,256]{1,2,0:T(8,128)}, u32[]{:S(2)}) copy-start(f32[3,128,256]{1,2,0:T(8,128)} %copy-done.13) | copy-start | bytes 1179652
  1045.7 100.5 %copy-start.8 = (bf16[1,512,1024]{2,1,0:T(8,128)(2,1)S(1)}, bf16[1,512,1024]{2,1,0:T(8,128)(2,1)}, u32[]{:S(2)}) copy-start(bf16[1,512,1024]{2,1,0:T(8,128)(2,1)} %param.23) | copy-start | bytes 3145732
  1045.7 100.5 %copy-start.38 = (f32[1,1024]{1,0:T(1,128)S(1)}, f32[1,1024]{1,0:T(1,128)}, u32[]{:S(2)}) copy-start(f32[1,1024]{1,0:T(1,128)} %copy-done.37) | copy-start | bytes 12292
  1045.7 100.5 %copy-start.42 = (f32[512]{0:T(512)S(1)}, f32[512]{0:T(512)}, u32[]{:S(2)}) copy-start(f32[512]{0:T(512)} %copy-done.41) | copy-start | bytes 6148
  1069.4 156.2 %copy-start.5 = (f32[512,1024]{1,0:T(8,128)S(1)}, f32[512,1024]{1,0:T(8,128)}, u32[]{:S(2)}) copy-start(f32[512,1024]{1,0:T(8,128)} %copy-done.4) | copy-start | bytes 6291460
  1069.4 156.2 %copy-start.34 = (f32[1,1024]{1,0:T(1,128)S(1)}, f32[1,1024]{1,0:T(1,128)}, u32[]{:S(2)}) copy-start(f32[1,1024]{1,0:T(1,128)} %get-tuple-element.364) | copy-start | bytes 12292
  1069.4 156.2 %copy-start.40 = (f32[512]{0:T(512)S(1)}, f32[512]{0:T(512)}, u32[]{:S(2)}) copy-start(f32[512]{0:T(512)} %copy-done.39) | copy-start | bytes 6148
  1150.0 125.9 %copy-start.44 = (f32[2,128]{1,0:T(2,128)S(1)}, f32[2,128]{1,0:T(2,128)}, u32[]{:S(2)}) copy-start(f32[2,128]{1,0:T(2,128)} %param.39) | copy-start | bytes 3076
  1150.0 125.8 %copy-start.45 = (f32[2,128]{1,0:T(2,128)S(1)}, f32[2,128]{1,0:T(2,128)}, u32[]{:S(2)}) copy-start(f32[2,128]{1,0:T(2,128)} %param.40) | copy-start | bytes 3076
  1150.0 125.8 %copy-start.46 = (f32[2,128]{1,0:T(2,128)S(1)}, f32[2,128]{1,0:T(2,128)}, u32[]{:S(2)}) copy-start(f32[2,128]{1,0:T(2,128)} %param.41) | copy-start | bytes 3076
  (24 other events, 32.7 us)
Sparse Core Ops, SparseCore 0:
  10.5 29.9 all-gather.10
  42.6 80.7 all-gather.8
  244.0 143.0 reduce-scatter.11
  389.4 32.1 all-gather.14
  423.6 80.7 all-gather.12
  506.7 23.6 all-gather.16
  532.0 80.7 all-gather.20
  636.7 75.2 reduce-scatter.15
  716.6 81.2 all-gather.18
  801.1 43.2 reduce-scatter.25
  847.8 58.8 reduce-scatter.23
  909.7 35.9 reduce-scatter.21
  1021.7 45.4 reduce-scatter.19
  1069.4 76.7 reduce-scatter.17
  1148.3 77.2 reduce-scatter.13
  1228.6 34.6 reduce-scatter.27
where the time goes:
time: 1290 us; the launch traced here: 1280 us
  waiting for transfers between devices  771 us (60%)
  matrix products  260 us (20%)
  other arithmetic  101 us (8%)
  local copies, waits for them, and re-layouts  99.7 us (8%)
  blocking collectives  34.4 us (3%)
  between operations  15.3 us (1%)
    reduce_scatter x1, waiting for transfers between devices, on_device(): lax.psum_scatter(jnp.dot(attended, full_out, preferred_element_type=jnp.f...  141 us
    all_gather x1, waiting for transfers between devices, on_device(): lax.all_gather(normed_one, 'mp', axis=0, tiled=True)  82.9 us
    all_gather x1, waiting for transfers between devices, on_device(): lax.all_gather(normed_two, 'mp', axis=0, tiled=True)  82.8 us
    all_gather x1, waiting for transfers between devices, on_device(): lax.all_gather(cotangent[0], 'mp', axis=0, tiled=True)  82.3 us
    reduce_scatter x1, waiting for transfers between devices, on_device(): lax.psum_scatter(jnp.dot(hidden, full_down, preferred_element_type=jnp.fl...  75.6 us
    reduce_scatter x1, waiting for transfers between devices, on_device(): lax.psum_scatter(jnp.einsum('ctf,cdf->td', part, full_gate_up, preferred_...  75.4 us
    reduce_scatter x1, waiting for transfers between devices, on_device(): lax.psum_scatter(jnp.einsum('tcf,cdf->td', part, full_qkv, preferred_elem...  70.1 us
    all_gather x1, waiting for transfers between devices, on_device(): lax.all_gather(d_branch, 'mp', axis=0, tiled=True)  61.6 us
  transfers between devices with their start and end apart: 16, of which 13 were waited for; matrix products, arithmetic and copies ran while one was open for 24% of the time, Pallas kernels for 0%

commit v1 on v0

--- a/solution.py
+++ b/solution.py
@@ -1,6 +1,10 @@
+import functools
+
 import jax
 import jax.numpy as jnp
 from jax import lax
+from jax.experimental import pallas as pl
+from jax.experimental.pallas import tpu as pltpu
 from jax.sharding import PartitionSpec as P
 
 HEAD = 64
@@ -38,10 +42,165 @@
     return (updated, updated.astype(jnp.bfloat16), moment_new, second_new)
 
 
-def block_scores(query_blk, seg_blk, seg_row, keys_in):
-    scores = jnp.einsum("qhd,khd->hqk", query_blk, keys_in, preferred_element_type=jnp.float32)
-    same_doc = (seg_blk[:, None] == seg_row[None, :])[None]
-    return (scores, same_doc)
+NT = (((1,), (1,)), ((), ()))
+NN = (((1,), (0,)), ((), ()))
+
+
+def dot32(left, right, dims):
+    return lax.dot_general(left, right, dims, preferred_element_type=jnp.float32)
+
+
+def attend_kernel(lo_ref, hi_ref, q_ref, k_ref, vt_ref, seg_q, seg_k, o_ref, lse_ref, *, bk, heads):
+    i = pl.program_id(0)
+    bq = q_ref.shape[0]
+
+    def body(j, carry):
+        ks = pl.ds(pl.multiple_of(j * bk, bk), bk)
+        same = seg_k[ks, :] == seg_q[...]
+        out = []
+        for h in range(heads):
+            peak, total, acc = carry[h]
+            hs = slice(h * HEAD, (h + 1) * HEAD)
+            s = jnp.where(same, dot32(k_ref[ks, hs], q_ref[:, hs], NT), NEG_FILL)
+            peak_new = jnp.maximum(peak, jnp.max(s, axis=0, keepdims=True))
+            p = jnp.exp(s - peak_new)
+            keep = jnp.exp(peak - peak_new)
+            total = total * keep + jnp.sum(p, axis=0, keepdims=True)
+            acc = acc * keep + dot32(vt_ref[hs, ks], p.astype(jnp.bfloat16), NN)
+            out.append((peak_new, total, acc))
+        return tuple(out)
+
+    first = tuple(
+        (
+            jnp.full((1, bq), NEG_FILL, jnp.float32),
+            jnp.zeros((1, bq), jnp.float32),
+            jnp.zeros((HEAD, bq), jnp.float32),
+        )
+        for _ in range(heads)
+    )
+    found = lax.fori_loop(lo_ref[i], hi_ref[i], body, first)
+    totals = [jnp.where(total > 0, total, 1.0) for _, total, _ in found]
+    o_ref[...] = jnp.concatenate([acc / t for (_, _, acc), t in zip(found, totals)], axis=0).T
+    lse_ref[...] = jnp.concatenate([peak + jnp.log(t) for (peak, _, _), t in zip(found, totals)], axis=0)
+
+
+def attend(q, k, vt, seg, lo, hi, bq, bk):
+    rows, width = q.shape
+    heads = width // HEAD
+    keys = k.shape[0]
+    whole = lambda i, *_: (0, 0)
+    return pl.pallas_call(
+        functools.partial(attend_kernel, bk=bk, heads=heads),
+        out_shape=(
+            jax.ShapeDtypeStruct((rows, width), jnp.float32),
+            jax.ShapeDtypeStruct((heads, rows), jnp.float32),
+        ),
+        grid_spec=pltpu.PrefetchScalarGridSpec(
+            num_scalar_prefetch=2,
+            grid=(rows // bq,),
+            in_specs=[
+                pl.BlockSpec((bq, width), lambda i, *_: (i, 0)),
+                pl.BlockSpec((keys, width), whole),
+                pl.BlockSpec((width, keys), whole),
+                pl.BlockSpec((1, bq), lambda i, *_: (0, i)),
+                pl.BlockSpec((keys, 1), whole),
+            ],
+            out_specs=(
+                pl.BlockSpec((bq, width), lambda i, *_: (i, 0)),
+                pl.BlockSpec((heads, bq), lambda i, *_: (0, i)),
+            ),
+        ),
+        name="attend",
+    )(lo, hi, q, k, vt, seg[None, :], seg[:, None])
+
+
+def attend_back_kernel(
+    lo_ref, hi_ref, q_ref, do_ref, lse_ref, dot_ref, k_ref, kt_ref, v_ref, seg_q, seg_k,
+    dq_ref, dk_ref, dv_ref, dk_sum, dv_sum, *, bk, heads,
+):
+    i = pl.program_id(0)
+    bq = q_ref.shape[0]
+
+    @pl.when(i == 0)
+    def _():
+        dk_sum[...] = jnp.zeros_like(dk_sum)
+        dv_sum[...] = jnp.zeros_like(dv_sum)
+
+    def body(j, carry):
+        ks = pl.ds(pl.multiple_of(j * bk, bk), bk)
+        same = seg_k[ks, :] == seg_q[...]
+        out, dks, dvs = [], [], []
+        for h in range(heads):
+            hs = slice(h * HEAD, (h + 1) * HEAD)
+            qh = q_ref[:, hs]
+            doh = do_ref[:, hs]
+            s = dot32(k_ref[ks, hs], qh, NT)
+            p = jnp.exp(jnp.where(same, s - lse_ref[h : h + 1, :], NEG_FILL))
+            dp = dot32(v_ref[ks, hs], doh, NT)
+            ds = (p * (dp - dot_ref[h : h + 1, :])).astype(jnp.bfloat16)
+            dvs.append(dot32(p.astype(jnp.bfloat16), doh, NN))
+            dks.append(dot32(ds, qh, NN))
+            out.append(carry[h] + dot32(kt_ref[hs, ks], ds, NN))
+        dk_sum[ks, :] += jnp.concatenate(dks, axis=1)
+        dv_sum[ks, :] += jnp.concatenate(dvs, axis=1)
+        return tuple(out)
+
+    first = tuple(jnp.zeros((HEAD, bq), jnp.float32) for _ in range(heads))
+    found = lax.fori_loop(lo_ref[i], hi_ref[i], body, first)
+    dq_ref[...] = jnp.concatenate(found, axis=0).T.astype(dq_ref.dtype)
+
+    @pl.when(i == pl.num_programs(0) - 1)
+    def _():
+        dk_ref[...] = dk_sum[...].astype(dk_ref.dtype)
+        dv_ref[...] = dv_sum[...].astype(dv_ref.dtype)
+
+
+def attend_back(q, k, kt, v, d_out, lse, row_dot, seg, lo, hi, bq, bk):
+    rows, width = q.shape
+    heads = width // HEAD
+    keys = k.shape[0]
+    whole = lambda i, *_: (0, 0)
+    by_row = lambda i, *_: (i, 0)
+    by_col = lambda i, *_: (0, i)
+    return pl.pallas_call(
+        functools.partial(attend_back_kernel, bk=bk, heads=heads),
+        out_shape=(
+            jax.ShapeDtypeStruct((rows, width), jnp.bfloat16),
+            jax.ShapeDtypeStruct((keys, width), jnp.bfloat16),
+            jax.ShapeDtypeStruct((keys, width), jnp.bfloat16),
+        ),
+        grid_spec=pltpu.PrefetchScalarGridSpec(
+            num_scalar_prefetch=2,
+            grid=(rows // bq,),
+            in_specs=[
+                pl.BlockSpec((bq, width), by_row),
+                pl.BlockSpec((bq, width), by_row),
+                pl.BlockSpec((heads, bq), by_col),
+                pl.BlockSpec((heads, bq), by_col),
+                pl.BlockSpec((keys, width), whole),
+                pl.BlockSpec((width, keys), whole),
+                pl.BlockSpec((keys, width), whole),
+                pl.BlockSpec((1, bq), by_col),
+                pl.BlockSpec((keys, 1), whole),
+            ],
+            out_specs=(
+                pl.BlockSpec((bq, width), by_row),
+                pl.BlockSpec((keys, width), whole),
+                pl.BlockSpec((keys, width), whole),
+            ),
+            scratch_shapes=[pltpu.VMEM((keys, width), jnp.float32)] * 2,
+        ),
+        name="attend_back",
+    )(lo, hi, q, d_out, lse, row_dot, k, kt, v, seg[None, :], seg[:, None])
+
+
+def key_blocks(seg, length, bq, bk):
+    lo = jnp.sum(seg[None, :] < seg[::bq][:, None], axis=1)
+    hi = jnp.minimum(jnp.sum(seg[None, :] <= seg[bq - 1 :: bq][:, None], axis=1), length)
+    lo = lo // bk
+    hi = (hi + bk - 1) // bk
+    dead = jnp.arange(seg.shape[0] // bq) * bq >= length
+    return lo.astype(jnp.int32), jnp.where(dead, lo, hi).astype(jnp.int32)
 
 
 def on_device(
@@ -82,12 +241,9 @@
     seq_len = segment_ids.shape[1]
     width = full_qkv.shape[2]
     heads_here = width // HEAD
-    block_rows = min(512, seq_len)
-    blocks = seq_len // block_rows
     seg_row = segment_ids[0]
     positions = jnp.arange(seq_len, dtype=jnp.int32)
     live_row = (positions < row_length[0]).astype(jnp.float32)
-    seg_blocks = seg_row.reshape(blocks, block_rows)
     resid_in = inputs[0].astype(jnp.float32)
     scale_one = rms_scale(resid_in)
     hat_one = resid_in * scale_one
@@ -98,33 +254,18 @@
         full_qkv,
         preferred_element_type=jnp.float32,
     ).astype(jnp.bfloat16)
-    queries = qkv_rows[:, 0].reshape(seq_len, heads_here, HEAD)
-    keys_all = qkv_rows[:, 1].reshape(seq_len, heads_here, HEAD)
-    values_all = qkv_rows[:, 2].reshape(seq_len, heads_here, HEAD)
-
-    def forward_block(block_in):
-        query_blk, seg_blk = block_in
-        scores, same_doc = block_scores(query_blk, seg_blk, seg_row, keys_all)
-        scores = jnp.where(same_doc, scores, NEG_FILL)
-        row_peak = jnp.max(scores, axis=-1, keepdims=True)
-        raised = jnp.exp(scores - row_peak)
-        summed = jnp.sum(raised, axis=-1, keepdims=True)
-        probs = (raised / summed).astype(jnp.bfloat16)
-        attended_blk = jnp.einsum(
-            "hqk,khd->qhd", probs, values_all, preferred_element_type=jnp.float32
-        )
-        return (attended_blk, (row_peak + jnp.log(summed))[..., 0])
-
-    attended, log_sums = lax.map(
-        forward_block, (queries.reshape(blocks, block_rows, heads_here, HEAD), seg_blocks)
-    )
-    attended = (attended.reshape(seq_len, width) * live_row[:, None]).astype(jnp.bfloat16)
+    queries, keys_all, values_all = qkv_rows[:, 0], qkv_rows[:, 1], qkv_rows[:, 2]
+    wide, narrow = min(1024, seq_len), min(512, seq_len)
+    lo, hi = key_blocks(seg_row, row_length[0], wide, narrow)
+    raw_out, log_sums = attend(queries, keys_all, values_all.T, seg_row, lo, hi, wide, narrow)
+    log_sums = jnp.where(live_row[None, :] > 0, log_sums, -NEG_FILL)
+    attended = (raw_out * live_row[:, None]).astype(jnp.bfloat16)
     after_attn = resid_in + lax.psum_scatter(
-        jnp.dot(attended, full_out, preferred_element_type=jnp.float32),
+        jnp.dot(attended, full_out, preferred_element_type=jnp.float32).astype(jnp.bfloat16),
         "mp",
         scatter_dimension=0,
         tiled=True,
-    )
+    ).astype(jnp.float32)
     scale_two = rms_scale(after_attn)
     hat_two = after_attn * scale_two
     normed_two = (hat_two * gain_two).astype(jnp.bfloat16)
@@ -175,56 +316,18 @@
         lax.all_gather(d_branch, "mp", axis=0, tiled=True),
         lax.all_gather(normed_one, "mp", axis=0, tiled=True),
     )
-    qkv_again = jnp.einsum(
-        "td,cdf->tcf", normed_one_all, full_qkv, preferred_element_type=jnp.float32
-    ).astype(jnp.bfloat16)
-    queries_new = qkv_again[:, 0].reshape(seq_len, heads_here, HEAD)
-    keys_new = qkv_again[:, 1].reshape(seq_len, heads_here, HEAD)
-    values_new = qkv_again[:, 2].reshape(seq_len, heads_here, HEAD)
     grad_out = jnp.einsum("tf,td->fd", attended, d_branch_all, preferred_element_type=jnp.float32)
     d_attended = jnp.einsum(
         "td,fd->tf", d_branch_all, full_out, preferred_element_type=jnp.float32
     ).astype(jnp.bfloat16)
     d_attended = d_attended * live_row[:, None].astype(jnp.bfloat16)
 
-    def back_block(carry, block_in):
-        d_keys, d_values = carry
-        query_blk, seg_blk, log_blk, d_out_blk = block_in
-        scores, same_doc = block_scores(query_blk, seg_blk, seg_row, keys_new)
-        probs = jnp.exp(jnp.where(same_doc, scores - log_blk[..., None], NEG_FILL))
-        d_probs = jnp.einsum(
-            "qhd,khd->hqk", d_out_blk, values_new, preferred_element_type=jnp.float32
-        )
-        row_dot = jnp.sum(probs * d_probs, axis=-1, keepdims=True)
-        d_scores = (probs * (d_probs - row_dot)).astype(jnp.bfloat16)
-        d_query = jnp.einsum("hqk,khd->qhd", d_scores, keys_new, preferred_element_type=jnp.float32)
-        d_keys = d_keys + jnp.einsum(
-            "hqk,qhd->khd", d_scores, query_blk, preferred_element_type=jnp.float32
-        )
-        d_values = d_values + jnp.einsum(
-            "hqk,qhd->khd",
-            probs.astype(jnp.bfloat16),
-            d_out_blk,
-            preferred_element_type=jnp.float32,
-        )
-        return ((d_keys, d_values), d_query)
-
-    initial = jnp.zeros((seq_len, heads_here, HEAD), jnp.float32)
-    scan_in = (
-        queries_new.reshape(blocks, block_rows, heads_here, HEAD),
-        seg_blocks,
-        log_sums,
-        d_attended.reshape(blocks, block_rows, heads_here, HEAD),
-    )
-    (d_keys, d_values), d_queries = lax.scan(back_block, (initial, initial), scan_in)
-    d_qkv = jnp.stack(
-        [
-            d_queries.reshape(seq_len, width),
-            d_keys.reshape(seq_len, width),
-            d_values.reshape(seq_len, width),
-        ],
-        axis=1,
-    ).astype(jnp.bfloat16)
+    row_dot = jnp.sum((raw_out * d_attended).reshape(seq_len, heads_here, HEAD), axis=-1).T
+    lo, hi = key_blocks(seg_row, row_length[0], narrow, narrow)
+    d_queries, d_keys, d_values = attend_back(
+        queries, keys_all, keys_all.T, values_all, d_attended, log_sums, row_dot, seg_row, lo, hi, narrow, narrow
+    )
+    d_qkv = jnp.stack([d_queries, d_keys, d_values], axis=1)
     grad_qkv = jnp.einsum("td,tcf->cdf", normed_one_all, d_qkv, preferred_element_type=jnp.float32)
     part = d_qkv
     d_normed_one = lax.psum_scatter(
@@ -239,10 +342,18 @@
     grad_gain_one = jnp.sum(d_normed_one * hat_one, axis=0)
     grad_gains = lax.psum(jnp.stack([grad_gain_one, grad_gain_two]), "mp")
     red_qkv, red_out, red_gate_up, red_down, red_gains = (
-        lax.psum_scatter(grad_qkv, "dp", scatter_dimension=1, tiled=True),
-        lax.psum_scatter(grad_out, "dp", scatter_dimension=1, tiled=True),
-        lax.psum_scatter(grad_gate_up, "dp", scatter_dimension=1, tiled=True),
-        lax.psum_scatter(grad_down, "dp", scatter_dimension=1, tiled=True),
+        lax.psum_scatter(grad_qkv.astype(jnp.bfloat16), "dp", scatter_dimension=1, tiled=True).astype(
+            jnp.float32
+        ),
+        lax.psum_scatter(grad_out.astype(jnp.bfloat16), "dp", scatter_dimension=1, tiled=True).astype(
+            jnp.float32
+        ),
+        lax.psum_scatter(grad_gate_up.astype(jnp.bfloat16), "dp", scatter_dimension=1, tiled=True).astype(
+            jnp.float32
+        ),
+        lax.psum_scatter(grad_down.astype(jnp.bfloat16), "dp", scatter_dimension=1, tiled=True).astype(
+            jnp.float32
+        ),
         lax.psum_scatter(grad_gains, "dp", scatter_dimension=1, tiled=True),
     )
     new_qkv = adam_update(w_qkv, m_qkv, v_qkv, red_qkv, RATES[0], DECAY_RATE)

time: 1290 us -> 1050 us (0.81)
  matrix products: 260 us -> 96.5 us
  Pallas kernels: 0 us -> 72.4 us
  other arithmetic: 101 us -> 38.7 us
  waiting for transfers between devices: 771 us -> 718 us
  local copies, waits for them, and re-layouts: 99.7 us -> 67 us
    dot_general x28 -> x0, matrix products: 167 us -> none  [the longest x4 44.1 us: back_block(): jnp.einsum('qhd,khd->hqk', d_out_blk, values_new, preferred_element_type=...]
    pallas_call x0 -> x2, Pallas kernels: none -> 72.4 us  [the longest x1 40.8 us: attend_back(): pl.pallas_call(functools.partial(attend_back_kernel, bk=bk, heads=heads),...]
    reduce_scatter x1, waiting for transfers between devices: 141 us -> 76.4 us  [on_device(): lax.psum_scatter(jnp.dot(attended, full_out, preferred_element_type=jnp.f...]
    unnamed x17 -> x21, waiting for transfers between devices: 34.3 us -> 92 us
    dynamic_update_slice x8 -> x0, local copies, waits for them, and re-layouts: 46.5 us -> none  [on_device(): lax.map(forward_block, (queries.reshape(blocks, block_rows, heads_here, H...]
    convert_element_type x4 -> x0, other arithmetic: 42.9 us -> none  [back_block(): d_scores = (probs * (d_probs - row_dot)).astype(jnp.bfloat16)]
    unnamed x100 -> x65, local copies, waits for them, and re-layouts: 27 us -> 56.4 us
    all_gather x1, waiting for transfers between devices: 61.6 us -> 39.8 us  [on_device(): lax.all_gather(d_branch, 'mp', axis=0, tiled=True)]
  transfers between devices with their start and end apart: 16 -> 16, of which waited for: 13 -> 14; matrix products, arithmetic and copies ran while one was open for 24% -> 15% of each run, Pallas kernels for 0% -> 4%
where the time goes in v1:
time: 1050 us; the launch traced here: 1040 us
  waiting for transfers between devices  718 us (68%)
  matrix products  96.5 us (9%)
  Pallas kernels  72.4 us (7%)
  local copies, waits for them, and re-layouts  67 us (6%)
  other arithmetic  38.7 us (4%)
  blocking collectives  33.5 us (3%)
  between operations  15.3 us (1%)
    unnamed x21, waiting for transfers between devices  92 us
    all_gather x1, waiting for transfers between devices, on_device(): lax.all_gather(normed_one, 'mp', axis=0, tiled=True)  82.9 us
    all_gather x1, waiting for transfers between devices, on_device(): lax.all_gather(normed_two, 'mp', axis=0, tiled=True)  82.8 us
    all_gather x1, waiting for transfers between devices, on_device(): lax.all_gather(cotangent[0], 'mp', axis=0, tiled=True)  82.3 us
    reduce_scatter x1, waiting for transfers between devices, on_device(): lax.psum_scatter(jnp.dot(attended, full_out, preferred_element_type=jnp.f...  76.4 us
    reduce_scatter x1, waiting for transfers between devices, on_device(): lax.psum_scatter(jnp.dot(hidden, full_down, preferred_element_type=jnp.fl...  76.3 us
    reduce_scatter x1, waiting for transfers between devices, on_device(): lax.psum_scatter(jnp.einsum('ctf,cdf->td', part, full_gate_up, preferred_...  75.2 us
    reduce_scatter x1, waiting for transfers between devices, on_device(): lax.psum_scatter(jnp.einsum('tcf,cdf->td', part, full_qkv, preferred_elem...  65.4 us
  transfers between devices with their start and end apart: 16, of which 14 were waited for; matrix products, arithmetic and copies ran while one was open for 15% of the time, Pallas kernels for 4%

profile of v1, /device:TPU:0, one launch (start us, length us, event | category | flops | bytes accessed | tf_op | source)
XLA Modules:
  0.0 1042.7 jit_solution(11920044958239340545)
XLA Ops:
  7.2 1.7 convert_element_type.163
  9.7 10.3 all_gather.29
  20.0 1.5 fusion.43
  21.5 2.5 fusion.40
  26.3 11.6 %all_gather.32 = bf16[256,1024]{1,0:T(8,128)(2,1)S(1)} all-gather(bf16[256,128]{1,0:T(8,128)(2,1)S(1)} %convert_element_type.167), channel_id=1, replica_groups=mesh['dp'=8,'mp'=4] {'dp'}, dimensions={1}, use_global_device_ids=true | all-gather | bytes 589824 | tf_op jit(solution)/shard_map/all_gather | solution.py:234
  38.7 1.5 all-gather.11.cloned.1.call-done
  40.2 82.9 %all-gather.9.cloned.1.call-done = bf16[2048,1024]{1,0:T(8,128)(2,1)} async-done(((bf16[512,1024]{1,0:T(8,128)(2,1)}), bf16[2048,1024]{1,0:T(8,128)(2,1)}) %all-gather.9.cloned.1.call-update) | async-done | bytes 4194320 | tf_op jit(solution)/shard_map/all_gather | solution.py:253
  123.1 6.1 fusion.18
  129.2 2.2 slice_bitcast_fusion.4
  132.8 31.6 %attend.1 = (f32[2048,256]{1,0:T(8,128)}, f32[4,2048]{1,0:T(4,128)}) custom-call(s32[2]{0:T(128)} %get-tuple-element.151.lo_ref, s32[2]{0:T(128)} %get-tuple-element.150.hi_ref, bf16[2048,256]{1,0:T(8,128)(2,1)} %get-tuple-element.159.q_ref, bf16[2048,256]{1,0:T(8,128)(2,1)} %get-tuple-element.158.k_ref, bf16[256,2048]{1,0:T(8,128)(2,1)} %copy.83.vt_ref, ...), custom_call_target="tpu_custom_call" | custom-call | tf_op jit(solution)/shard_map/attend/pallas_call | solution.py:92
  164.4 4.8 convolution_convert_fusion.1
  171.7 76.4 %reduce-scatter.20.cloned.1.call-done = bf16[512,1024]{1,0:T(8,128)(2,1)} async-done(((bf16[2048,1024]{1,0:T(8,128)(2,1)}), bf16[512,1024]{1,0:T(8,128)(2,1)}) %reduce-scatter.20.cloned.1.call-update) | async-done | bytes 1048592 | tf_op jit(solution)/shard_map/reduce_scatter | solution.py:263
  248.1 1.6 multiply_reduce_fusion
  249.7 2.6 multiply_convert_fusion.2
  253.9 28.6 %all-gather.15.cloned.1.call-done = bf16[2,1024,704]{1,2,0:T(8,128)(2,1)} async-done(((bf16[2,128,704]{1,2,0:T(8,128)(2,1)}), bf16[2,1024,704]{1,2,0:T(8,128)(2,1)}) %all-gather.15.cloned.1.call-update) | async-done | bytes 2883600 | tf_op jit(solution)/shard_map/all_gather | solution.py:235
  282.5 82.8 %all-gather.13.cloned.1.call-done = bf16[2048,1024]{1,0:T(8,128)(2,1)} async-done(((bf16[512,1024]{1,0:T(8,128)(2,1)}), bf16[2048,1024]{1,0:T(8,128)(2,1)}) %all-gather.13.cloned.1.call-update) | async-done | bytes 4194320 | tf_op jit(solution)/shard_map/all_gather | solution.py:274
  365.2 11.6 %convolution_bitcast_fusion = f32[2,2048,704]{1,2,0:T(8,128)} fusion(bf16[2,1024,704]{1,2,0:T(8,128)(2,1)} %all-gather.15.cloned.1.call-done, bf16[2048,1024]{1,0:T(8,128)(2,1)} %all-gather.13.cloned.1.call-done), kind=kOutput, calls=%fused_computation.17 | convolution fusion | flops 5905580032 | bytes 18612224 | tf_op jit(solution)/shard_map/td,cdf->ctf/dot_general | solution.py:272
  376.8 14.5 %all-gather.17.cloned.1.call-done = bf16[704,1024]{1,0:T(8,128)(2,1)} async-done(((bf16[704,128]{1,0:T(8,128)(2,1)}), bf16[704,1024]{1,0:T(8,128)(2,1)}) %all-gather.17.cloned.1.call-update) | async-done | bytes 1441808 | tf_op jit(solution)/shard_map/all_gather | solution.py:236
  391.3 82.3 %all-gather.21.cloned.1.call-done = bf16[1,2048,1024]{2,1,0:T(8,128)(2,1)} async-done(((bf16[1,512,1024]{2,1,0:T(8,128)(2,1)}), bf16[1,2048,1024]{2,1,0:T(8,128)(2,1)}) %all-gather.21.cloned.1.call-update) | async-done | bytes 4194320 | tf_op jit(solution)/shard_map/all_gather | solution.py:286
  473.6 13.1 %fusion.26 = (bf16[1,2048,704]{1,2,0:T(8,128)(2,1)S(1)}, bf16[1,2048,704]{1,2,0:T(8,128)(2,1)S(1)}, bf16[2048,704]{0,1:T(8,128)(2,1)}) fusion(f32[2,2048,704]{1,2,0:T(8,128)} %convolution_bitcast_fusion, bf16[704,1024]{1,0:T(8,128)(2,1)} %all-gather.17.cloned.1.call-done, bf16[1,2048,1024]{2,1,0:T(8,128)(2,1)} %all-gather.21.cloned.1.call-done), kind=kOutput, calls=%fused_computation.42 | convolution fusion | flops 2990276608 | bytes 25821184 | tf_op jit(solution)/shard_map/td,fd->tf/dot_general | solution.py:294
  486.7 1.6 copy-done.20
  489.3 8.3 bitcast_convert_fusion.1
  497.8 75.2 %reduce-scatter.24.cloned.1.call-done = bf16[512,1024]{1,0:T(8,128)(2,1)} async-done(((bf16[2048,1024]{1,0:T(8,128)(2,1)}), bf16[512,1024]{1,0:T(8,128)(2,1)}) %reduce-scatter.24.cloned.1.call-update) | async-done | bytes 1048592 | tf_op jit(solution)/shard_map/reduce_scatter | solution.py:302
  573.0 2.8 fusion.39
  575.8 1.8 fusion.72
  577.7 7.3 fusion.48
  585.0 2.6 copy.106
  587.7 10.6 %convert_bitcast_fusion = bf16[2,1024,704]{1,2,0:T(8,128)(2,1)} fusion(bf16[2048,1024]{1,0:T(8,128)(2,1)} %all-gather.13.cloned.1.call-done, bf16[1,2048,704]{1,2,0:T(8,128)(2,1)} %copy-done.21, bf16[1,2048,704]{1,2,0:T(8,128)(2,1)} %copy-done.20), kind=kOutput, calls=%fused_computation.41 | convolution fusion | flops 5909905408 | bytes 12845056 | tf_op jit(solution)/shard_map/td,ctf->cdf/dot_general | solution.py:298
  598.4 8.7 copy.104
  607.1 7.6 reshape.107
  616.4 2.3 copy.87.kt_ref
  619.3 39.8 %all-gather.19.cloned.1.call-done = bf16[2048,1024]{1,0:T(8,128)(2,1)} async-done(((bf16[512,1024]{1,0:T(8,128)(2,1)}), bf16[2048,1024]{1,0:T(8,128)(2,1)}) %all-gather.19.cloned.1.call-update) | async-done | bytes 4194320 | tf_op jit(solution)/shard_map/all_gather | solution.py:316
  659.1 6.0 convert_multiply_fusion.5
  665.1 3.0 copy.86
  668.1 5.2 convolution_convert_fusion.3
  673.3 2.0 copy.102
  675.3 2.4 bitcast_reduce_fusion
  678.0 40.8 %attend_back.1 = (bf16[2048,256]{1,0:T(8,128)(2,1)}, bf16[2048,256]{1,0:T(8,128)(2,1)}, bf16[2048,256]{1,0:T(8,128)(2,1)}) custom-call(s32[4]{0:T(128)} %get-tuple-element.149.lo_ref, s32[4]{0:T(128)} %get-tuple-element.148.hi_ref, bf16[2048,256]{1,0:T(8,128)(2,1)} %get-tuple-element.159.q_ref, bf16[2048,256]{1,0:T(8,128)(2,1)} %get-tuple-element.165.do_ref, ...), custom_call_target="tpu_custom_call" | custom-call | tf_op jit(solution)/shard_map/attend_back/pallas_call | solution.py:165
  718.8 7.8 fusion.51
  726.7 4.1 copy.100
  730.8 3.1 copy.110
  734.0 7.8 bitcast_convert_fusion
  742.2 7.7 convolution_convert_fusion
  751.8 1.9 copy.89
  753.7 1.9 copy.91
  756.7 2.4 fusion.75
  761.7 3.5 fusion.78
  765.2 19.1 %reduce-scatter.30.cloned.1.call-done = bf16[128,256]{1,0:T(8,128)(2,1)} async-done(((bf16[1024,256]{1,0:T(8,128)(2,1)}), bf16[128,256]{1,0:T(8,128)(2,1)}) %reduce-scatter.30.cloned.1.call-update) | async-done | bytes 65552
  784.3 1.6 copy.103
  785.9 1.9 fusion.81
  787.7 38.8 %reduce-scatter.28.cloned.1.call-done = bf16[128,768]{1,0:T(8,128)(2,1)} async-done(((bf16[1024,768]{1,0:T(8,128)(2,1)}), bf16[128,768]{1,0:T(8,128)(2,1)}) %reduce-scatter.28.cloned.1.call-update) | async-done | bytes 196624
  826.5 1.7 reshape.104
  828.2 1.8 copy.101
  830.0 2.5 fusion.84
  832.5 1.9 copy.94
  834.4 2.0 copy.96
  836.4 1.9 copy.97
  838.4 1.7 copy.95
  840.1 65.4 %reduce-scatter.26.cloned.1.call-done = bf16[512,1024]{1,0:T(8,128)(2,1)} async-done(((bf16[2048,1024]{1,0:T(8,128)(2,1)}), bf16[512,1024]{1,0:T(8,128)(2,1)}) %reduce-scatter.26.cloned.1.call-update) | async-done | bytes 1048592 | tf_op jit(solution)/shard_map/reduce_scatter | solution.py:333
  905.5 2.0 fusion.42
  908.7 76.3 %reduce-scatter.22.cloned.1.call-done = bf16[512,1024]{1,0:T(8,128)(2,1)} async-done(((bf16[2048,1024]{1,0:T(8,128)(2,1)}), bf16[512,1024]{1,0:T(8,128)(2,1)}) %reduce-scatter.22.cloned.1.call-update) | async-done | bytes 1048592 | tf_op jit(solution)/shard_map/reduce_scatter | solution.py:279
  985.0 4.4 fusion.35
  989.4 33.2 %reduce-scatter.36.cloned.1.call-done = f32[128,2]{1,0:T(8,128)} async-done(((f32[1024,2]{1,0:T(8,128)}), f32[128,2]{1,0:T(8,128)}) %reduce-scatter.36.cloned.1.call-update) | async-done | bytes 1040
  1023.5 11.7 %psum.8 = f32[2,128]{1,0:T(2,128)S(1)} all-reduce(f32[2,128]{1,0:T(2,128)S(1)} %copy.109), channel_id=1, replica_groups=mesh['dp'=8,'mp'=4] {'mp'}, use_global_device_ids=true, to_apply=%region_19.20 | all-reduce | flops 256 | bytes 2048 | tf_op jit(solution)/shard_map/psum | solution.py:343
  (108 shorter events, 20.9 us)
Async XLA Ops:
  7.2 16.9 %copy-start.10 = (s32[1,2048]{1,0:T(1,128)S(1)}, s32[1,2048]{1,0:T(1,128)}, u32[]{:S(2)}) copy-start(s32[1,2048]{1,0:T(1,128)} %seg_q.3) | copy-start | bytes 24580
  7.2 33.0 %all-gather.11.cloned.1.call-start = ((), (), s32[]{:S(2)}) async-start(), calls=%async_computation.10 | async-start | bytes 1769472 | tf_op jit(solution)/shard_map/all_gather | solution.py:233
  8.9 17.4 %copy-start.9 = (f32[256,128]{1,0:T(8,128)S(1)}, f32[256,128]{1,0:T(8,128)}, u32[]{:S(2)}) copy-start(f32[256,128]{1,0:T(8,128)} %param.26) | copy-start | bytes 393220
  9.0 114.1 %all-gather.9.cloned.1.call-start = ((), (), s32[]{:S(2)}) async-start(), calls=%async_computation.9 | async-start | bytes 5242880 | tf_op jit(solution)/shard_map/all_gather | solution.py:253
  24.1 224.0 %reduce-scatter.20.cloned.1.call-start = ((), (), s32[]{:S(2)}) async-start(), calls=%async_computation.11 | async-start | bytes 5242880 | tf_op jit(solution)/shard_map/reduce_scatter | solution.py:263
  37.9 126.5 %copy-start.4 = (bf16[256,1024]{1,0:T(8,128)(2,1)}, bf16[256,1024]{1,0:T(8,128)(2,1)S(1)}, u32[]{:S(2)}) copy-start(bf16[256,1024]{1,0:T(8,128)(2,1)S(1)} %all_gather.32) | copy-start | bytes 1572868
  169.3 1.1 copy-start.5
  169.3 78.8 %copy-start = (bf16[1,512,1024]{2,1,0:T(8,128)(2,1)S(1)}, bf16[1,512,1024]{2,1,0:T(8,128)(2,1)}, u32[]{:S(2)}) copy-start(bf16[1,512,1024]{2,1,0:T(8,128)(2,1)} %param.19) | copy-start | bytes 3145732
  169.3 113.2 %all-gather.15.cloned.1.call-start = ((), (), s32[]{:S(2)}) async-start(), calls=%async_computation.13 | async-start | bytes 3244032 | tf_op jit(solution)/shard_map/all_gather | solution.py:235
  171.2 81.2 %copy-start.8 = (f32[704,128]{1,0:T(8,128)S(1)}, f32[704,128]{1,0:T(8,128)}, u32[]{:S(2)}) copy-start(f32[704,128]{1,0:T(8,128)} %param.32) | copy-start | bytes 1081348
  171.2 194.0 %all-gather.13.cloned.1.call-start = ((), (), s32[]{:S(2)}) async-start(), calls=%async_computation.12 | async-start | bytes 5242880 | tf_op jit(solution)/shard_map/all_gather | solution.py:274
  252.3 138.9 %all-gather.17.cloned.1.call-start = ((), (), s32[]{:S(2)}) async-start(), calls=%async_computation.14 | async-start | bytes 1622016 | tf_op jit(solution)/shard_map/all_gather | solution.py:236
  253.1 220.5 %all-gather.21.cloned.1.call-start = ((), (), s32[]{:S(2)}) async-start(), calls=%async_computation.19 | async-start | bytes 5242880 | tf_op jit(solution)/shard_map/all_gather | solution.py:286
  253.8 319.2 %reduce-scatter.24.cloned.1.call-start = ((), (), s32[]{:S(2)}) async-start(), calls=%async_computation.16 | async-start | bytes 5242880 | tf_op jit(solution)/shard_map/reduce_scatter | solution.py:302
  473.6 15.7 %copy-start.19 = (bf16[2,1024,704]{1,2,0:T(8,128)(2,1)S(1)}, bf16[2,1024,704]{1,2,0:T(8,128)(2,1)}, u32[]{:S(2)}) copy-start(bf16[2,1024,704]{1,2,0:T(8,128)(2,1)} %all-gather.15.cloned.1.call-done) | copy-start | bytes 8650756
  486.7 1.6 copy-start.20
  486.7 2.5 copy-start.21
  497.5 75.5 %copy-start.1 = (bf16[512,1024]{1,0:T(8,128)(2,1)S(1)}, bf16[512,1024]{1,0:T(8,128)(2,1)}, u32[]{:S(2)}) copy-start(bf16[512,1024]{1,0:T(8,128)(2,1)} %reduce-scatter.20.cloned.1.call-done) | copy-start | bytes 3145732
  497.5 78.3 %copy-start.2 = (bf16[1,512,1024]{2,1,0:T(8,128)(2,1)S(1)}, bf16[1,512,1024]{2,1,0:T(8,128)(2,1)}, u32[]{:S(2)}) copy-start(bf16[1,512,1024]{2,1,0:T(8,128)(2,1)} %param.20) | copy-start | bytes 3145732
  497.6 161.5 %all-gather.19.cloned.1.call-start = ((), (), s32[]{:S(2)}) async-start(), calls=%async_computation.17 | async-start | bytes 5242880 | tf_op jit(solution)/shard_map/all_gather | solution.py:316
  573.0 2.8 copy-start.3
  575.8 1.8 copy-start.13
  577.7 177.9 %reduce-scatter.34.cloned.1.call-start = ((), (), s32[]{:S(2)}) async-start(), calls=%async_computation.23 | async-start | bytes 1769472
  587.7 171.5 %reduce-scatter.32.cloned.1.call-start = ((), (), s32[]{:S(2)}) async-start(), calls=%async_computation.22 | async-start | bytes 3244032
  614.7 0.7 copy-start.11
  614.7 3.9 copy-start.12
  614.8 169.5 %reduce-scatter.30.cloned.1.call-start = ((), (), s32[]{:S(2)}) async-start(), calls=%async_computation.21 | async-start | bytes 589824
  677.8 148.8 %reduce-scatter.28.cloned.1.call-start = ((), (), s32[]{:S(2)}) async-start(), calls=%async_computation.20 | async-start | bytes 1769472
  734.0 171.6 %reduce-scatter.26.cloned.1.call-start = ((), (), s32[]{:S(2)}) async-start(), calls=%async_computation.18 | async-start | bytes 5242880 | tf_op jit(solution)/shard_map/reduce_scatter | solution.py:333
  741.9 243.1 %reduce-scatter.22.cloned.1.call-start = ((), (), s32[]{:S(2)}) async-start(), calls=%async_computation.15 | async-start | bytes 5242880 | tf_op jit(solution)/shard_map/reduce_scatter | solution.py:279
  749.9 1.0 copy-start.6
  749.9 272.7 %reduce-scatter.36.cloned.1.call-start = ((), (), s32[]{:S(2)}) async-start(), calls=%async_computation.24 | async-start | bytes 589824
  761.7 68.4 %copy-start.7 = (f32[3,128,256]{1,2,0:T(8,128)S(1)}, f32[3,128,256]{1,2,0:T(8,128)}, u32[]{:S(2)}) copy-start(f32[3,128,256]{1,2,0:T(8,128)} %copy.93) | copy-start | bytes 1179652
  832.5 75.0 %copy-start.15 = (f32[1024]{0:T(1024)S(1)}, f32[1024]{0:T(1024)}, u32[]{:S(2)}) copy-start(f32[1024]{0:T(1024)} %get-tuple-element.120) | copy-start | bytes 12292
  832.5 152.5 %copy-start.14 = (f32[512]{0:T(512)S(1)}, f32[512]{0:T(512)}, u32[]{:S(2)}) copy-start(f32[512]{0:T(512)} %copy-done.13) | copy-start | bytes 6148
  908.7 126.5 %copy-start.16 = (f32[2,128]{1,0:T(2,128)S(1)}, f32[2,128]{1,0:T(2,128)}, u32[]{:S(2)}) copy-start(f32[2,128]{1,0:T(2,128)} %param.35) | copy-start | bytes 3076
  908.7 126.5 %copy-start.17 = (f32[2,128]{1,0:T(2,128)S(1)}, f32[2,128]{1,0:T(2,128)}, u32[]{:S(2)}) copy-start(f32[2,128]{1,0:T(2,128)} %param.36) | copy-start | bytes 3076
  908.7 126.5 %copy-start.18 = (f32[2,128]{1,0:T(2,128)S(1)}, f32[2,128]{1,0:T(2,128)}, u32[]{:S(2)}) copy-start(f32[2,128]{1,0:T(2,128)} %param.37) | copy-start | bytes 3076
Sparse Core Ops, SparseCore 0:
  10.5 29.6 all-gather.10
  42.4 80.7 all-gather.8
  169.4 78.6 reduce-scatter.19
  250.4 32.0 all-gather.14
  284.4 80.7 all-gather.12
  367.5 23.6 all-gather.16
  392.8 80.7 all-gather.20
  497.7 75.2 reduce-scatter.23
  577.8 81.2 all-gather.18
  662.2 36.7 reduce-scatter.33
  702.4 44.7 reduce-scatter.31
  750.1 34.0 reduce-scatter.29
  788.1 38.3 reduce-scatter.27
  828.7 76.7 reduce-scatter.25
  907.6 77.2 reduce-scatter.21
  987.9 34.6 reduce-scatter.35

commit v2 on v1

v2 whole, which is shorter than its diff:
```python
import functools
import math

import jax
import jax.numpy as jnp
from jax import lax
from jax.experimental import pallas as pl
from jax.experimental.pallas import tpu as pltpu
from jax.sharding import PartitionSpec as P

HEAD = 64
ADAM_STEP = 5
LANES = 128


EPS_NORM = 1e-06
BETA_ONE = 0.9
BETA_TWO = 0.999
ADAM_EPS = 1e-08
DECAY_RATE = 0.1
RATES = (0.03, 0.5, 0.06, 0.04, 0.4)
NEG_FILL = -1e30
GELU_IN = 0.7978845608028654
GELU_CUBE = 0.044715


def rms_scale(values_in):
    return lax.rsqrt(jnp.mean(values_in * values_in, axis=-1, keepdims=True) + EPS_NORM)


def norm_back(d_normed, hat, scale, gain):
    scaled = gain * d_normed
    return scale * (scaled - hat * jnp.mean(scaled * hat, axis=-1, keepdims=True))


def adam_update(weight, moment, second, grad, step_rate, decay):
    moment_new = BETA_ONE * moment + (1.0 - BETA_ONE) * grad
    second_new = BETA_TWO * second + (1.0 - BETA_TWO) * grad * grad
    moment_hat = moment_new / (1.0 - BETA_ONE**ADAM_STEP)
    second_hat = second_new / (1.0 - BETA_TWO**ADAM_STEP)
    updated = weight - step_rate * (moment_hat / (jnp.sqrt(second_hat) + ADAM_EPS) + decay * weight)
    return (updated, updated.astype(jnp.bfloat16), moment_new, second_new)


NT = (((1,), (1,)), ((), ()))
NN = (((1,), (0,)), ((), ()))


def dot32(left, right, dims):
    return lax.dot_general(left, right, dims, preferred_element_type=jnp.float32)


def attend_kernel(lo_ref, hi_ref, q_ref, k_ref, v_ref, seg_q, seg_k, o_ref, lse_ref, vt_ref, *, bk, heads):
    i = pl.program_id(0)
    bq = q_ref.shape[0]

    @pl.when(i == 0)
    def _():
        vt_ref[...] = v_ref[...].T

    def body(j, carry):
        ks = pl.ds(pl.multiple_of(j * bk, bk), bk)
        same = seg_k[ks, :] == seg_q[...]
        out = []
        for h in range(heads):
            peak, total, acc = carry[h]
            hs = slice(h * HEAD, (h + 1) * HEAD)
            s = jnp.where(same, dot32(k_ref[ks, hs], q_ref[:, hs], NT), NEG_FILL)
            peak_new = jnp.maximum(peak, jnp.max(s, axis=0, keepdims=True))
            p = jnp.exp(s - peak_new)
            keep = jnp.exp(peak - peak_new)
            total = total * keep + jnp.sum(p, axis=0, keepdims=True)
            acc = acc * keep + dot32(vt_ref[hs, ks], p.astype(jnp.bfloat16), NN)
            out.append((peak_new, total, acc))
        return tuple(out)

    first = tuple(
        (
            jnp.full((1, bq), NEG_FILL, jnp.float32),
            jnp.zeros((1, bq), jnp.float32),
            jnp.zeros((HEAD, bq), jnp.float32),
        )
        for _ in range(heads)
    )
    found = lax.fori_loop(lo_ref[i], hi_ref[i], body, first)
    totals = [jnp.where(total > 0, total, 1.0) for _, total, _ in found]
    o_ref[...] = jnp.concatenate([acc / t for (_, _, acc), t in zip(found, totals)], axis=0).T
    lse_ref[...] = jnp.concatenate([peak + jnp.log(t) for (peak, _, _), t in zip(found, totals)], axis=0)


def attend(qkv, seg, lo, hi, bq, bk):
    rows, width = qkv.shape[0], qkv.shape[1] // 3
    heads = width // HEAD
    return pl.pallas_call(
        functools.partial(attend_kernel, bk=bk, heads=heads),
        out_shape=(
            jax.ShapeDtypeStruct((rows, width), jnp.float32),
            jax.ShapeDtypeStruct((heads, rows), jnp.float32),
        ),
        grid_spec=pltpu.PrefetchScalarGridSpec(
            num_scalar_prefetch=2,
            grid=(rows // bq,),
            in_specs=[
                pl.BlockSpec((bq, width), lambda i, *_: (i, 0)),
                pl.BlockSpec((rows, width), lambda i, *_: (0, 1)),
                pl.BlockSpec((rows, width), lambda i, *_: (0, 2)),
                pl.BlockSpec((1, bq), lambda i, *_: (0, i)),
                pl.BlockSpec((rows, 1), lambda i, *_: (0, 0)),
            ],
            out_specs=(
                pl.BlockSpec((bq, width), lambda i, *_: (i, 0)),
                pl.BlockSpec((heads, bq), lambda i, *_: (0, i)),
            ),
            scratch_shapes=[pltpu.VMEM((width, rows), jnp.bfloat16)],
        ),
        name="attend",
    )(lo, hi, qkv, qkv, qkv, seg[None, :], seg[:, None])


def attend_back_kernel(
    lo_ref, hi_ref, q_ref, do_ref, lse_ref, dot_ref, k_ref, v_ref, seg_q, seg_k,
    d_ref, dk_sum, dv_sum, kt_ref, *, bk, heads,
):
    i = pl.program_id(0)
    bq, width = q_ref.shape

    @pl.when(i == 0)
    def _():
        kt_ref[...] = k_ref[...].T
        dk_sum[...] = jnp.zeros_like(dk_sum)
        dv_sum[...] = jnp.zeros_like(dv_sum)

    def body(j, carry):
        ks = pl.ds(pl.multiple_of(j * bk, bk), bk)
        same = seg_k[ks, :] == seg_q[...]
        out, dks, dvs = [], [], []
        for h in range(heads):
            hs = slice(h * HEAD, (h + 1) * HEAD)
            qh = q_ref[:, hs]
            doh = do_ref[:, hs]
            s = dot32(k_ref[ks, hs], qh, NT)
            p = jnp.exp(jnp.where(same, s - lse_ref[h : h + 1, :], NEG_FILL))
            dp = dot32(v_ref[ks, hs], doh, NT)
            ds = (p * (dp - dot_ref[h : h + 1, :])).astype(jnp.bfloat16)
            dvs.append(dot32(p.astype(jnp.bfloat16), doh, NN))
            dks.append(dot32(ds, qh, NN))
            out.append(carry[h] + dot32(kt_ref[hs, ks], ds, NN))
        dk_sum[ks, :] += jnp.concatenate(dks, axis=1)
        dv_sum[ks, :] += jnp.concatenate(dvs, axis=1)
        return tuple(out)

    first = tuple(jnp.zeros((HEAD, bq), jnp.float32) for _ in range(heads))
    found = lax.fori_loop(lo_ref[i], hi_ref[i], body, first)
    d_ref[pl.ds(pl.multiple_of(i * bq, bq), bq), :width] = jnp.concatenate(found, axis=0).T.astype(d_ref.dtype)

    @pl.when(i == pl.num_programs(0) - 1)
    def _():
        d_ref[:, width : 2 * width] = dk_sum[...].astype(d_ref.dtype)
        d_ref[:, 2 * width :] = dv_sum[...].astype(d_ref.dtype)


def attend_back(qkv, d_out, lse, row_dot, seg, lo, hi, bq, bk):
    rows, width = d_out.shape
    heads = width // HEAD
    by_row = lambda i, *_: (i, 0)
    by_col = lambda i, *_: (0, i)
    return pl.pallas_call(
        functools.partial(attend_back_kernel, bk=bk, heads=heads),
        out_shape=jax.ShapeDtypeStruct((rows, 3 * width), jnp.bfloat16),
        grid_spec=pltpu.PrefetchScalarGridSpec(
            num_scalar_prefetch=2,
            grid=(rows // bq,),
            in_specs=[
                pl.BlockSpec((bq, width), by_row),
                pl.BlockSpec((bq, width), by_row),
                pl.BlockSpec((heads, bq), by_col),
                pl.BlockSpec((heads, bq), by_col),
                pl.BlockSpec((rows, width), lambda i, *_: (0, 1)),
                pl.BlockSpec((rows, width), lambda i, *_: (0, 2)),
                pl.BlockSpec((1, bq), by_col),
                pl.BlockSpec((rows, 1), lambda i, *_: (0, 0)),
            ],
            out_specs=pl.BlockSpec((rows, 3 * width), lambda i, *_: (0, 0)),
            scratch_shapes=[
                pltpu.VMEM((rows, width), jnp.float32),
                pltpu.VMEM((rows, width), jnp.float32),
                pltpu.VMEM((width, rows), jnp.bfloat16),
            ],
        ),
        name="attend_back",
    )(lo, hi, qkv, d_out, lse, row_dot, qkv, qkv, seg[None, :], seg[:, None])


def key_blocks(seg, length, bq, bk):
    lo = jnp.sum(seg[None, :] < seg[::bq][:, None], axis=1)
    hi = jnp.minimum(jnp.sum(seg[None, :] <= seg[bq - 1 :: bq][:, None], axis=1), length)
    lo = lo // bk
    hi = (hi + bk - 1) // bk
    dead = jnp.arange(seg.shape[0] // bq) * bq >= length
    return lo.astype(jnp.int32), jnp.where(dead, lo, hi).astype(jnp.int32)


TN = (((0,), (0,)), ((), ()))
PIECES = 8


def feed_kernel(spots, *refs, slices):
    n_ref, g_ref = refs[:2]
    w_in = [refs[2 + 4 * s : 6 + 4 * s] for s in range(slices)]
    at = 2 + 4 * slices
    out_ref, dn_ref = refs[at : at + 2]
    d_out = [refs[at + 2 + 4 * s : at + 6 + 4 * s] for s in range(slices)]
    w_buf, d_buf, w_sem, d_sem = refs[at + 2 + 4 * slices :]
    step = pl.program_id(0)
    slot = lax.rem(step, 2)

    def pieces(arrays, s, buf, sem, outward):
        held = s % 2
        for p in range(PIECES):
            lanes = pl.ds(pl.multiple_of(spots[s * PIECES + p] * LANES, LANES), LANES)
            far = arrays[p // 2].at[p % 2]
            near = buf.at[held, :, :, lanes]
            src, dst = (near, far) if outward else (far, near)
            yield pltpu.make_async_copy(src, dst, sem.at[held])

    for s in range(slices):

        @pl.when(step == s)
        def _(s=s):
            if s == 0:
                for first in range(min(2, slices)):
                    for copy in pieces(w_in[first], first, w_buf, w_sem, False):
                        copy.start()
            for copy in pieces(w_in[s], s, w_buf, w_sem, False):
                copy.wait()

    @pl.when(step == 0)
    def _():
        out_ref[...] = jnp.zeros_like(out_ref)
        dn_ref[...] = jnp.zeros_like(dn_ref)

    n = n_ref[...]
    g = g_ref[...]
    gate = dot32(n, w_buf[slot, 0], NT)
    up = dot32(n, w_buf[slot, 1], NT)
    d_hidden = dot32(g, w_buf[slot, 2], NT)
    square = gate * gate
    bent = jnp.tanh(gate * (GELU_IN + (GELU_IN * GELU_CUBE) * square))
    half = 0.5 + 0.5 * bent
    lifted = gate * half
    slope = half + (0.5 * gate) * (1.0 - bent * bent) * (GELU_IN + (3.0 * GELU_IN * GELU_CUBE) * square)
    hidden = (lifted * up).astype(jnp.bfloat16)
    d_gate = (d_hidden * up * slope).astype(jnp.bfloat16)
    d_up = (d_hidden * lifted).astype(jnp.bfloat16)
    out_ref[...] += dot32(hidden, w_buf[slot, 2], NN)
    dn_ref[...] += dot32(d_gate, w_buf[slot, 0], NN) + dot32(d_up, w_buf[slot, 1], NN)

    for s in range(2, slices):

        @pl.when(step == s)
        def _(s=s):
            for copy in pieces(d_out[s - 2], s - 2, d_buf, d_sem, True):
                copy.wait()

    d_buf[slot, 2] = dot32(hidden, g, TN).astype(jnp.bfloat16)
    d_buf[slot, 0] = dot32(d_gate, n, TN).astype(jnp.bfloat16)
    d_buf[slot, 1] = dot32(d_up, n, TN).astype(jnp.bfloat16)

    for s in range(slices):

        @pl.when(step == s)
        def _(s=s):
            for copy in pieces(d_out[s], s, d_buf, d_sem, True):
                copy.start()
            if s + 2 < slices:
                for copy in pieces(w_in[s + 2], s + 2, w_buf, w_sem, False):
                    copy.start()
            if s == slices - 1:
                for last in range(max(0, slices - 2), slices):
                    for copy in pieces(d_out[last], last, d_buf, d_sem, True):
                        copy.wait()


def feed(n, g, weights, spots):
    slices = len(weights)
    rows, width = n.shape
    hidden = weights[0][0].shape[2]
    whole = pl.BlockSpec((rows, width), lambda i, *_: (0, 0))
    there = pl.BlockSpec(memory_space=pl.ANY)
    acc = jax.ShapeDtypeStruct((rows, width), jnp.float32)
    part = jax.ShapeDtypeStruct((2, 3, hidden, LANES), jnp.bfloat16)
    found = pl.pallas_call(
        functools.partial(feed_kernel, slices=slices),
        out_shape=(acc, acc) + (part,) * (4 * slices),
        grid_spec=pltpu.PrefetchScalarGridSpec(
            num_scalar_prefetch=1,
            grid=(slices,),
            in_specs=[whole, whole] + [there] * (4 * slices),
            out_specs=(whole, whole) + (there,) * (4 * slices),
            scratch_shapes=[
                pltpu.VMEM((2, 3, hidden, width), jnp.bfloat16),
                pltpu.VMEM((2, 3, hidden, width), jnp.bfloat16),
                pltpu.SemaphoreType.DMA((2,)),
                pltpu.SemaphoreType.DMA((2,)),
            ],
        ),
        name="feed",
    )(spots, n, g, *[array for slice_ in weights for array in slice_])
    return found[0], found[1], [found[2 + 4 * s : 6 + 4 * s] for s in range(slices)]


def swap_over(axis, count, bit):
    return [(i, i ^ bit) for i in range(count)]


def spots_of(me, chip_bits):
    rows = []
    for first, second in chip_bits:
        rows += [0, first, second, first | second, 1, 1 | first, 1 | second, 1 | first | second]
    return jnp.bitwise_xor(me, jnp.array(rows, jnp.int32))


def gather_slice(piece, count, first, second):
    swap = lambda value, bit: lax.ppermute(value, "dp", swap_over("dp", count, bit))
    pair = jnp.stack([piece, swap(piece, first)])
    other = swap(pair, second)
    return [pair, other, swap(pair, 1), swap(other, 1)]


def scatter_slice(parts, count, first, second):
    swap = lambda value, bit: lax.ppermute(value, "dp", swap_over("dp", count, bit))
    low = lambda value: value.astype(jnp.bfloat16)
    wide = lambda value: value.astype(jnp.float32)
    away = low(wide(parts[1]) + wide(swap(parts[3], 1)))
    near = wide(parts[0]) + wide(swap(parts[2], 1))
    near = near + wide(swap(away, second))
    return near[0] + wide(swap(low(near[1]), first))


def on_device(
    inputs, cotangent, segment_ids, row_length,
    w_qkv, m_qkv, v_qkv, w_out, m_out, v_out, w_gate_up, m_gate_up, v_gate_up, w_down, m_down, v_down,
    norm_gains, m_gains, v_gains,
    *, dp, mp,
):
    f32, bf16 = jnp.float32, jnp.bfloat16
    z = lax.axis_index("mp")
    me = lax.axis_index("dp")
    onward = [(i, (i + 1) % mp) for i in range(mp)]
    ring = lambda value: lax.ppermute(value, "mp", onward)
    rows, width = inputs.shape[1:]
    seq_len = segment_ids.shape[1]
    hidden_here = w_down.shape[0]
    lanes_here = w_down.shape[1]
    heads_width = w_out.shape[0]
    exchange = dp == PIECES and lanes_here == LANES

    copy_qkv = w_qkv.astype(bf16).transpose(0, 2, 1).reshape(3 * heads_width, lanes_here)
    copy_out = w_out.astype(bf16)
    copy_feed = jnp.concatenate([w_gate_up.astype(bf16).transpose(0, 2, 1), w_down.astype(bf16)[None]])
    copy_gains = jnp.pad(norm_gains.astype(bf16), ((0, 14), (0, 0)))

    blocks = [inputs[0]]
    for _ in range(mp - 1):
        blocks.append(ring(blocks[-1]))

    full_first = lax.all_gather(jnp.concatenate([copy_qkv, copy_gains]), "dp", axis=1, tiled=True)
    full_qkv = full_first[: 3 * heads_width]
    gain_one = full_first[3 * heads_width].astype(f32)
    gain_two = full_first[3 * heads_width + 1].astype(f32)
    full_out = lax.all_gather(copy_out, ("dp", "mp"), axis=0)
    full_out = full_out.reshape(dp, mp, heads_width, lanes_here).transpose(1, 2, 0, 3).reshape(mp * heads_width, width)

    copy_feed, _ = lax.optimization_barrier((copy_feed, blocks[-1]))
    feed_own = [copy_feed]
    for _ in range(mp - 1):
        feed_own.append(ring(feed_own[-1]))
    if exchange:
        chip_bits = [(2, 4) if s % 2 == 0 else (4, 2) for s in range(mp)]
        feed_full = [gather_slice(piece, dp, *bits) for piece, bits in zip(feed_own, chip_bits)]
        spots = spots_of(me, chip_bits)
    else:
        chip_bits = [(2, 4)] * mp
        spots = spots_of(0, chip_bits)
        turn = jnp.array([0, 2, 4, 6, 1, 3, 5, 7])
        feed_full = []
        for piece in feed_own:
            whole = lax.all_gather(piece, "dp", axis=2, tiled=True)
            whole = whole.reshape(3, hidden_here, PIECES, LANES).transpose(2, 0, 1, 3)[turn]
            feed_full.append([whole[2 * i : 2 * i + 2] for i in range(4)])

    seg_row = segment_ids[0]
    live_row = jnp.arange(seq_len, dtype=jnp.int32) < row_length[0]
    live = live_row.astype(f32)[:, None]

    resid_in = inputs[0].astype(f32)
    scale_one = rms_scale(resid_in)
    hat_one = resid_in * scale_one
    hats = []
    normed_one = jnp.zeros((seq_len, width), bf16)
    for s, block in enumerate(blocks):
        block = block.astype(f32)
        hats.append(block * rms_scale(block))
        at = lax.rem(z + mp - s, mp) * rows
        normed_one = lax.dynamic_update_slice(normed_one, (hats[-1] * gain_one).astype(bf16), (at, 0))
    qkv = dot32(normed_one, full_qkv, NT).astype(bf16)

    wide, narrow = min(1024, seq_len), min(512, seq_len)
    lo, hi = key_blocks(seg_row, row_length[0], wide, narrow)
    raw_out, log_sums = attend(qkv, seg_row, lo, hi, wide, narrow)
    log_sums = jnp.where(live_row[None, :], log_sums, -NEG_FILL)
    attended = (raw_out * live).astype(bf16)
    attended = lax.all_to_all(attended, "mp", split_axis=0, concat_axis=1, tiled=True)

    after_attn = resid_in + dot32(attended, full_out, NN)
    scale_two = rms_scale(after_attn)
    hat_two = after_attn * scale_two
    normed_two = (hat_two * gain_two).astype(bf16)

    fed, d_normed_two, d_feed = [], [], []
    for start in range(0, mp, 2):
        stop = min(start + 2, mp)
        out_part, d_part, grads = feed(
            normed_two, cotangent[0], feed_full[start:stop], spots[PIECES * start : PIECES * stop]
        )
        fed.append(out_part)
        d_normed_two.append(d_part)
        d_feed += grads
    block_output = after_attn + functools.reduce(jnp.add, fed)
    d_normed_two = functools.reduce(jnp.add, d_normed_two)
    d_after = cotangent[0].astype(f32) + norm_back(d_normed_two, hat_two, scale_two, gain_two)
    grad_gain_two = jnp.sum(d_normed_two * hat_two, axis=0)

    d_branch = d_after.astype(bf16)
    d_attended = dot32(d_branch, full_out, NT).astype(bf16)
    d_attended = lax.all_to_all(d_attended, "mp", split_axis=1, concat_axis=0, tiled=True)
    d_attended = jnp.where(live_row[:, None], d_attended, jnp.zeros((), bf16))
    grad_out = dot32(attended, d_branch, TN).astype(bf16)
    grad_out = lax.psum_scatter(grad_out, "dp", scatter_dimension=1, tiled=True)
    grad_out = lax.psum_scatter(grad_out, "mp", scatter_dimension=0, tiled=True).astype(f32)

    row_dot = jnp.sum((raw_out * d_attended).reshape(seq_len, heads_width // HEAD, HEAD), axis=-1).T
    lo, hi = key_blocks(seg_row, row_length[0], narrow, narrow)
    d_qkv = attend_back(qkv, d_attended, log_sums, row_dot, seg_row, lo, hi, narrow, narrow)

    total = None
    grad_gain_one = jnp.zeros((width,), f32)
    for s in [*range(1, mp), 0]:
        at = lax.rem(z + mp - s, mp) * rows
        part = dot32(lax.dynamic_slice(d_qkv, (at, 0), (rows, d_qkv.shape[1])), full_qkv, NN)
        grad_gain_one = grad_gain_one + jnp.sum(part * hats[s], axis=0)
        total = part if total is None else ring(total.astype(bf16)).astype(f32) + part
    d_normed_one = total
    input_grad = d_after + norm_back(d_normed_one, hat_one, scale_one, gain_one)

    grad_qkv = dot32(d_qkv, normed_one, TN).astype(bf16)
    grad_qkv = lax.psum_scatter(grad_qkv, "dp", scatter_dimension=1, tiled=True).astype(f32)
    grad_qkv = grad_qkv.reshape(3, heads_width, lanes_here).transpose(0, 2, 1)

    if exchange:
        owned = [scatter_slice(parts, dp, *bits) for parts, bits in zip(d_feed, chip_bits)]
    else:
        back = jnp.array([0, 4, 1, 5, 2, 6, 3, 7])
        owned = []
        for parts in d_feed:
            whole = jnp.concatenate(parts)[back].transpose(1, 2, 0, 3).reshape(3, hidden_here, width)
            owned.append(lax.psum_scatter(whole, "dp", scatter_dimension=2, tiled=True).astype(f32))
    total = owned[1]
    for s in [*range(2, mp), 0]:
        total = ring(total.astype(bf16)).astype(f32) + owned[s]
    grad_gate_up = total[:2].transpose(0, 2, 1)
    grad_down = total[2]

    grad_gains = jnp.stack([grad_gain_one, grad_gain_two])
    for axis, count in (("mp", mp), ("dp", dp)):
        bit = 1
        while bit < count:
            grad_gains = grad_gains + lax.ppermute(grad_gains, axis, swap_over(axis, count, bit))
            bit *= 2
    grad_gains = lax.dynamic_slice(grad_gains, (0, me * lanes_here), (2, lanes_here))

    new_qkv = adam_update(w_qkv, m_qkv, v_qkv, grad_qkv, RATES[0], DECAY_RATE)
    new_out = adam_update(w_out, m_out, v_out, grad_out, RATES[1], DECAY_RATE)
    new_gate_up = adam_update(w_gate_up, m_gate_up, v_gate_up, grad_gate_up, RATES[2], DECAY_RATE)
    new_down = adam_update(w_down, m_down, v_down, grad_down, RATES[3], DECAY_RATE)
    new_gains = adam_update(norm_gains, m_gains, v_gains, grad_gains, RATES[4], 0.0)
    return (block_output[None], input_grad[None], *new_qkv, *new_out, *new_gate_up, *new_down, *new_gains)


def solution(mesh):
    tokens = P("dp", "mp", None)
    stacked = P(None, "dp", "mp")
    flat = P("mp", "dp")
    gains = P(None, "dp")
    return jax.shard_map(
        functools.partial(on_device, dp=mesh.shape["dp"], mp=mesh.shape["mp"]),
        mesh=mesh,
        in_specs=(tokens, tokens, P("dp", None), P("dp"))
        + (stacked,) * 3 + (flat,) * 3 + (stacked,) * 3 + (flat,) * 3 + (gains,) * 3,
        out_specs=(tokens, tokens) + (stacked,) * 4 + (flat,) * 4 + (stacked,) * 4 + (flat,) * 4 + (gains,) * 4,
        check_vma=False,
    )
```

time: 1050 us -> 583 us (0.56)
  waiting for transfers between devices: 718 us -> 225 us
  starting transfers between devices: 1.76 us -> 97.9 us
  matrix products: 96.5 us -> 26.3 us
  Pallas kernels: 72.4 us -> 112 us
  blocking collectives: 33.5 us -> 0 us
  other arithmetic: 38.7 us -> 71.9 us
  local copies, waits for them, and re-layouts: 67 us -> 35.3 us
    all_gather x7 -> x2, waiting for transfers between devices: 332 us -> 0.02 us  [the longest x1 0.02 us: on_device(): lax.all_gather(jnp.concatenate([copy_qkv, copy_gains]), 'dp', axis=1, til...]
    reduce_scatter x4 -> x1, waiting for transfers between devices: 293 us -> 28.6 us  [on_device(): lax.psum_scatter(grad_out, 'mp', scatter_dimension=0, tiled=True)]
    ppermute x0 -> x49, waiting for transfers between devices: none -> 172 us  [the longest x12 99.4 us: on_device(): ring = lambda value: lax.ppermute(value, 'mp', onward)]
    ppermute x0 -> x49, starting transfers between devices: none -> 86.2 us  [the longest x16 46.1 us: scatter_slice(): lax.ppermute(value, 'dp', swap_over('dp', count, bit))]
    dot_general x12 -> x9, matrix products: 96.5 us -> 26.3 us  [dot32(): lax.dot_general(left, right, dims, preferred_element_type=jnp.float32)]
    unnamed x21 -> x7, waiting for transfers between devices: 92 us -> 23.5 us
    pallas_call x0 -> x2, Pallas kernels: none -> 48.1 us  [feed(): pl.pallas_call(functools.partial(feed_kernel, slices=slices), out_shape=(...]
    unnamed x65 -> x121, local copies, waits for them, and re-layouts: 56.4 us -> 16.7 us
  transfers between devices with their start and end apart: 16 -> 56, of which waited for: 14 -> 17; matrix products, arithmetic and copies ran while one was open for 15% -> 21% of each run, Pallas kernels for 4% -> 19%
where the time goes in v2:
time: 583 us
  waiting for transfers between devices  225 us (39%)
  Pallas kernels  112 us (19%)
  starting transfers between devices  97.9 us (17%)
  other arithmetic  71.9 us (12%)
  local copies, waits for them, and re-layouts  35.3 us (6%)
  matrix products  26.3 us (5%)
  between operations  15.7 us (3%)
    ppermute x12, waiting for transfers between devices, on_device(): ring = lambda value: lax.ppermute(value, 'mp', onward)  99.4 us
    pallas_call x2, Pallas kernels, feed(): pl.pallas_call(functools.partial(feed_kernel, slices=slices), out_shape=(...  48.1 us
    ppermute x16, starting transfers between devices, scatter_slice(): lax.ppermute(value, 'dp', swap_over('dp', count, bit))  46.1 us
    ppermute x16, waiting for transfers between devices, gather_slice(): lax.ppermute(value, 'dp', swap_over('dp', count, bit))  41.2 us
    pallas_call x1, Pallas kernels, attend_back(): pl.pallas_call(functools.partial(attend_back_kernel, bk=bk, heads=heads),...  35.4 us
    ppermute x16, starting transfers between devices, gather_slice(): lax.ppermute(value, 'dp', swap_over('dp', count, bit))  29.2 us
    reduce_scatter x1, waiting for transfers between devices, on_device(): lax.psum_scatter(grad_out, 'mp', scatter_dimension=0, tiled=True)  28.6 us
    ppermute x16, waiting for transfers between devices, scatter_slice(): lax.ppermute(value, 'dp', swap_over('dp', count, bit))  28.6 us
  transfers between devices with their start and end apart: 56, of which 17 were waited for; matrix products, arithmetic and copies ran while one was open for 21% of the time, Pallas kernels for 19%

profile of v2, /device:TPU:0, one launch (start us, length us, event | category | flops | bytes accessed | tf_op | source)
XLA Modules:
  0.0 583.4 jit_solution(2279594669686663818)
XLA Ops:
  9.9 3.1 collective-permute-start
  19.7 18.8 %collective-permute-done = bf16[512,1024]{1,0:T(8,128)(2,1)S(1)} collective-permute-done((bf16[512,1024]{1,0:T(8,128)(2,1)}, bf16[512,1024]{1,0:T(8,128)(2,1)S(1)}, u32[]{:S(2)}, u32[]{:S(2)}) %collective-permute-start) | collective-permute-done | bytes 1048608 | tf_op jit(solution)/shard_map/ppermute | solution.py:350
  40.9 25.0 %collective-permute-done.1 = bf16[512,1024]{1,0:T(8,128)(2,1)S(1)} collective-permute-done((bf16[512,1024]{1,0:T(8,128)(2,1)S(1)}, bf16[512,1024]{1,0:T(8,128)(2,1)S(1)}, u32[]{:S(2)}, u32[]{:S(2)}) %collective-permute-start.1) | collective-permute-done | bytes 1048608 | tf_op jit(solution)/shard_map/ppermute | solution.py:350
  69.6 24.8 %collective-permute-done.2 = bf16[512,1024]{1,0:T(8,128)(2,1)S(1)} collective-permute-done((bf16[512,1024]{1,0:T(8,128)(2,1)S(1)}, bf16[512,1024]{1,0:T(8,128)(2,1)S(1)}, u32[]{:S(2)}, u32[]{:S(2)}) %collective-permute-start.2) | collective-permute-done | bytes 1048608 | tf_op jit(solution)/shard_map/ppermute | solution.py:350
  96.0 16.5 %collective-permute-done.7 = bf16[3,704,128]{2,1,0:T(8,128)(2,1)} collective-permute-done((bf16[3,704,128]{2,1,0:T(8,128)(2,1)}, bf16[3,704,128]{2,1,0:T(8,128)(2,1)}, u32[]{:S(2)}, u32[]{:S(2)}) %collective-permute-start.7) | collective-permute-done | bytes 540704 | tf_op jit(solution)/shard_map/ppermute | solution.py:350
  112.6 4.9 convolution_convert_fusion.q_ref.k_ref.v_ref
  117.5 28.1 %attend.1 = (f32[2048,256]{1,0:T(8,128)}, f32[4,2048]{1,0:T(4,128)}) custom-call(s32[2]{0:T(128)} %get-tuple-element.101.lo_ref, s32[2]{0:T(128)} %get-tuple-element.100.hi_ref, bf16[2048,768]{1,0:T(8,128)(2,1)} %convolution_convert_fusion.q_ref.k_ref.v_ref, bf16[2048,768]{1,0:T(8,128)(2,1)} %convolution_convert_fusion.q_ref.k_ref.v_ref, ...), custom_call_target="tpu_custom_call" | custom-call | tf_op jit(solution)/shard_map/attend/pallas_call | solution.py:94
  147.9 5.8 collective-permute-start.4
  155.4 6.2 %all-to-all-start = ((bf16[4,512,256]{1,2,0:T(8,128)(2,1)}), bf16[4,512,256]{1,2,0:T(8,128)(2,1)S(1)}, u32[]{:S(2)}, u32[]{:S(2)}) async-start(bf16[4,512,256]{1,2,0:T(8,128)(2,1)} %copy.62), calls=%async_computation | async-start | bytes 2097152 | tf_op jit(solution)/shard_map/all_to_all | solution.py:413
  161.7 6.3 %collective-permute-start.13 = (bf16[3,704,128]{2,1,0:T(8,128)(2,1)}, bf16[3,704,128]{2,1,0:T(8,128)(2,1)}, u32[]{:S(2)}, u32[]{:S(2)}) collective-permute-start(bf16[3,704,128]{2,1,0:T(8,128)(2,1)} %collective-permute-done.12), channel_id=1, source_target_pairs={{0,8},{4,12},{8,0},{12,4},{16,24},{20,28},{24,16},{28,20},{1,9},{5... | collective-permute-start | bytes 1622024 | tf_op jit(solution)/shard_map/ppermute | solution.py:324
  168.0 3.1 collective-permute-done.17
  171.1 1.9 collective-permute-start.18
  173.0 17.0 %collective-permute-done.8 = bf16[3,704,128]{2,1,0:T(8,128)(2,1)} collective-permute-done((bf16[3,704,128]{2,1,0:T(8,128)(2,1)}, bf16[3,704,128]{2,1,0:T(8,128)(2,1)}, u32[]{:S(2)}, u32[]{:S(2)}) %collective-permute-start.8) | collective-permute-done | bytes 540704 | tf_op jit(solution)/shard_map/ppermute | solution.py:324
  190.1 2.3 pad_maximum_fusion.1.refs_6_
  192.4 6.4 %collective-permute-start.9 = (bf16[2,3,704,128]{3,2,1,0:T(8,128)(2,1)}, bf16[2,3,704,128]{3,2,1,0:T(8,128)(2,1)}, u32[]{:S(2)}, u32[]{:S(2)}) collective-permute-start(bf16[2,3,704,128]{3,2,1,0:T(8,128)(2,1)} %pad_maximum_fusion.1.refs_6_), channel_id=1, source_target_pairs={{0,8},{4,12},{8,0},{12,4},{16,24},{20,28},{24,16},{28,20},{1,9},{5... | collective-permute-start | bytes 3244040 | tf_op jit(solution)/shard_map/ppermute | solution.py:324
  199.2 2.4 pad_maximum_fusion.2.refs_2_
  202.2 2.3 pad_maximum_fusion.3.refs_6_
  204.5 5.9 %collective-permute-start.19 = (bf16[2,3,704,128]{3,2,1,0:T(8,128)(2,1)}, bf16[2,3,704,128]{3,2,1,0:T(8,128)(2,1)}, u32[]{:S(2)}, u32[]{:S(2)}) collective-permute-start(bf16[2,3,704,128]{3,2,1,0:T(8,128)(2,1)} %pad_maximum_fusion.3.refs_6_), channel_id=1, source_target_pairs={{0,8},{4,12},{8,0},{12,4},{16,24},{20,28},{24,16},{28,20},{1,9},{5... | collective-permute-start | bytes 3244040 | tf_op jit(solution)/shard_map/ppermute | solution.py:324
  210.9 12.9 %collective-permute-done.9.refs_7_ = bf16[2,3,704,128]{3,2,1,0:T(8,128)(2,1)} collective-permute-done((bf16[2,3,704,128]{3,2,1,0:T(8,128)(2,1)}, bf16[2,3,704,128]{3,2,1,0:T(8,128)(2,1)}, u32[]{:S(2)}, u32[]{:S(2)}) %collective-permute-start.9) | collective-permute-done | bytes 1081376 | tf_op jit(solution)/shard_map/ppermute | solution.py:324
  224.3 4.3 copy.63
  229.7 3.3 multiply_reduce_fusion.2
  234.1 11.2 %collective-permute-done.19.refs_7_ = bf16[2,3,704,128]{3,2,1,0:T(8,128)(2,1)} collective-permute-done((bf16[2,3,704,128]{3,2,1,0:T(8,128)(2,1)}, bf16[2,3,704,128]{3,2,1,0:T(8,128)(2,1)}, u32[]{:S(2)}, u32[]{:S(2)}) %collective-permute-start.19) | collective-permute-done | bytes 1081376 | tf_op jit(solution)/shard_map/ppermute | solution.py:324
  246.5 24.1 %feed.2 = (f32[512,1024]{1,0:T(8,128)}, f32[512,1024]{1,0:T(8,128)}, bf16[2,3,704,128]{3,2,1,0:T(8,128)(2,1)}, bf16[2,3,704,128]{3,2,1,0:T(8,128)(2,1)}, bf16[2,...) custom-call(s32[16]{0:T(128)} %get-tuple-element.113.spots, ...), custom_call_target="tpu_custom_call" | custom-call | tf_op jit(solution)/shard_map/feed/pallas_call | solution.py:292
  272.4 24.1 %feed.3 = (f32[512,1024]{1,0:T(8,128)}, f32[512,1024]{1,0:T(8,128)}, bf16[2,3,704,128]{3,2,1,0:T(8,128)(2,1)}, bf16[2,3,704,128]{3,2,1,0:T(8,128)(2,1)}, bf16[2,...) custom-call(s32[16]{0:T(128)} %get-tuple-element.112.spots, ...), custom_call_target="tpu_custom_call" | custom-call | tf_op jit(solution)/shard_map/feed/pallas_call | solution.py:292
  297.0 3.0 multiply_reduce_fusion
  300.0 3.0 add_convert_fusion.3
  303.1 1.7 collective-permute-start.27
  304.9 2.2 multiply_add_fusion
  311.4 5.1 all-to-all-start.1
  316.5 2.5 copy.70
  321.9 7.3 %collective-permute-done.27 = bf16[2,3,704,128]{3,2,1,0:T(8,128)(2,1)} collective-permute-done((bf16[2,3,704,128]{3,2,1,0:T(8,128)(2,1)}, bf16[2,3,704,128]{3,2,1,0:T(8,128)(2,1)}, u32[]{:S(2)}, u32[]{:S(2)}) %collective-permute-start.27) | collective-permute-done | bytes 1081376 | tf_op jit(solution)/shard_map/ppermute | solution.py:331
  329.8 2.1 convert_add_fusion.4
  332.8 2.9 add_convert_fusion.2
  338.6 1.7 collective-permute-start.37
  340.4 21.2 %collective-permute-done.42 = bf16[2,3,704,128]{3,2,1,0:T(8,128)(2,1)S(1)} collective-permute-done((bf16[2,3,704,128]{3,2,1,0:T(8,128)(2,1)S(1)}, bf16[2,3,704,128]{3,2,1,0:T(8,128)(2,1)S(1)}, u32[]{:S(2)}, u32[]{:S(2)}) %collective-permute-start.42) | collective-permute-done | bytes 1081376 | tf_op jit(solution)/shard_map/ppermute | solution.py:331
  362.1 3.2 convert_add_fusion.1
  365.3 2.9 convert_multiply_fusion.8
  368.3 1.9 copy.65
  371.0 35.4 %attend_back.1 = bf16[2048,768]{1,0:T(8,128)(2,1)} custom-call(s32[4]{0:T(128)} %get-tuple-element.99.lo_ref, s32[4]{0:T(128)} %get-tuple-element.98.hi_ref, bf16[2048,768]{1,0:T(8,128)(2,1)} %convolution_convert_fusion.q_ref.k_ref.v_ref, bf16[2048,256]{1,0:T(8,128)(2,1)} %get-tuple-element.97.do_ref, f32[4,2048]{1,0:T(4,128)} %broadcast_select_fusion.lse_ref, ...), custom_call_target="tpu_custom_call" | custom-call | tf_op jit(solution)/shard_map/attend_back/pallas_call | solution.py:167
  406.4 2.8 fusion.15
  412.5 2.0 convert_add_fusion.3
  414.5 19.1 %collective-permute-start.33 = (bf16[3,704,128]{2,1,0:T(8,128)(2,1)S(1)}, bf16[3,704,128]{2,1,0:T(8,128)(2,1)S(1)}, u32[]{:S(2)}, u32[]{:S(2)}) collective-permute-start(bf16[3,704,128]{2,1,0:T(8,128)(2,1)S(1)} %fusion.67), channel_id=1, source_target_pairs={{0,8},{4,12},{8,0},{12,4},{16,24},{20,28},{24,16},{28,20},{1,9},{5... | collective-permute-start | bytes 1622024 | tf_op jit(solution)/shard_map/ppermute | solution.py:331
  433.7 2.0 convert_add_fusion.2
  438.9 3.9 collective-permute-start.23
  442.7 7.2 %collective-permute-done.29 = bf16[3,704,128]{2,1,0:T(8,128)(2,1)S(1)} collective-permute-done((bf16[3,704,128]{2,1,0:T(8,128)(2,1)S(1)}, bf16[3,704,128]{2,1,0:T(8,128)(2,1)S(1)}, u32[]{:S(2)}, u32[]{:S(2)}) %collective-permute-start.29) | collective-permute-done | bytes 540704 | tf_op jit(solution)/shard_map/ppermute | solution.py:350
  451.0 2.1 fusion.69
  453.1 19.0 %collective-permute-start.43 = (bf16[3,704,128]{2,1,0:T(8,128)(2,1)}, bf16[3,704,128]{2,1,0:T(8,128)(2,1)}, u32[]{:S(2)}, u32[]{:S(2)}) collective-permute-start(bf16[3,704,128]{2,1,0:T(8,128)(2,1)} %fusion.69), channel_id=1, source_target_pairs={{0,8},{4,12},{8,0},{12,4},{16,24},{20,28},{24,16},{28,20},{1,9},{5... | collective-permute-start | bytes 1622024 | tf_op jit(solution)/shard_map/ppermute | solution.py:331
  472.1 2.3 fusion.54
  474.4 1.9 copy.71
  476.4 3.5 collective-permute-done.34
  479.9 2.7 fusion.42
  482.8 3.5 fusion.11
  486.5 4.5 convolution_convert_fusion.2
  491.1 2.7 copy.68
  493.9 28.6 %reduce-scatter.8.cloned.1.call-done = bf16[256,128]{1,0:T(8,128)(2,1)} async-done(((bf16[1024,128]{1,0:T(8,128)(2,1)}), bf16[256,128]{1,0:T(8,128)(2,1)}) %reduce-scatter.8.cloned.1.call-update) | async-done | bytes 65552 | tf_op jit(solution)/shard_map/reduce_scatter | solution.py:440
  522.5 1.9 fusion.95
  525.8 5.0 fusion.25
  530.9 1.8 fusion.93
  532.8 1.8 collective-permute-done.44
  536.4 23.5 %reduce-scatter.10.cloned.1.call-done = bf16[128,768]{1,0:T(8,128)(2,1)} async-done(((bf16[1024,768]{1,0:T(8,128)(2,1)}), bf16[128,768]{1,0:T(8,128)(2,1)}) %reduce-scatter.10.cloned.1.call-update) | async-done | bytes 196624
  559.9 1.7 copy.69
  561.6 1.8 copy.67
  564.2 2.5 fusion.98
  571.9 3.8 fusion.24
  (269 shorter events, 58.8 us)
Async XLA Ops:
  7.2 59.1 %all-gather.4.cloned.1.call-start = ((), (), s32[]{:S(2)}) async-start(), calls=%async_computation.5 | async-start | bytes 1806336 | tf_op jit(solution)/shard_map/all_gather | solution.py:367
  9.9 214.4 %all-gather.6.cloned.1.call-start = ((), (), s32[]{:S(2)}) async-start(), calls=%async_computation.7 | async-start | bytes 2162688 | tf_op jit(solution)/shard_map/all_gather | solution.py:371
  9.9 28.5 %collective-permute-start = (bf16[512,1024]{1,0:T(8,128)(2,1)}, bf16[512,1024]{1,0:T(8,128)(2,1)S(1)}, u32[]{:S(2)}, u32[]{:S(2)}) collective-permute-start(bf16[512,1024]{1,0:T(8,128)(2,1)} %bitcast.140), channel_id=1, source_target_pairs={{0,1},{1,2},{2,3},{3,0},{4,5},{5,6},{6,7},{7,4},{8,9},{9,10},{10,1... | collective-permute-start | bytes 3145736 | tf_op jit(solution)/shard_map/ppermute | solution.py:350
  38.5 27.5 %collective-permute-start.1 = (bf16[512,1024]{1,0:T(8,128)(2,1)S(1)}, bf16[512,1024]{1,0:T(8,128)(2,1)S(1)}, u32[]{:S(2)}, u32[]{:S(2)}) collective-permute-start(bf16[512,1024]{1,0:T(8,128)(2,1)S(1)} %collective-permute-done), channel_id=1, source_target_pairs={{0,1},{1,2},{2,3},{3,0},{4,5},{5,6},{6,7},{7,4},{8,9},{9,10},{10,1... | collective-permute-start | bytes 3145736 | tf_op jit(solution)/shard_map/ppermute | solution.py:350
  66.3 28.1 %collective-permute-start.2 = (bf16[512,1024]{1,0:T(8,128)(2,1)S(1)}, bf16[512,1024]{1,0:T(8,128)(2,1)S(1)}, u32[]{:S(2)}, u32[]{:S(2)}) collective-permute-start(bf16[512,1024]{1,0:T(8,128)(2,1)S(1)} %collective-permute-done.1), channel_id=1, source_target_pairs={{0,1},{1,2},{2,3},{3,0},{4,5},{5,6},{6,7},{7,4},{8,9},{9,10},{10,1... | collective-permute-start | bytes 3145736 | tf_op jit(solution)/shard_map/ppermute | solution.py:350
  69.6 43.0 %copy-start.54 = (bf16[784,1024]{1,0:T(8,128)(2,1)S(1)}, bf16[784,1024]{1,0:T(8,128)(2,1)}, u32[]{:S(2)}) copy-start(bf16[784,1024]{1,0:T(8,128)(2,1)} %all-gather.4.cloned.1.call-done) | copy-start | bytes 4816900
  94.3 18.2 %collective-permute-start.7 = (bf16[3,704,128]{2,1,0:T(8,128)(2,1)}, bf16[3,704,128]{2,1,0:T(8,128)(2,1)}, u32[]{:S(2)}, u32[]{:S(2)}) collective-permute-start(bf16[3,704,128]{2,1,0:T(8,128)(2,1)} %pad_maximum_fusion.4), channel_id=1, source_target_pairs={{0,1},{1,2},{2,3},{3,0},{4,5},{5,6},{6,7},{7,4},{8,9},{9,10},{10,1... | collective-permute-start | bytes 1622024 | tf_op jit(solution)/shard_map/ppermute | solution.py:350
  94.3 51.3 %collective-permute-start.3 = (bf16[3,704,128]{2,1,0:T(8,128)(2,1)}, bf16[3,704,128]{2,1,0:T(8,128)(2,1)S(1)}, u32[]{:S(2)}, u32[]{:S(2)}) collective-permute-start(bf16[3,704,128]{2,1,0:T(8,128)(2,1)} %pad_maximum_fusion.4), channel_id=1, source_target_pairs={{0,8},{4,12},{8,0},{12,4},{16,24},{20,28},{24,16},{28,20},{1,9},{5... | collective-permute-start | bytes 1622024 | tf_op jit(solution)/shard_map/ppermute | solution.py:324
  112.6 41.2 %collective-permute-start.12 = (bf16[3,704,128]{2,1,0:T(8,128)(2,1)}, bf16[3,704,128]{2,1,0:T(8,128)(2,1)}, u32[]{:S(2)}, u32[]{:S(2)}) collective-permute-start(bf16[3,704,128]{2,1,0:T(8,128)(2,1)} %collective-permute-done.7), channel_id=1, source_target_pairs={{0,1},{1,2},{2,3},{3,0},{4,5},{5,6},{6,7},{7,4},{8,9},{9,10},{10,1... | collective-permute-start | bytes 1622024 | tf_op jit(solution)/shard_map/ppermute | solution.py:350
  147.8 56.7 %collective-permute-start.5 = (bf16[2,3,704,128]{3,2,1,0:T(8,128)(2,1)S(1)}, bf16[2,3,704,128]{3,2,1,0:T(8,128)(2,1)}, u32[]{:S(2)}, u32[]{:S(2)}) collective-permute-start(bf16[2,3,704,128]{3,2,1,0:T(8,128)(2,1)S(1)} %pad_maximum_fusion.refs_2_), channel_id=1, source_target_pairs={{0,4},{4,0},{8,12},{12,8},{16,20},{20,16},{24,28},{28,24},{1,5},{5... | collective-permute-start | bytes 3244040 | tf_op jit(solution)/shard_map/ppermute | solution.py:324
  147.9 53.7 %collective-permute-start.4 = (bf16[2,3,704,128]{3,2,1,0:T(8,128)(2,1)S(1)}, bf16[2,3,704,128]{3,2,1,0:T(8,128)(2,1)}, u32[]{:S(2)}, u32[]{:S(2)}) collective-permute-start(bf16[2,3,704,128]{3,2,1,0:T(8,128)(2,1)S(1)} %pad_maximum_fusion.refs_2_), channel_id=1, source_target_pairs={{0,16},{4,20},{8,24},{12,28},{16,0},{20,4},{24,8},{28,12},{1,17},{... | collective-permute-start | bytes 3244040 | tf_op jit(solution)/shard_map/ppermute | solution.py:324
  153.7 36.4 %collective-permute-start.8 = (bf16[3,704,128]{2,1,0:T(8,128)(2,1)}, bf16[3,704,128]{2,1,0:T(8,128)(2,1)}, u32[]{:S(2)}, u32[]{:S(2)}) collective-permute-start(bf16[3,704,128]{2,1,0:T(8,128)(2,1)} %collective-permute-done.7), channel_id=1, source_target_pairs={{0,16},{4,20},{8,24},{12,28},{16,0},{20,4},{24,8},{28,12},{1,17},{... | collective-permute-start | bytes 1622024 | tf_op jit(solution)/shard_map/ppermute | solution.py:324
  153.7 17.4 %collective-permute-start.17 = (bf16[3,704,128]{2,1,0:T(8,128)(2,1)}, bf16[3,704,128]{2,1,0:T(8,128)(2,1)}, u32[]{:S(2)}, u32[]{:S(2)}) collective-permute-start(bf16[3,704,128]{2,1,0:T(8,128)(2,1)} %collective-permute-done.12), channel_id=1, source_target_pairs={{0,1},{1,2},{2,3},{3,0},{4,5},{5,6},{6,7},{7,4},{8,9},{9,10},{10,1... | collective-permute-start | bytes 1622024 | tf_op jit(solution)/shard_map/ppermute | solution.py:350
  155.4 43.3 %copy-start.47 = (s32[1,2048]{1,0:T(1,128)S(1)}, s32[1,2048]{1,0:T(1,128)}, u32[]{:S(2)}) copy-start(s32[1,2048]{1,0:T(1,128)} %seg_q.3) | copy-start | bytes 24580
  155.4 73.3 %all-to-all-start = ((bf16[4,512,256]{1,2,0:T(8,128)(2,1)}), bf16[4,512,256]{1,2,0:T(8,128)(2,1)S(1)}, u32[]{:S(2)}, u32[]{:S(2)}) async-start(bf16[4,512,256]{1,2,0:T(8,128)(2,1)} %copy.62), calls=%async_computation | async-start | bytes 2097152 | tf_op jit(solution)/shard_map/all_to_all | solution.py:413
  161.7 37.5 %collective-permute-start.13 = (bf16[3,704,128]{2,1,0:T(8,128)(2,1)}, bf16[3,704,128]{2,1,0:T(8,128)(2,1)}, u32[]{:S(2)}, u32[]{:S(2)}) collective-permute-start(bf16[3,704,128]{2,1,0:T(8,128)(2,1)} %collective-permute-done.12), channel_id=1, source_target_pairs={{0,8},{4,12},{8,0},{12,4},{16,24},{20,28},{24,16},{28,20},{1,9},{5... | collective-permute-start | bytes 1622024 | tf_op jit(solution)/shard_map/ppermute | solution.py:324
  171.1 30.5 %collective-permute-start.18 = (bf16[3,704,128]{2,1,0:T(8,128)(2,1)}, bf16[3,704,128]{2,1,0:T(8,128)(2,1)}, u32[]{:S(2)}, u32[]{:S(2)}) collective-permute-start(bf16[3,704,128]{2,1,0:T(8,128)(2,1)} %collective-permute-done.17), channel_id=1, source_target_pairs={{0,16},{4,20},{8,24},{12,28},{16,0},{20,4},{24,8},{28,12},{1,17},{... | collective-permute-start | bytes 1622024 | tf_op jit(solution)/shard_map/ppermute | solution.py:324
  192.4 31.4 %collective-permute-start.9 = (bf16[2,3,704,128]{3,2,1,0:T(8,128)(2,1)}, bf16[2,3,704,128]{3,2,1,0:T(8,128)(2,1)}, u32[]{:S(2)}, u32[]{:S(2)}) collective-permute-start(bf16[2,3,704,128]{3,2,1,0:T(8,128)(2,1)} %pad_maximum_fusion.1.refs_6_), channel_id=1, source_target_pairs={{0,8},{4,12},{8,0},{12,4},{16,24},{20,28},{24,16},{28,20},{1,9},{5... | collective-permute-start | bytes 3244040 | tf_op jit(solution)/shard_map/ppermute | solution.py:324
  199.1 33.8 %collective-permute-start.10 = (bf16[2,3,704,128]{3,2,1,0:T(8,128)(2,1)}, bf16[2,3,704,128]{3,2,1,0:T(8,128)(2,1)}, u32[]{:S(2)}, u32[]{:S(2)}) collective-permute-start(bf16[2,3,704,128]{3,2,1,0:T(8,128)(2,1)} %pad_maximum_fusion.1.refs_6_), channel_id=1, source_target_pairs={{0,4},{4,0},{8,12},{12,8},{16,20},{20,16},{24,28},{28,24},{1,5},{5... | collective-permute-start | bytes 3244040 | tf_op jit(solution)/shard_map/ppermute | solution.py:324
  201.6 32.0 %collective-permute-start.14 = (bf16[2,3,704,128]{3,2,1,0:T(8,128)(2,1)}, bf16[2,3,704,128]{3,2,1,0:T(8,128)(2,1)}, u32[]{:S(2)}, u32[]{:S(2)}) collective-permute-start(bf16[2,3,704,128]{3,2,1,0:T(8,128)(2,1)} %pad_maximum_fusion.2.refs_2_), channel_id=1, source_target_pairs={{0,16},{4,20},{8,24},{12,28},{16,0},{20,4},{24,8},{28,12},{1,17},{... | collective-permute-start | bytes 3244040 | tf_op jit(solution)/shard_map/ppermute | solution.py:324
  201.6 31.9 %collective-permute-start.6 = (bf16[2,3,704,128]{3,2,1,0:T(8,128)(2,1)}, bf16[2,3,704,128]{3,2,1,0:T(8,128)(2,1)}, u32[]{:S(2)}, u32[]{:S(2)}) collective-permute-start(bf16[2,3,704,128]{3,2,1,0:T(8,128)(2,1)} %collective-permute-done.4.refs_3_), channel_id=1, source_target_pairs={{0,4},{4,0},{8,12},{12,8},{16,20},{20,16},{24,28},{28,24},{1,5},{5... | collective-permute-start | bytes 3244040 | tf_op jit(solution)/shard_map/ppermute | solution.py:324
  204.5 40.8 %collective-permute-start.19 = (bf16[2,3,704,128]{3,2,1,0:T(8,128)(2,1)}, bf16[2,3,704,128]{3,2,1,0:T(8,128)(2,1)}, u32[]{:S(2)}, u32[]{:S(2)}) collective-permute-start(bf16[2,3,704,128]{3,2,1,0:T(8,128)(2,1)} %pad_maximum_fusion.3.refs_6_), channel_id=1, source_target_pairs={{0,8},{4,12},{8,0},{12,4},{16,24},{20,28},{24,16},{28,20},{1,9},{5... | collective-permute-start | bytes 3244040 | tf_op jit(solution)/shard_map/ppermute | solution.py:324
  223.7 22.8 %collective-permute-start.11 = (bf16[2,3,704,128]{3,2,1,0:T(8,128)(2,1)}, bf16[2,3,704,128]{3,2,1,0:T(8,128)(2,1)}, u32[]{:S(2)}, u32[]{:S(2)}) collective-permute-start(bf16[2,3,704,128]{3,2,1,0:T(8,128)(2,1)} %collective-permute-done.9.refs_7_), channel_id=1, source_target_pairs={{0,4},{4,0},{8,12},{12,8},{16,20},{20,16},{24,28},{28,24},{1,5},{5... | collective-permute-start | bytes 3244040 | tf_op jit(solution)/shard_map/ppermute | solution.py:324
  233.0 38.8 %collective-permute-start.15 = (bf16[2,3,704,128]{3,2,1,0:T(8,128)(2,1)}, bf16[2,3,704,128]{3,2,1,0:T(8,128)(2,1)}, u32[]{:S(2)}, u32[]{:S(2)}) collective-permute-start(bf16[2,3,704,128]{3,2,1,0:T(8,128)(2,1)} %pad_maximum_fusion.2.refs_2_), channel_id=1, source_target_pairs={{0,4},{4,0},{8,12},{12,8},{16,20},{20,16},{24,28},{28,24},{1,5},{5... | collective-permute-start | bytes 3244040 | tf_op jit(solution)/shard_map/ppermute | solution.py:324
  233.5 38.3 %collective-permute-start.20 = (bf16[2,3,704,128]{3,2,1,0:T(8,128)(2,1)}, bf16[2,3,704,128]{3,2,1,0:T(8,128)(2,1)}, u32[]{:S(2)}, u32[]{:S(2)}) collective-permute-start(bf16[2,3,704,128]{3,2,1,0:T(8,128)(2,1)} %pad_maximum_fusion.3.refs_6_), channel_id=1, source_target_pairs={{0,4},{4,0},{8,12},{12,8},{16,20},{20,16},{24,28},{28,24},{1,5},{5... | collective-permute-start | bytes 3244040 | tf_op jit(solution)/shard_map/ppermute | solution.py:324
  233.6 38.7 %collective-permute-start.16 = (bf16[2,3,704,128]{3,2,1,0:T(8,128)(2,1)}, bf16[2,3,704,128]{3,2,1,0:T(8,128)(2,1)}, u32[]{:S(2)}, u32[]{:S(2)}) collective-permute-start(bf16[2,3,704,128]{3,2,1,0:T(8,128)(2,1)} %collective-permute-done.14.refs_3_), channel_id=1, source_target_pairs={{0,4},{4,0},{8,12},{12,8},{16,20},{20,16},{24,28},{28,24},{1,5},{5... | collective-permute-start | bytes 3244040 | tf_op jit(solution)/shard_map/ppermute | solution.py:324
  245.3 27.1 %collective-permute-start.21 = (bf16[2,3,704,128]{3,2,1,0:T(8,128)(2,1)}, bf16[2,3,704,128]{3,2,1,0:T(8,128)(2,1)}, u32[]{:S(2)}, u32[]{:S(2)}) collective-permute-start(bf16[2,3,704,128]{3,2,1,0:T(8,128)(2,1)} %collective-permute-done.19.refs_7_), channel_id=1, source_target_pairs={{0,4},{4,0},{8,12},{12,8},{16,20},{20,16},{24,28},{28,24},{1,5},{5... | collective-permute-start | bytes 3244040 | tf_op jit(solution)/shard_map/ppermute | solution.py:324
  270.6 29.4 %collective-permute-start.26 = (bf16[2,3,704,128]{3,2,1,0:T(8,128)(2,1)}, bf16[2,3,704,128]{3,2,1,0:T(8,128)(2,1)}, u32[]{:S(2)}, u32[]{:S(2)}) collective-permute-start(bf16[2,3,704,128]{3,2,1,0:T(8,128)(2,1)} %get-tuple-element.55), channel_id=1, source_target_pairs={{0,4},{4,0},{8,12},{12,8},{16,20},{20,16},{24,28},{28,24},{1,5},{5... | collective-permute-start | bytes 3244040 | tf_op jit(solution)/shard_map/ppermute | solution.py:331
  271.8 50.0 %collective-permute-start.25 = (bf16[2,3,704,128]{3,2,1,0:T(8,128)(2,1)}, bf16[2,3,704,128]{3,2,1,0:T(8,128)(2,1)}, u32[]{:S(2)}, u32[]{:S(2)}) collective-permute-start(bf16[2,3,704,128]{3,2,1,0:T(8,128)(2,1)} %get-tuple-element.53), channel_id=1, source_target_pairs={{0,4},{4,0},{8,12},{12,8},{16,20},{20,16},{24,28},{28,24},{1,5},{5... | collective-permute-start | bytes 3244040 | tf_op jit(solution)/shard_map/ppermute | solution.py:331
  271.8 66.8 %collective-permute-start.40 = (bf16[2,3,704,128]{3,2,1,0:T(8,128)(2,1)}, bf16[2,3,704,128]{3,2,1,0:T(8,128)(2,1)}, u32[]{:S(2)}, u32[]{:S(2)}) collective-permute-start(bf16[2,3,704,128]{3,2,1,0:T(8,128)(2,1)} %get-tuple-element.65), channel_id=1, source_target_pairs={{0,4},{4,0},{8,12},{12,8},{16,20},{20,16},{24,28},{28,24},{1,5},{5... | collective-permute-start | bytes 3244040 | tf_op jit(solution)/shard_map/ppermute | solution.py:331
  272.3 47.0 %collective-permute-start.41 = (bf16[2,3,704,128]{3,2,1,0:T(8,128)(2,1)}, bf16[2,3,704,128]{3,2,1,0:T(8,128)(2,1)}, u32[]{:S(2)}, u32[]{:S(2)}) collective-permute-start(bf16[2,3,704,128]{3,2,1,0:T(8,128)(2,1)} %get-tuple-element.67), channel_id=1, source_target_pairs={{0,4},{4,0},{8,12},{12,8},{16,20},{20,16},{24,28},{28,24},{1,5},{5... | collective-permute-start | bytes 3244040 | tf_op jit(solution)/shard_map/ppermute | solution.py:331
  296.5 36.4 %collective-permute-start.31 = (bf16[2,3,704,128]{3,2,1,0:T(8,128)(2,1)}, bf16[2,3,704,128]{3,2,1,0:T(8,128)(2,1)}, u32[]{:S(2)}, u32[]{:S(2)}) collective-permute-start(bf16[2,3,704,128]{3,2,1,0:T(8,128)(2,1)} %get-tuple-element.59), channel_id=1, source_target_pairs={{0,4},{4,0},{8,12},{12,8},{16,20},{20,16},{24,28},{28,24},{1,5},{5... | collective-permute-start | bytes 3244040 | tf_op jit(solution)/shard_map/ppermute | solution.py:331
  303.1 26.2 %collective-permute-start.27 = (bf16[2,3,704,128]{3,2,1,0:T(8,128)(2,1)}, bf16[2,3,704,128]{3,2,1,0:T(8,128)(2,1)}, u32[]{:S(2)}, u32[]{:S(2)}) collective-permute-start(bf16[2,3,704,128]{3,2,1,0:T(8,128)(2,1)} %add_convert_fusion.3), channel_id=1, source_target_pairs={{0,8},{4,12},{8,0},{12,4},{16,24},{20,28},{24,16},{28,20},{1,9},{5... | collective-permute-start | bytes 3244040 | tf_op jit(solution)/shard_map/ppermute | solution.py:331
  311.4 53.9 %all-to-all-start.1 = ((bf16[512,4,256]{2,0,1:T(8,128)(2,1)}), bf16[512,4,256]{2,0,1:T(8,128)(2,1)}, u32[]{:S(2)}, u32[]{:S(2)}) async-start(bf16[512,4,256]{2,0,1:T(8,128)(2,1)} %bitcast.135), calls=%async_computation.1 | async-start | bytes 2097152 | tf_op jit(solution)/shard_map/all_to_all | solution.py:436
  316.5 157.9 %reduce-scatter.12.cloned.1.call-start = ((), (), s32[]{:S(2)}) async-start(), calls=%async_computation.9 | async-start | bytes 2359296
  319.1 203.4 %reduce-scatter.8.cloned.1.call-start = ((), (), s32[]{:S(2)}) async-start(), calls=%async_computation.6 | async-start | bytes 327680 | tf_op jit(solution)/shard_map/reduce_scatter | solution.py:440
  319.4 16.4 %collective-permute-start.36 = (bf16[2,3,704,128]{3,2,1,0:T(8,128)(2,1)}, bf16[2,3,704,128]{3,2,1,0:T(8,128)(2,1)S(1)}, u32[]{:S(2)}, u32[]{:S(2)}) collective-permute-start(bf16[2,3,704,128]{3,2,1,0:T(8,128)(2,1)} %get-tuple-element.63), channel_id=1, source_target_pairs={{0,4},{4,0},{8,12},{12,8},{16,20},{20,16},{24,28},{28,24},{1,5},{5... | collective-permute-start | bytes 3244040 | tf_op jit(solution)/shard_map/ppermute | solution.py:331
  321.8 90.5 %collective-permute-start.30 = (bf16[2,3,704,128]{3,2,1,0:T(8,128)(2,1)}, bf16[2,3,704,128]{3,2,1,0:T(8,128)(2,1)}, u32[]{:S(2)}, u32[]{:S(2)}) collective-permute-start(bf16[2,3,704,128]{3,2,1,0:T(8,128)(2,1)} %get-tuple-element.57), channel_id=1, source_target_pairs={{0,4},{4,0},{8,12},{12,8},{16,20},{20,16},{24,28},{28,24},{1,5},{5... | collective-permute-start | bytes 3244040 | tf_op jit(solution)/shard_map/ppermute | solution.py:331
  329.2 32.3 %collective-permute-start.42 = (bf16[2,3,704,128]{3,2,1,0:T(8,128)(2,1)S(1)}, bf16[2,3,704,128]{3,2,1,0:T(8,128)(2,1)S(1)}, u32[]{:S(2)}, u32[]{:S(2)}) collective-permute-start(bf16[2,3,704,128]{3,2,1,0:T(8,128)(2,1)S(1)} %add_convert_fusion), channel_id=1, source_target_pairs={{0,16},{4,20},{8,24},{12,28},{16,0},{20,4},{24,8},{28,12},{1,17},{... | collective-permute-start | bytes 3244040 | tf_op jit(solution)/shard_map/ppermute | solution.py:331
  332.8 100.9 %collective-permute-start.35 = (bf16[2,3,704,128]{3,2,1,0:T(8,128)(2,1)}, bf16[2,3,704,128]{3,2,1,0:T(8,128)(2,1)}, u32[]{:S(2)}, u32[]{:S(2)}) collective-permute-start(bf16[2,3,704,128]{3,2,1,0:T(8,128)(2,1)} %get-tuple-element.61), channel_id=1, source_target_pairs={{0,4},{4,0},{8,12},{12,8},{16,20},{20,16},{24,28},{28,24},{1,5},{5... | collective-permute-start | bytes 3244040 | tf_op jit(solution)/shard_map/ppermute | solution.py:331
  335.8 76.7 %collective-permute-start.32 = (bf16[2,3,704,128]{3,2,1,0:T(8,128)(2,1)}, bf16[2,3,704,128]{3,2,1,0:T(8,128)(2,1)}, u32[]{:S(2)}, u32[]{:S(2)}) collective-permute-start(bf16[2,3,704,128]{3,2,1,0:T(8,128)(2,1)} %add_convert_fusion.2), channel_id=1, source_target_pairs={{0,16},{4,20},{8,24},{12,28},{16,0},{20,4},{24,8},{28,12},{1,17},{... | collective-permute-start | bytes 3244040 | tf_op jit(solution)/shard_map/ppermute | solution.py:331
  338.6 95.0 %collective-permute-start.37 = (bf16[2,3,704,128]{3,2,1,0:T(8,128)(2,1)}, bf16[2,3,704,128]{3,2,1,0:T(8,128)(2,1)}, u32[]{:S(2)}, u32[]{:S(2)}) collective-permute-start(bf16[2,3,704,128]{3,2,1,0:T(8,128)(2,1)} %add_convert_fusion.1), channel_id=1, source_target_pairs={{0,8},{4,12},{8,0},{12,4},{16,24},{20,28},{24,16},{28,20},{1,9},{5... | collective-permute-start | bytes 3244040 | tf_op jit(solution)/shard_map/ppermute | solution.py:331
  361.6 48.9 %collective-permute-start.28 = (bf16[3,704,128]{2,1,0:T(8,128)(2,1)}, bf16[3,704,128]{2,1,0:T(8,128)(2,1)}, u32[]{:S(2)}, u32[]{:S(2)}) collective-permute-start(bf16[3,704,128]{2,1,0:T(8,128)(2,1)} %fusion.66), channel_id=1, source_target_pairs={{0,16},{4,20},{8,24},{12,28},{16,0},{20,4},{24,8},{28,12},{1,17},{... | collective-permute-start | bytes 1622024 | tf_op jit(solution)/shard_map/ppermute | solution.py:331
  371.0 35.4 %copy-start.21 = (bf16[512,1024]{1,0:T(8,128)(2,1)S(1)}, bf16[512,1024]{1,0:T(8,128)(2,1)}, u32[]{:S(2)}) copy-start(bf16[512,1024]{1,0:T(8,128)(2,1)} %copy-done.19) | copy-start | bytes 3145732
  410.5 27.9 %collective-permute-start.22 = (bf16[512,1024]{1,0:T(8,128)(2,1)S(1)}, bf16[512,1024]{1,0:T(8,128)(2,1)S(1)}, u32[]{:S(2)}, u32[]{:S(2)}) collective-permute-start(bf16[512,1024]{1,0:T(8,128)(2,1)S(1)} %get-tuple-element.105), channel_id=1, source_target_pairs={{0,1},{1,2},{2,3},{3,0},{4,5},{5,6},{6,7},{7,4},{8,9},{9,10},{10,1... | collective-permute-start | bytes 3145736 | tf_op jit(solution)/shard_map/ppermute | solution.py:350
  412.3 37.7 %collective-permute-start.29 = (bf16[3,704,128]{2,1,0:T(8,128)(2,1)S(1)}, bf16[3,704,128]{2,1,0:T(8,128)(2,1)S(1)}, u32[]{:S(2)}, u32[]{:S(2)}) collective-permute-start(bf16[3,704,128]{2,1,0:T(8,128)(2,1)S(1)} %fusion.47), channel_id=1, source_target_pairs={{0,1},{1,2},{2,3},{3,0},{4,5},{5,6},{6,7},{7,4},{8,9},{9,10},{10,1... | collective-permute-start | bytes 1622024 | tf_op jit(solution)/shard_map/ppermute | solution.py:350
  414.5 35.4 %collective-permute-start.33 = (bf16[3,704,128]{2,1,0:T(8,128)(2,1)S(1)}, bf16[3,704,128]{2,1,0:T(8,128)(2,1)S(1)}, u32[]{:S(2)}, u32[]{:S(2)}) collective-permute-start(bf16[3,704,128]{2,1,0:T(8,128)(2,1)S(1)} %fusion.67), channel_id=1, source_target_pairs={{0,8},{4,12},{8,0},{12,4},{16,24},{20,28},{24,16},{28,20},{1,9},{5... | collective-permute-start | bytes 1622024 | tf_op jit(solution)/shard_map/ppermute | solution.py:331
  437.9 38.4 %collective-permute-start.38 = (bf16[3,704,128]{2,1,0:T(8,128)(2,1)}, bf16[3,704,128]{2,1,0:T(8,128)(2,1)}, u32[]{:S(2)}, u32[]{:S(2)}) collective-permute-start(bf16[3,704,128]{2,1,0:T(8,128)(2,1)} %fusion.68), channel_id=1, source_target_pairs={{0,16},{4,20},{8,24},{12,28},{16,0},{20,4},{24,8},{28,12},{1,17},{... | collective-permute-start | bytes 1622024 | tf_op jit(solution)/shard_map/ppermute | solution.py:331
  438.9 43.9 %collective-permute-start.23 = (bf16[512,1024]{1,0:T(8,128)(2,1)S(1)}, bf16[512,1024]{1,0:T(8,128)(2,1)}, u32[]{:S(2)}, u32[]{:S(2)}) collective-permute-start(bf16[512,1024]{1,0:T(8,128)(2,1)S(1)} %get-tuple-element.103), channel_id=1, source_target_pairs={{0,1},{1,2},{2,3},{3,0},{4,5},{5,6},{6,7},{7,4},{8,9},{9,10},{10,1... | collective-permute-start | bytes 3145736 | tf_op jit(solution)/shard_map/ppermute | solution.py:350
  450.9 28.9 %collective-permute-start.34 = (bf16[3,704,128]{2,1,0:T(8,128)(2,1)}, bf16[3,704,128]{2,1,0:T(8,128)(2,1)}, u32[]{:S(2)}, u32[]{:S(2)}) collective-permute-start(bf16[3,704,128]{2,1,0:T(8,128)(2,1)} %fusion.45), channel_id=1, source_target_pairs={{0,1},{1,2},{2,3},{3,0},{4,5},{5,6},{6,7},{7,4},{8,9},{9,10},{10,1... | collective-permute-start | bytes 1622024 | tf_op jit(solution)/shard_map/ppermute | solution.py:350
  453.1 71.3 %collective-permute-start.43 = (bf16[3,704,128]{2,1,0:T(8,128)(2,1)}, bf16[3,704,128]{2,1,0:T(8,128)(2,1)}, u32[]{:S(2)}, u32[]{:S(2)}) collective-permute-start(bf16[3,704,128]{2,1,0:T(8,128)(2,1)} %fusion.69), channel_id=1, source_target_pairs={{0,8},{4,12},{8,0},{12,4},{16,24},{20,28},{24,16},{28,20},{1,9},{5... | collective-permute-start | bytes 1622024 | tf_op jit(solution)/shard_map/ppermute | solution.py:331
  476.3 83.6 %reduce-scatter.10.cloned.1.call-start = ((), (), s32[]{:S(2)}) async-start(), calls=%async_computation.8 | async-start | bytes 1769472
  482.5 41.8 %collective-permute-start.39 = (bf16[3,704,128]{2,1,0:T(8,128)(2,1)}, bf16[3,704,128]{2,1,0:T(8,128)(2,1)}, u32[]{:S(2)}, u32[]{:S(2)}) collective-permute-start(bf16[3,704,128]{2,1,0:T(8,128)(2,1)} %fusion.42), channel_id=1, source_target_pairs={{0,1},{1,2},{2,3},{3,0},{4,5},{5,6},{6,7},{7,4},{8,9},{9,10},{10,1... | collective-permute-start | bytes 1622024 | tf_op jit(solution)/shard_map/ppermute | solution.py:350
  486.3 39.5 %collective-permute-start.24 = (bf16[512,1024]{1,0:T(8,128)(2,1)}, bf16[512,1024]{1,0:T(8,128)(2,1)}, u32[]{:S(2)}, u32[]{:S(2)}) collective-permute-start(bf16[512,1024]{1,0:T(8,128)(2,1)} %get-tuple-element.107), channel_id=1, source_target_pairs={{0,1},{1,2},{2,3},{3,0},{4,5},{5,6},{6,7},{7,4},{8,9},{9,10},{10,1... | collective-permute-start | bytes 3145736 | tf_op jit(solution)/shard_map/ppermute | solution.py:350
  491.1 31.4 %copy-start.43 = (f32[256,128]{1,0:T(8,128)S(1)}, f32[256,128]{1,0:T(8,128)}, u32[]{:S(2)}) copy-start(f32[256,128]{1,0:T(8,128)} %param.27) | copy-start | bytes 393220
  491.1 31.4 %copy-start.48 = (f32[256,128]{1,0:T(8,128)S(1)}, f32[256,128]{1,0:T(8,128)}, u32[]{:S(2)}) copy-start(f32[256,128]{1,0:T(8,128)} %param.28) | copy-start | bytes 393220
  491.1 33.3 %copy-start.12 = (f32[2,3,704,128]{3,2,1,0:T(8,128)S(1)}, f32[2,3,704,128]{3,2,1,0:T(8,128)}, u32[]{:S(2)}) copy-start(f32[2,3,704,128]{3,2,1,0:T(8,128)} %convert_add_fusion.1) | copy-start | bytes 6488068
  530.8 3.7 collective-permute-start.44
  532.8 31.5 %copy-start.29 = (f32[3,128,256]{2,1,0:T(8,128)S(1)}, f32[3,128,256]{2,1,0:T(8,128)}, u32[]{:S(2)}) copy-start(f32[3,128,256]{2,1,0:T(8,128)} %param.24) | copy-start | bytes 1179652
  535.2 28.3 %collective-permute-start.45 = (f32[2,1024]{1,0:T(2,128)}, f32[2,1024]{1,0:T(2,128)}, u32[]{:S(2)}, u32[]{:S(2)}) collective-permute-start(f32[2,1024]{1,0:T(2,128)} %fusion.88), channel_id=1, source_target_pairs={{0,2},{1,3},{2,0},{3,1},{4,6},{5,7},{6,4},{7,5},{8,10},{9,11},{10,... | collective-permute-start | bytes 24584 | tf_op jit(solution)/shard_map/ppermute | solution.py:478
  536.4 35.5 %copy-start.7 = (f32[512,1024]{1,0:T(8,128)S(1)}, f32[512,1024]{1,0:T(8,128)}, u32[]{:S(2)}) copy-start(f32[512,1024]{1,0:T(8,128)} %copy-done.6) | copy-start | bytes 6291460
  564.1 2.6 collective-permute-start.46
  566.7 3.7 collective-permute-start.47
  570.5 5.3 collective-permute-start.48
  (50 other events, 394.7 us)
Sparse Core Ops, SparseCore 0:
  10.5 28.6 all-gather.3
  42.6 84.5 all-gather.5
  320.6 49.3 reduce-scatter.11
  476.4 46.0 reduce-scatter.7
  525.6 34.1 reduce-scatter.9

commit v3 on v2

--- a/solution.py
+++ b/solution.py
@@ -88,8 +88,8 @@
     lse_ref[...] = jnp.concatenate([peak + jnp.log(t) for (peak, _, _), t in zip(found, totals)], axis=0)
 
 
-def attend(qkv, seg, lo, hi, bq, bk):
-    rows, width = qkv.shape[0], qkv.shape[1] // 3
+def attend(qkv, group, width, seg, lo, hi, bq, bk):
+    rows = qkv.shape[0]
     heads = width // HEAD
     return pl.pallas_call(
         functools.partial(attend_kernel, bk=bk, heads=heads),
@@ -101,9 +101,9 @@
             num_scalar_prefetch=2,
             grid=(rows // bq,),
             in_specs=[
-                pl.BlockSpec((bq, width), lambda i, *_: (i, 0)),
-                pl.BlockSpec((rows, width), lambda i, *_: (0, 1)),
-                pl.BlockSpec((rows, width), lambda i, *_: (0, 2)),
+                pl.BlockSpec((bq, width), lambda i, *_: (i, 3 * group)),
+                pl.BlockSpec((rows, width), lambda i, *_: (0, 3 * group + 1)),
+                pl.BlockSpec((rows, width), lambda i, *_: (0, 3 * group + 2)),
                 pl.BlockSpec((1, bq), lambda i, *_: (0, i)),
                 pl.BlockSpec((rows, 1), lambda i, *_: (0, 0)),
             ],
@@ -112,6 +112,9 @@
                 pl.BlockSpec((heads, bq), lambda i, *_: (0, i)),
             ),
             scratch_shapes=[pltpu.VMEM((width, rows), jnp.bfloat16)],
+        ),
+        cost_estimate=pl.CostEstimate(
+            flops=16 * heads * rows * rows * HEAD, transcendentals=heads * rows * rows, bytes_accessed=10 * rows * width
         ),
         name="attend",
     )(lo, hi, qkv, qkv, qkv, seg[None, :], seg[:, None])
@@ -159,7 +162,7 @@
         d_ref[:, 2 * width :] = dv_sum[...].astype(d_ref.dtype)
 
 
-def attend_back(qkv, d_out, lse, row_dot, seg, lo, hi, bq, bk):
+def attend_back(qkv, group, d_out, lse, row_dot, seg, lo, hi, bq, bk):
     rows, width = d_out.shape
     heads = width // HEAD
     by_row = lambda i, *_: (i, 0)
@@ -171,12 +174,12 @@
             num_scalar_prefetch=2,
             grid=(rows // bq,),
             in_specs=[
-                pl.BlockSpec((bq, width), by_row),
+                pl.BlockSpec((bq, width), lambda i, *_: (i, 3 * group)),
                 pl.BlockSpec((bq, width), by_row),
                 pl.BlockSpec((heads, bq), by_col),
                 pl.BlockSpec((heads, bq), by_col),
-                pl.BlockSpec((rows, width), lambda i, *_: (0, 1)),
-                pl.BlockSpec((rows, width), lambda i, *_: (0, 2)),
+                pl.BlockSpec((rows, width), lambda i, *_: (0, 3 * group + 1)),
+                pl.BlockSpec((rows, width), lambda i, *_: (0, 3 * group + 2)),
                 pl.BlockSpec((1, bq), by_col),
                 pl.BlockSpec((rows, 1), lambda i, *_: (0, 0)),
             ],
@@ -187,6 +190,9 @@
                 pltpu.VMEM((width, rows), jnp.bfloat16),
             ],
         ),
+        cost_estimate=pl.CostEstimate(
+            flops=40 * heads * rows * rows * HEAD, transcendentals=heads * rows * rows, bytes_accessed=16 * rows * width
+        ),
         name="attend_back",
     )(lo, hi, qkv, d_out, lse, row_dot, qkv, qkv, seg[None, :], seg[:, None])
 
@@ -206,8 +212,8 @@
 
 def feed_kernel(spots, *refs, slices):
     n_ref, g_ref = refs[:2]
-    w_in = [refs[2 + 4 * s : 6 + 4 * s] for s in range(slices)]
-    at = 2 + 4 * slices
+    w_in = [refs[2 + PIECES * s : 2 + PIECES * (s + 1)] for s in range(slices)]
+    at = 2 + PIECES * slices
     out_ref, dn_ref = refs[at : at + 2]
     d_out = [refs[at + 2 + 4 * s : at + 6 + 4 * s] for s in range(slices)]
     w_buf, d_buf, w_sem, d_sem = refs[at + 2 + 4 * slices :]
@@ -218,9 +224,8 @@
         held = s % 2
         for p in range(PIECES):
             lanes = pl.ds(pl.multiple_of(spots[s * PIECES + p] * LANES, LANES), LANES)
-            far = arrays[p // 2].at[p % 2]
             near = buf.at[held, :, :, lanes]
-            src, dst = (near, far) if outward else (far, near)
+            src, dst = (near, arrays[p // 2].at[p % 2]) if outward else (arrays[p], near)
             yield pltpu.make_async_copy(src, dst, sem.at[held])
 
     for s in range(slices):
@@ -284,7 +289,7 @@
 def feed(n, g, weights, spots):
     slices = len(weights)
     rows, width = n.shape
-    hidden = weights[0][0].shape[2]
+    hidden = weights[0][0].shape[1]
     whole = pl.BlockSpec((rows, width), lambda i, *_: (0, 0))
     there = pl.BlockSpec(memory_space=pl.ANY)
     acc = jax.ShapeDtypeStruct((rows, width), jnp.float32)
@@ -295,7 +300,7 @@
         grid_spec=pltpu.PrefetchScalarGridSpec(
             num_scalar_prefetch=1,
             grid=(slices,),
-            in_specs=[whole, whole] + [there] * (4 * slices),
+            in_specs=[whole, whole] + [there] * (PIECES * slices),
             out_specs=(whole, whole) + (there,) * (4 * slices),
             scratch_shapes=[
                 pltpu.VMEM((2, 3, hidden, width), jnp.bfloat16),
@@ -304,6 +309,11 @@
                 pltpu.SemaphoreType.DMA((2,)),
             ],
         ),
+        cost_estimate=pl.CostEstimate(
+            flops=27 * slices * rows * hidden * width,
+            transcendentals=slices * rows * hidden,
+            bytes_accessed=12 * slices * hidden * width + 12 * rows * width,
+        ),
         name="feed",
     )(spots, n, g, *[array for slice_ in weights for array in slice_])
     return found[0], found[1], [found[2 + 4 * s : 6 + 4 * s] for s in range(slices)]
@@ -320,11 +330,20 @@
     return jnp.bitwise_xor(me, jnp.array(rows, jnp.int32))
 
 
-def gather_slice(piece, count, first, second):
+def after(value, *others):
+    return lax.optimization_barrier((value, *others))[0]
+
+
+def cross_first(piece, count, first, second):
     swap = lambda value, bit: lax.ppermute(value, "dp", swap_over("dp", count, bit))
-    pair = jnp.stack([piece, swap(piece, first)])
-    other = swap(pair, second)
-    return [pair, other, swap(pair, 1), swap(other, 1)]
+    return piece, swap(piece, first), swap(piece, second), swap(piece, 1)
+
+
+def cross_last(found, count, second):
+    swap = lambda value, bit: lax.ppermute(value, "dp", swap_over("dp", count, bit))
+    own, one, two, core = found
+    both = swap(one, second)
+    return [own, one, two, both, core, swap(one, 1), swap(two, 1), swap(both, 1)]
 
 
 def scatter_slice(parts, count, first, second):
@@ -355,43 +374,46 @@
     heads_width = w_out.shape[0]
     exchange = dp == PIECES and lanes_here == LANES
 
-    copy_qkv = w_qkv.astype(bf16).transpose(0, 2, 1).reshape(3 * heads_width, lanes_here)
+    groups = 2 if heads_width % (4 * HEAD) == 0 else 1
+    share = heads_width // groups
+
+    seg_row = segment_ids[0]
+    live_row = jnp.arange(seq_len, dtype=jnp.int32) < row_length[0]
+    live = live_row.astype(f32)[:, None]
+
+    wide, narrow = min(1024, seq_len), min(512, seq_len)
+    lo, hi = key_blocks(seg_row, row_length[0], wide, narrow)
+    lo_back, hi_back = key_blocks(seg_row, row_length[0], narrow, narrow)
+
+    copy_qkv = w_qkv.astype(bf16).reshape(3, lanes_here, groups, share).transpose(2, 0, 3, 1).reshape(3 * heads_width, lanes_here)
     copy_out = w_out.astype(bf16)
     copy_feed = jnp.concatenate([w_gate_up.astype(bf16).transpose(0, 2, 1), w_down.astype(bf16)[None]])
     copy_gains = jnp.pad(norm_gains.astype(bf16), ((0, 14), (0, 0)))
-
+    chip_bits = [(2, 4) if s % 2 == 0 or not exchange else (4, 2) for s in range(mp)]
+    spots = spots_of(me if exchange else 0, chip_bits)
+
+    def start_cross(piece, s):
+        if exchange:
+            return cross_first(piece, dp, *chip_bits[s])
+        return lax.all_gather(piece, "dp", axis=2, tiled=True)
+
+    def end_cross(found, s):
+        if exchange:
+            return cross_last(found, dp, chip_bits[s][1])
+        whole = found.reshape(3, hidden_here, PIECES, LANES)
+        return [whole[:, :, block] for block in (0, 2, 4, 6, 1, 3, 5, 7)]
+
+    feed_own = [copy_feed, ring(copy_feed)]
     blocks = [inputs[0]]
     for _ in range(mp - 1):
         blocks.append(ring(blocks[-1]))
-
     full_first = lax.all_gather(jnp.concatenate([copy_qkv, copy_gains]), "dp", axis=1, tiled=True)
     full_qkv = full_first[: 3 * heads_width]
     gain_one = full_first[3 * heads_width].astype(f32)
     gain_two = full_first[3 * heads_width + 1].astype(f32)
-    full_out = lax.all_gather(copy_out, ("dp", "mp"), axis=0)
-    full_out = full_out.reshape(dp, mp, heads_width, lanes_here).transpose(1, 2, 0, 3).reshape(mp * heads_width, width)
-
-    copy_feed, _ = lax.optimization_barrier((copy_feed, blocks[-1]))
-    feed_own = [copy_feed]
-    for _ in range(mp - 1):
-        feed_own.append(ring(feed_own[-1]))
-    if exchange:
-        chip_bits = [(2, 4) if s % 2 == 0 else (4, 2) for s in range(mp)]
-        feed_full = [gather_slice(piece, dp, *bits) for piece, bits in zip(feed_own, chip_bits)]
-        spots = spots_of(me, chip_bits)
-    else:
-        chip_bits = [(2, 4)] * mp
-        spots = spots_of(0, chip_bits)
-        turn = jnp.array([0, 2, 4, 6, 1, 3, 5, 7])
-        feed_full = []
-        for piece in feed_own:
-            whole = lax.all_gather(piece, "dp", axis=2, tiled=True)
-            whole = whole.reshape(3, hidden_here, PIECES, LANES).transpose(2, 0, 1, 3)[turn]
-            feed_full.append([whole[2 * i : 2 * i + 2] for i in range(4)])
-
-    seg_row = segment_ids[0]
-    live_row = jnp.arange(seq_len, dtype=jnp.int32) < row_length[0]
-    live = live_row.astype(f32)[:, None]
+    full_out = lax.all_gather(copy_out, ("dp", "mp"), axis=0).reshape(dp, mp, groups, share, lanes_here)
+    full_out = [full_out[:, :, i].transpose(1, 2, 0, 3).reshape(mp * share, width) for i in range(groups)]
+    feed_full = [end_cross(start_cross(feed_own[s], s), s) for s in range(2)]
 
     resid_in = inputs[0].astype(f32)
     scale_one = rms_scale(resid_in)
@@ -405,14 +427,29 @@
         normed_one = lax.dynamic_update_slice(normed_one, (hats[-1] * gain_one).astype(bf16), (at, 0))
     qkv = dot32(normed_one, full_qkv, NT).astype(bf16)
 
-    wide, narrow = min(1024, seq_len), min(512, seq_len)
-    lo, hi = key_blocks(seg_row, row_length[0], wide, narrow)
-    raw_out, log_sums = attend(qkv, seg_row, lo, hi, wide, narrow)
-    log_sums = jnp.where(live_row[None, :], log_sums, -NEG_FILL)
-    attended = (raw_out * live).astype(bf16)
-    attended = lax.all_to_all(attended, "mp", split_axis=0, concat_axis=1, tiled=True)
-
-    after_attn = resid_in + dot32(attended, full_out, NN)
+    pending = ring(after(feed_own[1], blocks[-1]))
+    crossing = []
+    raw_out, log_sums, attended = [], [], []
+    for i in range(groups):
+        raw, logs = attend(qkv, i, share, seg_row, lo, hi, wide, narrow)
+        raw_out.append(raw)
+        log_sums.append(jnp.where(live_row[None, :], logs, -NEG_FILL))
+        mine = (raw * live).astype(bf16)
+        pending, mine = lax.optimization_barrier((pending, mine))
+        feed_own.append(pending)
+        crossing.append(start_cross(pending, len(feed_own) - 1))
+        if len(feed_own) < mp:
+            pending = ring(pending)
+        attended.append(lax.all_to_all(mine, "mp", split_axis=0, concat_axis=1, tiled=True))
+    while len(feed_own) < mp:
+        feed_own.append(pending)
+        crossing.append(start_cross(pending, len(feed_own) - 1))
+        pending = ring(pending)
+    feed_full += [end_cross(found, s + 2) for s, found in enumerate(crossing)]
+
+    after_attn = resid_in
+    for part, weight in zip(attended, full_out):
+        after_attn = after_attn + dot32(part, weight, NN)
     scale_two = rms_scale(after_attn)
     hat_two = after_attn * scale_two
     normed_two = (hat_two * gain_two).astype(bf16)
@@ -426,22 +463,27 @@
         fed.append(out_part)
         d_normed_two.append(d_part)
         d_feed += grads
-    block_output = after_attn + functools.reduce(jnp.add, fed)
     d_normed_two = functools.reduce(jnp.add, d_normed_two)
     d_after = cotangent[0].astype(f32) + norm_back(d_normed_two, hat_two, scale_two, gain_two)
-    grad_gain_two = jnp.sum(d_normed_two * hat_two, axis=0)
 
     d_branch = d_after.astype(bf16)
-    d_attended = dot32(d_branch, full_out, NT).astype(bf16)
-    d_attended = lax.all_to_all(d_attended, "mp", split_axis=1, concat_axis=0, tiled=True)
-    d_attended = jnp.where(live_row[:, None], d_attended, jnp.zeros((), bf16))
-    grad_out = dot32(attended, d_branch, TN).astype(bf16)
+    d_attended = [
+        lax.all_to_all(dot32(d_branch, weight, NT).astype(bf16), "mp", split_axis=1, concat_axis=0, tiled=True)
+        for weight in full_out
+    ]
+    grad_out = [dot32(part, d_branch, TN).astype(bf16).reshape(mp, share, width) for part in attended]
+    grad_out = jnp.stack(grad_out, axis=1).reshape(mp * heads_width, width)
     grad_out = lax.psum_scatter(grad_out, "dp", scatter_dimension=1, tiled=True)
     grad_out = lax.psum_scatter(grad_out, "mp", scatter_dimension=0, tiled=True).astype(f32)
 
-    row_dot = jnp.sum((raw_out * d_attended).reshape(seq_len, heads_width // HEAD, HEAD), axis=-1).T
-    lo, hi = key_blocks(seg_row, row_length[0], narrow, narrow)
-    d_qkv = attend_back(qkv, d_attended, log_sums, row_dot, seg_row, lo, hi, narrow, narrow)
+    d_qkv = []
+    for i in range(groups):
+        d_here = jnp.where(live_row[:, None], d_attended[i], jnp.zeros((), bf16))
+        row_dot = jnp.sum((raw_out[i] * d_here).reshape(seq_len, share // HEAD, HEAD), axis=-1).T
+        d_qkv.append(attend_back(qkv, i, d_here, log_sums[i], row_dot, seg_row, lo_back, hi_back, narrow, narrow))
+    d_qkv = jnp.concatenate(d_qkv, axis=1)
+    block_output = after_attn + functools.reduce(jnp.add, fed)
+    grad_gain_two = jnp.sum(d_normed_two * hat_two, axis=0)
 
     total = None
     grad_gain_one = jnp.zeros((width,), f32)
@@ -455,7 +497,7 @@
 
     grad_qkv = dot32(d_qkv, normed_one, TN).astype(bf16)
     grad_qkv = lax.psum_scatter(grad_qkv, "dp", scatter_dimension=1, tiled=True).astype(f32)
-    grad_qkv = grad_qkv.reshape(3, heads_width, lanes_here).transpose(0, 2, 1)
+    grad_qkv = grad_qkv.reshape(groups, 3, share, lanes_here).transpose(1, 3, 0, 2).reshape(w_qkv.shape)
 
     if exchange:
         owned = [scatter_slice(parts, dp, *bits) for parts, bits in zip(d_feed, chip_bits)]

time: 583 us -> 590 us (1.012); the launches traced: 583 us -> 581 us
  other arithmetic: 71.9 us -> 56.3 us
  starting transfers between devices: 97.9 us -> 82.6 us
  waiting for transfers between devices: 225 us -> 237 us
  Pallas kernels: 112 us -> 120 us
  matrix products: 26.3 us -> 33.7 us
    ppermute x12, waiting for transfers between devices: 99.4 us -> 146 us  [on_device(): ring = lambda value: lax.ppermute(value, 'mp', onward)]
    unnamed x7, waiting for transfers between devices: 23.5 us -> 0.1 us
    ppermute x16, starting transfers between devices: 46.1 us -> 26.6 us  [scatter_slice(): lax.ppermute(value, 'dp', swap_over('dp', count, bit))]
    reduce_scatter x1, waiting for transfers between devices: 28.6 us -> 9.97 us  [on_device(): lax.psum_scatter(grad_out, 'mp', scatter_dimension=0, tiled=True)]
    ppermute x16 -> x28, starting transfers between devices: 29.2 us -> 18.9 us  [the longest x16 11.3 us: cross_last(): lax.ppermute(value, 'dp', swap_over('dp', count, bit))]
    another operation x4 -> x1, other arithmetic: 8.3 us -> 0.19 us  [on_device(): grad_out = jnp.stack(grad_out, axis=1).reshape(mp * heads_width, width)]
    all_to_all x2 -> x4, starting transfers between devices: 11.3 us -> 18.9 us  [the longest x2 10.1 us: on_device(): lax.all_to_all(mine, 'mp', split_axis=0, concat_axis=1, tiled=True)]
    ppermute x16, waiting for transfers between devices: 28.6 us -> 21 us  [scatter_slice(): lax.ppermute(value, 'dp', swap_over('dp', count, bit))]
  transfers between devices with their start and end apart: 56 -> 70, of which waited for: 17 -> 22; matrix products, arithmetic and copies ran while one was open for 21% -> 20% of each run, Pallas kernels for 19% -> 21%
where the time goes in v3:
time: 590 us; the launch traced here: 581 us
  waiting for transfers between devices  237 us (40%)
  Pallas kernels  120 us (20%)
  starting transfers between devices  82.6 us (14%)
  other arithmetic  56.3 us (10%)
  local copies, waits for them, and re-layouts  36 us (6%)
  matrix products  33.7 us (6%)
  between operations  15.8 us (3%)
    ppermute x12, waiting for transfers between devices, on_device(): ring = lambda value: lax.ppermute(value, 'mp', onward)  146 us
    pallas_call x2, Pallas kernels, feed(): pl.pallas_call(functools.partial(feed_kernel, slices=slices), out_shape=(...  48 us
    pallas_call x2, Pallas kernels, attend_back(): pl.pallas_call(functools.partial(attend_back_kernel, bk=bk, heads=heads),...  40 us
    dot_general x12, matrix products, dot32(): lax.dot_general(left, right, dims, preferred_element_type=jnp.float32)  33.7 us
    pallas_call x2, Pallas kernels, attend(): pl.pallas_call(functools.partial(attend_kernel, bk=bk, heads=heads), out_...  31.9 us
    ppermute x16, starting transfers between devices, scatter_slice(): lax.ppermute(value, 'dp', swap_over('dp', count, bit))  26.6 us
    ppermute x12, waiting for transfers between devices, cross_first(): lax.ppermute(value, 'dp', swap_over('dp', count, bit))  24.7 us
    ppermute x16, waiting for transfers between devices, cross_last(): lax.ppermute(value, 'dp', swap_over('dp', count, bit))  23.7 us
  transfers between devices with their start and end apart: 70, of which 22 were waited for; matrix products, arithmetic and copies ran while one was open for 20% of the time, Pallas kernels for 21%

profile of v3, /device:TPU:0, one launch (start us, length us, event | category | flops | bytes accessed | tf_op | source)
XLA Modules:
  0.0 581.0 jit_solution(16719557157786008270)
XLA Ops:
  10.0 3.1 collective-permute-start.1
  22.8 16.6 %collective-permute-done.1 = bf16[512,1024]{1,0:T(8,128)(2,1)S(1)} collective-permute-done((bf16[512,1024]{1,0:T(8,128)(2,1)}, bf16[512,1024]{1,0:T(8,128)(2,1)S(1)}, u32[]{:S(2)}, u32[]{:S(2)}) %collective-permute-start.1) | collective-permute-done | bytes 1048608 | tf_op jit(solution)/shard_map/ppermute | solution.py:369
  40.6 33.3 %collective-permute-done.2 = bf16[512,1024]{1,0:T(8,128)(2,1)S(1)} collective-permute-done((bf16[512,1024]{1,0:T(8,128)(2,1)S(1)}, bf16[512,1024]{1,0:T(8,128)(2,1)S(1)}, u32[]{:S(2)}, u32[]{:S(2)}) %collective-permute-start.2) | collective-permute-done | bytes 1048608 | tf_op jit(solution)/shard_map/ppermute | solution.py:369
  77.6 25.6 %collective-permute-done.3 = bf16[512,1024]{1,0:T(8,128)(2,1)S(1)} collective-permute-done((bf16[512,1024]{1,0:T(8,128)(2,1)S(1)}, bf16[512,1024]{1,0:T(8,128)(2,1)S(1)}, u32[]{:S(2)}, u32[]{:S(2)}) %collective-permute-start.3) | collective-permute-done | bytes 1048608 | tf_op jit(solution)/shard_map/ppermute | solution.py:369
  103.9 4.8 convolution_convert_fusion.q_ref.k_ref.v_ref
  108.8 15.9 %attend.3 = (f32[2048,128]{1,0:T(8,128)}, f32[2,2048]{1,0:T(2,128)}) custom-call(s32[2]{0:T(128)} %get-tuple-element.117.lo_ref, s32[2]{0:T(128)} %get-tuple-element.116.hi_ref, bf16[2048,768]{1,0:T(8,128)(2,1)} %convolution_convert_fusion.q_ref.k_ref.v_ref, bf16[2048,768]{1,0:T(8,128)(2,1)} %convolution_convert_fusion.q_ref.k_ref.v_ref, ...), custom_call_target="tpu_custom_call" | custom-call | flops 8589934592 | bytes 2621440 | tf_op jit(solution)/shard_map/attend/pallas_call | solution.py:94
  124.7 16.0 %attend.2 = (f32[2048,128]{1,0:T(8,128)}, f32[2,2048]{1,0:T(2,128)}) custom-call(s32[2]{0:T(128)} %get-tuple-element.117.lo_ref, s32[2]{0:T(128)} %get-tuple-element.116.hi_ref, bf16[2048,768]{1,0:T(8,128)(2,1)} %convolution_convert_fusion.q_ref.k_ref.v_ref, bf16[2048,768]{1,0:T(8,128)(2,1)} %convolution_convert_fusion.q_ref.k_ref.v_ref, ...), custom_call_target="tpu_custom_call" | custom-call | flops 8589934592 | bytes 2621440 | tf_op jit(solution)/shard_map/attend/pallas_call | solution.py:94
  143.3 5.1 all-to-all-start
  148.4 5.7 collective-permute-start.10
  154.1 2.0 collective-permute-start.8
  156.2 2.0 collective-permute-start.5
  159.1 10.5 %collective-permute-done.13.refs_11_ = bf16[3,704,128]{2,1,0:T(8,128)(2,1)} collective-permute-done((bf16[3,704,128]{2,1,0:T(8,128)(2,1)}, bf16[3,704,128]{2,1,0:T(8,128)(2,1)}, u32[]{:S(2)}, u32[]{:S(2)}) %collective-permute-start.13) | collective-permute-done | bytes 540704 | tf_op jit(solution)/shard_map/ppermute | solution.py:338
  169.6 10.7 %collective-permute-done.8.refs_5_ = bf16[3,704,128]{2,1,0:T(8,128)(2,1)} collective-permute-done((bf16[3,704,128]{2,1,0:T(8,128)(2,1)}, bf16[3,704,128]{2,1,0:T(8,128)(2,1)}, u32[]{:S(2)}, u32[]{:S(2)}) %collective-permute-start.8) | collective-permute-done | bytes 540704 | tf_op jit(solution)/shard_map/ppermute | solution.py:343
  181.8 5.0 all-to-all-start.1
  187.5 6.5 %collective-permute-done.15.refs_13_ = bf16[3,704,128]{2,1,0:T(8,128)(2,1)} collective-permute-done((bf16[3,704,128]{2,1,0:T(8,128)(2,1)}, bf16[3,704,128]{2,1,0:T(8,128)(2,1)}, u32[]{:S(2)}, u32[]{:S(2)}) %collective-permute-start.15) | collective-permute-done | bytes 540704 | tf_op jit(solution)/shard_map/ppermute | solution.py:343
  201.9 2.1 fusion.47
  204.0 1.7 collective-permute-start.28
  205.7 4.9 collective-permute-done.20.refs_3_
  212.3 9.3 %collective-permute-done.27.refs_11_ = bf16[3,704,128]{2,1,0:T(8,128)(2,1)} collective-permute-done((bf16[3,704,128]{2,1,0:T(8,128)(2,1)}, bf16[3,704,128]{2,1,0:T(8,128)(2,1)}, u32[]{:S(2)}, u32[]{:S(2)}) %collective-permute-start.27) | collective-permute-done | bytes 540704 | tf_op jit(solution)/shard_map/ppermute | solution.py:338
  222.7 2.9 multiply_reduce_fusion.2
  227.4 4.9 collective-permute-done.22.refs_5_
  234.4 23.9 %feed.2 = (f32[512,1024]{1,0:T(8,128)}, f32[512,1024]{1,0:T(8,128)}, bf16[2,3,704,128]{3,2,1,0:T(8,128)(2,1)}, bf16[2,3,704,128]{3,2,1,0:T(8,128)(2,1)}, bf16[2,...) custom-call(s32[16]{0:T(128)} %get-tuple-element.136.spots, ...), custom_call_target="tpu_custom_call" | custom-call | flops 19931332608 | bytes 23592960 | tf_op jit(solution)/shard_map/feed/pallas_call | solution.py:297
  258.9 24.1 %feed.3 = (f32[512,1024]{1,0:T(8,128)}, f32[512,1024]{1,0:T(8,128)}, bf16[2,3,704,128]{3,2,1,0:T(8,128)(2,1)}, bf16[2,3,704,128]{3,2,1,0:T(8,128)(2,1)}, bf16[2,...) custom-call(s32[16]{0:T(128)} %get-tuple-element.135.spots, ...), custom_call_target="tpu_custom_call" | custom-call | flops 19931332608 | bytes 23592960 | tf_op jit(solution)/shard_map/feed/pallas_call | solution.py:297
  283.0 3.0 multiply_reduce_fusion
  287.1 5.1 fusion.107
  294.1 4.7 all-to-all-start.3
  300.0 2.8 convolution_convert_fusion.4
  302.8 2.1 copy.100
  304.9 3.0 convolution_convert_fusion.1
  307.9 5.6 all-to-all-done.3
  313.5 4.1 all-to-all-start.2
  317.7 1.9 convolution_convert_fusion.2
  320.1 3.0 copy.110
  324.4 2.5 add_convert_fusion.3
  327.7 2.6 add_convert_fusion
  331.8 3.0 convert_multiply_fusion.8
  337.1 20.0 %attend_back.3 = bf16[2048,384]{1,0:T(8,128)(2,1)} custom-call(s32[4]{0:T(128)} %get-tuple-element.115.lo_ref, s32[4]{0:T(128)} %get-tuple-element.114.hi_ref, bf16[2048,768]{1,0:T(8,128)(2,1)} %convolution_convert_fusion.q_ref.k_ref.v_ref, bf16[2048,128]{1,0:T(8,128)(2,1)} %get-tuple-element.109.do_ref, f32[2,2048]{1,0:T(2,128)} %get-tuple-element.131.lse_ref, ...), custom_call_target="tpu_custom_call" | custom-call | flops 21474836480 | bytes 4194304 | tf_op jit(solution)/shard_map/attend_back/pallas_call | solution.py:170
  358.1 20.0 %attend_back.2 = bf16[2048,384]{1,0:T(8,128)(2,1)} custom-call(s32[4]{0:T(128)} %get-tuple-element.115.lo_ref, s32[4]{0:T(128)} %get-tuple-element.114.hi_ref, bf16[2048,768]{1,0:T(8,128)(2,1)} %convolution_convert_fusion.q_ref.k_ref.v_ref, bf16[2048,128]{1,0:T(8,128)(2,1)} %get-tuple-element.134.do_ref, f32[2,2048]{1,0:T(2,128)} %get-tuple-element.132.lse_ref, ...), custom_call_target="tpu_custom_call" | custom-call | flops 21474836480 | bytes 4194304 | tf_op jit(solution)/shard_map/attend_back/pallas_call | solution.py:170
  378.1 7.4 %fusion.29 = bf16[768,1024]{1,0:T(8,128)(2,1)} fusion(bf16[2048,1024]{1,0:T(8,128)(2,1)} %copy-done.17, bf16[2048,384]{1,0:T(8,128)(2,1)S(1)} %copy-done.10, bf16[2048,384]{1,0:T(8,128)(2,1)} %attend_back.2), kind=kOutput, calls=%fused_computation.66 | convolution fusion | flops 3228303360 | bytes 8912896 | tf_op jit(solution)/shard_map/dot_general | solution.py:50
  385.4 2.6 copy.108
  388.3 2.7 fusion.57
  395.5 17.2 %collective-permute-start.42 = (bf16[2,3,704,128]{3,2,1,0:T(8,128)(2,1)S(1)}, bf16[2,3,704,128]{3,2,1,0:T(8,128)(2,1)S(1)}, u32[]{:S(2)}, u32[]{:S(2)}) collective-permute-start(bf16[2,3,704,128]{3,2,1,0:T(8,128)(2,1)S(1)} %copy-done.70), channel_id=1, source_target_pairs={{0,4},{4,0},{8,12},{12,8},{16,20},{20,16},{24,28},{28,24},{1,5},{5... | collective-permute-start | bytes 3244040 | tf_op jit(solution)/shard_map/ppermute | solution.py:350
  416.2 2.0 convert_add_fusion.4
  423.0 18.8 %collective-permute-done.34 = bf16[512,1024]{1,0:T(8,128)(2,1)S(1)} collective-permute-done((bf16[512,1024]{1,0:T(8,128)(2,1)S(1)}, bf16[512,1024]{1,0:T(8,128)(2,1)S(1)}, u32[]{:S(2)}, u32[]{:S(2)}) %collective-permute-start.34) | collective-permute-done | bytes 1048608 | tf_op jit(solution)/shard_map/ppermute | solution.py:369
  442.3 20.7 %collective-permute-done.40 = bf16[3,704,128]{2,1,0:T(8,128)(2,1)S(1)} collective-permute-done((bf16[3,704,128]{2,1,0:T(8,128)(2,1)S(1)}, bf16[3,704,128]{2,1,0:T(8,128)(2,1)S(1)}, u32[]{:S(2)}, u32[]{:S(2)}) %collective-permute-start.40) | collective-permute-done | bytes 540704 | tf_op jit(solution)/shard_map/ppermute | solution.py:350
  466.6 2.1 collective-permute-start.45
  471.5 1.9 collective-permute-start.50
  473.4 27.3 %collective-permute-done.41 = bf16[3,704,128]{2,1,0:T(8,128)(2,1)S(1)} collective-permute-done((bf16[3,704,128]{2,1,0:T(8,128)(2,1)S(1)}, bf16[3,704,128]{2,1,0:T(8,128)(2,1)S(1)}, u32[]{:S(2)}, u32[]{:S(2)}) %collective-permute-start.41) | collective-permute-done | bytes 540704 | tf_op jit(solution)/shard_map/ppermute | solution.py:369
  504.2 1.8 copy.111
  507.9 1.9 copy.106
  509.8 2.1 reshape.199
  511.9 2.8 fusion.105
  514.6 3.7 collective-permute-done.46
  518.3 2.2 fusion.34
  520.7 10.0 %reduce-scatter.8.cloned.1.call-done = bf16[256,128]{1,0:T(8,128)(2,1)} async-done(((bf16[1024,128]{1,0:T(8,128)(2,1)}), bf16[256,128]{1,0:T(8,128)(2,1)}) %reduce-scatter.8.cloned.1.call-update) | async-done | bytes 65552 | tf_op jit(solution)/shard_map/reduce_scatter | solution.py:477
  530.7 1.8 fusion.102
  532.4 12.4 %collective-permute-done.36 = bf16[512,1024]{1,0:T(8,128)(2,1)} collective-permute-done((bf16[512,1024]{1,0:T(8,128)(2,1)}, bf16[512,1024]{1,0:T(8,128)(2,1)}, u32[]{:S(2)}, u32[]{:S(2)}) %collective-permute-start.36) | collective-permute-done | bytes 1048608 | tf_op jit(solution)/shard_map/ppermute | solution.py:369
  544.9 3.3 fusion.26
  548.3 8.1 %collective-permute-done.51 = bf16[3,704,128]{2,1,0:T(8,128)(2,1)} collective-permute-done((bf16[3,704,128]{2,1,0:T(8,128)(2,1)}, bf16[3,704,128]{2,1,0:T(8,128)(2,1)}, u32[]{:S(2)}, u32[]{:S(2)}) %collective-permute-start.51) | collective-permute-done | bytes 540704 | tf_op jit(solution)/shard_map/ppermute | solution.py:369
  558.0 1.8 fusion.100
  559.8 2.7 collective-permute-done.57
  563.8 2.6 collective-permute-start.59
  568.1 2.3 collective-permute-start.60
  570.4 3.2 fusion.25
  (339 shorter events, 79.8 us)
Async XLA Ops:
  7.2 67.1 %all-gather.4.cloned.1.call-start = ((), (), s32[]{:S(2)}) async-start(), calls=%async_computation.7 | async-start | bytes 1806336 | tf_op jit(solution)/shard_map/all_gather | solution.py:410
  9.9 186.9 %all-gather.6.cloned.1.call-start = ((), (), s32[]{:S(2)}) async-start(), calls=%async_computation.9 | async-start | bytes 2162688 | tf_op jit(solution)/shard_map/all_gather | solution.py:414
  10.0 29.4 %collective-permute-start.1 = (bf16[512,1024]{1,0:T(8,128)(2,1)}, bf16[512,1024]{1,0:T(8,128)(2,1)S(1)}, u32[]{:S(2)}, u32[]{:S(2)}) collective-permute-start(bf16[512,1024]{1,0:T(8,128)(2,1)} %bitcast.155), channel_id=1, source_target_pairs={{0,1},{1,2},{2,3},{3,0},{4,5},{5,6},{6,7},{7,4},{8,9},{9,10},{10,1... | collective-permute-start | bytes 3145736 | tf_op jit(solution)/shard_map/ppermute | solution.py:369
  15.0 141.1 %collective-permute-start.9 = (bf16[3,704,128]{2,1,0:T(8,128)(2,1)}, bf16[3,704,128]{2,1,0:T(8,128)(2,1)}, u32[]{:S(2)}, u32[]{:S(2)}) collective-permute-start(bf16[3,704,128]{2,1,0:T(8,128)(2,1)} %pad_maximum_fusion.5.refs_2_), channel_id=1, source_target_pairs={{0,4},{4,0},{8,12},{12,8},{16,20},{20,16},{24,28},{28,24},{1,5},{5... | collective-permute-start | bytes 1622024 | tf_op jit(solution)/shard_map/ppermute | solution.py:338
  15.0 25.2 %collective-permute-start.7 = (bf16[3,704,128]{2,1,0:T(8,128)(2,1)}, bf16[3,704,128]{2,1,0:T(8,128)(2,1)}, u32[]{:S(2)}, u32[]{:S(2)}) collective-permute-start(bf16[3,704,128]{2,1,0:T(8,128)(2,1)} %pad_maximum_fusion.5.refs_2_), channel_id=1, source_target_pairs={{0,16},{4,20},{8,24},{12,28},{16,0},{20,4},{24,8},{28,12},{1,17},{... | collective-permute-start | bytes 1622024 | tf_op jit(solution)/shard_map/ppermute | solution.py:338
  16.5 131.9 %collective-permute-start.6 = (bf16[3,704,128]{2,1,0:T(8,128)(2,1)}, bf16[3,704,128]{2,1,0:T(8,128)(2,1)}, u32[]{:S(2)}, u32[]{:S(2)}) collective-permute-start(bf16[3,704,128]{2,1,0:T(8,128)(2,1)} %pad_maximum_fusion.5.refs_2_), channel_id=1, source_target_pairs={{0,8},{4,12},{8,0},{12,4},{16,24},{20,28},{24,16},{28,20},{1,9},{5... | collective-permute-start | bytes 1622024 | tf_op jit(solution)/shard_map/ppermute | solution.py:338
  18.0 59.5 %collective-permute-start = (bf16[3,704,128]{2,1,0:T(8,128)(2,1)}, bf16[3,704,128]{2,1,0:T(8,128)(2,1)}, u32[]{:S(2)}, u32[]{:S(2)}) collective-permute-start(bf16[3,704,128]{2,1,0:T(8,128)(2,1)} %pad_maximum_fusion.5.refs_2_), channel_id=1, source_target_pairs={{0,1},{1,2},{2,3},{3,0},{4,5},{5,6},{6,7},{7,4},{8,9},{9,10},{10,1... | collective-permute-start | bytes 1622024 | tf_op jit(solution)/shard_map/ppermute | solution.py:369
  39.4 34.6 %collective-permute-start.2 = (bf16[512,1024]{1,0:T(8,128)(2,1)S(1)}, bf16[512,1024]{1,0:T(8,128)(2,1)S(1)}, u32[]{:S(2)}, u32[]{:S(2)}) collective-permute-start(bf16[512,1024]{1,0:T(8,128)(2,1)S(1)} %collective-permute-done.1), channel_id=1, source_target_pairs={{0,1},{1,2},{2,3},{3,0},{4,5},{5,6},{6,7},{7,4},{8,9},{9,10},{10,1... | collective-permute-start | bytes 3145736 | tf_op jit(solution)/shard_map/ppermute | solution.py:369
  40.2 116.0 %collective-permute-start.11 = (bf16[3,704,128]{2,1,0:T(8,128)(2,1)}, bf16[3,704,128]{2,1,0:T(8,128)(2,1)}, u32[]{:S(2)}, u32[]{:S(2)}) collective-permute-start(bf16[3,704,128]{2,1,0:T(8,128)(2,1)} %collective-permute-done.7.refs_4_), channel_id=1, source_target_pairs={{0,4},{4,0},{8,12},{12,8},{16,20},{20,16},{24,28},{28,24},{1,5},{5... | collective-permute-start | bytes 1622024 | tf_op jit(solution)/shard_map/ppermute | solution.py:343
  74.3 28.9 %collective-permute-start.3 = (bf16[512,1024]{1,0:T(8,128)(2,1)S(1)}, bf16[512,1024]{1,0:T(8,128)(2,1)S(1)}, u32[]{:S(2)}, u32[]{:S(2)}) collective-permute-start(bf16[512,1024]{1,0:T(8,128)(2,1)S(1)} %collective-permute-done.2), channel_id=1, source_target_pairs={{0,1},{1,2},{2,3},{3,0},{4,5},{5,6},{6,7},{7,4},{8,9},{9,10},{10,1... | collective-permute-start | bytes 3145736 | tf_op jit(solution)/shard_map/ppermute | solution.py:369
  103.5 38.8 %collective-permute-start.4 = (bf16[3,704,128]{2,1,0:T(8,128)(2,1)}, bf16[3,704,128]{2,1,0:T(8,128)(2,1)}, u32[]{:S(2)}, u32[]{:S(2)}) collective-permute-start(bf16[3,704,128]{2,1,0:T(8,128)(2,1)} %collective-permute-done.refs_10_), channel_id=1, source_target_pairs={{0,1},{1,2},{2,3},{3,0},{4,5},{5,6},{6,7},{7,4},{8,9},{9,10},{10,1... | collective-permute-start | bytes 1622024 | tf_op jit(solution)/shard_map/ppermute | solution.py:369
  143.3 38.5 %all-to-all-start = ((bf16[4,512,128]{1,2,0:T(8,128)(2,1)}), bf16[4,512,128]{1,2,0:T(8,128)(2,1)S(1)}, u32[]{:S(2)}, u32[]{:S(2)}) async-start(bf16[4,512,128]{1,2,0:T(8,128)(2,1)} %copy.95), calls=%async_computation | async-start | bytes 1048576 | tf_op jit(solution)/shard_map/all_to_all | solution.py:443
  148.4 10.7 %collective-permute-start.10 = (bf16[3,704,128]{2,1,0:T(8,128)(2,1)}, bf16[3,704,128]{2,1,0:T(8,128)(2,1)}, u32[]{:S(2)}, u32[]{:S(2)}) collective-permute-start(bf16[3,704,128]{2,1,0:T(8,128)(2,1)} %collective-permute-done.6.refs_3_), channel_id=1, source_target_pairs={{0,4},{4,0},{8,12},{12,8},{16,20},{20,16},{24,28},{28,24},{1,5},{5... | collective-permute-start | bytes 1622024 | tf_op jit(solution)/shard_map/ppermute | solution.py:343
  154.1 15.5 %collective-permute-start.13 = (bf16[3,704,128]{2,1,0:T(8,128)(2,1)}, bf16[3,704,128]{2,1,0:T(8,128)(2,1)}, u32[]{:S(2)}, u32[]{:S(2)}) collective-permute-start(bf16[3,704,128]{2,1,0:T(8,128)(2,1)} %collective-permute-done.refs_10_), channel_id=1, source_target_pairs={{0,16},{4,20},{8,24},{12,28},{16,0},{20,4},{24,8},{28,12},{1,17},{... | collective-permute-start | bytes 1622024 | tf_op jit(solution)/shard_map/ppermute | solution.py:338
  154.1 26.1 %collective-permute-start.8 = (bf16[3,704,128]{2,1,0:T(8,128)(2,1)}, bf16[3,704,128]{2,1,0:T(8,128)(2,1)}, u32[]{:S(2)}, u32[]{:S(2)}) collective-permute-start(bf16[3,704,128]{2,1,0:T(8,128)(2,1)} %collective-permute-done.6.refs_3_), channel_id=1, source_target_pairs={{0,16},{4,20},{8,24},{12,28},{16,0},{20,4},{24,8},{28,12},{1,17},{... | collective-permute-start | bytes 1622024 | tf_op jit(solution)/shard_map/ppermute | solution.py:343
  156.2 24.1 %collective-permute-start.14 = (bf16[3,704,128]{2,1,0:T(8,128)(2,1)}, bf16[3,704,128]{2,1,0:T(8,128)(2,1)}, u32[]{:S(2)}, u32[]{:S(2)}) collective-permute-start(bf16[3,704,128]{2,1,0:T(8,128)(2,1)} %collective-permute-done.refs_10_), channel_id=1, source_target_pairs={{0,8},{4,12},{8,0},{12,4},{16,24},{20,28},{24,16},{28,20},{1,9},{5... | collective-permute-start | bytes 1622024 | tf_op jit(solution)/shard_map/ppermute | solution.py:338
  156.2 24.1 %collective-permute-start.5 = (bf16[3,704,128]{2,1,0:T(8,128)(2,1)}, bf16[3,704,128]{2,1,0:T(8,128)(2,1)}, u32[]{:S(2)}, u32[]{:S(2)}) collective-permute-start(bf16[3,704,128]{2,1,0:T(8,128)(2,1)} %collective-permute-done.4.refs_2_), channel_id=1, source_target_pairs={{0,1},{1,2},{2,3},{3,0},{4,5},{5,6},{6,7},{7,4},{8,9},{9,10},{10,1... | collective-permute-start | bytes 1622024 | tf_op jit(solution)/shard_map/ppermute | solution.py:369
  159.1 34.9 %collective-permute-start.16 = (bf16[3,704,128]{2,1,0:T(8,128)(2,1)}, bf16[3,704,128]{2,1,0:T(8,128)(2,1)}, u32[]{:S(2)}, u32[]{:S(2)}) collective-permute-start(bf16[3,704,128]{2,1,0:T(8,128)(2,1)} %collective-permute-done.refs_10_), channel_id=1, source_target_pairs={{0,4},{4,0},{8,12},{12,8},{16,20},{20,16},{24,28},{28,24},{1,5},{5... | collective-permute-start | bytes 1622024 | tf_op jit(solution)/shard_map/ppermute | solution.py:338
  169.6 26.7 %collective-permute-start.17 = (bf16[3,704,128]{2,1,0:T(8,128)(2,1)}, bf16[3,704,128]{2,1,0:T(8,128)(2,1)}, u32[]{:S(2)}, u32[]{:S(2)}) collective-permute-start(bf16[3,704,128]{2,1,0:T(8,128)(2,1)} %collective-permute-done.13.refs_11_), channel_id=1, source_target_pairs={{0,4},{4,0},{8,12},{12,8},{16,20},{20,16},{24,28},{28,24},{1,5},{5... | collective-permute-start | bytes 1622024 | tf_op jit(solution)/shard_map/ppermute | solution.py:343
  180.3 13.7 %collective-permute-start.15 = (bf16[3,704,128]{2,1,0:T(8,128)(2,1)}, bf16[3,704,128]{2,1,0:T(8,128)(2,1)}, u32[]{:S(2)}, u32[]{:S(2)}) collective-permute-start(bf16[3,704,128]{2,1,0:T(8,128)(2,1)} %collective-permute-done.13.refs_11_), channel_id=1, source_target_pairs={{0,8},{4,12},{8,0},{12,4},{16,24},{20,28},{24,16},{28,20},{1,9},{5... | collective-permute-start | bytes 1622024 | tf_op jit(solution)/shard_map/ppermute | solution.py:343
  180.3 14.2 %collective-permute-start.12 = (bf16[3,704,128]{2,1,0:T(8,128)(2,1)}, bf16[3,704,128]{2,1,0:T(8,128)(2,1)}, u32[]{:S(2)}, u32[]{:S(2)}) collective-permute-start(bf16[3,704,128]{2,1,0:T(8,128)(2,1)} %collective-permute-done.8.refs_5_), channel_id=1, source_target_pairs={{0,4},{4,0},{8,12},{12,8},{16,20},{20,16},{24,28},{28,24},{1,5},{5... | collective-permute-start | bytes 1622024 | tf_op jit(solution)/shard_map/ppermute | solution.py:343
  180.3 14.8 %collective-permute-start.18 = (bf16[3,704,128]{2,1,0:T(8,128)(2,1)}, bf16[3,704,128]{2,1,0:T(8,128)(2,1)}, u32[]{:S(2)}, u32[]{:S(2)}) collective-permute-start(bf16[3,704,128]{2,1,0:T(8,128)(2,1)} %collective-permute-done.14.refs_12_), channel_id=1, source_target_pairs={{0,4},{4,0},{8,12},{12,8},{16,20},{20,16},{24,28},{28,24},{1,5},{5... | collective-permute-start | bytes 1622024 | tf_op jit(solution)/shard_map/ppermute | solution.py:343
  181.8 40.0 %all-to-all-start.1 = ((bf16[4,512,128]{1,2,0:T(8,128)(2,1)}), bf16[4,512,128]{1,2,0:T(8,128)(2,1)S(1)}, u32[]{:S(2)}, u32[]{:S(2)}) async-start(bf16[4,512,128]{1,2,0:T(8,128)(2,1)} %copy.98), calls=%async_computation.1 | async-start | bytes 1048576 | tf_op jit(solution)/shard_map/all_to_all | solution.py:443
  194.0 16.6 %collective-permute-start.23 = (bf16[3,704,128]{2,1,0:T(8,128)(2,1)}, bf16[3,704,128]{2,1,0:T(8,128)(2,1)S(1)}, u32[]{:S(2)}, u32[]{:S(2)}) collective-permute-start(bf16[3,704,128]{2,1,0:T(8,128)(2,1)} %collective-permute-done.4.refs_2_), channel_id=1, source_target_pairs={{0,4},{4,0},{8,12},{12,8},{16,20},{20,16},{24,28},{28,24},{1,5},{5... | collective-permute-start | bytes 1622024 | tf_op jit(solution)/shard_map/ppermute | solution.py:338
  194.5 17.6 %collective-permute-start.21 = (bf16[3,704,128]{2,1,0:T(8,128)(2,1)}, bf16[3,704,128]{2,1,0:T(8,128)(2,1)}, u32[]{:S(2)}, u32[]{:S(2)}) collective-permute-start(bf16[3,704,128]{2,1,0:T(8,128)(2,1)} %collective-permute-done.4.refs_2_), channel_id=1, source_target_pairs={{0,16},{4,20},{8,24},{12,28},{16,0},{20,4},{24,8},{28,12},{1,17},{... | collective-permute-start | bytes 1622024 | tf_op jit(solution)/shard_map/ppermute | solution.py:338
  195.1 15.5 %collective-permute-start.20 = (bf16[3,704,128]{2,1,0:T(8,128)(2,1)}, bf16[3,704,128]{2,1,0:T(8,128)(2,1)}, u32[]{:S(2)}, u32[]{:S(2)}) collective-permute-start(bf16[3,704,128]{2,1,0:T(8,128)(2,1)} %collective-permute-done.4.refs_2_), channel_id=1, source_target_pairs={{0,8},{4,12},{8,0},{12,4},{16,24},{20,28},{24,16},{28,20},{1,9},{5... | collective-permute-start | bytes 1622024 | tf_op jit(solution)/shard_map/ppermute | solution.py:338
  196.3 25.2 %collective-permute-start.27 = (bf16[3,704,128]{2,1,0:T(8,128)(2,1)}, bf16[3,704,128]{2,1,0:T(8,128)(2,1)}, u32[]{:S(2)}, u32[]{:S(2)}) collective-permute-start(bf16[3,704,128]{2,1,0:T(8,128)(2,1)} %collective-permute-done.5.refs_10_), channel_id=1, source_target_pairs={{0,16},{4,20},{8,24},{12,28},{16,0},{20,4},{24,8},{28,12},{1,17},{... | collective-permute-start | bytes 1622024 | tf_op jit(solution)/shard_map/ppermute | solution.py:338
  204.0 28.3 %collective-permute-start.28 = (bf16[3,704,128]{2,1,0:T(8,128)(2,1)}, bf16[3,704,128]{2,1,0:T(8,128)(2,1)}, u32[]{:S(2)}, u32[]{:S(2)}) collective-permute-start(bf16[3,704,128]{2,1,0:T(8,128)(2,1)} %collective-permute-done.5.refs_10_), channel_id=1, source_target_pairs={{0,8},{4,12},{8,0},{12,4},{16,24},{20,28},{24,16},{28,20},{1,9},{5... | collective-permute-start | bytes 1622024 | tf_op jit(solution)/shard_map/ppermute | solution.py:338
  210.6 16.3 %collective-permute-start.24 = (bf16[3,704,128]{2,1,0:T(8,128)(2,1)}, bf16[3,704,128]{2,1,0:T(8,128)(2,1)}, u32[]{:S(2)}, u32[]{:S(2)}) collective-permute-start(bf16[3,704,128]{2,1,0:T(8,128)(2,1)} %collective-permute-done.20.refs_3_), channel_id=1, source_target_pairs={{0,4},{4,0},{8,12},{12,8},{16,20},{20,16},{24,28},{28,24},{1,5},{5... | collective-permute-start | bytes 1622024 | tf_op jit(solution)/shard_map/ppermute | solution.py:343
  210.6 21.7 %collective-permute-start.22 = (bf16[3,704,128]{2,1,0:T(8,128)(2,1)}, bf16[3,704,128]{2,1,0:T(8,128)(2,1)}, u32[]{:S(2)}, u32[]{:S(2)}) collective-permute-start(bf16[3,704,128]{2,1,0:T(8,128)(2,1)} %collective-permute-done.20.refs_3_), channel_id=1, source_target_pairs={{0,16},{4,20},{8,24},{12,28},{16,0},{20,4},{24,8},{28,12},{1,17},{... | collective-permute-start | bytes 1622024 | tf_op jit(solution)/shard_map/ppermute | solution.py:343
  212.1 14.8 %collective-permute-start.25 = (bf16[3,704,128]{2,1,0:T(8,128)(2,1)}, bf16[3,704,128]{2,1,0:T(8,128)(2,1)}, u32[]{:S(2)}, u32[]{:S(2)}) collective-permute-start(bf16[3,704,128]{2,1,0:T(8,128)(2,1)} %collective-permute-done.21.refs_4_), channel_id=1, source_target_pairs={{0,4},{4,0},{8,12},{12,8},{16,20},{20,16},{24,28},{28,24},{1,5},{5... | collective-permute-start | bytes 1622024 | tf_op jit(solution)/shard_map/ppermute | solution.py:343
  221.6 12.8 %collective-permute-start.29 = (bf16[3,704,128]{2,1,0:T(8,128)(2,1)}, bf16[3,704,128]{2,1,0:T(8,128)(2,1)}, u32[]{:S(2)}, u32[]{:S(2)}) collective-permute-start(bf16[3,704,128]{2,1,0:T(8,128)(2,1)} %collective-permute-done.27.refs_11_), channel_id=1, source_target_pairs={{0,8},{4,12},{8,0},{12,4},{16,24},{20,28},{24,16},{28,20},{1,9},{5... | collective-permute-start | bytes 1622024 | tf_op jit(solution)/shard_map/ppermute | solution.py:343
  226.9 31.4 %collective-permute-start.30 = (bf16[3,704,128]{2,1,0:T(8,128)(2,1)}, bf16[3,704,128]{2,1,0:T(8,128)(2,1)}, u32[]{:S(2)}, u32[]{:S(2)}) collective-permute-start(bf16[3,704,128]{2,1,0:T(8,128)(2,1)} %collective-permute-done.5.refs_10_), channel_id=1, source_target_pairs={{0,4},{4,0},{8,12},{12,8},{16,20},{20,16},{24,28},{28,24},{1,5},{5... | collective-permute-start | bytes 1622024 | tf_op jit(solution)/shard_map/ppermute | solution.py:338
  226.9 32.0 %collective-permute-start.31 = (bf16[3,704,128]{2,1,0:T(8,128)(2,1)}, bf16[3,704,128]{2,1,0:T(8,128)(2,1)}, u32[]{:S(2)}, u32[]{:S(2)}) collective-permute-start(bf16[3,704,128]{2,1,0:T(8,128)(2,1)} %collective-permute-done.27.refs_11_), channel_id=1, source_target_pairs={{0,4},{4,0},{8,12},{12,8},{16,20},{20,16},{24,28},{28,24},{1,5},{5... | collective-permute-start | bytes 1622024 | tf_op jit(solution)/shard_map/ppermute | solution.py:343
  232.3 26.6 %collective-permute-start.26 = (bf16[3,704,128]{2,1,0:T(8,128)(2,1)}, bf16[3,704,128]{2,1,0:T(8,128)(2,1)}, u32[]{:S(2)}, u32[]{:S(2)}) collective-permute-start(bf16[3,704,128]{2,1,0:T(8,128)(2,1)} %collective-permute-done.22.refs_5_), channel_id=1, source_target_pairs={{0,4},{4,0},{8,12},{12,8},{16,20},{20,16},{24,28},{28,24},{1,5},{5... | collective-permute-start | bytes 1622024 | tf_op jit(solution)/shard_map/ppermute | solution.py:343
  232.3 26.6 %collective-permute-start.32 = (bf16[3,704,128]{2,1,0:T(8,128)(2,1)}, bf16[3,704,128]{2,1,0:T(8,128)(2,1)}, u32[]{:S(2)}, u32[]{:S(2)}) collective-permute-start(bf16[3,704,128]{2,1,0:T(8,128)(2,1)} %collective-permute-done.28.refs_12_), channel_id=1, source_target_pairs={{0,4},{4,0},{8,12},{12,8},{16,20},{20,16},{24,28},{28,24},{1,5},{5... | collective-permute-start | bytes 1622024 | tf_op jit(solution)/shard_map/ppermute | solution.py:343
  234.4 24.5 %collective-permute-start.33 = (bf16[3,704,128]{2,1,0:T(8,128)(2,1)}, bf16[3,704,128]{2,1,0:T(8,128)(2,1)}, u32[]{:S(2)}, u32[]{:S(2)}) collective-permute-start(bf16[3,704,128]{2,1,0:T(8,128)(2,1)} %collective-permute-done.29.refs_13_), channel_id=1, source_target_pairs={{0,4},{4,0},{8,12},{12,8},{16,20},{20,16},{24,28},{28,24},{1,5},{5... | collective-permute-start | bytes 1622024 | tf_op jit(solution)/shard_map/ppermute | solution.py:343
  258.3 64.9 %collective-permute-start.38 = (bf16[2,3,704,128]{3,2,1,0:T(8,128)(2,1)}, bf16[2,3,704,128]{3,2,1,0:T(8,128)(2,1)}, u32[]{:S(2)}, u32[]{:S(2)}) collective-permute-start(bf16[2,3,704,128]{3,2,1,0:T(8,128)(2,1)} %get-tuple-element.67), channel_id=1, source_target_pairs={{0,4},{4,0},{8,12},{12,8},{16,20},{20,16},{24,28},{28,24},{1,5},{5... | collective-permute-start | bytes 3244040 | tf_op jit(solution)/shard_map/ppermute | solution.py:350
  294.1 19.4 %all-to-all-start.3 = ((bf16[512,4,128]{2,0,1:T(8,128)(2,1)}), bf16[512,4,128]{2,0,1:T(8,128)(2,1)S(1)}, u32[]{:S(2)}, u32[]{:S(2)}) async-start(bf16[512,4,128]{2,0,1:T(8,128)(2,1)} %copy.103), calls=%async_computation.3 | async-start | bytes 1048576 | tf_op jit(solution)/shard_map/all_to_all | solution.py:471
  299.5 114.9 %collective-permute-start.37 = (bf16[2,3,704,128]{3,2,1,0:T(8,128)(2,1)}, bf16[2,3,704,128]{3,2,1,0:T(8,128)(2,1)}, u32[]{:S(2)}, u32[]{:S(2)}) collective-permute-start(bf16[2,3,704,128]{3,2,1,0:T(8,128)(2,1)} %get-tuple-element.65), channel_id=1, source_target_pairs={{0,4},{4,0},{8,12},{12,8},{16,20},{20,16},{24,28},{28,24},{1,5},{5... | collective-permute-start | bytes 3244040 | tf_op jit(solution)/shard_map/ppermute | solution.py:350
  299.5 118.8 %collective-permute-start.52 = (bf16[2,3,704,128]{3,2,1,0:T(8,128)(2,1)}, bf16[2,3,704,128]{3,2,1,0:T(8,128)(2,1)}, u32[]{:S(2)}, u32[]{:S(2)}) collective-permute-start(bf16[2,3,704,128]{3,2,1,0:T(8,128)(2,1)} %get-tuple-element.77), channel_id=1, source_target_pairs={{0,4},{4,0},{8,12},{12,8},{16,20},{20,16},{24,28},{28,24},{1,5},{5... | collective-permute-start | bytes 3244040 | tf_op jit(solution)/shard_map/ppermute | solution.py:350
  300.0 26.9 %collective-permute-start.53 = (bf16[2,3,704,128]{3,2,1,0:T(8,128)(2,1)}, bf16[2,3,704,128]{3,2,1,0:T(8,128)(2,1)}, u32[]{:S(2)}, u32[]{:S(2)}) collective-permute-start(bf16[2,3,704,128]{3,2,1,0:T(8,128)(2,1)} %get-tuple-element.79), channel_id=1, source_target_pairs={{0,4},{4,0},{8,12},{12,8},{16,20},{20,16},{24,28},{28,24},{1,5},{5... | collective-permute-start | bytes 3244040 | tf_op jit(solution)/shard_map/ppermute | solution.py:350
  313.5 18.3 %all-to-all-start.2 = ((bf16[512,4,128]{2,0,1:T(8,128)(2,1)}), bf16[512,4,128]{2,0,1:T(8,128)(2,1)}, u32[]{:S(2)}, u32[]{:S(2)}) async-start(bf16[512,4,128]{2,0,1:T(8,128)(2,1)} %copy.100), calls=%async_computation.2 | async-start | bytes 1048576 | tf_op jit(solution)/shard_map/all_to_all | solution.py:471
  317.7 186.5 %reduce-scatter.12.cloned.1.call-start = ((), (), s32[]{:S(2)}) async-start(), calls=%async_computation.11 | async-start | bytes 2359296
  319.7 73.6 %collective-permute-start.43 = (bf16[2,3,704,128]{3,2,1,0:T(8,128)(2,1)}, bf16[2,3,704,128]{3,2,1,0:T(8,128)(2,1)}, u32[]{:S(2)}, u32[]{:S(2)}) collective-permute-start(bf16[2,3,704,128]{3,2,1,0:T(8,128)(2,1)} %get-tuple-element.71), channel_id=1, source_target_pairs={{0,4},{4,0},{8,12},{12,8},{16,20},{20,16},{24,28},{28,24},{1,5},{5... | collective-permute-start | bytes 3244040 | tf_op jit(solution)/shard_map/ppermute | solution.py:350
  323.2 182.8 %reduce-scatter.10.cloned.1.call-start = ((), (), s32[]{:S(2)}) async-start(), calls=%async_computation.10 | async-start | bytes 1769472
  323.2 72.3 %collective-permute-start.48 = (bf16[2,3,704,128]{3,2,1,0:T(8,128)(2,1)}, bf16[2,3,704,128]{3,2,1,0:T(8,128)(2,1)}, u32[]{:S(2)}, u32[]{:S(2)}) collective-permute-start(bf16[2,3,704,128]{3,2,1,0:T(8,128)(2,1)} %get-tuple-element.75), channel_id=1, source_target_pairs={{0,4},{4,0},{8,12},{12,8},{16,20},{20,16},{24,28},{28,24},{1,5},{5... | collective-permute-start | bytes 3244040 | tf_op jit(solution)/shard_map/ppermute | solution.py:350
  326.9 87.7 %collective-permute-start.39 = (bf16[2,3,704,128]{3,2,1,0:T(8,128)(2,1)}, bf16[2,3,704,128]{3,2,1,0:T(8,128)(2,1)}, u32[]{:S(2)}, u32[]{:S(2)}) collective-permute-start(bf16[2,3,704,128]{3,2,1,0:T(8,128)(2,1)} %add_convert_fusion.3), channel_id=1, source_target_pairs={{0,8},{4,12},{8,0},{12,4},{16,24},{20,28},{24,16},{28,20},{1,9},{5... | collective-permute-start | bytes 3244040 | tf_op jit(solution)/shard_map/ppermute | solution.py:350
  388.0 142.6 %reduce-scatter.8.cloned.1.call-start = ((), (), s32[]{:S(2)}) async-start(), calls=%async_computation.8 | async-start | bytes 327680 | tf_op jit(solution)/shard_map/reduce_scatter | solution.py:477
  393.4 26.2 %collective-permute-start.54 = (bf16[2,3,704,128]{3,2,1,0:T(8,128)(2,1)S(1)}, bf16[2,3,704,128]{3,2,1,0:T(8,128)(2,1)S(1)}, u32[]{:S(2)}, u32[]{:S(2)}) collective-permute-start(bf16[2,3,704,128]{3,2,1,0:T(8,128)(2,1)S(1)} %copy-done.38), channel_id=1, source_target_pairs={{0,16},{4,20},{8,24},{12,28},{16,0},{20,4},{24,8},{28,12},{1,17},{... | collective-permute-start | bytes 3244040 | tf_op jit(solution)/shard_map/ppermute | solution.py:350
  395.5 67.6 %collective-permute-start.42 = (bf16[2,3,704,128]{3,2,1,0:T(8,128)(2,1)S(1)}, bf16[2,3,704,128]{3,2,1,0:T(8,128)(2,1)S(1)}, u32[]{:S(2)}, u32[]{:S(2)}) collective-permute-start(bf16[2,3,704,128]{3,2,1,0:T(8,128)(2,1)S(1)} %copy-done.70), channel_id=1, source_target_pairs={{0,4},{4,0},{8,12},{12,8},{16,20},{20,16},{24,28},{28,24},{1,5},{5... | collective-permute-start | bytes 3244040 | tf_op jit(solution)/shard_map/ppermute | solution.py:350
  414.4 52.2 %collective-permute-start.47 = (bf16[2,3,704,128]{3,2,1,0:T(8,128)(2,1)S(1)}, bf16[2,3,704,128]{3,2,1,0:T(8,128)(2,1)S(1)}, u32[]{:S(2)}, u32[]{:S(2)}) collective-permute-start(bf16[2,3,704,128]{3,2,1,0:T(8,128)(2,1)S(1)} %copy-done.69), channel_id=1, source_target_pairs={{0,4},{4,0},{8,12},{12,8},{16,20},{20,16},{24,28},{28,24},{1,5},{5... | collective-permute-start | bytes 3244040 | tf_op jit(solution)/shard_map/ppermute | solution.py:350
  414.6 27.2 %collective-permute-start.34 = (bf16[512,1024]{1,0:T(8,128)(2,1)S(1)}, bf16[512,1024]{1,0:T(8,128)(2,1)S(1)}, u32[]{:S(2)}, u32[]{:S(2)}) collective-permute-start(bf16[512,1024]{1,0:T(8,128)(2,1)S(1)} %get-tuple-element.121), channel_id=1, source_target_pairs={{0,1},{1,2},{2,3},{3,0},{4,5},{5,6},{6,7},{7,4},{8,9},{9,10},{10,1... | collective-permute-start | bytes 3145736 | tf_op jit(solution)/shard_map/ppermute | solution.py:369
  418.3 46.4 %collective-permute-start.44 = (bf16[2,3,704,128]{3,2,1,0:T(8,128)(2,1)S(1)}, bf16[2,3,704,128]{3,2,1,0:T(8,128)(2,1)S(1)}, u32[]{:S(2)}, u32[]{:S(2)}) collective-permute-start(bf16[2,3,704,128]{3,2,1,0:T(8,128)(2,1)S(1)} %add_convert_fusion.2), channel_id=1, source_target_pairs={{0,16},{4,20},{8,24},{12,28},{16,0},{20,4},{24,8},{28,12},{1,17},{... | collective-permute-start | bytes 3244040 | tf_op jit(solution)/shard_map/ppermute | solution.py:350
  419.6 43.4 %collective-permute-start.40 = (bf16[3,704,128]{2,1,0:T(8,128)(2,1)S(1)}, bf16[3,704,128]{2,1,0:T(8,128)(2,1)S(1)}, u32[]{:S(2)}, u32[]{:S(2)}) collective-permute-start(bf16[3,704,128]{2,1,0:T(8,128)(2,1)S(1)} %fusion.71), channel_id=1, source_target_pairs={{0,16},{4,20},{8,24},{12,28},{16,0},{20,4},{24,8},{28,12},{1,17},{... | collective-permute-start | bytes 1622024 | tf_op jit(solution)/shard_map/ppermute | solution.py:350
  441.8 27.1 %collective-permute-start.49 = (bf16[2,3,704,128]{3,2,1,0:T(8,128)(2,1)S(1)}, bf16[2,3,704,128]{3,2,1,0:T(8,128)(2,1)S(1)}, u32[]{:S(2)}, u32[]{:S(2)}) collective-permute-start(bf16[2,3,704,128]{3,2,1,0:T(8,128)(2,1)S(1)} %add_convert_fusion.1), channel_id=1, source_target_pairs={{0,8},{4,12},{8,0},{12,4},{16,24},{20,28},{24,16},{28,20},{1,9},{5... | collective-permute-start | bytes 3244040 | tf_op jit(solution)/shard_map/ppermute | solution.py:350
  463.0 85.3 %collective-permute-start.55 = (bf16[3,704,128]{2,1,0:T(8,128)(2,1)}, bf16[3,704,128]{2,1,0:T(8,128)(2,1)}, u32[]{:S(2)}, u32[]{:S(2)}) collective-permute-start(bf16[3,704,128]{2,1,0:T(8,128)(2,1)} %fusion.74), channel_id=1, source_target_pairs={{0,8},{4,12},{8,0},{12,4},{16,24},{20,28},{24,16},{28,20},{1,9},{5... | collective-permute-start | bytes 1622024 | tf_op jit(solution)/shard_map/ppermute | solution.py:350
  463.1 38.6 %collective-permute-start.35 = (bf16[512,1024]{1,0:T(8,128)(2,1)S(1)}, bf16[512,1024]{1,0:T(8,128)(2,1)S(1)}, u32[]{:S(2)}, u32[]{:S(2)}) collective-permute-start(bf16[512,1024]{1,0:T(8,128)(2,1)S(1)} %get-tuple-element.119), channel_id=1, source_target_pairs={{0,1},{1,2},{2,3},{3,0},{4,5},{5,6},{6,7},{7,4},{8,9},{9,10},{10,1... | collective-permute-start | bytes 3145736 | tf_op jit(solution)/shard_map/ppermute | solution.py:369
  464.7 36.0 %collective-permute-start.41 = (bf16[3,704,128]{2,1,0:T(8,128)(2,1)S(1)}, bf16[3,704,128]{2,1,0:T(8,128)(2,1)S(1)}, u32[]{:S(2)}, u32[]{:S(2)}) collective-permute-start(bf16[3,704,128]{2,1,0:T(8,128)(2,1)S(1)} %fusion.39), channel_id=1, source_target_pairs={{0,1},{1,2},{2,3},{3,0},{4,5},{5,6},{6,7},{7,4},{8,9},{9,10},{10,1... | collective-permute-start | bytes 1622024 | tf_op jit(solution)/shard_map/ppermute | solution.py:369
  466.6 34.1 %collective-permute-start.45 = (bf16[3,704,128]{2,1,0:T(8,128)(2,1)S(1)}, bf16[3,704,128]{2,1,0:T(8,128)(2,1)S(1)}, u32[]{:S(2)}, u32[]{:S(2)}) collective-permute-start(bf16[3,704,128]{2,1,0:T(8,128)(2,1)S(1)} %fusion.72), channel_id=1, source_target_pairs={{0,8},{4,12},{8,0},{12,4},{16,24},{20,28},{24,16},{28,20},{1,9},{5... | collective-permute-start | bytes 1622024 | tf_op jit(solution)/shard_map/ppermute | solution.py:350
  471.5 43.1 %collective-permute-start.50 = (bf16[3,704,128]{2,1,0:T(8,128)(2,1)}, bf16[3,704,128]{2,1,0:T(8,128)(2,1)}, u32[]{:S(2)}, u32[]{:S(2)}) collective-permute-start(bf16[3,704,128]{2,1,0:T(8,128)(2,1)} %fusion.73), channel_id=1, source_target_pairs={{0,16},{4,20},{8,24},{12,28},{16,0},{20,4},{24,8},{28,12},{1,17},{... | collective-permute-start | bytes 1622024 | tf_op jit(solution)/shard_map/ppermute | solution.py:350
  501.7 16.6 %collective-permute-start.46 = (bf16[3,704,128]{2,1,0:T(8,128)(2,1)}, bf16[3,704,128]{2,1,0:T(8,128)(2,1)}, u32[]{:S(2)}, u32[]{:S(2)}) collective-permute-start(bf16[3,704,128]{2,1,0:T(8,128)(2,1)} %fusion.37), channel_id=1, source_target_pairs={{0,1},{1,2},{2,3},{3,0},{4,5},{5,6},{6,7},{7,4},{8,9},{9,10},{10,1... | collective-permute-start | bytes 1622024 | tf_op jit(solution)/shard_map/ppermute | solution.py:369
  503.2 41.7 %collective-permute-start.36 = (bf16[512,1024]{1,0:T(8,128)(2,1)}, bf16[512,1024]{1,0:T(8,128)(2,1)}, u32[]{:S(2)}, u32[]{:S(2)}) collective-permute-start(bf16[512,1024]{1,0:T(8,128)(2,1)} %get-tuple-element.123), channel_id=1, source_target_pairs={{0,1},{1,2},{2,3},{3,0},{4,5},{5,6},{6,7},{7,4},{8,9},{9,10},{10,1... | collective-permute-start | bytes 3145736 | tf_op jit(solution)/shard_map/ppermute | solution.py:369
  520.5 36.0 %collective-permute-start.51 = (bf16[3,704,128]{2,1,0:T(8,128)(2,1)}, bf16[3,704,128]{2,1,0:T(8,128)(2,1)}, u32[]{:S(2)}, u32[]{:S(2)}) collective-permute-start(bf16[3,704,128]{2,1,0:T(8,128)(2,1)} %fusion.34), channel_id=1, source_target_pairs={{0,1},{1,2},{2,3},{3,0},{4,5},{5,6},{6,7},{7,4},{8,9},{9,10},{10,1... | collective-permute-start | bytes 1622024 | tf_op jit(solution)/shard_map/ppermute | solution.py:369
  (79 other events, 873.9 us)
Sparse Core Ops, SparseCore 0:
  10.5 30.8 all-gather.3
  44.9 80.7 all-gather.5
  323.3 47.5 reduce-scatter.11
  388.1 60.7 reduce-scatter.9
  506.1 24.5 reduce-scatter.7

commit v4 on v3

--- a/solution.py
+++ b/solution.py
@@ -356,6 +356,70 @@
     return near[0] + wide(swap(low(near[1]), first))
 
 
+def join_kernel(spots, *refs, count, sets, high):
+    pieces, whole, sem = refs[:count], refs[count], refs[count + 1]
+    copies = []
+    for k in range(count):
+        for s in range(sets):
+            lanes = pl.ds(pl.multiple_of(spots[k] * LANES, LANES), LANES)
+            rows = pl.ds(pl.multiple_of(spots[count + s] * high, high), high)
+            copies.append(pltpu.make_async_copy(pieces[k].at[s], whole.at[rows, lanes], sem))
+    for copy in copies:
+        copy.start()
+    for copy in copies:
+        copy.wait()
+
+
+def part_kernel(spots, whole, *refs, count, sets, high):
+    pieces, sem = refs[:count], refs[count]
+    copies = []
+    for k in range(count):
+        for s in range(sets):
+            lanes = pl.ds(pl.multiple_of(spots[k] * LANES, LANES), LANES)
+            rows = pl.ds(pl.multiple_of(spots[count + s] * high, high), high)
+            copies.append(pltpu.make_async_copy(whole.at[rows, lanes], pieces[k].at[s], sem))
+    for copy in copies:
+        copy.start()
+    for copy in copies:
+        copy.wait()
+
+
+def join(pieces, spots):
+    count = len(pieces)
+    sets, high, _ = pieces[0].shape
+    shape = (sets * high, count * LANES)
+    return pl.pallas_call(
+        functools.partial(join_kernel, count=count, sets=sets, high=high),
+        out_shape=jax.ShapeDtypeStruct(shape, pieces[0].dtype),
+        grid_spec=pltpu.PrefetchScalarGridSpec(
+            num_scalar_prefetch=1,
+            grid=(1,),
+            in_specs=[pl.BlockSpec(memory_space=pl.ANY)] * count,
+            out_specs=pl.BlockSpec(shape, lambda i, *_: (0, 0)),
+            scratch_shapes=[pltpu.SemaphoreType.DMA],
+        ),
+        name="join",
+    )(spots, *pieces)
+
+
+def part(whole, spots, sets):
+    high = whole.shape[0] // sets
+    count = whole.shape[1] // LANES
+    there = pl.BlockSpec(memory_space=pl.ANY)
+    return pl.pallas_call(
+        functools.partial(part_kernel, count=count, sets=sets, high=high),
+        out_shape=(jax.ShapeDtypeStruct((sets, high, LANES), whole.dtype),) * count,
+        grid_spec=pltpu.PrefetchScalarGridSpec(
+            num_scalar_prefetch=1,
+            grid=(1,),
+            in_specs=[pl.BlockSpec(whole.shape, lambda i, *_: (0, 0))],
+            out_specs=(there,) * count,
+            scratch_shapes=[pltpu.SemaphoreType.DMA],
+        ),
+        name="part",
+    )(spots, whole)
+
+
 def on_device(
     inputs, cotangent, segment_ids, row_length,
     w_qkv, m_qkv, v_qkv, w_out, m_out, v_out, w_gate_up, m_gate_up, v_gate_up, w_down, m_down, v_down,
@@ -363,32 +427,38 @@
     *, dp, mp,
 ):
     f32, bf16 = jnp.float32, jnp.bfloat16
+    low = lambda value: value.astype(bf16)
+    wide_of = lambda value: value.astype(f32)
     z = lax.axis_index("mp")
     me = lax.axis_index("dp")
-    onward = [(i, (i + 1) % mp) for i in range(mp)]
-    ring = lambda value: lax.ppermute(value, "mp", onward)
+    core = lax.rem(me, 2)
     rows, width = inputs.shape[1:]
     seq_len = segment_ids.shape[1]
     hidden_here = w_down.shape[0]
     lanes_here = w_down.shape[1]
     heads_width = w_out.shape[0]
     exchange = dp == PIECES and lanes_here == LANES
-
-    groups = 2 if heads_width % (4 * HEAD) == 0 else 1
-    share = heads_width // groups
-
-    seg_row = segment_ids[0]
-    live_row = jnp.arange(seq_len, dtype=jnp.int32) < row_length[0]
-    live = live_row.astype(f32)[:, None]
-
-    wide, narrow = min(1024, seq_len), min(512, seq_len)
-    lo, hi = key_blocks(seg_row, row_length[0], wide, narrow)
-    lo_back, hi_back = key_blocks(seg_row, row_length[0], narrow, narrow)
-
-    copy_qkv = w_qkv.astype(bf16).reshape(3, lanes_here, groups, share).transpose(2, 0, 3, 1).reshape(3 * heads_width, lanes_here)
-    copy_out = w_out.astype(bf16)
-    copy_feed = jnp.concatenate([w_gate_up.astype(bf16).transpose(0, 2, 1), w_down.astype(bf16)[None]])
-    copy_gains = jnp.pad(norm_gains.astype(bf16), ((0, 14), (0, 0)))
+    half = rows // 2
+    parts_of_heads = 2
+    share = heads_width // parts_of_heads
+
+    swap = lambda value, bit: lax.ppermute(value, "dp", swap_over("dp", dp, bit))
+    pair = lambda value: swap(value, 1)
+    line = lambda value, pairs: lax.ppermute(value, "mp", pairs)
+    onward = lambda value: line(value, [(i, (i + 1) % mp) for i in range(mp)])
+    backward = lambda value: line(value, [(i, (i - 1) % mp) for i in range(mp)])
+    across = lambda value: line(value, swap_over("mp", mp, 2))
+    tie = lax.optimization_barrier
+
+    home = z // 2
+    outer = (z == 0) | (z == mp - 1)
+    first = core == 0
+
+    copy_qkv = low(w_qkv).reshape(3, lanes_here, parts_of_heads, share).transpose(2, 0, 3, 1)
+    copy_qkv = copy_qkv.reshape(3 * heads_width, lanes_here)
+    copy_first = jnp.concatenate([copy_qkv, jnp.pad(low(norm_gains), ((0, 14), (0, 0)))])
+    copy_out = low(w_out)
+    copy_feed = jnp.concatenate([low(w_gate_up).transpose(0, 2, 1), low(w_down)[None]])
     chip_bits = [(2, 4) if s % 2 == 0 or not exchange else (4, 2) for s in range(mp)]
     spots = spots_of(me if exchange else 0, chip_bits)
 
@@ -403,81 +473,188 @@
         whole = found.reshape(3, hidden_here, PIECES, LANES)
         return [whole[:, :, block] for block in (0, 2, 4, 6, 1, 3, 5, 7)]
 
-    feed_own = [copy_feed, ring(copy_feed)]
-    blocks = [inputs[0]]
-    for _ in range(mp - 1):
-        blocks.append(ring(blocks[-1]))
-    full_first = lax.all_gather(jnp.concatenate([copy_qkv, copy_gains]), "dp", axis=1, tiled=True)
+    far_first = across(copy_first)
+
+    x_own = inputs[0]
+    keep = lax.dynamic_slice(x_own, (core * half, 0), (half, width))
+    got = pair(lax.dynamic_slice(x_own, ((1 - core) * half, 0), (half, width)))
+    ids = jnp.concatenate([segment_ids[0], jnp.broadcast_to(row_length, (LANES,))])
+    ids = jnp.where(home == core, ids, pair(ids))
+    row_a = jnp.where(first, keep, got)
+    row_b = jnp.where(first, got, keep)
+    down_one = line(row_a, [(3, 2), (2, 1), (1, 0)])
+    up_one = line(row_b, [(0, 1), (1, 2), (2, 3)])
+    down_two = line(down_one, [(2, 1), (1, 0)])
+    up_two = line(up_one, [(1, 2), (2, 3)])
+    side = line(after(jnp.where(z == 0, row_a, row_b), down_one, up_one), [(0, 1), (3, 2)])
+    far = line(jnp.where(z == 1, down_two, up_two), [(1, 0), (2, 3)])
+    held = [
+        (jnp.where(home == 0, row_a, row_b), z),
+        (jnp.where(z == 0, down_one, jnp.where(z == 3, up_one, side)), z ^ 1),
+        (jnp.where(outer, jnp.where(z == 0, down_two, up_two), jnp.where(z == 1, down_one, up_one)), 2 - home),
+        (jnp.where(outer, far, jnp.where(z == 1, down_two, up_two)), 3 * (1 - home)),
+    ]
+
+    if exchange:
+        two = [jnp.where(first, copy_first, far_first), pair(jnp.where(first, far_first, copy_first))]
+        two = jnp.stack(two)
+        four = swap(two, 2)
+        last_four = swap(jnp.stack([two, four]), 4)
+        spots_first = jnp.concatenate([me ^ jnp.arange(PIECES, dtype=jnp.int32), jnp.zeros((1,), jnp.int32)])
+        pieces = [two[:1], two[1:], four[:1], four[1:]]
+        pieces += [last_four[i, j : j + 1] for i in range(2) for j in range(2)]
+        full_first = join(pieces, spots_first)
+    else:
+        full_first = lax.all_gather(jnp.stack([copy_first, far_first]), "dp", axis=2, tiled=True)
+        full_first = jnp.where(first, full_first[0], full_first[1])
     full_qkv = full_first[: 3 * heads_width]
-    gain_one = full_first[3 * heads_width].astype(f32)
-    gain_two = full_first[3 * heads_width + 1].astype(f32)
-    full_out = lax.all_gather(copy_out, ("dp", "mp"), axis=0).reshape(dp, mp, groups, share, lanes_here)
-    full_out = [full_out[:, :, i].transpose(1, 2, 0, 3).reshape(mp * share, width) for i in range(groups)]
-    feed_full = [end_cross(start_cross(feed_own[s], s), s) for s in range(2)]
-
-    resid_in = inputs[0].astype(f32)
+    gain_one = wide_of(full_first[3 * heads_width])
+    gain_two = wide_of(full_first[3 * heads_width + 1])
+
+    crossing = [start_cross(copy_feed, 0)]
+    if exchange:
+        out_one = onward(copy_out)
+        out_all = jnp.stack([copy_out, out_one, onward(out_one), backward(copy_out)])
+    seg_row = ids[:seq_len]
+    length = ids[seq_len]
+    live_row = jnp.arange(seq_len, dtype=jnp.int32) < length
+    live = wide_of(live_row)[:, None]
+    wide, narrow = min(1024, seq_len), min(512, seq_len)
+    lo, hi = key_blocks(seg_row, length, wide, narrow)
+    lo_back, hi_back = key_blocks(seg_row, length, narrow, narrow)
+
+    hats = []
+    normed_one = jnp.zeros((seq_len, width), bf16)
+    for value, block in held:
+        for piece, side_of in ((value, core), (pair(value), 1 - core)):
+            piece = wide_of(piece)
+            hats.append(piece * rms_scale(piece))
+            at = block * rows + side_of * half
+            normed_one = lax.dynamic_update_slice(normed_one, low(hats[-1] * gain_one), (at, 0))
+    qkv = low(dot32(normed_one, full_qkv, NT))
+
+    feed_in = after(copy_feed, far)
+    plus = onward(feed_in)
+    minus = backward(feed_in)
+    if exchange:
+        out_in = after(out_all, last_four)
+        out_two = [out_in, swap(out_in, 2)]
+        out_four = out_two + [swap(value, 4) for value in out_two]
+
+    rank = 2 * lax.rem(z, 2) + core
+
+    def column_pairs(s):
+        found = []
+        for d in range(dp):
+            for c in range(mp):
+                to_dp = (d // 2) * 2 + c // 2
+                to_z = (2 * (c % 2) + d % 2) ^ s
+                found.append((d * mp + c, to_dp * mp + to_z))
+        return found
+
+    def group_at(s):
+        place = z ^ s
+        return (2 * core + place // 2) ^ (2 * lax.rem(place, 2))
+
+    def spread(value):
+        return [
+            lax.ppermute(lax.dynamic_slice(value, ((rank ^ s) * rows, 0), (rows, share)), ("dp", "mp"), column_pairs(s))
+            for s in range(mp)
+        ]
+
+    def collect(value, i):
+        found = jnp.zeros((seq_len, share), value.dtype)
+        for s in range(mp):
+            piece = lax.dynamic_slice(value, (0, group_at(s) * heads_width + i * share), (rows, share))
+            piece = lax.ppermute(piece, ("dp", "mp"), [(there, here) for here, there in column_pairs(s)])
+            found = lax.dynamic_update_slice(found, piece, ((rank ^ s) * rows, 0))
+        return found
+
+    raw_one, logs_one = attend(qkv, 0, share, seg_row, lo, hi, wide, narrow)
+    mine_one = low(raw_one * live)
+    if exchange:
+        qkv_next, plus, minus, mine_one, *out_four = tie((qkv, plus, minus, mine_one, *out_four))
+        out_eight = out_four + [pair(value) for value in out_four]
+    else:
+        qkv_next, plus, minus, mine_one = tie((qkv, plus, minus, mine_one))
+    spread_one = spread(mine_one)
+    twice = onward(plus)
+    crossing.append(start_cross(plus, 1))
+    slice_three = start_cross(minus, 3)
+    feed_full = [end_cross(crossing[0], 0)]
+
+    raw_two, logs_two = attend(qkv_next, 1, share, seg_row, lo, hi, wide, narrow)
+    mine_two = low(raw_two * live)
+    spread_two = spread(mine_two)
+    raw_out = [raw_one, raw_two]
+    log_sums = [jnp.where(live_row[None, :], logs, -NEG_FILL) for logs in (logs_one, logs_two)]
+    feed_full.append(end_cross(crossing[1], 1))
+    slice_two = start_cross(twice, 2)
+
+    if exchange:
+        place_out = jnp.array([0, 2, 4, 6, 1, 3, 5, 7], jnp.int32)
+        spots_out = jnp.concatenate([me ^ place_out, lax.rem(z + mp - jnp.arange(mp, dtype=jnp.int32), mp)])
+        full_out = join([out_eight[i] for i in range(PIECES)], spots_out)
+    else:
+        full_out = lax.all_gather(copy_out, ("dp", "mp"), axis=0)
+        full_out = full_out.reshape(dp, mp, heads_width, lanes_here).transpose(1, 2, 0, 3).reshape(mp * heads_width, width)
+
+    attended = jnp.zeros((rows, width), bf16)
+    for i, found in enumerate((spread_one, spread_two)):
+        for s in range(mp):
+            attended = lax.dynamic_update_slice(attended, found[s], (0, group_at(s) * heads_width + i * share))
+
+    resid_in = wide_of(x_own)
     scale_one = rms_scale(resid_in)
     hat_one = resid_in * scale_one
-    hats = []
-    normed_one = jnp.zeros((seq_len, width), bf16)
-    for s, block in enumerate(blocks):
-        block = block.astype(f32)
-        hats.append(block * rms_scale(block))
-        at = lax.rem(z + mp - s, mp) * rows
-        normed_one = lax.dynamic_update_slice(normed_one, (hats[-1] * gain_one).astype(bf16), (at, 0))
-    qkv = dot32(normed_one, full_qkv, NT).astype(bf16)
-
-    pending = ring(after(feed_own[1], blocks[-1]))
-    crossing = []
-    raw_out, log_sums, attended = [], [], []
-    for i in range(groups):
-        raw, logs = attend(qkv, i, share, seg_row, lo, hi, wide, narrow)
-        raw_out.append(raw)
-        log_sums.append(jnp.where(live_row[None, :], logs, -NEG_FILL))
-        mine = (raw * live).astype(bf16)
-        pending, mine = lax.optimization_barrier((pending, mine))
-        feed_own.append(pending)
-        crossing.append(start_cross(pending, len(feed_own) - 1))
-        if len(feed_own) < mp:
-            pending = ring(pending)
-        attended.append(lax.all_to_all(mine, "mp", split_axis=0, concat_axis=1, tiled=True))
-    while len(feed_own) < mp:
-        feed_own.append(pending)
-        crossing.append(start_cross(pending, len(feed_own) - 1))
-        pending = ring(pending)
-    feed_full += [end_cross(found, s + 2) for s, found in enumerate(crossing)]
-
-    after_attn = resid_in
-    for part, weight in zip(attended, full_out):
-        after_attn = after_attn + dot32(part, weight, NN)
+    after_attn = resid_in + dot32(attended, full_out, NN)
     scale_two = rms_scale(after_attn)
     hat_two = after_attn * scale_two
-    normed_two = (hat_two * gain_two).astype(bf16)
+    normed_two = low(hat_two * gain_two)
 
     fed, d_normed_two, d_feed = [], [], []
-    for start in range(0, mp, 2):
-        stop = min(start + 2, mp)
-        out_part, d_part, grads = feed(
-            normed_two, cotangent[0], feed_full[start:stop], spots[PIECES * start : PIECES * stop]
-        )
-        fed.append(out_part)
-        d_normed_two.append(d_part)
-        d_feed += grads
+    out_part, d_part, grads = feed(normed_two, cotangent[0], feed_full, spots[: 2 * PIECES])
+    fed.append(out_part)
+    d_normed_two.append(d_part)
+    d_feed += grads
+    feed_full = [end_cross(slice_two, 2), end_cross(slice_three, 3)]
+    out_part, d_part, grads = feed(normed_two, cotangent[0], feed_full, spots[2 * PIECES :])
+    fed.append(out_part)
+    d_normed_two.append(d_part)
+    d_feed += grads
     d_normed_two = functools.reduce(jnp.add, d_normed_two)
-    d_after = cotangent[0].astype(f32) + norm_back(d_normed_two, hat_two, scale_two, gain_two)
-
-    d_branch = d_after.astype(bf16)
-    d_attended = [
-        lax.all_to_all(dot32(d_branch, weight, NT).astype(bf16), "mp", split_axis=1, concat_axis=0, tiled=True)
-        for weight in full_out
-    ]
-    grad_out = [dot32(part, d_branch, TN).astype(bf16).reshape(mp, share, width) for part in attended]
-    grad_out = jnp.stack(grad_out, axis=1).reshape(mp * heads_width, width)
-    grad_out = lax.psum_scatter(grad_out, "dp", scatter_dimension=1, tiled=True)
-    grad_out = lax.psum_scatter(grad_out, "mp", scatter_dimension=0, tiled=True).astype(f32)
+    d_after = wide_of(cotangent[0]) + norm_back(d_normed_two, hat_two, scale_two, gain_two)
+
+    d_branch = low(d_after)
+    d_attended = low(dot32(d_branch, full_out, NT))
+    d_attended = [collect(d_attended, i) for i in range(parts_of_heads)]
+    grad_out = low(dot32(attended, d_branch, TN))
+    if exchange:
+        away = part(grad_out, spots_out, mp)
+        near = [low(wide_of(away[k]) + wide_of(pair(away[k + 4]))) for k in range(4)]
+        near = [low(wide_of(near[k]) + wide_of(swap(near[k + 2], 4))) for k in range(2)]
+        owned_out = wide_of(near[0]) + wide_of(swap(near[1], 2))
+        grad_out = wide_of(onward(low(wide_of(onward(low(owned_out[2]))) + owned_out[3])))
+        grad_out = grad_out + wide_of(backward(low(owned_out[1]))) + owned_out[0]
+    else:
+        grad_out = lax.psum_scatter(grad_out, "dp", scatter_dimension=1, tiled=True)
+        grad_out = wide_of(lax.psum_scatter(grad_out, "mp", scatter_dimension=0, tiled=True))
+
+    if exchange:
+        owned = [scatter_slice(pieces, dp, *bits) for pieces, bits in zip(d_feed, chip_bits)]
+    else:
+        back = jnp.array([0, 4, 1, 5, 2, 6, 3, 7])
+        owned = []
+        for pieces in d_feed:
+            whole = jnp.concatenate(pieces)[back].transpose(1, 2, 0, 3).reshape(3, hidden_here, width)
+            owned.append(wide_of(lax.psum_scatter(whole, "dp", scatter_dimension=2, tiled=True)))
+    total = owned[0] + wide_of(backward(low(owned[1])))
+    total = total + wide_of(onward(low(owned[3] + wide_of(onward(low(owned[2]))))))
+    grad_gate_up = total[:2].transpose(0, 2, 1)
+    grad_down = total[2]
 
     d_qkv = []
-    for i in range(groups):
+    for i in range(parts_of_heads):
         d_here = jnp.where(live_row[:, None], d_attended[i], jnp.zeros((), bf16))
         row_dot = jnp.sum((raw_out[i] * d_here).reshape(seq_len, share // HEAD, HEAD), axis=-1).T
         d_qkv.append(attend_back(qkv, i, d_here, log_sums[i], row_dot, seg_row, lo_back, hi_back, narrow, narrow))
@@ -485,33 +662,48 @@
     block_output = after_attn + functools.reduce(jnp.add, fed)
     grad_gain_two = jnp.sum(d_normed_two * hat_two, axis=0)
 
-    total = None
     grad_gain_one = jnp.zeros((width,), f32)
-    for s in [*range(1, mp), 0]:
-        at = lax.rem(z + mp - s, mp) * rows
-        part = dot32(lax.dynamic_slice(d_qkv, (at, 0), (rows, d_qkv.shape[1])), full_qkv, NN)
-        grad_gain_one = grad_gain_one + jnp.sum(part * hats[s], axis=0)
-        total = part if total is None else ring(total.astype(bf16)).astype(f32) + part
-    d_normed_one = total
+    sums = [None] * mp
+    for k in range(mp - 1, -1, -1):
+        block = held[k][1]
+        halves = []
+        for j, side_of in enumerate((core, 1 - core)):
+            at = block * rows + side_of * half
+            found = dot32(lax.dynamic_slice(d_qkv, (at, 0), (half, d_qkv.shape[1])), full_qkv, NN)
+            grad_gain_one = grad_gain_one + jnp.sum(found * hats[2 * k + j], axis=0)
+            halves.append(found)
+        sums[k] = halves[0] + wide_of(pair(low(halves[1])))
+    inward = wide_of(line(low(sums[3]), [(0, 1), (3, 2)]))
+    passed = low(jnp.where(outer, sums[2], sums[3] + inward))
+    up_two = line(passed, [(0, 1), (1, 2)])
+    down_two = line(passed, [(3, 2), (2, 1)])
+    third = sums[2] + wide_of(jnp.where(z == 1, up_two, down_two))
+    up_three = line(jnp.where(z == 2, up_two, low(jnp.where(z == 0, sums[1], third))), [(0, 1), (1, 2), (2, 3)])
+    down_three = line(jnp.where(z == 1, down_two, low(jnp.where(z == 3, sums[1], third))), [(3, 2), (2, 1), (1, 0)])
+    side = line(low(sums[1]), [(1, 0), (2, 3)])
+    mine = sums[0] + wide_of(jnp.where(outer, side, jnp.where(z == 1, up_three, down_three)))
+    theirs = wide_of(jnp.where(home == 0, down_three, up_three))
+    stay = jnp.where(home == core, mine, theirs)
+    moved = wide_of(pair(low(jnp.where(home == core, theirs, mine))))
+    d_normed_one = jnp.concatenate([jnp.where(first, stay, moved), jnp.where(first, moved, stay)])
     input_grad = d_after + norm_back(d_normed_one, hat_one, scale_one, gain_one)
 
-    grad_qkv = dot32(d_qkv, normed_one, TN).astype(bf16)
-    grad_qkv = lax.psum_scatter(grad_qkv, "dp", scatter_dimension=1, tiled=True).astype(f32)
-    grad_qkv = grad_qkv.reshape(groups, 3, share, lanes_here).transpose(1, 3, 0, 2).reshape(w_qkv.shape)
-
+    grad_qkv = low(dot32(d_qkv, normed_one, TN))
     if exchange:
-        owned = [scatter_slice(parts, dp, *bits) for parts, bits in zip(d_feed, chip_bits)]
+        away = part(grad_qkv, spots_first, 1)
+        near = [low(wide_of(away[k]) + wide_of(swap(away[k + 4], 4))) for k in range(4)]
+        near = [wide_of(near[k]) + wide_of(swap(near[k + 2], 2)) for k in range(2)]
+        moved = wide_of(pair(low(near[1][0])))
+        stay = near[0][0]
+        here = jnp.where(first, stay, moved)
+        there = jnp.where(first, moved, stay)
     else:
-        back = jnp.array([0, 4, 1, 5, 2, 6, 3, 7])
-        owned = []
-        for parts in d_feed:
-            whole = jnp.concatenate(parts)[back].transpose(1, 2, 0, 3).reshape(3, hidden_here, width)
-            owned.append(lax.psum_scatter(whole, "dp", scatter_dimension=2, tiled=True).astype(f32))
-    total = owned[1]
-    for s in [*range(2, mp), 0]:
-        total = ring(total.astype(bf16)).astype(f32) + owned[s]
-    grad_gate_up = total[:2].transpose(0, 2, 1)
-    grad_down = total[2]
+        nothing = jnp.zeros_like(grad_qkv)
+        both = jnp.stack([jnp.where(first, grad_qkv, nothing), jnp.where(first, nothing, grad_qkv)])
+        both = wide_of(lax.psum_scatter(both, "dp", scatter_dimension=2, tiled=True))
+        here, there = both[0], both[1]
+    grad_qkv = here + wide_of(across(low(there)))
+    grad_qkv = grad_qkv.reshape(parts_of_heads, 3, share, lanes_here).transpose(1, 3, 0, 2).reshape(w_qkv.shape)
 
     grad_gains = jnp.stack([grad_gain_one, grad_gain_two])
     for axis, count in (("mp", mp), ("dp", dp)):

time: 590 us -> 671 us (1.14)
  starting transfers between devices: 82.6 us -> 166 us
  Pallas kernels: 120 us -> 144 us
  waiting for transfers between devices: 237 us -> 214 us
  other arithmetic: 56.3 us -> 70.5 us
  between operations: 15.8 us -> 3.63 us
    ppermute x12 -> x77, starting transfers between devices: 12.6 us -> 136 us  [the longest x26 61.8 us: on_device(): line = lambda value, pairs: lax.ppermute(value, 'mp', pairs)]
    all_to_all x4 -> x0, starting transfers between devices: 18.9 us -> none  [the longest x2 10.1 us: on_device(): lax.all_to_all(mine, 'mp', split_axis=0, concat_axis=1, tiled=True)]
    ppermute x5, waiting for transfers between devices: 4.32 us -> 22.5 us  [on_device(): lax.ppermute(grad_gains, axis, swap_over(axis, count, bit))]
    ppermute x16, starting transfers between devices: 26.6 us -> 9.89 us  [scatter_slice(): lax.ppermute(value, 'dp', swap_over('dp', count, bit))]
    ppermute x12 -> x77, waiting for transfers between devices: 146 us -> 162 us  [the longest x26 96.1 us: on_device(): line = lambda value, pairs: lax.ppermute(value, 'mp', pairs)]
    ppermute x16, waiting for transfers between devices: 21 us -> 4.83 us  [scatter_slice(): lax.ppermute(value, 'dp', swap_over('dp', count, bit))]
    pallas_call x0 -> x4, Pallas kernels: none -> 13.7 us  [the longest x2 6.86 us: part(): pl.pallas_call(functools.partial(part_kernel, count=count, sets=sets, hig...]
    dynamic_update_slice x0 -> x16, local copies, waits for them, and re-layouts: none -> 12.8 us  [the longest x8 12.7 us: on_device(): lax.dynamic_update_slice(attended, found[s], (0, group_at(s) * heads_widt...]
  transfers between devices with their start and end apart: 70 -> 126, of which waited for: 22 -> 36; matrix products, arithmetic and copies ran while one was open for 20% -> 19% of each run, Pallas kernels for 21% -> 22%
where the time goes in v4:
time: 671 us; the launch traced here: 665 us
  waiting for transfers between devices  214 us (32%)
  starting transfers between devices  166 us (25%)
  Pallas kernels  144 us (21%)
  other arithmetic  70.5 us (11%)
  local copies, waits for them, and re-layouts  34.1 us (5%)
  matrix products  33 us (5%)
    ppermute x26, waiting for transfers between devices, on_device(): line = lambda value, pairs: lax.ppermute(value, 'mp', pairs)  96.1 us
    ppermute x26, starting transfers between devices, on_device(): line = lambda value, pairs: lax.ppermute(value, 'mp', pairs)  61.8 us
    ppermute x35, waiting for transfers between devices, on_device(): lax.ppermute(value, 'dp', swap_over('dp', dp, bit))  56.6 us
    pallas_call x2, Pallas kernels, feed(): pl.pallas_call(functools.partial(feed_kernel, slices=slices), out_shape=(...  48.4 us
    pallas_call x2, Pallas kernels, attend_back(): pl.pallas_call(functools.partial(attend_back_kernel, bk=bk, heads=heads),...  45.8 us
    pallas_call x2, Pallas kernels, attend(): pl.pallas_call(functools.partial(attend_kernel, bk=bk, heads=heads), out_...  35.8 us
    dot_general x13, matrix products, dot32(): lax.dot_general(left, right, dims, preferred_element_type=jnp.float32)  33 us
    ppermute x35, starting transfers between devices, on_device(): lax.ppermute(value, 'dp', swap_over('dp', dp, bit))  31.3 us
  transfers between devices with their start and end apart: 126, of which 36 were waited for; matrix products, arithmetic and copies ran while one was open for 19% of the time, Pallas kernels for 22%

profile of v4, /device:TPU:0, one launch (start us, length us, event | category | flops | bytes accessed | tf_op | source)
XLA Modules:
  0.0 665.3 jit_solution(6186247204076291492)
XLA Ops:
  1.7 3.1 collective-permute-start.18
  22.6 3.8 collective-permute-done.19
  33.3 8.9 %collective-permute-done.7 = bf16[256,1024]{1,0:T(8,128)(2,1)S(1)} collective-permute-done((bf16[256,1024]{1,0:T(8,128)(2,1)S(1)}, bf16[256,1024]{1,0:T(8,128)(2,1)S(1)}, u32[]{:S(2)}, u32[]{:S(2)}) %collective-permute-start.7) | collective-permute-done | bytes 524320 | tf_op jit(solution)/shard_map/ppermute | solution.py:447
  42.2 4.1 collective-permute-done.6
  46.4 3.0 collective-permute-start.8
  56.2 3.9 collective-permute-done.8
  60.0 4.9 collective-permute-done.10
  67.8 26.8 %collective-permute-done.4 = bf16[2,2,784,128]{3,2,1,0:T(8,128)(2,1)S(1)} collective-permute-done((bf16[2,2,784,128]{3,2,1,0:T(8,128)(2,1)S(1)}, bf16[2,2,784,128]{3,2,1,0:T(8,128)(2,1)S(1)}, u32[]{:S(2)}, u32[]{:S(2)}) %collective-permute-start.4) | collective-permute-done | bytes 802848 | tf_op jit(solution)/shard_map/ppermute | solution.py:445
  96.8 3.3 join.2
  104.2 4.6 collective-permute-done.13
  116.4 4.8 convolution_convert_fusion.q_ref.k_ref.v_ref
  121.2 17.9 %attend.2 = (f32[2048,128]{1,0:T(8,128)}, f32[2,2048]{1,0:T(2,128)}) custom-call(s32[2]{0:T(128)} %get-tuple-element.162.lo_ref, s32[2]{0:T(128)} %get-tuple-element.161.hi_ref, bf16[2048,768]{1,0:T(8,128)(2,1)} %convolution_convert_fusion.q_ref.k_ref.v_ref, bf16[2048,768]{1,0:T(8,128)(2,1)} %convolution_convert_fusion.q_ref.k_ref.v_ref, ...), custom_call_target="tpu_custom_call" | custom-call | flops 8589934592 | bytes 2621440 | tf_op jit(solution)/shard_map/attend/pallas_call | solution.py:94
  142.9 5.5 collective-permute-done.22.refs_2_
  148.4 4.8 collective-permute-done.23.refs_3_
  154.5 7.1 %collective-permute-start.27 = (bf16[512,128]{1,0:T(8,128)(2,1)}, bf16[512,128]{1,0:T(8,128)(2,1)}, u32[]{:S(2)}, u32[]{:S(2)}) collective-permute-start(bf16[512,128]{1,0:T(8,128)(2,1)} %get-tuple-element.213), channel_id=1, source_target_pairs={{0,3},{1,1},{2,7},{3,5},{4,2},{5,0},{6,6},{7,4},{8,11},{9,9},{10,1... | collective-permute-start | bytes 393224 | tf_op jit(solution)/shard_map/ppermute | solution.py:561
  161.6 17.9 %attend.3 = (f32[2048,128]{1,0:T(8,128)}, f32[2,2048]{1,0:T(2,128)}) custom-call(s32[2]{0:T(128)} %get-tuple-element.162.lo_ref, s32[2]{0:T(128)} %get-tuple-element.161.hi_ref, bf16[2048,768]{1,0:T(8,128)(2,1)} %convolution_convert_fusion.q_ref.k_ref.v_ref, bf16[2048,768]{1,0:T(8,128)(2,1)} %convolution_convert_fusion.q_ref.k_ref.v_ref, ...), custom_call_target="tpu_custom_call" | custom-call | flops 8589934592 | bytes 2621440 | tf_op jit(solution)/shard_map/attend/pallas_call | solution.py:94
  186.3 5.3 collective-permute-start.31
  192.3 3.4 collective-permute-done.31
  195.8 3.9 collective-permute-start.29
  202.8 2.9 collective-permute-start.33
  209.3 2.6 collective-permute-start.50
  229.0 6.8 %collective-permute-done.43.refs_11_ = bf16[3,704,128]{2,1,0:T(8,128)(2,1)} collective-permute-done((bf16[3,704,128]{2,1,0:T(8,128)(2,1)}, bf16[3,704,128]{2,1,0:T(8,128)(2,1)}, u32[]{:S(2)}, u32[]{:S(2)}) %collective-permute-start.43) | collective-permute-done | bytes 540704 | tf_op jit(solution)/shard_map/ppermute | solution.py:338
  245.3 3.5 join.3
  249.7 3.8 collective-permute-done.51.refs_3_
  255.2 8.7 %collective-permute-done.45.refs_13_ = bf16[3,704,128]{2,1,0:T(8,128)(2,1)} collective-permute-done((bf16[3,704,128]{2,1,0:T(8,128)(2,1)}, bf16[3,704,128]{2,1,0:T(8,128)(2,1)}, u32[]{:S(2)}, u32[]{:S(2)}) %collective-permute-start.45) | collective-permute-done | bytes 540704 | tf_op jit(solution)/shard_map/ppermute | solution.py:343
  263.9 3.3 multiply_reduce_fusion.2
  271.3 3.0 collective-permute-done.53.refs_5_
  274.8 24.1 %feed.2 = (f32[512,1024]{1,0:T(8,128)}, f32[512,1024]{1,0:T(8,128)}, bf16[2,3,704,128]{3,2,1,0:T(8,128)(2,1)}, bf16[2,3,704,128]{3,2,1,0:T(8,128)(2,1)}, bf16[2,...) custom-call(s32[16]{0:T(128)} %get-tuple-element.230.spots, ...), custom_call_target="tpu_custom_call" | custom-call | flops 19931332608 | bytes 23592960 | tf_op jit(solution)/shard_map/feed/pallas_call | solution.py:297
  299.7 24.4 %feed.3 = (f32[512,1024]{1,0:T(8,128)}, f32[512,1024]{1,0:T(8,128)}, bf16[2,3,704,128]{3,2,1,0:T(8,128)(2,1)}, bf16[2,3,704,128]{3,2,1,0:T(8,128)(2,1)}, bf16[2,...) custom-call(s32[16]{0:T(128)} %get-tuple-element.229.spots, ...), custom_call_target="tpu_custom_call" | custom-call | flops 19931332608 | bytes 23592960 | tf_op jit(solution)/shard_map/feed/pallas_call | solution.py:297
  324.1 3.7 multiply_reduce_fusion
  328.8 4.7 multiply_add_fusion
  335.9 3.9 convolution_convert_fusion.1.whole
  339.7 7.1 %collective-permute-start.72 = (bf16[512,128]{1,0:T(8,128)(2,1)S(1)}, bf16[512,128]{1,0:T(8,128)(2,1)S(1)}, u32[]{:S(2)}, u32[]{:S(2)}) collective-permute-start(bf16[512,128]{1,0:T(8,128)(2,1)S(1)} %get-tuple-element.195), channel_id=1, source_target_pairs={{3,0},{1,1},{7,2},{5,3},{2,4},{0,5},{6,6},{4,7},{11,8},{9,9},{15,1... | collective-permute-start | bytes 393224 | tf_op jit(solution)/shard_map/ppermute | solution.py:569
  346.9 3.5 part.3
  350.6 4.2 collective-permute-start.68
  354.9 2.8 collective-permute-done.71
  359.3 6.5 collective-permute-start.67
  366.1 3.4 collective-permute-done.67
  376.8 22.8 %attend_back.3 = bf16[2048,384]{1,0:T(8,128)(2,1)} custom-call(s32[4]{0:T(128)} %get-tuple-element.160.lo_ref, s32[4]{0:T(128)} %get-tuple-element.159.hi_ref, bf16[2048,768]{1,0:T(8,128)(2,1)} %convolution_convert_fusion.q_ref.k_ref.v_ref, bf16[2048,128]{1,0:T(8,128)(2,1)} %get-tuple-element.156.do_ref, f32[2,2048]{1,0:T(2,128)} %get-tuple-element.225.lse_ref, ...), custom_call_target="tpu_custom_call" | custom-call | flops 21474836480 | bytes 4194304 | tf_op jit(solution)/shard_map/attend_back/pallas_call | solution.py:170
  399.7 22.9 %attend_back.2 = bf16[2048,384]{1,0:T(8,128)(2,1)} custom-call(s32[4]{0:T(128)} %get-tuple-element.160.lo_ref, s32[4]{0:T(128)} %get-tuple-element.159.hi_ref, bf16[2048,768]{1,0:T(8,128)(2,1)} %convolution_convert_fusion.q_ref.k_ref.v_ref, bf16[2048,128]{1,0:T(8,128)(2,1)} %get-tuple-element.228.do_ref, f32[2,2048]{1,0:T(2,128)} %get-tuple-element.226.lse_ref, ...), custom_call_target="tpu_custom_call" | custom-call | flops 21474836480 | bytes 4194304 | tf_op jit(solution)/shard_map/attend_back/pallas_call | solution.py:170
  422.6 7.5 %fusion.9.whole = bf16[768,1024]{1,0:T(8,128)(2,1)} fusion(bf16[2048,1024]{1,0:T(8,128)(2,1)} %copy-done.27, bf16[2048,384]{1,0:T(8,128)(2,1)S(1)} %copy-done.1, bf16[2048,384]{1,0:T(8,128)(2,1)} %attend_back.2), kind=kOutput, calls=%fused_computation.46 | convolution fusion | flops 3228303360 | bytes 8912896 | tf_op jit(solution)/shard_map/dot_general | solution.py:50
  440.0 3.3 part.2
  447.7 7.0 %collective-permute-done.88 = bf16[1,768,128]{2,1,0:T(8,128)(2,1)S(1)} collective-permute-done((bf16[1,768,128]{2,1,0:T(8,128)(2,1)}, bf16[1,768,128]{2,1,0:T(8,128)(2,1)S(1)}, u32[]{:S(2)}, u32[]{:S(2)}) %collective-permute-start.88) | collective-permute-done | bytes 196640 | tf_op jit(solution)/shard_map/ppermute | solution.py:445
  457.8 4.9 collective-permute-done.87
  462.7 11.1 %collective-permute-start.89 = (bf16[1,768,128]{2,1,0:T(8,128)(2,1)S(1)}, bf16[1,768,128]{2,1,0:T(8,128)(2,1)S(1)}, u32[]{:S(2)}, u32[]{:S(2)}) collective-permute-start(bf16[1,768,128]{2,1,0:T(8,128)(2,1)S(1)} %add_convert_fusion.11), channel_id=1, source_target_pairs={{0,8},{4,12},{8,0},{12,4},{16,24},{20,28},{24,16},{28,20},{1,9},{5... | collective-permute-start | bytes 589832 | tf_op jit(solution)/shard_map/ppermute | solution.py:445
  473.8 3.6 collective-permute-done.89
  484.0 2.8 add_convert_fusion.2
  491.5 2.6 collective-permute-done.86
  494.1 3.3 collective-permute-start.78
  502.2 2.7 collective-permute-start.99
  504.9 4.7 collective-permute-done.78
  509.6 3.0 collective-permute-start.101
  515.0 3.7 collective-permute-done.99
  519.3 3.0 collective-permute-done.121
  524.0 4.1 collective-permute-done.122
  542.5 15.5 %collective-permute-done.125 = f32[2,1024]{1,0:T(2,128)S(1)} collective-permute-done((f32[2,1024]{1,0:T(2,128)S(1)}, f32[2,1024]{1,0:T(2,128)S(1)}, u32[]{:S(2)}, u32[]{:S(2)}) %collective-permute-start.125) | collective-permute-done | bytes 8224 | tf_op jit(solution)/shard_map/ppermute | solution.py:712
  563.8 14.6 %collective-permute-start.79 = (bf16[256,1024]{1,0:T(8,128)(2,1)S(1)}, bf16[256,1024]{1,0:T(8,128)(2,1)S(1)}, u32[]{:S(2)}, u32[]{:S(2)}) collective-permute-start(bf16[256,1024]{1,0:T(8,128)(2,1)S(1)} %copy-done.59), channel_id=1, source_target_pairs={{0,1},{1,2},{4,5},{5,6},{8,9},{9,10},{12,13},{13,14},{16,17},{17,1... | collective-permute-start | bytes 1572872 | tf_op jit(solution)/shard_map/ppermute | solution.py:447
  578.5 10.3 %collective-permute-done.79 = bf16[256,1024]{1,0:T(8,128)(2,1)S(1)} collective-permute-done((bf16[256,1024]{1,0:T(8,128)(2,1)S(1)}, bf16[256,1024]{1,0:T(8,128)(2,1)S(1)}, u32[]{:S(2)}, u32[]{:S(2)}) %collective-permute-start.79) | collective-permute-done | bytes 524320 | tf_op jit(solution)/shard_map/ppermute | solution.py:447
  592.1 4.6 collective-permute-start.81
  599.7 6.9 %collective-permute-done.75 = bf16[256,1024]{1,0:T(8,128)(2,1)S(1)} collective-permute-done((bf16[256,1024]{1,0:T(8,128)(2,1)S(1)}, bf16[256,1024]{1,0:T(8,128)(2,1)S(1)}, u32[]{:S(2)}, u32[]{:S(2)}) %collective-permute-start.75) | collective-permute-done | bytes 524320 | tf_op jit(solution)/shard_map/ppermute | solution.py:447
  609.1 8.3 %collective-permute-done.82 = bf16[256,1024]{1,0:T(8,128)(2,1)S(1)} collective-permute-done((bf16[256,1024]{1,0:T(8,128)(2,1)S(1)}, bf16[256,1024]{1,0:T(8,128)(2,1)S(1)}, u32[]{:S(2)}, u32[]{:S(2)}) %collective-permute-start.82) | collective-permute-done | bytes 524320 | tf_op jit(solution)/shard_map/ppermute | solution.py:447
  620.5 3.7 collective-permute-done.118
  628.5 17.0 %collective-permute-done.119 = bf16[3,704,128]{2,1,0:T(8,128)(2,1)S(1)} collective-permute-done((bf16[3,704,128]{2,1,0:T(8,128)(2,1)S(1)}, bf16[3,704,128]{2,1,0:T(8,128)(2,1)S(1)}, u32[]{:S(2)}, u32[]{:S(2)}) %collective-permute-start.119) | collective-permute-done | bytes 540704 | tf_op jit(solution)/shard_map/ppermute | solution.py:447
  649.0 12.1 %collective-permute-done.120 = bf16[3,704,128]{2,1,0:T(8,128)(2,1)S(1)} collective-permute-done((bf16[3,704,128]{2,1,0:T(8,128)(2,1)S(1)}, bf16[3,704,128]{2,1,0:T(8,128)(2,1)S(1)}, u32[]{:S(2)}, u32[]{:S(2)}) %collective-permute-start.120) | collective-permute-done | bytes 540704 | tf_op jit(solution)/shard_map/ppermute | solution.py:447
  (569 shorter events, 195.9 us)
Async XLA Ops:
  1.7 18.7 %collective-permute-start.18 = (bf16[256,128]{1,0:T(8,128)(2,1)S(1)}, bf16[256,128]{1,0:T(8,128)(2,1)S(1)}, u32[]{:S(2)}, u32[]{:S(2)}) collective-permute-start(bf16[256,128]{1,0:T(8,128)(2,1)S(1)} %convert_element_type.487), channel_id=1, source_target_pairs={{0,1},{1,2},{2,3},{3,0},{4,5},{5,6},{6,7},{7,4},{8,9},{9,10},{10,1... | collective-permute-start | bytes 196616 | tf_op jit(solution)/shard_map/ppermute | solution.py:447
  4.8 17.8 %collective-permute-start.20 = (bf16[256,128]{1,0:T(8,128)(2,1)S(1)}, bf16[256,128]{1,0:T(8,128)(2,1)S(1)}, u32[]{:S(2)}, u32[]{:S(2)}) collective-permute-start(bf16[256,128]{1,0:T(8,128)(2,1)S(1)} %convert_element_type.487), channel_id=1, source_target_pairs={{0,3},{1,0},{2,1},{3,2},{4,7},{5,4},{6,5},{7,6},{8,11},{9,8},{10,9... | collective-permute-start | bytes 196616 | tf_op jit(solution)/shard_map/ppermute | solution.py:447
  15.4 36.9 %collective-permute-start.36 = (bf16[3,704,128]{2,1,0:T(8,128)(2,1)}, bf16[3,704,128]{2,1,0:T(8,128)(2,1)}, u32[]{:S(2)}, u32[]{:S(2)}) collective-permute-start(bf16[3,704,128]{2,1,0:T(8,128)(2,1)} %pad_maximum_fusion.5.refs_2_), channel_id=1, source_target_pairs={{0,8},{4,12},{8,0},{12,4},{16,24},{20,28},{24,16},{28,20},{1,9},{5... | collective-permute-start | bytes 1622024 | tf_op jit(solution)/shard_map/ppermute | solution.py:338
  32.4 17.7 %collective-permute-start.3 = (bf16[2,784,128]{2,1,0:T(8,128)(2,1)S(1)}, bf16[2,784,128]{2,1,0:T(8,128)(2,1)S(1)}, u32[]{:S(2)}, u32[]{:S(2)}) collective-permute-start(bf16[2,784,128]{2,1,0:T(8,128)(2,1)S(1)} %get-tuple-element.218), channel_id=1, source_target_pairs={{0,8},{4,12},{8,0},{12,4},{16,24},{20,28},{24,16},{28,20},{1,9},{5... | collective-permute-start | bytes 1204232 | tf_op jit(solution)/shard_map/ppermute | solution.py:445
  33.3 20.6 %collective-permute-start.5 = (bf16[256,1024]{1,0:T(8,128)(2,1)S(1)}, bf16[256,1024]{1,0:T(8,128)(2,1)S(1)}, u32[]{:S(2)}, u32[]{:S(2)}) collective-permute-start(bf16[256,1024]{1,0:T(8,128)(2,1)S(1)} %get-tuple-element.173), channel_id=1, source_target_pairs={{0,4},{4,0},{8,12},{12,8},{16,20},{20,16},{24,28},{28,24},{1,5},{5... | collective-permute-start | bytes 1572872 | tf_op jit(solution)/shard_map/ppermute | solution.py:445
  52.3 86.8 %collective-permute-start.37 = (bf16[3,704,128]{2,1,0:T(8,128)(2,1)}, bf16[3,704,128]{2,1,0:T(8,128)(2,1)}, u32[]{:S(2)}, u32[]{:S(2)}) collective-permute-start(bf16[3,704,128]{2,1,0:T(8,128)(2,1)} %pad_maximum_fusion.5.refs_2_), channel_id=1, source_target_pairs={{0,16},{4,20},{8,24},{12,28},{16,0},{20,4},{24,8},{28,12},{1,17},{... | collective-permute-start | bytes 1622024 | tf_op jit(solution)/shard_map/ppermute | solution.py:338
  53.9 88.9 %collective-permute-start.38 = (bf16[3,704,128]{2,1,0:T(8,128)(2,1)}, bf16[3,704,128]{2,1,0:T(8,128)(2,1)}, u32[]{:S(2)}, u32[]{:S(2)}) collective-permute-start(bf16[3,704,128]{2,1,0:T(8,128)(2,1)} %collective-permute-done.36.refs_3_), channel_id=1, source_target_pairs={{0,16},{4,20},{8,24},{12,28},{16,0},{20,4},{24,8},{28,12},{1,17},{... | collective-permute-start | bytes 1622024 | tf_op jit(solution)/shard_map/ppermute | solution.py:343
  54.6 40.0 %collective-permute-start.4 = (bf16[2,2,784,128]{3,2,1,0:T(8,128)(2,1)S(1)}, bf16[2,2,784,128]{3,2,1,0:T(8,128)(2,1)S(1)}, u32[]{:S(2)}, u32[]{:S(2)}) collective-permute-start(bf16[2,2,784,128]{3,2,1,0:T(8,128)(2,1)S(1)} %pad_maximum_fusion.4), channel_id=1, source_target_pairs={{0,16},{4,20},{8,24},{12,28},{16,0},{20,4},{24,8},{28,12},{1,17},{... | collective-permute-start | bytes 2408456 | tf_op jit(solution)/shard_map/ppermute | solution.py:445
  66.4 35.7 %collective-permute-start.12 = (bf16[256,1024]{1,0:T(8,128)(2,1)}, bf16[256,1024]{1,0:T(8,128)(2,1)S(1)}, u32[]{:S(2)}, u32[]{:S(2)}) collective-permute-start(bf16[256,1024]{1,0:T(8,128)(2,1)} %get-tuple-element.166), channel_id=1, source_target_pairs={{0,4},{4,0},{8,12},{12,8},{16,20},{20,16},{24,28},{28,24},{1,5},{5... | collective-permute-start | bytes 1572872 | tf_op jit(solution)/shard_map/ppermute | solution.py:445
  66.4 36.6 %collective-permute-start.9 = (bf16[256,1024]{1,0:T(8,128)(2,1)S(1)}, bf16[256,1024]{1,0:T(8,128)(2,1)}, u32[]{:S(2)}, u32[]{:S(2)}) collective-permute-start(bf16[256,1024]{1,0:T(8,128)(2,1)S(1)} %get-tuple-element.204), channel_id=1, source_target_pairs={{0,4},{4,0},{8,12},{12,8},{16,20},{20,16},{24,28},{28,24},{1,5},{5... | collective-permute-start | bytes 1572872 | tf_op jit(solution)/shard_map/ppermute | solution.py:445
  102.4 38.3 %collective-permute-start.21 = (bf16[4,256,128]{2,1,0:T(8,128)(2,1)S(1)}, bf16[4,256,128]{2,1,0:T(8,128)(2,1)}, u32[]{:S(2)}, u32[]{:S(2)}) collective-permute-start(bf16[4,256,128]{2,1,0:T(8,128)(2,1)S(1)} %copy-done.51), channel_id=1, source_target_pairs={{0,8},{4,12},{8,0},{12,4},{16,24},{20,28},{24,16},{28,20},{1,9},{5... | collective-permute-start | bytes 786440 | tf_op jit(solution)/shard_map/ppermute | solution.py:445
  110.2 42.9 %collective-permute-start.16 = (bf16[3,704,128]{2,1,0:T(8,128)(2,1)}, bf16[3,704,128]{2,1,0:T(8,128)(2,1)}, u32[]{:S(2)}, u32[]{:S(2)}) collective-permute-start(bf16[3,704,128]{2,1,0:T(8,128)(2,1)} %pad_maximum_fusion.5.refs_2_), channel_id=1, source_target_pairs={{0,3},{1,0},{2,1},{3,2},{4,7},{5,4},{6,5},{7,6},{8,11},{9,8},{10,9... | collective-permute-start | bytes 1622024 | tf_op jit(solution)/shard_map/ppermute | solution.py:447
  115.3 38.4 %collective-permute-start.15 = (bf16[3,704,128]{2,1,0:T(8,128)(2,1)}, bf16[3,704,128]{2,1,0:T(8,128)(2,1)}, u32[]{:S(2)}, u32[]{:S(2)}) collective-permute-start(bf16[3,704,128]{2,1,0:T(8,128)(2,1)} %pad_maximum_fusion.5.refs_2_), channel_id=1, source_target_pairs={{0,1},{1,2},{2,3},{3,0},{4,5},{5,6},{6,7},{7,4},{8,9},{9,10},{10,1... | collective-permute-start | bytes 1622024 | tf_op jit(solution)/shard_map/ppermute | solution.py:447
  142.8 39.1 %collective-permute-start.39 = (bf16[3,704,128]{2,1,0:T(8,128)(2,1)}, bf16[3,704,128]{2,1,0:T(8,128)(2,1)}, u32[]{:S(2)}, u32[]{:S(2)}) collective-permute-start(bf16[3,704,128]{2,1,0:T(8,128)(2,1)} %pad_maximum_fusion.5.refs_2_), channel_id=1, source_target_pairs={{0,4},{4,0},{8,12},{12,8},{16,20},{20,16},{24,28},{28,24},{1,5},{5... | collective-permute-start | bytes 1622024 | tf_op jit(solution)/shard_map/ppermute | solution.py:338
  148.4 35.7 %collective-permute-start.40 = (bf16[3,704,128]{2,1,0:T(8,128)(2,1)}, bf16[3,704,128]{2,1,0:T(8,128)(2,1)}, u32[]{:S(2)}, u32[]{:S(2)}) collective-permute-start(bf16[3,704,128]{2,1,0:T(8,128)(2,1)} %collective-permute-done.36.refs_3_), channel_id=1, source_target_pairs={{0,4},{4,0},{8,12},{12,8},{16,20},{20,16},{24,28},{28,24},{1,5},{5... | collective-permute-start | bytes 1622024 | tf_op jit(solution)/shard_map/ppermute | solution.py:343
  153.2 30.9 %collective-permute-start.41 = (bf16[3,704,128]{2,1,0:T(8,128)(2,1)}, bf16[3,704,128]{2,1,0:T(8,128)(2,1)}, u32[]{:S(2)}, u32[]{:S(2)}) collective-permute-start(bf16[3,704,128]{2,1,0:T(8,128)(2,1)} %collective-permute-done.37.refs_4_), channel_id=1, source_target_pairs={{0,4},{4,0},{8,12},{12,8},{16,20},{20,16},{24,28},{28,24},{1,5},{5... | collective-permute-start | bytes 1622024 | tf_op jit(solution)/shard_map/ppermute | solution.py:343
  153.2 33.1 %collective-permute-start.42 = (bf16[3,704,128]{2,1,0:T(8,128)(2,1)}, bf16[3,704,128]{2,1,0:T(8,128)(2,1)}, u32[]{:S(2)}, u32[]{:S(2)}) collective-permute-start(bf16[3,704,128]{2,1,0:T(8,128)(2,1)} %collective-permute-done.38.refs_5_), channel_id=1, source_target_pairs={{0,4},{4,0},{8,12},{12,8},{16,20},{20,16},{24,28},{28,24},{1,5},{5... | collective-permute-start | bytes 1622024 | tf_op jit(solution)/shard_map/ppermute | solution.py:343
  154.5 37.0 %collective-permute-start.27 = (bf16[512,128]{1,0:T(8,128)(2,1)}, bf16[512,128]{1,0:T(8,128)(2,1)}, u32[]{:S(2)}, u32[]{:S(2)}) collective-permute-start(bf16[512,128]{1,0:T(8,128)(2,1)} %get-tuple-element.213), channel_id=1, source_target_pairs={{0,3},{1,1},{2,7},{3,5},{4,2},{5,0},{6,6},{7,4},{8,11},{9,9},{10,1... | collective-permute-start | bytes 393224 | tf_op jit(solution)/shard_map/ppermute | solution.py:561
  191.8 20.2 %collective-permute-start.61 = (bf16[3,704,128]{2,1,0:T(8,128)(2,1)}, bf16[3,704,128]{2,1,0:T(8,128)(2,1)}, u32[]{:S(2)}, u32[]{:S(2)}) collective-permute-start(bf16[3,704,128]{2,1,0:T(8,128)(2,1)} %collective-permute-done.16.refs_10_), channel_id=1, source_target_pairs={{0,4},{4,0},{8,12},{12,8},{16,20},{20,16},{24,28},{28,24},{1,5},{5... | collective-permute-start | bytes 1622024 | tf_op jit(solution)/shard_map/ppermute | solution.py:338
  192.3 21.8 %collective-permute-start.59 = (bf16[3,704,128]{2,1,0:T(8,128)(2,1)}, bf16[3,704,128]{2,1,0:T(8,128)(2,1)}, u32[]{:S(2)}, u32[]{:S(2)}) collective-permute-start(bf16[3,704,128]{2,1,0:T(8,128)(2,1)} %collective-permute-done.16.refs_10_), channel_id=1, source_target_pairs={{0,8},{4,12},{8,0},{12,4},{16,24},{20,28},{24,16},{28,20},{1,9},{5... | collective-permute-start | bytes 1622024 | tf_op jit(solution)/shard_map/ppermute | solution.py:338
  214.1 21.7 %collective-permute-start.43 = (bf16[3,704,128]{2,1,0:T(8,128)(2,1)}, bf16[3,704,128]{2,1,0:T(8,128)(2,1)}, u32[]{:S(2)}, u32[]{:S(2)}) collective-permute-start(bf16[3,704,128]{2,1,0:T(8,128)(2,1)} %collective-permute-done.15.refs_10_), channel_id=1, source_target_pairs={{0,16},{4,20},{8,24},{12,28},{16,0},{20,4},{24,8},{28,12},{1,17},{... | collective-permute-start | bytes 1622024 | tf_op jit(solution)/shard_map/ppermute | solution.py:338
  224.7 24.5 %collective-permute-start.62 = (bf16[3,704,128]{2,1,0:T(8,128)(2,1)}, bf16[3,704,128]{2,1,0:T(8,128)(2,1)}, u32[]{:S(2)}, u32[]{:S(2)}) collective-permute-start(bf16[3,704,128]{2,1,0:T(8,128)(2,1)} %collective-permute-done.58.refs_11_), channel_id=1, source_target_pairs={{0,4},{4,0},{8,12},{12,8},{16,20},{20,16},{24,28},{28,24},{1,5},{5... | collective-permute-start | bytes 1622024 | tf_op jit(solution)/shard_map/ppermute | solution.py:343
  226.5 22.7 %collective-permute-start.60 = (bf16[3,704,128]{2,1,0:T(8,128)(2,1)}, bf16[3,704,128]{2,1,0:T(8,128)(2,1)}, u32[]{:S(2)}, u32[]{:S(2)}) collective-permute-start(bf16[3,704,128]{2,1,0:T(8,128)(2,1)} %collective-permute-done.58.refs_11_), channel_id=1, source_target_pairs={{0,8},{4,12},{8,0},{12,4},{16,24},{20,28},{24,16},{28,20},{1,9},{5... | collective-permute-start | bytes 1622024 | tf_op jit(solution)/shard_map/ppermute | solution.py:343
  228.5 20.3 %collective-permute-start.63 = (bf16[3,704,128]{2,1,0:T(8,128)(2,1)}, bf16[3,704,128]{2,1,0:T(8,128)(2,1)}, u32[]{:S(2)}, u32[]{:S(2)}) collective-permute-start(bf16[3,704,128]{2,1,0:T(8,128)(2,1)} %collective-permute-done.59.refs_12_), channel_id=1, source_target_pairs={{0,4},{4,0},{8,12},{12,8},{16,20},{20,16},{24,28},{28,24},{1,5},{5... | collective-permute-start | bytes 1622024 | tf_op jit(solution)/shard_map/ppermute | solution.py:343
  228.5 25.0 %collective-permute-start.51 = (bf16[3,704,128]{2,1,0:T(8,128)(2,1)}, bf16[3,704,128]{2,1,0:T(8,128)(2,1)}, u32[]{:S(2)}, u32[]{:S(2)}) collective-permute-start(bf16[3,704,128]{2,1,0:T(8,128)(2,1)} %collective-permute-done.50.refs_2_), channel_id=1, source_target_pairs={{0,8},{4,12},{8,0},{12,4},{16,24},{20,28},{24,16},{28,20},{1,9},{5... | collective-permute-start | bytes 1622024 | tf_op jit(solution)/shard_map/ppermute | solution.py:338
  235.8 28.2 %collective-permute-start.45 = (bf16[3,704,128]{2,1,0:T(8,128)(2,1)}, bf16[3,704,128]{2,1,0:T(8,128)(2,1)}, u32[]{:S(2)}, u32[]{:S(2)}) collective-permute-start(bf16[3,704,128]{2,1,0:T(8,128)(2,1)} %collective-permute-done.43.refs_11_), channel_id=1, source_target_pairs={{0,8},{4,12},{8,0},{12,4},{16,24},{20,28},{24,16},{28,20},{1,9},{5... | collective-permute-start | bytes 1622024 | tf_op jit(solution)/shard_map/ppermute | solution.py:343
  248.8 21.0 %collective-permute-start.52 = (bf16[3,704,128]{2,1,0:T(8,128)(2,1)}, bf16[3,704,128]{2,1,0:T(8,128)(2,1)S(1)}, u32[]{:S(2)}, u32[]{:S(2)}) collective-permute-start(bf16[3,704,128]{2,1,0:T(8,128)(2,1)} %collective-permute-done.50.refs_2_), channel_id=1, source_target_pairs={{0,16},{4,20},{8,24},{12,28},{16,0},{20,4},{24,8},{28,12},{1,17},{... | collective-permute-start | bytes 1622024 | tf_op jit(solution)/shard_map/ppermute | solution.py:338
  249.2 21.2 %collective-permute-start.47 = (bf16[3,704,128]{2,1,0:T(8,128)(2,1)}, bf16[3,704,128]{2,1,0:T(8,128)(2,1)S(1)}, u32[]{:S(2)}, u32[]{:S(2)}) collective-permute-start(bf16[3,704,128]{2,1,0:T(8,128)(2,1)} %collective-permute-done.43.refs_11_), channel_id=1, source_target_pairs={{0,4},{4,0},{8,12},{12,8},{16,20},{20,16},{24,28},{28,24},{1,5},{5... | collective-permute-start | bytes 1622024 | tf_op jit(solution)/shard_map/ppermute | solution.py:343
  249.2 21.1 %collective-permute-start.48 = (bf16[3,704,128]{2,1,0:T(8,128)(2,1)}, bf16[3,704,128]{2,1,0:T(8,128)(2,1)S(1)}, u32[]{:S(2)}, u32[]{:S(2)}) collective-permute-start(bf16[3,704,128]{2,1,0:T(8,128)(2,1)} %collective-permute-done.44.refs_12_), channel_id=1, source_target_pairs={{0,4},{4,0},{8,12},{12,8},{16,20},{20,16},{24,28},{28,24},{1,5},{5... | collective-permute-start | bytes 1622024 | tf_op jit(solution)/shard_map/ppermute | solution.py:343
  253.6 20.7 %collective-permute-start.53 = (bf16[3,704,128]{2,1,0:T(8,128)(2,1)}, bf16[3,704,128]{2,1,0:T(8,128)(2,1)}, u32[]{:S(2)}, u32[]{:S(2)}) collective-permute-start(bf16[3,704,128]{2,1,0:T(8,128)(2,1)} %collective-permute-done.51.refs_3_), channel_id=1, source_target_pairs={{0,16},{4,20},{8,24},{12,28},{16,0},{20,4},{24,8},{28,12},{1,17},{... | collective-permute-start | bytes 1622024 | tf_op jit(solution)/shard_map/ppermute | solution.py:343
  269.8 29.1 %collective-permute-start.54 = (bf16[3,704,128]{2,1,0:T(8,128)(2,1)}, bf16[3,704,128]{2,1,0:T(8,128)(2,1)S(1)}, u32[]{:S(2)}, u32[]{:S(2)}) collective-permute-start(bf16[3,704,128]{2,1,0:T(8,128)(2,1)} %collective-permute-done.50.refs_2_), channel_id=1, source_target_pairs={{0,4},{4,0},{8,12},{12,8},{16,20},{20,16},{24,28},{28,24},{1,5},{5... | collective-permute-start | bytes 1622024 | tf_op jit(solution)/shard_map/ppermute | solution.py:338
  270.3 29.2 %collective-permute-start.55 = (bf16[3,704,128]{2,1,0:T(8,128)(2,1)}, bf16[3,704,128]{2,1,0:T(8,128)(2,1)}, u32[]{:S(2)}, u32[]{:S(2)}) collective-permute-start(bf16[3,704,128]{2,1,0:T(8,128)(2,1)} %collective-permute-done.51.refs_3_), channel_id=1, source_target_pairs={{0,4},{4,0},{8,12},{12,8},{16,20},{20,16},{24,28},{28,24},{1,5},{5... | collective-permute-start | bytes 1622024 | tf_op jit(solution)/shard_map/ppermute | solution.py:343
  270.4 28.6 %collective-permute-start.64 = (bf16[3,704,128]{2,1,0:T(8,128)(2,1)}, bf16[3,704,128]{2,1,0:T(8,128)(2,1)}, u32[]{:S(2)}, u32[]{:S(2)}) collective-permute-start(bf16[3,704,128]{2,1,0:T(8,128)(2,1)} %collective-permute-done.60.refs_13_), channel_id=1, source_target_pairs={{0,4},{4,0},{8,12},{12,8},{16,20},{20,16},{24,28},{28,24},{1,5},{5... | collective-permute-start | bytes 1622024 | tf_op jit(solution)/shard_map/ppermute | solution.py:343
  274.3 25.2 %collective-permute-start.56 = (bf16[3,704,128]{2,1,0:T(8,128)(2,1)S(1)}, bf16[3,704,128]{2,1,0:T(8,128)(2,1)}, u32[]{:S(2)}, u32[]{:S(2)}) collective-permute-start(bf16[3,704,128]{2,1,0:T(8,128)(2,1)S(1)} %collective-permute-done.52.refs_4_), channel_id=1, source_target_pairs={{0,4},{4,0},{8,12},{12,8},{16,20},{20,16},{24,28},{28,24},{1,5},{5... | collective-permute-start | bytes 1622024 | tf_op jit(solution)/shard_map/ppermute | solution.py:343
  274.3 25.2 %collective-permute-start.57 = (bf16[3,704,128]{2,1,0:T(8,128)(2,1)}, bf16[3,704,128]{2,1,0:T(8,128)(2,1)}, u32[]{:S(2)}, u32[]{:S(2)}) collective-permute-start(bf16[3,704,128]{2,1,0:T(8,128)(2,1)} %collective-permute-done.53.refs_5_), channel_id=1, source_target_pairs={{0,4},{4,0},{8,12},{12,8},{16,20},{20,16},{24,28},{28,24},{1,5},{5... | collective-permute-start | bytes 1622024 | tf_op jit(solution)/shard_map/ppermute | solution.py:343
  298.9 181.8 %collective-permute-start.103 = (bf16[2,3,704,128]{3,2,1,0:T(8,128)(2,1)}, bf16[2,3,704,128]{3,2,1,0:T(8,128)(2,1)}, u32[]{:S(2)}, u32[]{:S(2)}) collective-permute-start(bf16[2,3,704,128]{3,2,1,0:T(8,128)(2,1)} %get-tuple-element.111), channel_id=1, source_target_pairs={{0,4},{4,0},{8,12},{12,8},{16,20},{20,16},{24,28},{28,24},{1,5},{5... | collective-permute-start | bytes 3244040 | tf_op jit(solution)/shard_map/ppermute | solution.py:350
  299.0 184.6 %collective-permute-start.107 = (bf16[2,3,704,128]{3,2,1,0:T(8,128)(2,1)}, bf16[2,3,704,128]{3,2,1,0:T(8,128)(2,1)}, u32[]{:S(2)}, u32[]{:S(2)}) collective-permute-start(bf16[2,3,704,128]{3,2,1,0:T(8,128)(2,1)} %get-tuple-element.115), channel_id=1, source_target_pairs={{0,4},{4,0},{8,12},{12,8},{16,20},{20,16},{24,28},{28,24},{1,5},{5... | collective-permute-start | bytes 3244040 | tf_op jit(solution)/shard_map/ppermute | solution.py:350
  339.7 18.6 %collective-permute-start.72 = (bf16[512,128]{1,0:T(8,128)(2,1)S(1)}, bf16[512,128]{1,0:T(8,128)(2,1)S(1)}, u32[]{:S(2)}, u32[]{:S(2)}) collective-permute-start(bf16[512,128]{1,0:T(8,128)(2,1)S(1)} %get-tuple-element.195), channel_id=1, source_target_pairs={{3,0},{1,1},{7,2},{5,3},{2,4},{0,5},{6,6},{4,7},{11,8},{9,9},{15,1... | collective-permute-start | bytes 393224 | tf_op jit(solution)/shard_map/ppermute | solution.py:569
  350.6 18.9 %collective-permute-start.68 = (bf16[512,128]{1,0:T(8,128)(2,1)S(1)}, bf16[512,128]{1,0:T(8,128)(2,1)S(1)}, u32[]{:S(2)}, u32[]{:S(2)}) collective-permute-start(bf16[512,128]{1,0:T(8,128)(2,1)S(1)} %get-tuple-element.199), channel_id=1, source_target_pairs={{3,0},{1,1},{7,2},{5,3},{2,4},{0,5},{6,6},{4,7},{11,8},{9,9},{15,1... | collective-permute-start | bytes 393224 | tf_op jit(solution)/shard_map/ppermute | solution.py:569
  366.0 77.4 %collective-permute-start.93 = (bf16[4,256,128]{2,1,0:T(8,128)(2,1)}, bf16[4,256,128]{2,1,0:T(8,128)(2,1)}, u32[]{:S(2)}, u32[]{:S(2)}) collective-permute-start(bf16[4,256,128]{2,1,0:T(8,128)(2,1)} %get-tuple-element.103), channel_id=1, source_target_pairs={{0,4},{4,0},{8,12},{12,8},{16,20},{20,16},{24,28},{28,24},{1,5},{5... | collective-permute-start | bytes 786440 | tf_op jit(solution)/shard_map/ppermute | solution.py:445
  369.5 108.0 %collective-permute-start.95 = (bf16[4,256,128]{2,1,0:T(8,128)(2,1)}, bf16[4,256,128]{2,1,0:T(8,128)(2,1)}, u32[]{:S(2)}, u32[]{:S(2)}) collective-permute-start(bf16[4,256,128]{2,1,0:T(8,128)(2,1)} %get-tuple-element.105), channel_id=1, source_target_pairs={{0,4},{4,0},{8,12},{12,8},{16,20},{20,16},{24,28},{28,24},{1,5},{5... | collective-permute-start | bytes 786440 | tf_op jit(solution)/shard_map/ppermute | solution.py:445
  369.6 75.6 %collective-permute-start.96 = (bf16[4,256,128]{2,1,0:T(8,128)(2,1)}, bf16[4,256,128]{2,1,0:T(8,128)(2,1)}, u32[]{:S(2)}, u32[]{:S(2)}) collective-permute-start(bf16[4,256,128]{2,1,0:T(8,128)(2,1)} %get-tuple-element.107), channel_id=1, source_target_pairs={{0,4},{4,0},{8,12},{12,8},{16,20},{20,16},{24,28},{28,24},{1,5},{5... | collective-permute-start | bytes 786440 | tf_op jit(solution)/shard_map/ppermute | solution.py:445
  456.2 23.1 %collective-permute-start.97 = (bf16[4,256,128]{2,1,0:T(8,128)(2,1)S(1)}, bf16[4,256,128]{2,1,0:T(8,128)(2,1)S(1)}, u32[]{:S(2)}, u32[]{:S(2)}) collective-permute-start(bf16[4,256,128]{2,1,0:T(8,128)(2,1)S(1)} %add_convert_fusion.5), channel_id=1, source_target_pairs={{0,16},{4,20},{8,24},{12,28},{16,0},{20,4},{24,8},{28,12},{1,17},{... | collective-permute-start | bytes 786440 | tf_op jit(solution)/shard_map/ppermute | solution.py:445
  477.4 20.0 %collective-permute-start.92 = (bf16[4,256,128]{2,1,0:T(8,128)(2,1)S(1)}, bf16[4,256,128]{2,1,0:T(8,128)(2,1)S(1)}, u32[]{:S(2)}, u32[]{:S(2)}) collective-permute-start(bf16[4,256,128]{2,1,0:T(8,128)(2,1)S(1)} %copy-done.100), channel_id=1, source_target_pairs={{0,4},{4,0},{8,12},{12,8},{16,20},{20,16},{24,28},{28,24},{1,5},{5... | collective-permute-start | bytes 786440 | tf_op jit(solution)/shard_map/ppermute | solution.py:445
  497.5 39.1 %collective-permute-start.112 = (bf16[2,3,704,128]{3,2,1,0:T(8,128)(2,1)}, bf16[2,3,704,128]{3,2,1,0:T(8,128)(2,1)}, u32[]{:S(2)}, u32[]{:S(2)}) collective-permute-start(bf16[2,3,704,128]{3,2,1,0:T(8,128)(2,1)} %get-tuple-element.119), channel_id=1, source_target_pairs={{0,4},{4,0},{8,12},{12,8},{16,20},{20,16},{24,28},{28,24},{1,5},{5... | collective-permute-start | bytes 3244040 | tf_op jit(solution)/shard_map/ppermute | solution.py:350
  497.8 42.4 %collective-permute-start.116 = (bf16[2,3,704,128]{3,2,1,0:T(8,128)(2,1)}, bf16[2,3,704,128]{3,2,1,0:T(8,128)(2,1)}, u32[]{:S(2)}, u32[]{:S(2)}) collective-permute-start(bf16[2,3,704,128]{3,2,1,0:T(8,128)(2,1)} %get-tuple-element.123), channel_id=1, source_target_pairs={{0,4},{4,0},{8,12},{12,8},{16,20},{20,16},{24,28},{28,24},{1,5},{5... | collective-permute-start | bytes 3244040 | tf_op jit(solution)/shard_map/ppermute | solution.py:350
  499.4 23.8 %collective-permute-start.91 = (bf16[768,128]{1,0:T(8,128)(2,1)S(1)}, bf16[768,128]{1,0:T(8,128)(2,1)S(1)}, u32[]{:S(2)}, u32[]{:S(2)}) collective-permute-start(bf16[768,128]{1,0:T(8,128)(2,1)S(1)} %fusion.106), channel_id=1, source_target_pairs={{0,2},{1,3},{2,0},{3,1},{4,6},{5,7},{6,4},{7,5},{8,10},{9,11},{10,... | collective-permute-start | bytes 589832 | tf_op jit(solution)/shard_map/ppermute | solution.py:447
  509.6 22.1 %collective-permute-start.101 = (bf16[256,128]{1,0:T(8,128)(2,1)}, bf16[256,128]{1,0:T(8,128)(2,1)}, u32[]{:S(2)}, u32[]{:S(2)}) collective-permute-start(bf16[256,128]{1,0:T(8,128)(2,1)} %get-tuple-element.224), channel_id=1, source_target_pairs={{0,3},{1,0},{2,1},{3,2},{4,7},{5,4},{6,5},{7,6},{8,11},{9,8},{10,9... | collective-permute-start | bytes 196616 | tf_op jit(solution)/shard_map/ppermute | solution.py:447
  531.2 27.4 %collective-permute-start.102 = (bf16[2,3,704,128]{3,2,1,0:T(8,128)(2,1)}, bf16[2,3,704,128]{3,2,1,0:T(8,128)(2,1)S(1)}, u32[]{:S(2)}, u32[]{:S(2)}) collective-permute-start(bf16[2,3,704,128]{3,2,1,0:T(8,128)(2,1)} %get-tuple-element.109), channel_id=1, source_target_pairs={{0,4},{4,0},{8,12},{12,8},{16,20},{20,16},{24,28},{28,24},{1,5},{5... | collective-permute-start | bytes 3244040 | tf_op jit(solution)/shard_map/ppermute | solution.py:350
  531.7 27.4 %collective-permute-start.104 = (bf16[2,3,704,128]{3,2,1,0:T(8,128)(2,1)}, bf16[2,3,704,128]{3,2,1,0:T(8,128)(2,1)S(1)}, u32[]{:S(2)}, u32[]{:S(2)}) collective-permute-start(bf16[2,3,704,128]{3,2,1,0:T(8,128)(2,1)} %add_convert_fusion.3), channel_id=1, source_target_pairs={{0,16},{4,20},{8,24},{12,28},{16,0},{20,4},{24,8},{28,12},{1,17},{... | collective-permute-start | bytes 3244040 | tf_op jit(solution)/shard_map/ppermute | solution.py:350
  536.5 23.7 %collective-permute-start.106 = (bf16[2,3,704,128]{3,2,1,0:T(8,128)(2,1)S(1)}, bf16[2,3,704,128]{3,2,1,0:T(8,128)(2,1)S(1)}, u32[]{:S(2)}, u32[]{:S(2)}) collective-permute-start(bf16[2,3,704,128]{3,2,1,0:T(8,128)(2,1)S(1)} %copy-done.95), channel_id=1, source_target_pairs={{0,4},{4,0},{8,12},{12,8},{16,20},{20,16},{24,28},{28,24},{1,5},{5... | collective-permute-start | bytes 3244040 | tf_op jit(solution)/shard_map/ppermute | solution.py:350
  536.6 26.2 %collective-permute-start.108 = (bf16[2,3,704,128]{3,2,1,0:T(8,128)(2,1)S(1)}, bf16[2,3,704,128]{3,2,1,0:T(8,128)(2,1)S(1)}, u32[]{:S(2)}, u32[]{:S(2)}) collective-permute-start(bf16[2,3,704,128]{3,2,1,0:T(8,128)(2,1)S(1)} %copy-done.45), channel_id=1, source_target_pairs={{0,8},{4,12},{8,0},{12,4},{16,24},{20,28},{24,16},{28,20},{1,9},{5... | collective-permute-start | bytes 3244040 | tf_op jit(solution)/shard_map/ppermute | solution.py:350
  540.2 17.8 %collective-permute-start.125 = (f32[2,1024]{1,0:T(2,128)S(1)}, f32[2,1024]{1,0:T(2,128)S(1)}, u32[]{:S(2)}, u32[]{:S(2)}) collective-permute-start(f32[2,1024]{1,0:T(2,128)S(1)} %add.726), channel_id=1, source_target_pairs={{0,16},{4,20},{8,24},{12,28},{16,0},{20,4},{24,8},{28,12},{1,17},{... | collective-permute-start | bytes 24584 | tf_op jit(solution)/shard_map/ppermute | solution.py:712
  558.0 31.5 %collective-permute-start.111 = (bf16[2,3,704,128]{3,2,1,0:T(8,128)(2,1)S(1)}, bf16[2,3,704,128]{3,2,1,0:T(8,128)(2,1)S(1)}, u32[]{:S(2)}, u32[]{:S(2)}) collective-permute-start(bf16[2,3,704,128]{3,2,1,0:T(8,128)(2,1)S(1)} %copy-done.94), channel_id=1, source_target_pairs={{0,4},{4,0},{8,12},{12,8},{16,20},{20,16},{24,28},{28,24},{1,5},{5... | collective-permute-start | bytes 3244040 | tf_op jit(solution)/shard_map/ppermute | solution.py:350
  558.6 33.5 %collective-permute-start.115 = (bf16[2,3,704,128]{3,2,1,0:T(8,128)(2,1)S(1)}, bf16[2,3,704,128]{3,2,1,0:T(8,128)(2,1)S(1)}, u32[]{:S(2)}, u32[]{:S(2)}) collective-permute-start(bf16[2,3,704,128]{3,2,1,0:T(8,128)(2,1)S(1)} %copy-done.93), channel_id=1, source_target_pairs={{0,4},{4,0},{8,12},{12,8},{16,20},{20,16},{24,28},{28,24},{1,5},{5... | collective-permute-start | bytes 3244040 | tf_op jit(solution)/shard_map/ppermute | solution.py:350
  560.2 31.0 %collective-permute-start.113 = (bf16[2,3,704,128]{3,2,1,0:T(8,128)(2,1)S(1)}, bf16[2,3,704,128]{3,2,1,0:T(8,128)(2,1)S(1)}, u32[]{:S(2)}, u32[]{:S(2)}) collective-permute-start(bf16[2,3,704,128]{3,2,1,0:T(8,128)(2,1)S(1)} %add_convert_fusion.1), channel_id=1, source_target_pairs={{0,8},{4,12},{8,0},{12,4},{16,24},{20,28},{24,16},{28,20},{1,9},{5... | collective-permute-start | bytes 3244040 | tf_op jit(solution)/shard_map/ppermute | solution.py:350
  562.9 33.8 %collective-permute-start.117 = (bf16[2,3,704,128]{3,2,1,0:T(8,128)(2,1)S(1)}, bf16[2,3,704,128]{3,2,1,0:T(8,128)(2,1)S(1)}, u32[]{:S(2)}, u32[]{:S(2)}) collective-permute-start(bf16[2,3,704,128]{3,2,1,0:T(8,128)(2,1)S(1)} %add_convert_fusion), channel_id=1, source_target_pairs={{0,16},{4,20},{8,24},{12,28},{16,0},{20,4},{24,8},{28,12},{1,17},{... | collective-permute-start | bytes 3244040 | tf_op jit(solution)/shard_map/ppermute | solution.py:350
  563.8 25.1 %collective-permute-start.79 = (bf16[256,1024]{1,0:T(8,128)(2,1)S(1)}, bf16[256,1024]{1,0:T(8,128)(2,1)S(1)}, u32[]{:S(2)}, u32[]{:S(2)}) collective-permute-start(bf16[256,1024]{1,0:T(8,128)(2,1)S(1)} %copy-done.59), channel_id=1, source_target_pairs={{0,1},{1,2},{4,5},{5,6},{8,9},{9,10},{12,13},{13,14},{16,17},{17,1... | collective-permute-start | bytes 1572872 | tf_op jit(solution)/shard_map/ppermute | solution.py:447
  591.2 26.9 %collective-permute-start.109 = (bf16[3,704,128]{2,1,0:T(8,128)(2,1)S(1)}, bf16[3,704,128]{2,1,0:T(8,128)(2,1)S(1)}, u32[]{:S(2)}, u32[]{:S(2)}) collective-permute-start(bf16[3,704,128]{2,1,0:T(8,128)(2,1)S(1)} %fusion.64), channel_id=1, source_target_pairs={{0,16},{4,20},{8,24},{12,28},{16,0},{20,4},{24,8},{28,12},{1,17},{... | collective-permute-start | bytes 1622024 | tf_op jit(solution)/shard_map/ppermute | solution.py:350
  596.7 20.7 %collective-permute-start.82 = (bf16[256,1024]{1,0:T(8,128)(2,1)S(1)}, bf16[256,1024]{1,0:T(8,128)(2,1)S(1)}, u32[]{:S(2)}, u32[]{:S(2)}) collective-permute-start(bf16[256,1024]{1,0:T(8,128)(2,1)S(1)} %get-tuple-element.175), channel_id=1, source_target_pairs={{3,2},{2,1},{1,0},{7,6},{6,5},{5,4},{11,10},{10,9},{9,8},{15,14},{... | collective-permute-start | bytes 1572872 | tf_op jit(solution)/shard_map/ppermute | solution.py:447
  598.6 50.4 %collective-permute-start.105 = (bf16[3,704,128]{2,1,0:T(8,128)(2,1)S(1)}, bf16[3,704,128]{2,1,0:T(8,128)(2,1)S(1)}, u32[]{:S(2)}, u32[]{:S(2)}) collective-permute-start(bf16[3,704,128]{2,1,0:T(8,128)(2,1)S(1)} %fusion.63), channel_id=1, source_target_pairs={{0,8},{4,12},{8,0},{12,4},{16,24},{20,28},{24,16},{28,20},{1,9},{5... | collective-permute-start | bytes 1622024 | tf_op jit(solution)/shard_map/ppermute | solution.py:350
  606.6 21.9 %collective-permute-start.114 = (bf16[3,704,128]{2,1,0:T(8,128)(2,1)S(1)}, bf16[3,704,128]{2,1,0:T(8,128)(2,1)S(1)}, u32[]{:S(2)}, u32[]{:S(2)}) collective-permute-start(bf16[3,704,128]{2,1,0:T(8,128)(2,1)S(1)} %fusion.65), channel_id=1, source_target_pairs={{0,16},{4,20},{8,24},{12,28},{16,0},{20,4},{24,8},{28,12},{1,17},{... | collective-permute-start | bytes 1622024 | tf_op jit(solution)/shard_map/ppermute | solution.py:350
  618.2 30.7 %collective-permute-start.110 = (bf16[3,704,128]{2,1,0:T(8,128)(2,1)S(1)}, bf16[3,704,128]{2,1,0:T(8,128)(2,1)S(1)}, u32[]{:S(2)}, u32[]{:S(2)}) collective-permute-start(bf16[3,704,128]{2,1,0:T(8,128)(2,1)S(1)} %fusion.32), channel_id=1, source_target_pairs={{0,3},{1,0},{2,1},{3,2},{4,7},{5,4},{6,5},{7,6},{8,11},{9,8},{10,9... | collective-permute-start | bytes 1622024 | tf_op jit(solution)/shard_map/ppermute | solution.py:447
  624.3 21.2 %collective-permute-start.119 = (bf16[3,704,128]{2,1,0:T(8,128)(2,1)S(1)}, bf16[3,704,128]{2,1,0:T(8,128)(2,1)S(1)}, u32[]{:S(2)}, u32[]{:S(2)}) collective-permute-start(bf16[3,704,128]{2,1,0:T(8,128)(2,1)S(1)} %fusion.27), channel_id=1, source_target_pairs={{0,1},{1,2},{2,3},{3,0},{4,5},{5,6},{6,7},{7,4},{8,9},{9,10},{10,1... | collective-permute-start | bytes 1622024 | tf_op jit(solution)/shard_map/ppermute | solution.py:447
  (166 other events, 2224.4 us)

commit v5 on v4

--- a/solution.py
+++ b/solution.py
@@ -212,8 +212,8 @@
 
 def feed_kernel(spots, *refs, slices):
     n_ref, g_ref = refs[:2]
-    w_in = [refs[2 + PIECES * s : 2 + PIECES * (s + 1)] for s in range(slices)]
-    at = 2 + PIECES * slices
+    w_in = [refs[2 + 4 * s : 6 + 4 * s] for s in range(slices)]
+    at = 2 + 4 * slices
     out_ref, dn_ref = refs[at : at + 2]
     d_out = [refs[at + 2 + 4 * s : at + 6 + 4 * s] for s in range(slices)]
     w_buf, d_buf, w_sem, d_sem = refs[at + 2 + 4 * slices :]
@@ -224,8 +224,9 @@
         held = s % 2
         for p in range(PIECES):
             lanes = pl.ds(pl.multiple_of(spots[s * PIECES + p] * LANES, LANES), LANES)
+            far = arrays[p // 2].at[p % 2]
             near = buf.at[held, :, :, lanes]
-            src, dst = (near, arrays[p // 2].at[p % 2]) if outward else (arrays[p], near)
+            src, dst = (near, far) if outward else (far, near)
             yield pltpu.make_async_copy(src, dst, sem.at[held])
 
     for s in range(slices):
@@ -289,7 +290,7 @@
 def feed(n, g, weights, spots):
     slices = len(weights)
     rows, width = n.shape
-    hidden = weights[0][0].shape[1]
+    hidden = weights[0][0].shape[2]
     whole = pl.BlockSpec((rows, width), lambda i, *_: (0, 0))
     there = pl.BlockSpec(memory_space=pl.ANY)
     acc = jax.ShapeDtypeStruct((rows, width), jnp.float32)
@@ -300,7 +301,7 @@
         grid_spec=pltpu.PrefetchScalarGridSpec(
             num_scalar_prefetch=1,
             grid=(slices,),
-            in_specs=[whole, whole] + [there] * (PIECES * slices),
+            in_specs=[whole, whole] + [there] * (4 * slices),
             out_specs=(whole, whole) + (there,) * (4 * slices),
             scratch_shapes=[
                 pltpu.VMEM((2, 3, hidden, width), jnp.bfloat16),
@@ -334,67 +335,40 @@
     return lax.optimization_barrier((value, *others))[0]
 
 
-def cross_first(piece, count, first, second):
-    swap = lambda value, bit: lax.ppermute(value, "dp", swap_over("dp", count, bit))
-    return piece, swap(piece, first), swap(piece, second), swap(piece, 1)
-
-
-def cross_last(found, count, second):
-    swap = lambda value, bit: lax.ppermute(value, "dp", swap_over("dp", count, bit))
-    own, one, two, core = found
-    both = swap(one, second)
-    return [own, one, two, both, core, swap(one, 1), swap(two, 1), swap(both, 1)]
-
-
-def scatter_slice(parts, count, first, second):
-    swap = lambda value, bit: lax.ppermute(value, "dp", swap_over("dp", count, bit))
-    low = lambda value: value.astype(jnp.bfloat16)
-    wide = lambda value: value.astype(jnp.float32)
-    away = low(wide(parts[1]) + wide(swap(parts[3], 1)))
-    near = wide(parts[0]) + wide(swap(parts[2], 1))
-    near = near + wide(swap(away, second))
-    return near[0] + wide(swap(low(near[1]), first))
-
-
-def join_kernel(spots, *refs, count, sets, high):
-    pieces, whole, sem = refs[:count], refs[count], refs[count + 1]
+def place_kernel(spots, *refs, split, sets, high, outward):
+    if outward:
+        whole, pieces, sem = refs[0], refs[1:-1], refs[-1]
+    else:
+        pieces, whole, sem = refs[:-2], refs[-2], refs[-1]
+    count = sum(split)
     copies = []
-    for k in range(count):
-        for s in range(sets):
-            lanes = pl.ds(pl.multiple_of(spots[k] * LANES, LANES), LANES)
-            rows = pl.ds(pl.multiple_of(spots[count + s] * high, high), high)
-            copies.append(pltpu.make_async_copy(pieces[k].at[s], whole.at[rows, lanes], sem))
+    k = 0
+    for piece, size in zip(pieces, split):
+        for j in range(size):
+            for s in range(sets):
+                lanes = pl.ds(pl.multiple_of(spots[k] * LANES, LANES), LANES)
+                rows = pl.ds(pl.multiple_of(spots[count + s] * high, high), high)
+                near, far = whole.at[rows, lanes], piece.at[j, s]
+                src, dst = (near, far) if outward else (far, near)
+                copies.append(pltpu.make_async_copy(src, dst, sem))
+            k += 1
     for copy in copies:
         copy.start()
     for copy in copies:
         copy.wait()
 
 
-def part_kernel(spots, whole, *refs, count, sets, high):
-    pieces, sem = refs[:count], refs[count]
-    copies = []
-    for k in range(count):
-        for s in range(sets):
-            lanes = pl.ds(pl.multiple_of(spots[k] * LANES, LANES), LANES)
-            rows = pl.ds(pl.multiple_of(spots[count + s] * high, high), high)
-            copies.append(pltpu.make_async_copy(whole.at[rows, lanes], pieces[k].at[s], sem))
-    for copy in copies:
-        copy.start()
-    for copy in copies:
-        copy.wait()
-
-
 def join(pieces, spots):
-    count = len(pieces)
-    sets, high, _ = pieces[0].shape
-    shape = (sets * high, count * LANES)
+    split = tuple(piece.shape[0] for piece in pieces)
+    _, sets, high, _ = pieces[0].shape
+    shape = (sets * high, sum(split) * LANES)
     return pl.pallas_call(
-        functools.partial(join_kernel, count=count, sets=sets, high=high),
+        functools.partial(place_kernel, split=split, sets=sets, high=high, outward=False),
         out_shape=jax.ShapeDtypeStruct(shape, pieces[0].dtype),
         grid_spec=pltpu.PrefetchScalarGridSpec(
             num_scalar_prefetch=1,
             grid=(1,),
-            in_specs=[pl.BlockSpec(memory_space=pl.ANY)] * count,
+            in_specs=[pl.BlockSpec(memory_space=pl.ANY)] * len(pieces),
             out_specs=pl.BlockSpec(shape, lambda i, *_: (0, 0)),
             scratch_shapes=[pltpu.SemaphoreType.DMA],
         ),
@@ -402,18 +376,17 @@
     )(spots, *pieces)
 
 
-def part(whole, spots, sets):
+def part(whole, spots, split, sets):
     high = whole.shape[0] // sets
-    count = whole.shape[1] // LANES
     there = pl.BlockSpec(memory_space=pl.ANY)
     return pl.pallas_call(
-        functools.partial(part_kernel, count=count, sets=sets, high=high),
-        out_shape=(jax.ShapeDtypeStruct((sets, high, LANES), whole.dtype),) * count,
+        functools.partial(place_kernel, split=split, sets=sets, high=high, outward=True),
+        out_shape=tuple(jax.ShapeDtypeStruct((size, sets, high, LANES), whole.dtype) for size in split),
         grid_spec=pltpu.PrefetchScalarGridSpec(
             num_scalar_prefetch=1,
             grid=(1,),
             in_specs=[pl.BlockSpec(whole.shape, lambda i, *_: (0, 0))],
-            out_specs=(there,) * count,
+            out_specs=(there,) * len(split),
             scratch_shapes=[pltpu.SemaphoreType.DMA],
         ),
         name="part",
@@ -438,7 +411,6 @@
     lanes_here = w_down.shape[1]
     heads_width = w_out.shape[0]
     exchange = dp == PIECES and lanes_here == LANES
-    half = rows // 2
     parts_of_heads = 2
     share = heads_width // parts_of_heads
 
@@ -448,62 +420,49 @@
     onward = lambda value: line(value, [(i, (i + 1) % mp) for i in range(mp)])
     backward = lambda value: line(value, [(i, (i - 1) % mp) for i in range(mp)])
     across = lambda value: line(value, swap_over("mp", mp, 2))
-    tie = lax.optimization_barrier
+    tie = lambda *values: lax.optimization_barrier(values)
+
+    def toward(value, first_row, back=False):
+        pairs = []
+        for d in range(dp):
+            for a, b in first_row:
+                a, b = (a, b) if d % 2 == 0 else (mp - 1 - a, mp - 1 - b)
+                pairs.append((d * mp + b, d * mp + a) if back else (d * mp + a, d * mp + b))
+        return lax.ppermute(value, ("dp", "mp"), pairs)
 
     home = z // 2
-    outer = (z == 0) | (z == mp - 1)
+    at_home = home == core
     first = core == 0
+    edge = (z == 0) | (z == mp - 1)
+    mirrored = jnp.where(home == 0, z, mp - 1 - z)
+    at_edge = at_home & edge
+    steps = ([(3, 2), (2, 1), (1, 0)], [(2, 1), (1, 0)], [(1, 0), (0, 1)])
 
     copy_qkv = low(w_qkv).reshape(3, lanes_here, parts_of_heads, share).transpose(2, 0, 3, 1)
     copy_qkv = copy_qkv.reshape(3 * heads_width, lanes_here)
     copy_first = jnp.concatenate([copy_qkv, jnp.pad(low(norm_gains), ((0, 14), (0, 0)))])
     copy_out = low(w_out)
     copy_feed = jnp.concatenate([low(w_gate_up).transpose(0, 2, 1), low(w_down)[None]])
-    chip_bits = [(2, 4) if s % 2 == 0 or not exchange else (4, 2) for s in range(mp)]
-    spots = spots_of(me if exchange else 0, chip_bits)
-
-    def start_cross(piece, s):
-        if exchange:
-            return cross_first(piece, dp, *chip_bits[s])
-        return lax.all_gather(piece, "dp", axis=2, tiled=True)
-
-    def end_cross(found, s):
-        if exchange:
-            return cross_last(found, dp, chip_bits[s][1])
-        whole = found.reshape(3, hidden_here, PIECES, LANES)
-        return [whole[:, :, block] for block in (0, 2, 4, 6, 1, 3, 5, 7)]
-
+    chip_bits = [(2, 4), (4, 2), (4, 2), (2, 4)] if exchange else [(2, 4)] * mp
+    spots = spots_of(me if exchange else 0, chip_bits).reshape(mp, PIECES)
+
+    x_own = inputs[0]
+    x_one = toward(x_own, steps[0])
     far_first = across(copy_first)
-
-    x_own = inputs[0]
-    keep = lax.dynamic_slice(x_own, (core * half, 0), (half, width))
-    got = pair(lax.dynamic_slice(x_own, ((1 - core) * half, 0), (half, width)))
     ids = jnp.concatenate([segment_ids[0], jnp.broadcast_to(row_length, (LANES,))])
-    ids = jnp.where(home == core, ids, pair(ids))
-    row_a = jnp.where(first, keep, got)
-    row_b = jnp.where(first, got, keep)
-    down_one = line(row_a, [(3, 2), (2, 1), (1, 0)])
-    up_one = line(row_b, [(0, 1), (1, 2), (2, 3)])
-    down_two = line(down_one, [(2, 1), (1, 0)])
-    up_two = line(up_one, [(1, 2), (2, 3)])
-    side = line(after(jnp.where(z == 0, row_a, row_b), down_one, up_one), [(0, 1), (3, 2)])
-    far = line(jnp.where(z == 1, down_two, up_two), [(1, 0), (2, 3)])
-    held = [
-        (jnp.where(home == 0, row_a, row_b), z),
-        (jnp.where(z == 0, down_one, jnp.where(z == 3, up_one, side)), z ^ 1),
-        (jnp.where(outer, jnp.where(z == 0, down_two, up_two), jnp.where(z == 1, down_one, up_one)), 2 - home),
-        (jnp.where(outer, far, jnp.where(z == 1, down_two, up_two)), 3 * (1 - home)),
-    ]
-
-    if exchange:
-        two = [jnp.where(first, copy_first, far_first), pair(jnp.where(first, far_first, copy_first))]
-        two = jnp.stack(two)
-        four = swap(two, 2)
-        last_four = swap(jnp.stack([two, four]), 4)
+    ids = jnp.where(at_home, ids, pair(ids))
+    x_two = toward(x_one, steps[1])
+    x_far = toward(jnp.where(at_edge, x_own, x_two), steps[2])
+    blocks = [mirrored, mirrored + 1, jnp.where(edge, 2, 3), jnp.where(edge, 3, 0)]
+    blocks = [jnp.where(home == 0, block, mp - 1 - block) for block in blocks]
+
+    if exchange:
+        own_first = jnp.where(first, copy_first, far_first)
+        two = jnp.stack([own_first, pair(jnp.where(first, far_first, copy_first))])
+        by_x, by_y = swap(two, 2), swap(two, 4)
+        corner = [swap(by_x[:1], 4), swap(by_y[1:], 2)]
         spots_first = jnp.concatenate([me ^ jnp.arange(PIECES, dtype=jnp.int32), jnp.zeros((1,), jnp.int32)])
-        pieces = [two[:1], two[1:], four[:1], four[1:]]
-        pieces += [last_four[i, j : j + 1] for i in range(2) for j in range(2)]
-        full_first = join(pieces, spots_first)
+        full_first = join([value[:, None] for value in (two, by_x, by_y, *corner)], spots_first)
     else:
         full_first = lax.all_gather(jnp.stack([copy_first, far_first]), "dp", axis=2, tiled=True)
         full_first = jnp.where(first, full_first[0], full_first[1])
@@ -511,10 +470,6 @@
     gain_one = wide_of(full_first[3 * heads_width])
     gain_two = wide_of(full_first[3 * heads_width + 1])
 
-    crossing = [start_cross(copy_feed, 0)]
-    if exchange:
-        out_one = onward(copy_out)
-        out_all = jnp.stack([copy_out, out_one, onward(out_one), backward(copy_out)])
     seg_row = ids[:seq_len]
     length = ids[seq_len]
     live_row = jnp.arange(seq_len, dtype=jnp.int32) < length
@@ -523,23 +478,33 @@
     lo, hi = key_blocks(seg_row, length, wide, narrow)
     lo_back, hi_back = key_blocks(seg_row, length, narrow, narrow)
 
+    def hop_one(piece, s):
+        return jnp.stack([piece, swap(piece, chip_bits[s][0])]) if exchange else piece
+
+    def hop_two(found, s):
+        return swap(found, chip_bits[s][1]) if exchange else found
+
+    def hop_core(found, other, s):
+        if exchange:
+            return [found, other, pair(found), pair(other)]
+        whole = lax.all_gather(found, "dp", axis=2, tiled=True)
+        whole = whole.reshape(3, hidden_here, PIECES, LANES)
+        whole = [whole[:, :, block] for block in (0, 2, 4, 6, 1, 3, 5, 7)]
+        return [jnp.stack(whole[2 * i : 2 * i + 2]) for i in range(4)]
+
+    copy_late = after(copy_feed, by_x, by_y) if exchange else copy_feed
+    near_zero = hop_one(copy_late, 0)
+    if exchange:
+        out_one = onward(copy_out)
+        out_all = jnp.stack([copy_out, out_one, onward(out_one), backward(copy_out)])[None]
+
     hats = []
     normed_one = jnp.zeros((seq_len, width), bf16)
-    for value, block in held:
-        for piece, side_of in ((value, core), (pair(value), 1 - core)):
-            piece = wide_of(piece)
-            hats.append(piece * rms_scale(piece))
-            at = block * rows + side_of * half
-            normed_one = lax.dynamic_update_slice(normed_one, low(hats[-1] * gain_one), (at, 0))
+    for value, block in zip((x_own, x_one, x_two, x_far), blocks):
+        piece = wide_of(jnp.where(at_home, value, pair(value)))
+        hats.append(piece * rms_scale(piece))
+        normed_one = lax.dynamic_update_slice(normed_one, low(hats[-1] * gain_one), (block * rows, 0))
     qkv = low(dot32(normed_one, full_qkv, NT))
-
-    feed_in = after(copy_feed, far)
-    plus = onward(feed_in)
-    minus = backward(feed_in)
-    if exchange:
-        out_in = after(out_all, last_four)
-        out_two = [out_in, swap(out_in, 2)]
-        out_four = out_two + [swap(value, 4) for value in out_two]
 
     rank = 2 * lax.rem(z, 2) + core
 
@@ -552,10 +517,6 @@
                 found.append((d * mp + c, to_dp * mp + to_z))
         return found
 
-    def group_at(s):
-        place = z ^ s
-        return (2 * core + place // 2) ^ (2 * lax.rem(place, 2))
-
     def spread(value):
         return [
             lax.ppermute(lax.dynamic_slice(value, ((rank ^ s) * rows, 0), (rows, share)), ("dp", "mp"), column_pairs(s))
@@ -563,140 +524,143 @@
         ]
 
     def collect(value, i):
-        found = jnp.zeros((seq_len, share), value.dtype)
+        found = []
         for s in range(mp):
-            piece = lax.dynamic_slice(value, (0, group_at(s) * heads_width + i * share), (rows, share))
-            piece = lax.ppermute(piece, ("dp", "mp"), [(there, here) for here, there in column_pairs(s)])
-            found = lax.dynamic_update_slice(found, piece, ((rank ^ s) * rows, 0))
+            piece = value[:, s * heads_width + i * share : s * heads_width + (i + 1) * share]
+            found.append(lax.ppermute(piece, ("dp", "mp"), [(there, here) for here, there in column_pairs(s)]))
         return found
 
+    def in_row_order(found):
+        found = jnp.stack(found)
+        return jnp.concatenate([lax.dynamic_index_in_dim(found, rank ^ block, 0, False) for block in range(mp)])
+
+    feed_in = after(copy_feed, x_far)
+    plus, minus = onward(feed_in), backward(feed_in)
+    far_zero = hop_two(near_zero, 0)
+    out_x = swap(out_all, 2) if exchange else copy_out
     raw_one, logs_one = attend(qkv, 0, share, seg_row, lo, hi, wide, narrow)
-    mine_one = low(raw_one * live)
-    if exchange:
-        qkv_next, plus, minus, mine_one, *out_four = tie((qkv, plus, minus, mine_one, *out_four))
-        out_eight = out_four + [pair(value) for value in out_four]
+    raw_one, logs_one, plus, minus, far_zero, out_x, qkv_next = tie(raw_one, logs_one, plus, minus, far_zero, out_x, qkv)
+    twice = onward(plus)
+    near_plus, near_minus = hop_one(plus, 1), hop_one(minus, 3)
+    spread_one = spread(low(raw_one * live))
+    feed_zero = hop_core(near_zero, far_zero, 0)
+    if exchange:
+        out_two = jnp.concatenate([out_all, out_x])
+        out_y = swap(out_two, 4)
     else:
-        qkv_next, plus, minus, mine_one = tie((qkv, plus, minus, mine_one))
-    spread_one = spread(mine_one)
-    twice = onward(plus)
-    crossing.append(start_cross(plus, 1))
-    slice_three = start_cross(minus, 3)
-    feed_full = [end_cross(crossing[0], 0)]
-
+        out_y = out_x
     raw_two, logs_two = attend(qkv_next, 1, share, seg_row, lo, hi, wide, narrow)
-    mine_two = low(raw_two * live)
-    spread_two = spread(mine_two)
+    raw_two, logs_two, twice, near_plus, near_minus, out_y, *spread_one = tie(
+        raw_two, logs_two, twice, near_plus, near_minus, out_y, *spread_one
+    )
+    spread_two = spread(low(raw_two * live))
+    far_plus = hop_two(near_plus, 1)
+    near_twice = hop_one(twice, 2)
+    far_minus = hop_two(near_minus, 3)
     raw_out = [raw_one, raw_two]
     log_sums = [jnp.where(live_row[None, :], logs, -NEG_FILL) for logs in (logs_one, logs_two)]
-    feed_full.append(end_cross(crossing[1], 1))
-    slice_two = start_cross(twice, 2)
-
-    if exchange:
-        place_out = jnp.array([0, 2, 4, 6, 1, 3, 5, 7], jnp.int32)
-        spots_out = jnp.concatenate([me ^ place_out, lax.rem(z + mp - jnp.arange(mp, dtype=jnp.int32), mp)])
-        full_out = join([out_eight[i] for i in range(PIECES)], spots_out)
+
+    places = jnp.arange(mp, dtype=jnp.int32)
+    group_place = lambda group: (2 * lax.rem(group, 2) + (core ^ (group // 2))) ^ z
+    if exchange:
+        spots_out = jnp.concatenate([
+            me ^ jnp.array([0, 2, 4, 6, 1, 3, 5, 7], jnp.int32), group_place(lax.rem(z + mp - places, mp))
+        ])
+        out_four = jnp.concatenate([out_two, out_y])
+        full_out = join([out_four, pair(out_four)], spots_out)
     else:
+        place = z ^ places
+        groups_here = (2 * core + place // 2) ^ (2 * lax.rem(place, 2))
         full_out = lax.all_gather(copy_out, ("dp", "mp"), axis=0)
-        full_out = full_out.reshape(dp, mp, heads_width, lanes_here).transpose(1, 2, 0, 3).reshape(mp * heads_width, width)
-
-    attended = jnp.zeros((rows, width), bf16)
-    for i, found in enumerate((spread_one, spread_two)):
-        for s in range(mp):
-            attended = lax.dynamic_update_slice(attended, found[s], (0, group_at(s) * heads_width + i * share))
-
+        full_out = full_out.reshape(dp, mp, heads_width, lanes_here).transpose(1, 2, 0, 3)[groups_here]
+        full_out = full_out.reshape(mp * heads_width, width)
+
+    attended = jnp.concatenate([spread_one[s // 2] if s % 2 == 0 else spread_two[s // 2] for s in range(2 * mp)], axis=1)
     resid_in = wide_of(x_own)
-    scale_one = rms_scale(resid_in)
-    hat_one = resid_in * scale_one
     after_attn = resid_in + dot32(attended, full_out, NN)
     scale_two = rms_scale(after_attn)
     hat_two = after_attn * scale_two
     normed_two = low(hat_two * gain_two)
 
-    fed, d_normed_two, d_feed = [], [], []
-    out_part, d_part, grads = feed(normed_two, cotangent[0], feed_full, spots[: 2 * PIECES])
-    fed.append(out_part)
-    d_normed_two.append(d_part)
-    d_feed += grads
-    feed_full = [end_cross(slice_two, 2), end_cross(slice_three, 3)]
-    out_part, d_part, grads = feed(normed_two, cotangent[0], feed_full, spots[2 * PIECES :])
-    fed.append(out_part)
-    d_normed_two.append(d_part)
-    d_feed += grads
-    d_normed_two = functools.reduce(jnp.add, d_normed_two)
+    spots_one = jnp.concatenate([spots[0], spots[1]])
+    spots_two = jnp.concatenate([spots[3], spots[2]])
+    feed_one = [feed_zero, hop_core(near_plus, far_plus, 1)]
+    normed_two, far_minus, near_twice = tie(normed_two, far_minus, near_twice)
+    far_twice = hop_two(near_twice, 2)
+    feed_minus = hop_core(near_minus, far_minus, 3)
+    fed_one, back_one, grads_one = feed(normed_two, cotangent[0], feed_one, spots_one)
+    fed_one, back_one, far_twice, *feed_minus = tie(fed_one, back_one, far_twice, *feed_minus)
+    feed_two = [feed_minus, hop_core(near_twice, far_twice, 2)]
+    held = [pair(grads[k]) for grads in grads_one for k in (3, 2)] if exchange else []
+    fed_two, back_two, grads_two = feed(normed_two, cotangent[0], feed_two, spots_two)
+    if exchange:
+        fed_two, back_two, *held = tie(fed_two, back_two, *held)
+        away = [low(wide_of(grads_one[i][1]) + wide_of(held[2 * i])) for i in range(2)]
+        near = [wide_of(grads_one[i][0]) + wide_of(held[2 * i + 1]) for i in range(2)]
+        away = [swap(away[i], chip_bits[(0, 1)[i]][1]) for i in range(2)]
+        held = [pair(grads[k]) for grads in grads_two for k in (3, 2)]
+
+    d_normed_two = back_one + back_two
     d_after = wide_of(cotangent[0]) + norm_back(d_normed_two, hat_two, scale_two, gain_two)
-
     d_branch = low(d_after)
     d_attended = low(dot32(d_branch, full_out, NT))
-    d_attended = [collect(d_attended, i) for i in range(parts_of_heads)]
+    d_first = collect(d_attended, 0)
+    d_second = collect(d_attended, 1)
     grad_out = low(dot32(attended, d_branch, TN))
-    if exchange:
-        away = part(grad_out, spots_out, mp)
-        near = [low(wide_of(away[k]) + wide_of(pair(away[k + 4]))) for k in range(4)]
-        near = [low(wide_of(near[k]) + wide_of(swap(near[k + 2], 4))) for k in range(2)]
-        owned_out = wide_of(near[0]) + wide_of(swap(near[1], 2))
-        grad_out = wide_of(onward(low(wide_of(onward(low(owned_out[2]))) + owned_out[3])))
-        grad_out = grad_out + wide_of(backward(low(owned_out[1]))) + owned_out[0]
-    else:
-        grad_out = lax.psum_scatter(grad_out, "dp", scatter_dimension=1, tiled=True)
-        grad_out = wide_of(lax.psum_scatter(grad_out, "mp", scatter_dimension=0, tiled=True))
-
-    if exchange:
-        owned = [scatter_slice(pieces, dp, *bits) for pieces, bits in zip(d_feed, chip_bits)]
-    else:
-        back = jnp.array([0, 4, 1, 5, 2, 6, 3, 7])
-        owned = []
-        for pieces in d_feed:
-            whole = jnp.concatenate(pieces)[back].transpose(1, 2, 0, 3).reshape(3, hidden_here, width)
-            owned.append(wide_of(lax.psum_scatter(whole, "dp", scatter_dimension=2, tiled=True)))
-    total = owned[0] + wide_of(backward(low(owned[1])))
-    total = total + wide_of(onward(low(owned[3] + wide_of(onward(low(owned[2]))))))
-    grad_gate_up = total[:2].transpose(0, 2, 1)
-    grad_down = total[2]
-
-    d_qkv = []
-    for i in range(parts_of_heads):
-        d_here = jnp.where(live_row[:, None], d_attended[i], jnp.zeros((), bf16))
+
+    def heads_back(found, i):
+        d_here = jnp.where(live_row[:, None], in_row_order(found), jnp.zeros((), bf16))
         row_dot = jnp.sum((raw_out[i] * d_here).reshape(seq_len, share // HEAD, HEAD), axis=-1).T
-        d_qkv.append(attend_back(qkv, i, d_here, log_sums[i], row_dot, seg_row, lo_back, hi_back, narrow, narrow))
-    d_qkv = jnp.concatenate(d_qkv, axis=1)
-    block_output = after_attn + functools.reduce(jnp.add, fed)
+        return d_here, row_dot
+
+    d_here, row_dot = heads_back(d_first, 0)
+    if exchange:
+        out_near, out_core = part(grad_out, spots_out, (4, 4), mp)
+        d_here, row_dot, out_near, out_core, *away = tie(d_here, row_dot, out_near, out_core, *away)
+        near = [near[i] + wide_of(away[i]) for i in range(2)]
+        ends = [swap(low(near[i][1]), chip_bits[(0, 1)[i]][0]) for i in range(2)]
+        away = [low(wide_of(grads_two[i][1]) + wide_of(held[2 * i])) for i in range(2)]
+        near_two = [wide_of(grads_two[i][0]) + wide_of(held[2 * i + 1]) for i in range(2)]
+        away = [swap(away[i], chip_bits[(3, 2)[i]][1]) for i in range(2)]
+        out_core = pair(out_core)
+    d_qkv_one = attend_back(qkv, 0, d_here, log_sums[0], row_dot, seg_row, lo_back, hi_back, narrow, narrow)
+    d_here, row_dot = heads_back(d_second, 1)
+    if exchange:
+        d_qkv_one, d_here, out_core, *found = tie(d_qkv_one, d_here, out_core, *ends, *away)
+        owned = [near[i][0] + wide_of(found[i]) for i in range(2)]
+        near_two = [near_two[i] + wide_of(found[2 + i]) for i in range(2)]
+        ends = [swap(low(near_two[i][1]), chip_bits[(3, 2)[i]][0]) for i in range(2)]
+        from_one = backward(low(owned[1]))
+        out_near = wide_of(out_near) + wide_of(out_core)
+        out_away = swap(low(out_near[2:]), 4)
+    d_qkv_two = attend_back(qkv, 1, d_here, log_sums[1], row_dot, seg_row, lo_back, hi_back, narrow, narrow)
+    if exchange:
+        d_qkv_two, from_one, out_away, *ends = tie(d_qkv_two, from_one, out_away, *ends)
+    d_qkv = jnp.concatenate([d_qkv_one, d_qkv_two], axis=1)
+    block_output = after_attn + (fed_one + fed_two)
     grad_gain_two = jnp.sum(d_normed_two * hat_two, axis=0)
 
     grad_gain_one = jnp.zeros((width,), f32)
     sums = [None] * mp
     for k in range(mp - 1, -1, -1):
-        block = held[k][1]
-        halves = []
-        for j, side_of in enumerate((core, 1 - core)):
-            at = block * rows + side_of * half
-            found = dot32(lax.dynamic_slice(d_qkv, (at, 0), (half, d_qkv.shape[1])), full_qkv, NN)
-            grad_gain_one = grad_gain_one + jnp.sum(found * hats[2 * k + j], axis=0)
-            halves.append(found)
-        sums[k] = halves[0] + wide_of(pair(low(halves[1])))
-    inward = wide_of(line(low(sums[3]), [(0, 1), (3, 2)]))
-    passed = low(jnp.where(outer, sums[2], sums[3] + inward))
-    up_two = line(passed, [(0, 1), (1, 2)])
-    down_two = line(passed, [(3, 2), (2, 1)])
-    third = sums[2] + wide_of(jnp.where(z == 1, up_two, down_two))
-    up_three = line(jnp.where(z == 2, up_two, low(jnp.where(z == 0, sums[1], third))), [(0, 1), (1, 2), (2, 3)])
-    down_three = line(jnp.where(z == 1, down_two, low(jnp.where(z == 3, sums[1], third))), [(3, 2), (2, 1), (1, 0)])
-    side = line(low(sums[1]), [(1, 0), (2, 3)])
-    mine = sums[0] + wide_of(jnp.where(outer, side, jnp.where(z == 1, up_three, down_three)))
-    theirs = wide_of(jnp.where(home == 0, down_three, up_three))
-    stay = jnp.where(home == core, mine, theirs)
-    moved = wide_of(pair(low(jnp.where(home == core, theirs, mine))))
-    d_normed_one = jnp.concatenate([jnp.where(first, stay, moved), jnp.where(first, moved, stay)])
-    input_grad = d_after + norm_back(d_normed_one, hat_one, scale_one, gain_one)
+        found = dot32(lax.dynamic_slice(d_qkv, (blocks[k] * rows, 0), (rows, d_qkv.shape[1])), full_qkv, NN)
+        grad_gain_one = grad_gain_one + jnp.sum(found * hats[k], axis=0)
+        sums[k] = jnp.where(at_home, found + wide_of(pair(low(found))), 0.0)
+    inward = wide_of(toward(low(sums[3]), steps[2], back=True))
+    inward_two = toward(low(jnp.where(at_edge, sums[2], sums[2] + inward)), steps[1], back=True)
+    inward_one = toward(low(sums[1] + wide_of(inward_two)), steps[0], back=True)
+    d_normed_one = jnp.where(at_edge, sums[0] + inward, sums[0]) + wide_of(inward_one)
+    scale_one = rms_scale(resid_in)
+    input_grad = d_after + norm_back(d_normed_one, resid_in * scale_one, scale_one, gain_one)
 
     grad_qkv = low(dot32(d_qkv, normed_one, TN))
     if exchange:
-        away = part(grad_qkv, spots_first, 1)
-        near = [low(wide_of(away[k]) + wide_of(swap(away[k + 4], 4))) for k in range(4)]
-        near = [wide_of(near[k]) + wide_of(swap(near[k + 2], 2)) for k in range(2)]
-        moved = wide_of(pair(low(near[1][0])))
-        stay = near[0][0]
-        here = jnp.where(first, stay, moved)
-        there = jnp.where(first, moved, stay)
+        near, far = part(grad_qkv, spots_first, (4, 4), 1)
+        near = wide_of(near) + wide_of(swap(far, 4))
+        near = near[:2] + wide_of(swap(low(near[2:]), 2))
+        moved = wide_of(pair(low(near[1, 0])))
+        here = jnp.where(first, near[0, 0], moved)
+        there = jnp.where(first, moved, near[0, 0])
     else:
         nothing = jnp.zeros_like(grad_qkv)
         both = jnp.stack([jnp.where(first, grad_qkv, nothing), jnp.where(first, nothing, grad_qkv)])
@@ -704,6 +668,29 @@
         here, there = both[0], both[1]
     grad_qkv = here + wide_of(across(low(there)))
     grad_qkv = grad_qkv.reshape(parts_of_heads, 3, share, lanes_here).transpose(1, 3, 0, 2).reshape(w_qkv.shape)
+
+    if exchange:
+        owned += [near_two[i][0] + wide_of(ends[i]) for i in range(2)]
+        total = owned[0] + wide_of(from_one)
+        total = total + wide_of(onward(low(owned[2] + wide_of(onward(low(owned[3]))))))
+        out_near = out_near[:2] + wide_of(out_away)
+        out_owned = out_near[0] + wide_of(swap(low(out_near[1]), 2))
+        grad_out = wide_of(onward(low(wide_of(onward(low(out_owned[2]))) + out_owned[3])))
+        grad_out = grad_out + wide_of(backward(low(out_owned[1]))) + out_owned[0]
+    else:
+        total = 0.0
+        back = jnp.array([0, 4, 1, 5, 2, 6, 3, 7])
+        for s, pieces in zip((0, 1, 3, 2), grads_one + grads_two):
+            whole = jnp.concatenate(pieces)[back].transpose(1, 2, 0, 3).reshape(3, hidden_here, width)
+            whole = lax.psum_scatter(whole, "dp", scatter_dimension=2, tiled=True)
+            for _ in range(s):
+                whole = backward(whole)
+            total = total + wide_of(whole)
+        grad_out = grad_out.reshape(mp, heads_width, width)[group_place(places)].reshape(mp * heads_width, width)
+        grad_out = lax.psum_scatter(grad_out, "dp", scatter_dimension=1, tiled=True)
+        grad_out = wide_of(lax.psum_scatter(grad_out, "mp", scatter_dimension=0, tiled=True))
+    grad_gate_up = total[:2].transpose(0, 2, 1)
+    grad_down = total[2]
 
     grad_gains = jnp.stack([grad_gain_one, grad_gain_two])
     for axis, count in (("mp", mp), ("dp", dp)):

time: 671 us -> 569 us (0.85)
  waiting for transfers between devices: 214 us -> 137 us
  starting transfers between devices: 166 us -> 107 us
  other arithmetic: 70.5 us -> 105 us
  Pallas kernels: 144 us -> 159 us
  matrix products: 33 us -> 25.6 us
    ppermute x26 -> x14, starting transfers between devices: 61.8 us -> 12.6 us  [on_device(): line = lambda value, pairs: lax.ppermute(value, 'mp', pairs)]
    ppermute x26 -> x14, waiting for transfers between devices: 96.1 us -> 57.3 us  [on_device(): line = lambda value, pairs: lax.ppermute(value, 'mp', pairs)]
    ppermute x5, waiting for transfers between devices: 22.5 us -> 1.03 us  [on_device(): lax.ppermute(grad_gains, axis, swap_over(axis, count, bit))]
    dynamic_update_slice x16 -> x0, local copies, waits for them, and re-layouts: 12.8 us -> none  [the longest x8 12.7 us: on_device(): lax.dynamic_update_slice(attended, found[s], (0, group_at(s) * heads_widt...]
    ppermute x35 -> x55, waiting for transfers between devices: 56.6 us -> 44.1 us  [on_device(): lax.ppermute(value, 'dp', swap_over('dp', dp, bit))]
    ppermute x44 -> x6, starting transfers between devices: 26.8 us -> 14.8 us  [toward(): return lax.ppermute(value, ('dp', 'mp'), pairs)]
    pallas_call x2, Pallas kernels: 45.8 us -> 57.6 us  [attend_back(): pl.pallas_call(functools.partial(attend_back_kernel, bk=bk, heads=heads),...]
    add x6 -> x10, other arithmetic: 1.63 us -> 13.4 us  [the longest x2 4.86 us: on_device(): near_two = [near_two[i] + wide_of(found[2 + i]) for i in range(2)]]
  transfers between devices with their start and end apart: 126 -> 96, of which waited for: 36 -> 27; matrix products, arithmetic and copies ran while one was open for 19% -> 23% of each run, Pallas kernels for 22% -> 28%
where the time goes in v5:
time: 569 us; the launch traced here: 565 us
  Pallas kernels  159 us (28%)
  waiting for transfers between devices  137 us (24%)
  starting transfers between devices  107 us (19%)
  other arithmetic  105 us (18%)
  local copies, waits for them, and re-layouts  28.2 us (5%)
  matrix products  25.6 us (4%)
    pallas_call x2, Pallas kernels, attend_back(): pl.pallas_call(functools.partial(attend_back_kernel, bk=bk, heads=heads),...  57.6 us
    ppermute x14, waiting for transfers between devices, on_device(): line = lambda value, pairs: lax.ppermute(value, 'mp', pairs)  57.3 us
    pallas_call x2, Pallas kernels, feed(): pl.pallas_call(functools.partial(feed_kernel, slices=slices), out_shape=(...  48 us
    ppermute x55, waiting for transfers between devices, on_device(): lax.ppermute(value, 'dp', swap_over('dp', dp, bit))  44.1 us
    pallas_call x2, Pallas kernels, attend(): pl.pallas_call(functools.partial(attend_kernel, bk=bk, heads=heads), out_...  39.7 us
    ppermute x55, starting transfers between devices, on_device(): lax.ppermute(value, 'dp', swap_over('dp', dp, bit))  28.7 us
    dot_general x9, matrix products, dot32(): lax.dot_general(left, right, dims, preferred_element_type=jnp.float32)  25.6 us
    ppermute x6, waiting for transfers between devices, toward(): return lax.ppermute(value, ('dp', 'mp'), pairs)  25.6 us
  transfers between devices with their start and end apart: 96, of which 27 were waited for; matrix products, arithmetic and copies ran while one was open for 23% of the time, Pallas kernels for 28%

profile of v5, /device:TPU:0, one launch (start us, length us, event | category | flops | bytes accessed | tf_op | source)
XLA Modules:
  0.0 565.4 jit_solution(12853886141736099693)
XLA Ops:
  4.5 4.9 collective-permute-start.2
  16.9 13.4 %collective-permute-done.2 = bf16[784,128]{1,0:T(8,128)(2,1)S(1)} collective-permute-done((bf16[784,128]{1,0:T(8,128)(2,1)S(1)}, bf16[784,128]{1,0:T(8,128)(2,1)S(1)}, u32[]{:S(2)}, u32[]{:S(2)}) %collective-permute-start.2) | collective-permute-done | bytes 200736 | tf_op jit(solution)/shard_map/ppermute | solution.py:419
  40.7 3.7 collective-permute-done.4
  47.2 8.5 %collective-permute-done.20 = bf16[256,128]{1,0:T(8,128)(2,1)} collective-permute-done((bf16[256,128]{1,0:T(8,128)(2,1)}, bf16[256,128]{1,0:T(8,128)(2,1)}, u32[]{:S(2)}, u32[]{:S(2)}) %collective-permute-start.20) | collective-permute-done | bytes 65568 | tf_op jit(solution)/shard_map/ppermute | solution.py:419
  59.9 3.3 collective-permute-done.7
  63.9 3.3 join.2
  77.3 8.3 %collective-permute-done.12 = bf16[512,1024]{1,0:T(8,128)(2,1)S(1)} collective-permute-done((bf16[512,1024]{1,0:T(8,128)(2,1)S(1)}, bf16[512,1024]{1,0:T(8,128)(2,1)S(1)}, u32[]{:S(2)}, u32[]{:S(2)}) %collective-permute-start.12) | collective-permute-done | bytes 1048608 | tf_op jit(solution)/shard_map/ppermute | solution.py:431
  86.0 3.8 collective-permute-start.15
  92.6 4.9 convolution_convert_fusion.q_ref.k_ref.v_ref
  97.5 19.8 %attend.2 = (f32[2048,128]{1,0:T(8,128)}, f32[2,2048]{1,0:T(2,128)}) custom-call(s32[2]{0:T(128)} %get-tuple-element.229.lo_ref, s32[2]{0:T(128)} %get-tuple-element.228.hi_ref, bf16[2048,768]{1,0:T(8,128)(2,1)} %convolution_convert_fusion.q_ref.k_ref.v_ref, bf16[2048,768]{1,0:T(8,128)(2,1)} %convolution_convert_fusion.q_ref.k_ref.v_ref, ...), custom_call_target="tpu_custom_call" | custom-call | flops 8589934592 | bytes 2621440 | tf_op jit(solution)/shard_map/attend/pallas_call | solution.py:94
  123.6 2.6 collective-permute-start.26
  126.2 19.9 %attend.3 = (f32[2048,128]{1,0:T(8,128)}, f32[2,2048]{1,0:T(2,128)}) custom-call(s32[2]{0:T(128)} %get-tuple-element.229.lo_ref, s32[2]{0:T(128)} %get-tuple-element.228.hi_ref, bf16[2048,768]{1,0:T(8,128)(2,1)} %convolution_convert_fusion.q_ref.k_ref.v_ref, bf16[2048,768]{1,0:T(8,128)(2,1)} %convolution_convert_fusion.q_ref.k_ref.v_ref, ...), custom_call_target="tpu_custom_call" | custom-call | flops 8589934592 | bytes 2621440 | tf_op jit(solution)/shard_map/attend/pallas_call | solution.py:94
  146.1 2.3 pad_maximum_fusion.2.refs_2_
  148.5 5.3 collective-permute-start.28
  155.7 2.4 pad_maximum_fusion.1.refs_6_
  158.1 2.5 collective-permute-done.29
  168.8 2.6 collective-permute-start.31
  174.3 3.2 collective-permute-start.32
  178.4 2.7 collective-permute-done.32
  181.1 7.9 %collective-permute-start.33 = (bf16[512,128]{1,0:T(8,128)(2,1)}, bf16[512,128]{1,0:T(8,128)(2,1)S(1)}, u32[]{:S(2)}, u32[]{:S(2)}) collective-permute-start(bf16[512,128]{1,0:T(8,128)(2,1)} %get-tuple-element.257), channel_id=1, source_target_pairs={{0,3},{1,1},{2,7},{3,5},{4,2},{5,0},{6,6},{7,4},{8,11},{9,9},{10,1... | collective-permute-start | bytes 393224 | tf_op jit(solution)/shard_map/ppermute | solution.py:522
  195.1 3.5 join.3
  198.7 3.3 multiply_reduce_fusion.2
  204.5 15.3 %collective-permute-done.35.refs_3_ = bf16[2,3,704,128]{3,2,1,0:T(8,128)(2,1)} collective-permute-done((bf16[2,3,704,128]{3,2,1,0:T(8,128)(2,1)}, bf16[2,3,704,128]{3,2,1,0:T(8,128)(2,1)}, u32[]{:S(2)}, u32[]{:S(2)}) %collective-permute-start.35) | collective-permute-done | bytes 1081376 | tf_op jit(solution)/shard_map/ppermute | solution.py:417
  222.4 24.0 %feed.2 = (f32[512,1024]{1,0:T(8,128)}, f32[512,1024]{1,0:T(8,128)}, bf16[2,3,704,128]{3,2,1,0:T(8,128)(2,1)}, bf16[2,3,704,128]{3,2,1,0:T(8,128)(2,1)}, bf16[2,...) custom-call(s32[16]{0:T(128)} %bitcast.234, ...), custom_call_target="tpu_custom_call" | custom-call | flops 19931332608 | bytes 23592960 | tf_op jit(solution)/shard_map/feed/pallas_call | solution.py:298
  250.6 24.0 %feed.3 = (f32[512,1024]{1,0:T(8,128)}, f32[512,1024]{1,0:T(8,128)}, bf16[2,3,704,128]{3,2,1,0:T(8,128)(2,1)}, bf16[2,3,704,128]{3,2,1,0:T(8,128)(2,1)}, bf16[2,...) custom-call(s32[16]{0:T(128)} %pad_add_fusion.2.spots, ...), custom_call_target="tpu_custom_call" | custom-call | flops 19931332608 | bytes 23592960 | tf_op jit(solution)/shard_map/feed/pallas_call | solution.py:298
  274.7 3.7 multiply_reduce_fusion
  279.4 4.9 multiply_add_fusion
  284.4 2.6 convolution_convert_fusion.1.refs_0_
  292.7 3.9 collective-permute-start.54
  297.3 2.5 add_convert_fusion.2
  299.9 4.3 collective-permute-start.58
  304.6 5.1 collective-permute-start.60
  309.7 2.5 add_convert_fusion.3
  312.2 3.6 part.2
  321.1 4.2 convert_multiply_fusion.10
  325.2 2.6 copy.65
  327.8 2.5 copy.67
  334.3 9.7 %collective-permute-done.56 = bf16[2,3,704,128]{3,2,1,0:T(8,128)(2,1)} collective-permute-done((bf16[2,3,704,128]{3,2,1,0:T(8,128)(2,1)}, bf16[2,3,704,128]{3,2,1,0:T(8,128)(2,1)}, u32[]{:S(2)}, u32[]{:S(2)}) %collective-permute-start.56) | collective-permute-done | bytes 1081376 | tf_op jit(solution)/shard_map/ppermute | solution.py:417
  350.7 3.1 add_convert_fusion
  354.9 2.5 add_convert_fusion.1
  357.4 3.5 collective-permute-done.63
  361.1 4.3 collective-permute-done.62
  366.3 28.8 %attend_back.2 = bf16[2048,384]{1,0:T(8,128)(2,1)} custom-call(s32[4]{0:T(128)} %get-tuple-element.219.lo_ref, s32[4]{0:T(128)} %get-tuple-element.218.hi_ref, bf16[2048,768]{1,0:T(8,128)(2,1)} %convolution_convert_fusion.q_ref.k_ref.v_ref, bf16[2048,128]{1,0:T(8,128)(2,1)} %get-tuple-element.150.do_ref, f32[2,2048]{1,0:T(2,128)} %get-tuple-element.272.lse_ref, ...), custom_call_target="tpu_custom_call" | custom-call | flops 21474836480 | bytes 4194304 | tf_op jit(solution)/shard_map/attend_back/pallas_call | solution.py:170
  395.1 2.3 convert_add_fusion.1
  397.7 2.5 convert_add_fusion.2
  406.6 28.8 %attend_back.3 = bf16[2048,384]{1,0:T(8,128)(2,1)} custom-call(s32[4]{0:T(128)} %get-tuple-element.219.lo_ref, s32[4]{0:T(128)} %get-tuple-element.218.hi_ref, bf16[2048,768]{1,0:T(8,128)(2,1)} %convolution_convert_fusion.q_ref.k_ref.v_ref, bf16[2048,128]{1,0:T(8,128)(2,1)} %get-tuple-element.165.do_ref, f32[2,2048]{1,0:T(2,128)} %get-tuple-element.271.lse_ref, ...), custom_call_target="tpu_custom_call" | custom-call | flops 21474836480 | bytes 4194304 | tf_op jit(solution)/shard_map/attend_back/pallas_call | solution.py:170
  438.7 2.7 fusion.105
  443.2 2.6 fusion.106
  445.8 4.6 convolution_convert_fusion.2.refs_0_
  451.9 3.9 collective-permute-start.76
  455.8 2.7 fusion.107
  460.8 3.2 part.3
  464.1 12.9 %collective-permute-done.86 = bf16[256,128]{1,0:T(8,128)(2,1)S(1)} collective-permute-done((bf16[256,128]{1,0:T(8,128)(2,1)S(1)}, bf16[256,128]{1,0:T(8,128)(2,1)S(1)}, u32[]{:S(2)}, u32[]{:S(2)}) %collective-permute-start.86) | collective-permute-done | bytes 65568 | tf_op jit(solution)/shard_map/ppermute | solution.py:419
  477.0 6.3 %collective-permute-done.76 = bf16[512,1024]{1,0:T(8,128)(2,1)} collective-permute-done((bf16[512,1024]{1,0:T(8,128)(2,1)}, bf16[512,1024]{1,0:T(8,128)(2,1)}, u32[]{:S(2)}, u32[]{:S(2)}) %collective-permute-start.76) | collective-permute-done | bytes 1048608 | tf_op jit(solution)/shard_map/ppermute | solution.py:431
  483.3 3.1 fusion.18
  493.3 18.6 %collective-permute-done.90 = bf16[3,704,128]{2,1,0:T(8,128)(2,1)S(1)} collective-permute-done((bf16[3,704,128]{2,1,0:T(8,128)(2,1)S(1)}, bf16[3,704,128]{2,1,0:T(8,128)(2,1)S(1)}, u32[]{:S(2)}, u32[]{:S(2)}) %collective-permute-start.90) | collective-permute-done | bytes 540704 | tf_op jit(solution)/shard_map/ppermute | solution.py:419
  515.4 4.8 collective-permute-start.80
  523.4 11.0 %collective-permute-done.80 = bf16[512,1024]{1,0:T(8,128)(2,1)S(1)} collective-permute-done((bf16[512,1024]{1,0:T(8,128)(2,1)S(1)}, bf16[512,1024]{1,0:T(8,128)(2,1)S(1)}, u32[]{:S(2)}, u32[]{:S(2)}) %collective-permute-start.80) | collective-permute-done | bytes 1048608 | tf_op jit(solution)/shard_map/ppermute | solution.py:431
  534.5 3.5 fusion.22
  538.0 2.5 collective-permute-start.91
  542.8 3.4 collective-permute-start.92
  546.2 3.2 collective-permute-done.84
  553.4 2.6 fusion.100
  560.3 4.2 fusion.14
  (488 shorter events, 142.6 us)
Async XLA Ops:
  0.7 67.4 %collective-permute-start.1 = (bf16[512,1024]{1,0:T(8,128)(2,1)}, bf16[512,1024]{1,0:T(8,128)(2,1)}, u32[]{:S(2)}, u32[]{:S(2)}) collective-permute-start(bf16[512,1024]{1,0:T(8,128)(2,1)} %bitcast.190), channel_id=1, source_target_pairs={{0,4},{4,0},{8,12},{12,8},{16,20},{20,16},{24,28},{28,24},{1,5},{5... | collective-permute-start | bytes 3145736 | tf_op jit(solution)/shard_map/ppermute | solution.py:417
  1.3 35.3 %collective-permute-start.8 = (bf16[512,1024]{1,0:T(8,128)(2,1)}, bf16[512,1024]{1,0:T(8,128)(2,1)}, u32[]{:S(2)}, u32[]{:S(2)}) collective-permute-start(bf16[512,1024]{1,0:T(8,128)(2,1)} %bitcast.191), channel_id=1, source_target_pairs={{3,2},{2,1},{1,0},{4,5},{5,6},{6,7},{11,10},{10,9},{9,8},{12,13},{... | collective-permute-start | bytes 3145736 | tf_op jit(solution)/shard_map/ppermute | solution.py:431
  4.5 25.8 %collective-permute-start.2 = (bf16[784,128]{1,0:T(8,128)(2,1)S(1)}, bf16[784,128]{1,0:T(8,128)(2,1)S(1)}, u32[]{:S(2)}, u32[]{:S(2)}) collective-permute-start(bf16[784,128]{1,0:T(8,128)(2,1)S(1)} %fusion.72), channel_id=1, source_target_pairs={{0,2},{1,3},{2,0},{3,1},{4,6},{5,7},{6,4},{7,5},{8,10},{9,11},{10,... | collective-permute-start | bytes 602120 | tf_op jit(solution)/shard_map/ppermute | solution.py:419
  10.7 23.6 %collective-permute-start = (s32[2176]{0:T(1024)S(1)}, s32[2176]{0:T(1024)S(1)}, u32[]{:S(2)}, u32[]{:S(2)}) collective-permute-start(s32[2176]{0:T(1024)S(1)} %concatenate.40), channel_id=1, source_target_pairs={{0,4},{4,0},{8,12},{12,8},{16,20},{20,16},{24,28},{28,24},{1,5},{5... | collective-permute-start | bytes 26120 | tf_op jit(solution)/shard_map/ppermute | solution.py:417
  13.2 24.9 %collective-permute-start.18 = (bf16[256,128]{1,0:T(8,128)(2,1)}, bf16[256,128]{1,0:T(8,128)(2,1)}, u32[]{:S(2)}, u32[]{:S(2)}) collective-permute-start(bf16[256,128]{1,0:T(8,128)(2,1)} %convert_element_type.351), channel_id=1, source_target_pairs={{0,1},{1,2},{2,3},{3,0},{4,5},{5,6},{6,7},{7,4},{8,9},{9,10},{10,1... | collective-permute-start | bytes 196616 | tf_op jit(solution)/shard_map/ppermute | solution.py:419
  36.6 32.2 %collective-permute-start.10 = (bf16[512,1024]{1,0:T(8,128)(2,1)}, bf16[512,1024]{1,0:T(8,128)(2,1)S(1)}, u32[]{:S(2)}, u32[]{:S(2)}) collective-permute-start(bf16[512,1024]{1,0:T(8,128)(2,1)} %collective-permute-done.8), channel_id=1, source_target_pairs={{2,1},{1,0},{5,6},{6,7},{10,9},{9,8},{13,14},{14,15},{18,17},{17,1... | collective-permute-start | bytes 3145736 | tf_op jit(solution)/shard_map/ppermute | solution.py:431
  38.1 17.6 %collective-permute-start.20 = (bf16[256,128]{1,0:T(8,128)(2,1)}, bf16[256,128]{1,0:T(8,128)(2,1)}, u32[]{:S(2)}, u32[]{:S(2)}) collective-permute-start(bf16[256,128]{1,0:T(8,128)(2,1)} %convert_element_type.351), channel_id=1, source_target_pairs={{0,3},{1,0},{2,1},{3,2},{4,7},{5,4},{6,5},{7,6},{8,11},{9,8},{10,9... | collective-permute-start | bytes 196616 | tf_op jit(solution)/shard_map/ppermute | solution.py:419
  57.8 59.5 %collective-permute-start.21 = (bf16[1,4,256,128]{3,2,1,0:T(8,128)(2,1)S(1)}, bf16[1,4,256,128]{3,2,1,0:T(8,128)(2,1)}, u32[]{:S(2)}, u32[]{:S(2)}) collective-permute-start(bf16[1,4,256,128]{3,2,1,0:T(8,128)(2,1)S(1)} %maximum_bitcast_fusion), channel_id=1, source_target_pairs={{0,8},{4,12},{8,0},{12,4},{16,24},{20,28},{24,16},{28,20},{1,9},{5... | collective-permute-start | bytes 786440 | tf_op jit(solution)/shard_map/ppermute | solution.py:417
  68.9 16.7 %collective-permute-start.12 = (bf16[512,1024]{1,0:T(8,128)(2,1)S(1)}, bf16[512,1024]{1,0:T(8,128)(2,1)S(1)}, u32[]{:S(2)}, u32[]{:S(2)}) collective-permute-start(bf16[512,1024]{1,0:T(8,128)(2,1)S(1)} %broadcast_select_fusion), channel_id=1, source_target_pairs={{1,0},{0,1},{6,7},{7,6},{9,8},{8,9},{14,15},{15,14},{17,16},{16,17... | collective-permute-start | bytes 3145736 | tf_op jit(solution)/shard_map/ppermute | solution.py:431
  74.4 42.9 %collective-permute-start.17 = (bf16[2,3,704,128]{3,2,1,0:T(8,128)(2,1)}, bf16[2,3,704,128]{3,2,1,0:T(8,128)(2,1)}, u32[]{:S(2)}, u32[]{:S(2)}) collective-permute-start(bf16[2,3,704,128]{3,2,1,0:T(8,128)(2,1)} %pad_maximum_fusion.refs_2_), channel_id=1, source_target_pairs={{0,16},{4,20},{8,24},{12,28},{16,0},{20,4},{24,8},{28,12},{1,17},{... | collective-permute-start | bytes 3244040 | tf_op jit(solution)/shard_map/ppermute | solution.py:417
  85.9 31.4 %collective-permute-start.14 = (bf16[3,704,128]{2,1,0:T(8,128)(2,1)S(1)}, bf16[3,704,128]{2,1,0:T(8,128)(2,1)}, u32[]{:S(2)}, u32[]{:S(2)}) collective-permute-start(bf16[3,704,128]{2,1,0:T(8,128)(2,1)S(1)} %pad_maximum_fusion.5), channel_id=1, source_target_pairs={{0,1},{1,2},{2,3},{3,0},{4,5},{5,6},{6,7},{7,4},{8,9},{9,10},{10,1... | collective-permute-start | bytes 1622024 | tf_op jit(solution)/shard_map/ppermute | solution.py:419
  86.0 31.4 %collective-permute-start.15 = (bf16[3,704,128]{2,1,0:T(8,128)(2,1)S(1)}, bf16[3,704,128]{2,1,0:T(8,128)(2,1)}, u32[]{:S(2)}, u32[]{:S(2)}) collective-permute-start(bf16[3,704,128]{2,1,0:T(8,128)(2,1)S(1)} %pad_maximum_fusion.5), channel_id=1, source_target_pairs={{0,3},{1,0},{2,1},{3,2},{4,7},{5,4},{6,5},{7,6},{8,11},{9,8},{10,9... | collective-permute-start | bytes 1622024 | tf_op jit(solution)/shard_map/ppermute | solution.py:419
  117.3 36.5 %collective-permute-start.23 = (bf16[3,704,128]{2,1,0:T(8,128)(2,1)}, bf16[3,704,128]{2,1,0:T(8,128)(2,1)}, u32[]{:S(2)}, u32[]{:S(2)}) collective-permute-start(bf16[3,704,128]{2,1,0:T(8,128)(2,1)} %collective-permute-done.14), channel_id=1, source_target_pairs={{0,16},{4,20},{8,24},{12,28},{16,0},{20,4},{24,8},{28,12},{1,17},{... | collective-permute-start | bytes 1622024 | tf_op jit(solution)/shard_map/ppermute | solution.py:417
  117.4 43.2 %collective-permute-start.22 = (bf16[3,704,128]{2,1,0:T(8,128)(2,1)}, bf16[3,704,128]{2,1,0:T(8,128)(2,1)S(1)}, u32[]{:S(2)}, u32[]{:S(2)}) collective-permute-start(bf16[3,704,128]{2,1,0:T(8,128)(2,1)} %collective-permute-done.14), channel_id=1, source_target_pairs={{0,1},{1,2},{2,3},{3,0},{4,5},{5,6},{6,7},{7,4},{8,9},{9,10},{10,1... | collective-permute-start | bytes 1622024 | tf_op jit(solution)/shard_map/ppermute | solution.py:419
  117.5 28.6 %collective-permute-start.24 = (bf16[3,704,128]{2,1,0:T(8,128)(2,1)}, bf16[3,704,128]{2,1,0:T(8,128)(2,1)}, u32[]{:S(2)}, u32[]{:S(2)}) collective-permute-start(bf16[3,704,128]{2,1,0:T(8,128)(2,1)} %collective-permute-done.15), channel_id=1, source_target_pairs={{0,8},{4,12},{8,0},{12,4},{16,24},{20,28},{24,16},{28,20},{1,9},{5... | collective-permute-start | bytes 1622024 | tf_op jit(solution)/shard_map/ppermute | solution.py:417
  119.3 41.3 %collective-permute-start.25 = (bf16[2,4,256,128]{3,2,1,0:T(8,128)(2,1)}, bf16[2,4,256,128]{3,2,1,0:T(8,128)(2,1)}, u32[]{:S(2)}, u32[]{:S(2)}) collective-permute-start(bf16[2,4,256,128]{3,2,1,0:T(8,128)(2,1)} %pad_maximum_fusion.6), channel_id=1, source_target_pairs={{0,16},{4,20},{8,24},{12,28},{16,0},{20,4},{24,8},{28,12},{1,17},{... | collective-permute-start | bytes 1572872 | tf_op jit(solution)/shard_map/ppermute | solution.py:417
  123.6 24.9 %collective-permute-start.26 = (bf16[512,128]{1,0:T(8,128)(2,1)}, bf16[512,128]{1,0:T(8,128)(2,1)}, u32[]{:S(2)}, u32[]{:S(2)}) collective-permute-start(bf16[512,128]{1,0:T(8,128)(2,1)} %get-tuple-element.264), channel_id=1, source_target_pairs={{0,0},{1,2},{2,4},{3,6},{4,1},{5,3},{6,5},{7,7},{8,8},{9,10},{10,1... | collective-permute-start | bytes 393224 | tf_op jit(solution)/shard_map/ppermute | solution.py:522
  162.9 30.5 %collective-permute-start.34 = (bf16[4,4,256,128]{3,2,1,0:T(8,128)(2,1)}, bf16[4,4,256,128]{3,2,1,0:T(8,128)(2,1)}, u32[]{:S(2)}, u32[]{:S(2)}) collective-permute-start(bf16[4,4,256,128]{3,2,1,0:T(8,128)(2,1)} %pad_maximum_fusion.4.refs_0_), channel_id=1, source_target_pairs={{0,4},{4,0},{8,12},{12,8},{16,20},{20,16},{24,28},{28,24},{1,5},{5... | collective-permute-start | bytes 3145736 | tf_op jit(solution)/shard_map/ppermute | solution.py:417
  163.2 30.6 %collective-permute-start.39 = (bf16[2,3,704,128]{3,2,1,0:T(8,128)(2,1)}, bf16[2,3,704,128]{3,2,1,0:T(8,128)(2,1)}, u32[]{:S(2)}, u32[]{:S(2)}) collective-permute-start(bf16[2,3,704,128]{3,2,1,0:T(8,128)(2,1)} %pad_maximum_fusion.1.refs_6_), channel_id=1, source_target_pairs={{0,8},{4,12},{8,0},{12,4},{16,24},{20,28},{24,16},{28,20},{1,9},{5... | collective-permute-start | bytes 3244040 | tf_op jit(solution)/shard_map/ppermute | solution.py:417
  165.8 54.0 %collective-permute-start.37 = (bf16[2,3,704,128]{3,2,1,0:T(8,128)(2,1)}, bf16[2,3,704,128]{3,2,1,0:T(8,128)(2,1)}, u32[]{:S(2)}, u32[]{:S(2)}) collective-permute-start(bf16[2,3,704,128]{3,2,1,0:T(8,128)(2,1)} %pad_maximum_fusion.refs_2_), channel_id=1, source_target_pairs={{0,4},{4,0},{8,12},{12,8},{16,20},{20,16},{24,28},{28,24},{1,5},{5... | collective-permute-start | bytes 3244040 | tf_op jit(solution)/shard_map/ppermute | solution.py:417
  167.8 24.5 %collective-permute-start.36 = (bf16[3,704,128]{2,1,0:T(8,128)(2,1)S(1)}, bf16[3,704,128]{2,1,0:T(8,128)(2,1)S(1)}, u32[]{:S(2)}, u32[]{:S(2)}) collective-permute-start(bf16[3,704,128]{2,1,0:T(8,128)(2,1)S(1)} %collective-permute-done.22), channel_id=1, source_target_pairs={{0,16},{4,20},{8,24},{12,28},{16,0},{20,4},{24,8},{28,12},{1,17},{... | collective-permute-start | bytes 1622024 | tf_op jit(solution)/shard_map/ppermute | solution.py:417
  191.9 30.0 %collective-permute-start.38 = (bf16[2,3,704,128]{3,2,1,0:T(8,128)(2,1)}, bf16[2,3,704,128]{3,2,1,0:T(8,128)(2,1)}, u32[]{:S(2)}, u32[]{:S(2)}) collective-permute-start(bf16[2,3,704,128]{3,2,1,0:T(8,128)(2,1)} %collective-permute-done.17.refs_3_), channel_id=1, source_target_pairs={{0,4},{4,0},{8,12},{12,8},{16,20},{20,16},{24,28},{28,24},{1,5},{5... | collective-permute-start | bytes 3244040 | tf_op jit(solution)/shard_map/ppermute | solution.py:417
  193.3 28.8 %collective-permute-start.40 = (bf16[2,3,704,128]{3,2,1,0:T(8,128)(2,1)}, bf16[2,3,704,128]{3,2,1,0:T(8,128)(2,1)}, u32[]{:S(2)}, u32[]{:S(2)}) collective-permute-start(bf16[2,3,704,128]{3,2,1,0:T(8,128)(2,1)} %pad_maximum_fusion.1.refs_6_), channel_id=1, source_target_pairs={{0,4},{4,0},{8,12},{12,8},{16,20},{20,16},{24,28},{28,24},{1,5},{5... | collective-permute-start | bytes 3244040 | tf_op jit(solution)/shard_map/ppermute | solution.py:417
  193.4 26.5 %collective-permute-start.35 = (bf16[2,3,704,128]{3,2,1,0:T(8,128)(2,1)}, bf16[2,3,704,128]{3,2,1,0:T(8,128)(2,1)}, u32[]{:S(2)}, u32[]{:S(2)}) collective-permute-start(bf16[2,3,704,128]{3,2,1,0:T(8,128)(2,1)} %pad_maximum_fusion.2.refs_2_), channel_id=1, source_target_pairs={{0,16},{4,20},{8,24},{12,28},{16,0},{20,4},{24,8},{28,12},{1,17},{... | collective-permute-start | bytes 3244040 | tf_op jit(solution)/shard_map/ppermute | solution.py:417
  193.8 28.6 %collective-permute-start.41 = (bf16[2,3,704,128]{3,2,1,0:T(8,128)(2,1)}, bf16[2,3,704,128]{3,2,1,0:T(8,128)(2,1)}, u32[]{:S(2)}, u32[]{:S(2)}) collective-permute-start(bf16[2,3,704,128]{3,2,1,0:T(8,128)(2,1)} %collective-permute-done.39.refs_7_), channel_id=1, source_target_pairs={{0,4},{4,0},{8,12},{12,8},{16,20},{20,16},{24,28},{28,24},{1,5},{5... | collective-permute-start | bytes 3244040 | tf_op jit(solution)/shard_map/ppermute | solution.py:417
  219.9 26.6 %collective-permute-start.43 = (bf16[2,3,704,128]{3,2,1,0:T(8,128)(2,1)}, bf16[2,3,704,128]{3,2,1,0:T(8,128)(2,1)}, u32[]{:S(2)}, u32[]{:S(2)}) collective-permute-start(bf16[2,3,704,128]{3,2,1,0:T(8,128)(2,1)} %pad_maximum_fusion.2.refs_2_), channel_id=1, source_target_pairs={{0,4},{4,0},{8,12},{12,8},{16,20},{20,16},{24,28},{28,24},{1,5},{5... | collective-permute-start | bytes 3244040 | tf_op jit(solution)/shard_map/ppermute | solution.py:417
  219.9 26.8 %collective-permute-start.42 = (bf16[2,3,704,128]{3,2,1,0:T(8,128)(2,1)}, bf16[2,3,704,128]{3,2,1,0:T(8,128)(2,1)}, u32[]{:S(2)}, u32[]{:S(2)}) collective-permute-start(bf16[2,3,704,128]{3,2,1,0:T(8,128)(2,1)} %pad_maximum_fusion.3.refs_6_), channel_id=1, source_target_pairs={{0,8},{4,12},{8,0},{12,4},{16,24},{20,28},{24,16},{28,20},{1,9},{5... | collective-permute-start | bytes 3244040 | tf_op jit(solution)/shard_map/ppermute | solution.py:417
  221.9 28.7 %collective-permute-start.45 = (bf16[2,3,704,128]{3,2,1,0:T(8,128)(2,1)}, bf16[2,3,704,128]{3,2,1,0:T(8,128)(2,1)}, u32[]{:S(2)}, u32[]{:S(2)}) collective-permute-start(bf16[2,3,704,128]{3,2,1,0:T(8,128)(2,1)} %pad_maximum_fusion.3.refs_6_), channel_id=1, source_target_pairs={{0,4},{4,0},{8,12},{12,8},{16,20},{20,16},{24,28},{28,24},{1,5},{5... | collective-permute-start | bytes 3244040 | tf_op jit(solution)/shard_map/ppermute | solution.py:417
  222.1 24.6 %collective-permute-start.44 = (bf16[2,3,704,128]{3,2,1,0:T(8,128)(2,1)}, bf16[2,3,704,128]{3,2,1,0:T(8,128)(2,1)}, u32[]{:S(2)}, u32[]{:S(2)}) collective-permute-start(bf16[2,3,704,128]{3,2,1,0:T(8,128)(2,1)} %collective-permute-done.35.refs_3_), channel_id=1, source_target_pairs={{0,4},{4,0},{8,12},{12,8},{16,20},{20,16},{24,28},{28,24},{1,5},{5... | collective-permute-start | bytes 3244040 | tf_op jit(solution)/shard_map/ppermute | solution.py:417
  249.6 25.0 %collective-permute-start.47 = (bf16[2,3,704,128]{3,2,1,0:T(8,128)(2,1)}, bf16[2,3,704,128]{3,2,1,0:T(8,128)(2,1)}, u32[]{:S(2)}, u32[]{:S(2)}) collective-permute-start(bf16[2,3,704,128]{3,2,1,0:T(8,128)(2,1)} %get-tuple-element.137), channel_id=1, source_target_pairs={{0,4},{4,0},{8,12},{12,8},{16,20},{20,16},{24,28},{28,24},{1,5},{5... | collective-permute-start | bytes 3244040 | tf_op jit(solution)/shard_map/ppermute | solution.py:417
  250.1 24.6 %collective-permute-start.48 = (bf16[2,3,704,128]{3,2,1,0:T(8,128)(2,1)}, bf16[2,3,704,128]{3,2,1,0:T(8,128)(2,1)}, u32[]{:S(2)}, u32[]{:S(2)}) collective-permute-start(bf16[2,3,704,128]{3,2,1,0:T(8,128)(2,1)} %get-tuple-element.138), channel_id=1, source_target_pairs={{0,4},{4,0},{8,12},{12,8},{16,20},{20,16},{24,28},{28,24},{1,5},{5... | collective-permute-start | bytes 3244040 | tf_op jit(solution)/shard_map/ppermute | solution.py:417
  250.1 24.5 %collective-permute-start.49 = (bf16[2,3,704,128]{3,2,1,0:T(8,128)(2,1)}, bf16[2,3,704,128]{3,2,1,0:T(8,128)(2,1)}, u32[]{:S(2)}, u32[]{:S(2)}) collective-permute-start(bf16[2,3,704,128]{3,2,1,0:T(8,128)(2,1)} %get-tuple-element.139), channel_id=1, source_target_pairs={{0,4},{4,0},{8,12},{12,8},{16,20},{20,16},{24,28},{28,24},{1,5},{5... | collective-permute-start | bytes 3244040 | tf_op jit(solution)/shard_map/ppermute | solution.py:417
  250.6 24.1 %collective-permute-start.50 = (bf16[2,3,704,128]{3,2,1,0:T(8,128)(2,1)}, bf16[2,3,704,128]{3,2,1,0:T(8,128)(2,1)}, u32[]{:S(2)}, u32[]{:S(2)}) collective-permute-start(bf16[2,3,704,128]{3,2,1,0:T(8,128)(2,1)} %get-tuple-element.140), channel_id=1, source_target_pairs={{0,4},{4,0},{8,12},{12,8},{16,20},{20,16},{24,28},{28,24},{1,5},{5... | collective-permute-start | bytes 3244040 | tf_op jit(solution)/shard_map/ppermute | solution.py:417
  292.7 23.1 %collective-permute-start.54 = (bf16[512,128]{1,0:T(8,128)(2,1)S(1)}, bf16[512,128]{1,0:T(8,128)(2,1)}, u32[]{:S(2)}, u32[]{:S(2)}) collective-permute-start(bf16[512,128]{1,0:T(8,128)(2,1)S(1)} %get-tuple-element.245), channel_id=1, source_target_pairs={{3,0},{1,1},{7,2},{5,3},{2,4},{0,5},{6,6},{4,7},{11,8},{9,9},{15,1... | collective-permute-start | bytes 393224 | tf_op jit(solution)/shard_map/ppermute | solution.py:530
  296.6 20.6 %collective-permute-start.57 = (bf16[512,128]{1,0:T(8,128)(2,1)S(1)}, bf16[512,128]{1,0:T(8,128)(2,1)S(1)}, u32[]{:S(2)}, u32[]{:S(2)}) collective-permute-start(bf16[512,128]{1,0:T(8,128)(2,1)S(1)} %get-tuple-element.241), channel_id=1, source_target_pairs={{0,0},{2,1},{4,2},{6,3},{1,4},{3,5},{5,6},{7,7},{8,8},{10,9},{12,1... | collective-permute-start | bytes 393224 | tf_op jit(solution)/shard_map/ppermute | solution.py:530
  299.9 18.0 %collective-permute-start.58 = (bf16[512,128]{1,0:T(8,128)(2,1)S(1)}, bf16[512,128]{1,0:T(8,128)(2,1)}, u32[]{:S(2)}, u32[]{:S(2)}) collective-permute-start(bf16[512,128]{1,0:T(8,128)(2,1)S(1)} %get-tuple-element.244), channel_id=1, source_target_pairs={{1,0},{3,1},{5,2},{7,3},{0,4},{2,5},{4,6},{6,7},{9,8},{11,9},{13,1... | collective-permute-start | bytes 393224 | tf_op jit(solution)/shard_map/ppermute | solution.py:530
  304.1 15.4 %collective-permute-start.59 = (bf16[512,128]{1,0:T(8,128)(2,1)S(1)}, bf16[512,128]{1,0:T(8,128)(2,1)}, u32[]{:S(2)}, u32[]{:S(2)}) collective-permute-start(bf16[512,128]{1,0:T(8,128)(2,1)S(1)} %get-tuple-element.243), channel_id=1, source_target_pairs={{2,0},{0,1},{6,2},{4,3},{3,4},{1,5},{7,6},{5,7},{10,8},{8,9},{14,1... | collective-permute-start | bytes 393224 | tf_op jit(solution)/shard_map/ppermute | solution.py:530
  304.6 15.3 %collective-permute-start.60 = (bf16[512,128]{1,0:T(8,128)(2,1)S(1)}, bf16[512,128]{1,0:T(8,128)(2,1)}, u32[]{:S(2)}, u32[]{:S(2)}) collective-permute-start(bf16[512,128]{1,0:T(8,128)(2,1)S(1)} %get-tuple-element.242), channel_id=1, source_target_pairs={{3,0},{1,1},{7,2},{5,3},{2,4},{0,5},{6,6},{4,7},{11,8},{9,9},{15,1... | collective-permute-start | bytes 393224 | tf_op jit(solution)/shard_map/ppermute | solution.py:530
  315.9 34.4 %collective-permute-start.66 = (bf16[2,3,704,128]{3,2,1,0:T(8,128)(2,1)}, bf16[2,3,704,128]{3,2,1,0:T(8,128)(2,1)}, u32[]{:S(2)}, u32[]{:S(2)}) collective-permute-start(bf16[2,3,704,128]{3,2,1,0:T(8,128)(2,1)} %get-tuple-element.163), channel_id=1, source_target_pairs={{0,4},{4,0},{8,12},{12,8},{16,20},{20,16},{24,28},{28,24},{1,5},{5... | collective-permute-start | bytes 3244040 | tf_op jit(solution)/shard_map/ppermute | solution.py:417
  317.3 36.5 %collective-permute-start.64 = (bf16[2,3,704,128]{3,2,1,0:T(8,128)(2,1)}, bf16[2,3,704,128]{3,2,1,0:T(8,128)(2,1)}, u32[]{:S(2)}, u32[]{:S(2)}) collective-permute-start(bf16[2,3,704,128]{3,2,1,0:T(8,128)(2,1)} %get-tuple-element.161), channel_id=1, source_target_pairs={{0,4},{4,0},{8,12},{12,8},{16,20},{20,16},{24,28},{28,24},{1,5},{5... | collective-permute-start | bytes 3244040 | tf_op jit(solution)/shard_map/ppermute | solution.py:417
  317.8 26.2 %collective-permute-start.56 = (bf16[2,3,704,128]{3,2,1,0:T(8,128)(2,1)}, bf16[2,3,704,128]{3,2,1,0:T(8,128)(2,1)}, u32[]{:S(2)}, u32[]{:S(2)}) collective-permute-start(bf16[2,3,704,128]{3,2,1,0:T(8,128)(2,1)} %add_convert_fusion.2), channel_id=1, source_target_pairs={{0,8},{4,12},{8,0},{12,4},{16,24},{20,28},{24,16},{28,20},{1,9},{5... | collective-permute-start | bytes 3244040 | tf_op jit(solution)/shard_map/ppermute | solution.py:417
  319.5 25.9 %collective-permute-start.55 = (bf16[2,3,704,128]{3,2,1,0:T(8,128)(2,1)}, bf16[2,3,704,128]{3,2,1,0:T(8,128)(2,1)}, u32[]{:S(2)}, u32[]{:S(2)}) collective-permute-start(bf16[2,3,704,128]{3,2,1,0:T(8,128)(2,1)} %add_convert_fusion.3), channel_id=1, source_target_pairs={{0,16},{4,20},{8,24},{12,28},{16,0},{20,4},{24,8},{28,12},{1,17},{... | collective-permute-start | bytes 3244040 | tf_op jit(solution)/shard_map/ppermute | solution.py:417
  319.8 75.3 %collective-permute-start.72 = (bf16[2,3,704,128]{3,2,1,0:T(8,128)(2,1)}, bf16[2,3,704,128]{3,2,1,0:T(8,128)(2,1)}, u32[]{:S(2)}, u32[]{:S(2)}) collective-permute-start(bf16[2,3,704,128]{3,2,1,0:T(8,128)(2,1)} %get-tuple-element.174), channel_id=1, source_target_pairs={{0,4},{4,0},{8,12},{12,8},{16,20},{20,16},{24,28},{28,24},{1,5},{5... | collective-permute-start | bytes 3244040 | tf_op jit(solution)/shard_map/ppermute | solution.py:417
  344.0 53.7 %collective-permute-start.70 = (bf16[2,3,704,128]{3,2,1,0:T(8,128)(2,1)}, bf16[2,3,704,128]{3,2,1,0:T(8,128)(2,1)}, u32[]{:S(2)}, u32[]{:S(2)}) collective-permute-start(bf16[2,3,704,128]{3,2,1,0:T(8,128)(2,1)} %get-tuple-element.171), channel_id=1, source_target_pairs={{0,4},{4,0},{8,12},{12,8},{16,20},{20,16},{24,28},{28,24},{1,5},{5... | collective-permute-start | bytes 3244040 | tf_op jit(solution)/shard_map/ppermute | solution.py:417
  350.3 15.2 %collective-permute-start.62 = (bf16[3,704,128]{2,1,0:T(8,128)(2,1)S(1)}, bf16[3,704,128]{2,1,0:T(8,128)(2,1)S(1)}, u32[]{:S(2)}, u32[]{:S(2)}) collective-permute-start(bf16[3,704,128]{2,1,0:T(8,128)(2,1)S(1)} %fusion.59), channel_id=1, source_target_pairs={{0,8},{4,12},{8,0},{12,4},{16,24},{20,28},{24,16},{28,20},{1,9},{5... | collective-permute-start | bytes 1622024 | tf_op jit(solution)/shard_map/ppermute | solution.py:417
  353.8 41.3 %collective-permute-start.67 = (bf16[2,3,704,128]{3,2,1,0:T(8,128)(2,1)}, bf16[2,3,704,128]{3,2,1,0:T(8,128)(2,1)}, u32[]{:S(2)}, u32[]{:S(2)}) collective-permute-start(bf16[2,3,704,128]{3,2,1,0:T(8,128)(2,1)} %add_convert_fusion), channel_id=1, source_target_pairs={{0,8},{4,12},{8,0},{12,4},{16,24},{20,28},{24,16},{28,20},{1,9},{5... | collective-permute-start | bytes 3244040 | tf_op jit(solution)/shard_map/ppermute | solution.py:417
  360.9 34.3 %collective-permute-start.65 = (bf16[2,3,704,128]{3,2,1,0:T(8,128)(2,1)}, bf16[2,3,704,128]{3,2,1,0:T(8,128)(2,1)}, u32[]{:S(2)}, u32[]{:S(2)}) collective-permute-start(bf16[2,3,704,128]{3,2,1,0:T(8,128)(2,1)} %add_convert_fusion.1), channel_id=1, source_target_pairs={{0,16},{4,20},{8,24},{12,28},{16,0},{20,4},{24,8},{28,12},{1,17},{... | collective-permute-start | bytes 3244040 | tf_op jit(solution)/shard_map/ppermute | solution.py:417
  365.5 29.6 %collective-permute-start.61 = (bf16[4,4,256,128]{3,2,1,0:T(8,128)(2,1)}, bf16[4,4,256,128]{3,2,1,0:T(8,128)(2,1)}, u32[]{:S(2)}, u32[]{:S(2)}) collective-permute-start(bf16[4,4,256,128]{3,2,1,0:T(8,128)(2,1)} %get-tuple-element.153), channel_id=1, source_target_pairs={{0,4},{4,0},{8,12},{12,8},{16,20},{20,16},{24,28},{28,24},{1,5},{5... | collective-permute-start | bytes 3145736 | tf_op jit(solution)/shard_map/ppermute | solution.py:417
  397.6 39.6 %collective-permute-start.73 = (bf16[3,704,128]{2,1,0:T(8,128)(2,1)S(1)}, bf16[3,704,128]{2,1,0:T(8,128)(2,1)}, u32[]{:S(2)}, u32[]{:S(2)}) collective-permute-start(bf16[3,704,128]{2,1,0:T(8,128)(2,1)S(1)} %fusion.62), channel_id=1, source_target_pairs={{0,16},{4,20},{8,24},{12,28},{16,0},{20,4},{24,8},{28,12},{1,17},{... | collective-permute-start | bytes 1622024 | tf_op jit(solution)/shard_map/ppermute | solution.py:417
  401.2 36.0 %collective-permute-start.71 = (bf16[3,704,128]{2,1,0:T(8,128)(2,1)}, bf16[3,704,128]{2,1,0:T(8,128)(2,1)}, u32[]{:S(2)}, u32[]{:S(2)}) collective-permute-start(bf16[3,704,128]{2,1,0:T(8,128)(2,1)} %fusion.61), channel_id=1, source_target_pairs={{0,8},{4,12},{8,0},{12,4},{16,24},{20,28},{24,16},{28,20},{1,9},{5... | collective-permute-start | bytes 1622024 | tf_op jit(solution)/shard_map/ppermute | solution.py:417
  403.9 33.3 %collective-permute-start.69 = (bf16[2,4,256,128]{3,2,1,0:T(8,128)(2,1)}, bf16[2,4,256,128]{3,2,1,0:T(8,128)(2,1)}, u32[]{:S(2)}, u32[]{:S(2)}) collective-permute-start(bf16[2,4,256,128]{3,2,1,0:T(8,128)(2,1)} %slice.317), channel_id=1, source_target_pairs={{0,16},{4,20},{8,24},{12,28},{16,0},{20,4},{24,8},{28,12},{1,17},{... | collective-permute-start | bytes 1572872 | tf_op jit(solution)/shard_map/ppermute | solution.py:417
  406.2 30.9 %collective-permute-start.68 = (bf16[3,704,128]{2,1,0:T(8,128)(2,1)}, bf16[3,704,128]{2,1,0:T(8,128)(2,1)}, u32[]{:S(2)}, u32[]{:S(2)}) collective-permute-start(bf16[3,704,128]{2,1,0:T(8,128)(2,1)} %fusion.40), channel_id=1, source_target_pairs={{0,3},{1,0},{2,1},{3,2},{4,7},{5,4},{6,5},{7,6},{8,11},{9,8},{10,9... | collective-permute-start | bytes 1622024 | tf_op jit(solution)/shard_map/ppermute | solution.py:419
  441.4 35.6 %collective-permute-start.78 = (bf16[512,1024]{1,0:T(8,128)(2,1)}, bf16[512,1024]{1,0:T(8,128)(2,1)}, u32[]{:S(2)}, u32[]{:S(2)}) collective-permute-start(bf16[512,1024]{1,0:T(8,128)(2,1)} %get-tuple-element.281), channel_id=1, source_target_pairs={{0,4},{4,0},{8,12},{12,8},{16,20},{20,16},{24,28},{28,24},{1,5},{5... | collective-permute-start | bytes 3145736 | tf_op jit(solution)/shard_map/ppermute | solution.py:417
  443.1 15.4 %collective-permute-start.85 = (bf16[4,256,128]{2,1,0:T(8,128)(2,1)S(1)}, bf16[4,256,128]{2,1,0:T(8,128)(2,1)S(1)}, u32[]{:S(2)}, u32[]{:S(2)}) collective-permute-start(bf16[4,256,128]{2,1,0:T(8,128)(2,1)S(1)} %fusion.71), channel_id=1, source_target_pairs={{0,8},{4,12},{8,0},{12,4},{16,24},{20,28},{24,16},{28,20},{1,9},{5... | collective-permute-start | bytes 786440 | tf_op jit(solution)/shard_map/ppermute | solution.py:417
  451.9 31.4 %collective-permute-start.76 = (bf16[512,1024]{1,0:T(8,128)(2,1)}, bf16[512,1024]{1,0:T(8,128)(2,1)}, u32[]{:S(2)}, u32[]{:S(2)}) collective-permute-start(bf16[512,1024]{1,0:T(8,128)(2,1)} %get-tuple-element.233), channel_id=1, source_target_pairs={{0,1},{1,0},{7,6},{6,7},{8,9},{9,8},{15,14},{14,15},{16,17},{17,16... | collective-permute-start | bytes 3145736 | tf_op jit(solution)/shard_map/ppermute | solution.py:431
  458.5 54.7 %collective-permute-start.77 = (bf16[512,1024]{1,0:T(8,128)(2,1)}, bf16[512,1024]{1,0:T(8,128)(2,1)}, u32[]{:S(2)}, u32[]{:S(2)}) collective-permute-start(bf16[512,1024]{1,0:T(8,128)(2,1)} %get-tuple-element.283), channel_id=1, source_target_pairs={{0,4},{4,0},{8,12},{12,8},{16,20},{20,16},{24,28},{28,24},{1,5},{5... | collective-permute-start | bytes 3145736 | tf_op jit(solution)/shard_map/ppermute | solution.py:417
  458.7 18.3 %collective-permute-start.86 = (bf16[256,128]{1,0:T(8,128)(2,1)S(1)}, bf16[256,128]{1,0:T(8,128)(2,1)S(1)}, u32[]{:S(2)}, u32[]{:S(2)}) collective-permute-start(bf16[256,128]{1,0:T(8,128)(2,1)S(1)} %get-tuple-element.269), channel_id=1, source_target_pairs={{0,1},{1,2},{2,3},{3,0},{4,5},{5,6},{6,7},{7,4},{8,9},{9,10},{10,1... | collective-permute-start | bytes 196616 | tf_op jit(solution)/shard_map/ppermute | solution.py:419
  460.8 25.7 %collective-permute-start.89 = (bf16[3,704,128]{2,1,0:T(8,128)(2,1)}, bf16[3,704,128]{2,1,0:T(8,128)(2,1)S(1)}, u32[]{:S(2)}, u32[]{:S(2)}) collective-permute-start(bf16[3,704,128]{2,1,0:T(8,128)(2,1)} %fusion.32), channel_id=1, source_target_pairs={{0,1},{1,2},{2,3},{3,0},{4,5},{5,6},{6,7},{7,4},{8,9},{9,10},{10,1... | collective-permute-start | bytes 1622024 | tf_op jit(solution)/shard_map/ppermute | solution.py:419
  486.5 26.8 %collective-permute-start.79 = (bf16[512,1024]{1,0:T(8,128)(2,1)S(1)}, bf16[512,1024]{1,0:T(8,128)(2,1)S(1)}, u32[]{:S(2)}, u32[]{:S(2)}) collective-permute-start(bf16[512,1024]{1,0:T(8,128)(2,1)S(1)} %get-tuple-element.231), channel_id=1, source_target_pairs={{1,2},{0,1},{6,5},{7,6},{9,10},{8,9},{14,13},{15,14},{17,18},{16,1... | collective-permute-start | bytes 3145736 | tf_op jit(solution)/shard_map/ppermute | solution.py:431
  489.4 34.0 %collective-permute-start.74 = (bf16[512,1024]{1,0:T(8,128)(2,1)S(1)}, bf16[512,1024]{1,0:T(8,128)(2,1)S(1)}, u32[]{:S(2)}, u32[]{:S(2)}) collective-permute-start(bf16[512,1024]{1,0:T(8,128)(2,1)S(1)} %copy-done.51), channel_id=1, source_target_pairs={{0,4},{4,0},{8,12},{12,8},{16,20},{20,16},{24,28},{28,24},{1,5},{5... | collective-permute-start | bytes 3145736 | tf_op jit(solution)/shard_map/ppermute | solution.py:417
  490.1 21.8 %collective-permute-start.90 = (bf16[3,704,128]{2,1,0:T(8,128)(2,1)S(1)}, bf16[3,704,128]{2,1,0:T(8,128)(2,1)S(1)}, u32[]{:S(2)}, u32[]{:S(2)}) collective-permute-start(bf16[3,704,128]{2,1,0:T(8,128)(2,1)S(1)} %fusion.35), channel_id=1, source_target_pairs={{0,1},{1,2},{2,3},{3,0},{4,5},{5,6},{6,7},{7,4},{8,9},{9,10},{10,1... | collective-permute-start | bytes 1622024 | tf_op jit(solution)/shard_map/ppermute | solution.py:419
  491.5 31.7 %collective-permute-start.82 = (bf16[2,1,768,128]{3,2,1,0:T(8,128)(2,1)S(1)}, bf16[2,1,768,128]{3,2,1,0:T(8,128)(2,1)S(1)}, u32[]{:S(2)}, u32[]{:S(2)}) collective-permute-start(bf16[2,1,768,128]{3,2,1,0:T(8,128)(2,1)S(1)} %slice.318), channel_id=1, source_target_pairs={{0,8},{4,12},{8,0},{12,4},{16,24},{20,28},{24,16},{28,20},{1,9},{5... | collective-permute-start | bytes 1179656 | tf_op jit(solution)/shard_map/ppermute | solution.py:417
  515.4 19.1 %collective-permute-start.80 = (bf16[512,1024]{1,0:T(8,128)(2,1)S(1)}, bf16[512,1024]{1,0:T(8,128)(2,1)S(1)}, u32[]{:S(2)}, u32[]{:S(2)}) collective-permute-start(bf16[512,1024]{1,0:T(8,128)(2,1)S(1)} %get-tuple-element.235), channel_id=1, source_target_pairs={{2,3},{1,2},{0,1},{5,4},{6,5},{7,6},{10,11},{9,10},{8,9},{13,12},{... | collective-permute-start | bytes 3145736 | tf_op jit(solution)/shard_map/ppermute | solution.py:431
  523.3 17.2 %collective-permute-start.83 = (bf16[768,128]{1,0:T(8,128)(2,1)S(1)}, bf16[768,128]{1,0:T(8,128)(2,1)S(1)}, u32[]{:S(2)}, u32[]{:S(2)}) collective-permute-start(bf16[768,128]{1,0:T(8,128)(2,1)S(1)} %fusion.73), channel_id=1, source_target_pairs={{0,4},{4,0},{8,12},{12,8},{16,20},{20,16},{24,28},{28,24},{1,5},{5... | collective-permute-start | bytes 589832 | tf_op jit(solution)/shard_map/ppermute | solution.py:417
  (134 other events, 1197.9 us)
